TPU v7x, 32 devices: a whole 2x2x4 slice. The times are simulated.
32 devices in a mesh: blk: 4 (over y, x), dp: 8 (over z, core).
Axes of the slice: x: 2, y: 2, z: 4, core: 2. Of those that a mesh axis runs over, the one named last changes fastest.
Arguments:
- patches: bfloat16 [4096, 64, 256], P(('blk', 'dp')), may hold values from -6 to 6
- w_mix: bfloat16 [256, 128], replicated, may hold values from -0.375 to 0.375
- w_in: bfloat16 [2048, 512], replicated, may hold values from -0.125 to 0.125
- w_out: bfloat16 [512, 128], replicated, may hold values from -0.25 to 0.25
- partner_dev: int32 [4096], P(('blk', 'dp')), may hold values from 0 to 7, as said below
- partner_row: int32 [4096], P(('blk', 'dp')), may hold values from 0 to 127, as said below
Outputs:
- loss_rows: float32 [4096], P(('blk', 'dp'))
- grad_mix: float32 [256, 128], replicated
- grad_in: float32 [2048, 512], replicated
- grad_out: float32 [512, 128], replicated
Inputs may be any that keep to these rules, and one draw needn't show every extreme that they name: Among one device's rows every dp index appears as partner_dev exactly 128/8 times. Over the rows that share a blk index, the pairs (partner_dev, partner_row) name every pair of dp index and row of a device exactly once.
All inputs are finite; a program needn't handle non-finite values.
Results may differ from a plain program's by a relative error of at most 0.012.
The roundings to bfloat16 on the way count: a program that leaves them out, or rounds other values in their place, can miss the bound.
Values may be sent and summed in bfloat16 or wider, within the bound.
No kernel may reach another device: no remote copies, remote signals or barrier semaphores. Data moves between devices by JAX's collectives and lax.ppermute only.
A program may use at most 64 MiB of HBM per device.

v0:
```python
import functools
import math

import jax
import jax.numpy as jnp
import numpy as np
from jax import lax
from jax.experimental import pallas as pl
from jax.experimental.pallas import tpu as pltpu
from jax.sharding import PartitionSpec as P


SCALE = 10.0
SUB = 8
BF16 = jnp.bfloat16
F32 = jnp.float32
VMEM = pl.BlockSpec(memory_space=pltpu.VMEM)
ANY = pl.BlockSpec(memory_space=pl.ANY)


def shape(dims, dtype):
    return jax.ShapeDtypeStruct(tuple(dims), dtype)


def hbm(value):
    return pltpu.with_memory_space_constraint(value, pltpu.MemorySpace.HBM)


def mm(left, right):
    return jnp.dot(left, right, preferred_element_type=F32)


def mm_nt(left, right):
    return lax.dot_general(left, right, (((1,), (1,)), ((), ())), preferred_element_type=F32)


def mm_tn(left, right):
    return lax.dot_general(left, right, (((0,), (0,)), ((), ())), preferred_element_type=F32)


def params(mib):
    return pltpu.CompilerParams(vmem_limit_bytes=mib << 20)


def cost(flops, nbytes):
    return pl.CostEstimate(flops=int(flops), bytes_accessed=int(nbytes), transcendentals=0)


def angle_basis(length, freqs):
    phase = np.mod(np.outer(np.arange(freqs), np.arange(length)), length).astype(np.float32)
    phase = phase * np.float32(2.0 * math.pi / length)
    table = np.concatenate([np.cos(phase), -np.sin(phase)], axis=0).astype(np.float32)
    basis = np.einsum("ka,pq->kpqa", table, np.eye(SUB, dtype=np.float32))
    return jnp.asarray(basis.reshape(2 * freqs * SUB, SUB * length), BF16)


def encode_kernel(
    freqs,
    size,
    rounds,
    patch_hbm,
    basis_hbm,
    mix_hbm,
    out_hbm,
    in_hbm,
    spec_hbm,
    mixed_hbm,
    normed_hbm,
    *rest,
):
    piece_hbms, rest = rest[:size], rest[size:]
    units_ref, unit32_ref, norm_ref, rscale_ref, *rest = rest
    patches, basis, mix, out_w, in_w, spec, mixed, feat, normed, slope, hidden, *sems = rest
    table_sems, patch_sems, spec_sems, mixed_sems, out_sems = sems
    count, length, lanes = patches.shape
    filters = mix.shape[1]
    half = freqs * SUB
    per = count // rounds
    groups = per // SUB

    def table(i, source, target):
        return pltpu.make_async_copy(source, target, table_sems.at[i])

    tables = [
        table(i, *pair)
        for i, pair in enumerate(
            [(basis_hbm, basis), (mix_hbm, mix), (in_hbm, in_w), (out_hbm, out_w)]
        )
    ]

    def fetch(r):
        rows = pl.ds(r * per, per)
        return pltpu.make_async_copy(patch_hbm.at[rows], patches.at[rows], patch_sems.at[r])

    def keep(r):
        rows = pl.ds(r * groups, groups)
        return (
            pltpu.make_async_copy(spec.at[rows], spec_hbm.at[rows], spec_sems.at[r]),
            pltpu.make_async_copy(mixed.at[rows], mixed_hbm.at[rows], mixed_sems.at[r]),
        )

    tables[0].start()
    fetch(0).start()
    tables[1].start()
    for r in range(1, rounds):
        fetch(r).start()
    tables[2].start()
    tables[3].start()
    tables[0].wait()
    tables[1].wait()

    def one(r, carry):
        fetch(r).wait()
        for s in range(groups):
            g = r * groups + s
            base = pl.multiple_of(g * SUB, SUB)
            block = patches[pl.ds(base, SUB)].reshape(SUB * length, lanes)
            part = mm(basis[...], block).astype(BF16)
            spec[g] = part
            both = mm(part, mix[...])
            mixed[g] = both
            real_part, imag_part = both[:half], both[half:]
            piece = jnp.log1p(real_part * real_part + imag_part * imag_part)
            for k in range(freqs):
                feat[pl.ds(base, SUB), k * filters : (k + 1) * filters] = piece[
                    k * SUB : (k + 1) * SUB
                ]
        for each in keep(r):
            each.start()
        return carry

    lax.fori_loop(0, rounds, one, 0)
    features = feat[...]
    removed = features - jnp.mean(features, axis=1, keepdims=True)
    rscale = lax.rsqrt(jnp.mean(removed * removed, axis=1, keepdims=True) + 1e-05)
    normed[...] = (removed * rscale).astype(BF16)
    rscale_ref[...] = jnp.broadcast_to(rscale, rscale_ref.shape)
    deep, width, wide = piece_columns(normed.shape[1], hidden.shape[1], size)
    me = lax.axis_index("blk")
    outs = [pltpu.make_async_copy(normed, normed_hbm, out_sems.at[0])]
    for i, piece_hbm in enumerate(piece_hbms):
        columns = pl.ds(pl.multiple_of((me ^ i) * deep, 128), deep)
        outs.append(
            pltpu.make_async_copy(
                normed.at[:, columns], piece_hbm.at[:, :deep], out_sems.at[len(outs)]
            )
        )
    for each in outs:
        each.start()
    tables[2].wait()
    preact = mm(normed[...], in_w[...])
    sigm = jax.nn.sigmoid(preact)
    hidden[...] = (preact * sigm).astype(BF16)
    slope[...] = (sigm * (1.0 + preact * (1.0 - sigm))).astype(BF16)
    late = []
    for i, piece_hbm in enumerate(piece_hbms):
        if wide == hidden.shape[1]:
            columns = pl.ds(0, wide)
        else:
            columns = pl.ds(pl.multiple_of((me ^ i) * wide, 128), wide)
        for source, target in (
            (slope, piece_hbm.at[:, deep : deep + width]),
            (hidden.at[:, columns], piece_hbm.at[:, deep + width :]),
        ):
            late.append(
                pltpu.make_async_copy(source, target, out_sems.at[len(outs) + len(late)])
            )
    for each in late:
        each.start()
    tables[3].wait()
    raw = mm(hidden[...], out_w[...])
    norms = jnp.sqrt(jnp.sum(raw * raw, axis=1, keepdims=True) + 1e-06)
    norm_ref[...] = jnp.broadcast_to(norms, norm_ref.shape)
    unit32 = raw / norms
    unit32_ref[...] = unit32
    units_ref[...] = unit32.astype(BF16)
    for r in range(rounds):
        for each in keep(r):
            each.wait()
    for each in outs + late:
        each.wait()


def piece_columns(feats, width, size):
    wide = width // size
    return feats // size, width, wide if wide % 128 == 0 else width


def encode(patches, w_mix, w_in, w_out, size):
    count, length, lanes = patches.shape
    filters = w_mix.shape[1]
    feats, width = w_in.shape
    embed = w_out.shape[1]
    freqs = feats // filters
    rounds = 4
    assert count % (rounds * SUB) == 0
    groups = count // SUB
    rows = 2 * freqs * SUB
    piece = (count, sum(piece_columns(feats, width, size)))
    HBM = pltpu.MemorySpace.HBM
    kept = [
        HBM((groups, rows, lanes), BF16),
        HBM((groups, rows, filters), F32),
        HBM((count, feats), BF16),
    ] + [HBM(piece, BF16)] * size
    near = [shape((count, embed), BF16), shape((count, embed), F32)] + [shape((count, 128), F32)] * 2
    return pl.pallas_call(
        functools.partial(encode_kernel, freqs, size, rounds),
        in_specs=[ANY] * 5,
        out_shape=kept + near,
        out_specs=[ANY] * len(kept) + [VMEM] * len(near),
        scratch_shapes=[
            pltpu.VMEM(patches.shape, BF16),
            pltpu.VMEM((rows, SUB * length), BF16),
            pltpu.VMEM(w_mix.shape, BF16),
            pltpu.VMEM(w_out.shape, BF16),
            pltpu.VMEM(w_in.shape, BF16),
            pltpu.VMEM((groups, rows, lanes), BF16),
            pltpu.VMEM((groups, rows, filters), F32),
            pltpu.VMEM((count, feats), F32),
            pltpu.VMEM((count, feats), BF16),
            pltpu.VMEM((count, width), BF16),
            pltpu.VMEM((count, width), BF16),
            pltpu.SemaphoreType.DMA((4,)),
            pltpu.SemaphoreType.DMA((rounds,)),
            pltpu.SemaphoreType.DMA((rounds,)),
            pltpu.SemaphoreType.DMA((rounds,)),
            pltpu.SemaphoreType.DMA((1 + 3 * size,)),
        ],
        compiler_params=params(24),
        cost_estimate=cost(3e9, 14e6),
    )(*map(hbm, (patches, angle_basis(length, freqs), w_mix, w_out, w_in)))


def exponentials(units, keys, own):
    expo = jnp.exp(SCALE * mm_nt(units, keys))
    if own:
        row = lax.broadcasted_iota(jnp.int32, expo.shape, 0)
        col = lax.broadcasted_iota(jnp.int32, expo.shape, 1)
        expo = jnp.where(row == col, 0.0, expo)
    return expo


def negative_kernel(size, *refs):
    pieces, stacked, (zneg_ref, numer_ref, even_ref) = refs[:size], refs[size:-3], refs[-3:]
    units = pieces[0][...]
    count = units.shape[0]
    even_ref[:count, :] = units
    for i, each in enumerate(stacked):
        even_ref[(i + 1) * count : (i + 2) * count, :] = each[...]
    zneg = numer = None
    for i, piece in enumerate(pieces):
        keys = piece[...]
        expo = exponentials(units, keys, i == 0)
        total = jnp.sum(expo, axis=1, keepdims=True)
        term = mm(expo.astype(BF16), keys)
        zneg = total if zneg is None else zneg + total
        numer = term if numer is None else numer + term
    zneg_ref[...] = jnp.broadcast_to(zneg, zneg_ref.shape)
    numer_ref[...] = numer


def negatives(pieces, stacked):
    count, embed = pieces[0].shape
    size = len(pieces)
    return pl.pallas_call(
        functools.partial(negative_kernel, size),
        in_specs=[VMEM] * (size + len(stacked)),
        out_shape=[
            shape((count, 128), F32),
            shape((count, embed), F32),
            shape(((len(stacked) + 1) * count, embed), BF16),
        ],
        out_specs=[VMEM] * 3,
        compiler_params=params(8),
        cost_estimate=cost(4e8, 1e6),
    )(*pieces, *stacked)


def as_rows(column, count):
    return jnp.broadcast_to(column, (column.shape[0], count)).T


def positive_kernel(
    dev_ref, row_ref, even_ref, odd_ref, zneg_ref, numer_ref, local_ref, stats_ref, loss_ref
):
    count = dev_ref.shape[1]
    me = lax.axis_index("dp")
    step = dev_ref[...] ^ me
    place = ((step & 1) * even_ref.shape[0] + (step >> 1) * count + row_ref[...]).astype(F32)
    place = jnp.broadcast_to(place, (count, count)).T
    lane = lax.broadcasted_iota(jnp.int32, (count, count), 1).astype(F32)
    positive = None
    blocks = even_ref.shape[0] // count
    for i in range(2 * blocks):
        source = even_ref if i < blocks else odd_ref
        at = (i % blocks) * count
        hit = jnp.where(place - float(i * count) == lane, 1.0, 0.0).astype(BF16)
        term = mm(hit, source[at : at + count, :])
        positive = term if positive is None else positive + term
    units = even_ref[:count, :].astype(F32)
    spos = SCALE * jnp.sum(units * positive, axis=1, keepdims=True)
    top = jnp.exp(spos)
    totals = top + zneg_ref[:, :1]
    less = top / totals - 1.0
    coef = SCALE / count
    local_ref[...] = coef * (less * positive + numer_ref[...] / totals)
    loss_ref[...] = as_rows(jnp.log(totals) - spos, count)[:1]
    stats_ref[...] = jnp.zeros(stats_ref.shape, F32)
    stats_ref[0:1, :] = as_rows(totals, count)[:1]
    stats_ref[1:2, :] = as_rows(coef * less, count)[:1]
    stats_ref[2:3, :] = (dev_ref[...] * count + row_ref[...]).astype(F32)


def positives(partner_dev, partner_row, even, odd, zneg, numer):
    count, embed = numer.shape
    return pl.pallas_call(
        positive_kernel,
        in_specs=[VMEM] * 6,
        out_shape=[shape((count, embed), F32), shape((SUB, count), F32), shape((1, count), F32)],
        out_specs=[VMEM] * 3,
        compiler_params=params(8),
        cost_estimate=cost(4e8, 1e6),
    )(partner_dev.reshape(1, count), partner_row.reshape(1, count), even, odd, zneg, numer)


def upper_kernel(size, *refs):
    pieces, rest = refs[:size], refs[size:]
    stats, rest = rest[:size], rest[size:]
    (even_ref, odd_ref, even_stats, odd_stats, local_ref, unit32_ref, norm_ref, out_ref) = rest
    count, _ = local_ref.shape
    coef = SCALE / count
    units = pieces[0][...]
    keyterm = None
    for i in range(size):
        keys = pieces[i][...]
        expo = exponentials(units, keys, i == 0)
        weights = (expo / stats[i][0:1, :]).astype(BF16)
        term = mm(weights, keys)
        keyterm = term if keyterm is None else keyterm + term
    mine = lax.axis_index("dp") * count + lax.broadcasted_iota(jnp.int32, (count, count), 0)
    mine = mine.astype(F32)
    blocks = even_ref.shape[0] // count
    chosen = amount = None
    for i in range(2 * blocks):
        source, table = (even_ref, even_stats) if i < blocks else (odd_ref, odd_stats)
        j = i % blocks
        hit = table[j * SUB + 2 : j * SUB + 3, :] == mine
        share = jnp.where(hit, table[j * SUB + 1 : j * SUB + 2, :], 0.0)
        term = mm(jnp.where(hit, 1.0, 0.0).astype(BF16), source[j * count : (j + 1) * count, :])
        chosen = term if chosen is None else chosen + term
        amount = share if amount is None else amount + share
    back = jnp.sum(amount, axis=1, keepdims=True) * chosen
    grad_units = local_ref[...] + coef * keyterm + back
    unit32 = unit32_ref[...]
    along = jnp.sum(unit32 * grad_units, axis=1, keepdims=True)
    out_ref[...] = ((grad_units - unit32 * along) / norm_ref[:, :1]).astype(BF16)


def upper(pieces, stats, even, odd, even_stats, odd_stats, local, unit32, norms):
    count, embed = local.shape
    size = len(pieces)
    args = [*pieces, *stats, even, odd, even_stats, odd_stats, local, unit32, norms]
    return pl.pallas_call(
        functools.partial(upper_kernel, size),
        in_specs=[VMEM] * len(args),
        out_shape=shape((count, embed), BF16),
        out_specs=VMEM,
        compiler_params=params(8),
        cost_estimate=cost(4e8, 2e6),
    )(*args)


def pre_grads(grad_raw, out_w, slope):
    return (mm_nt(grad_raw, out_w) * slope.astype(F32)).astype(BF16)


def lower_kernel(
    freqs,
    columns,
    raw_ref,
    out_w_hbm,
    piece_hbm,
    normed_hbm,
    rscale_ref,
    in_hbm,
    mixed_hbm,
    spec_hbm,
    g_mix_ref,
    out_w,
    slope,
    in_w,
    normed,
    mixed,
    spec,
    grad_feat,
    sems,
):
    deep, width, _ = columns
    sources = [
        out_w_hbm,
        piece_hbm.at[:, deep : deep + width],
        in_hbm,
        normed_hbm,
        mixed_hbm,
        spec_hbm,
    ]
    targets = [out_w, slope, in_w, normed, mixed, spec]
    loads = [
        pltpu.make_async_copy(source, target, sems.at[i])
        for i, (source, target) in enumerate(zip(sources, targets))
    ]
    for each in loads:
        each.start()
    loads[0].wait()
    loads[1].wait()
    grad_pre = pre_grads(raw_ref[...], out_w[...], slope[...])
    loads[2].wait()
    grad_norm = mm_nt(grad_pre, in_w[...])
    loads[3].wait()
    xhat = normed[...].astype(F32)
    mean = jnp.mean(grad_norm, axis=1, keepdims=True)
    tilt = jnp.mean(grad_norm * xhat, axis=1, keepdims=True)
    grad_feat[...] = rscale_ref[:, :1] * (grad_norm - mean - xhat * tilt)
    loads[4].wait()
    loads[5].wait()
    groups, _, filters = mixed.shape
    half = freqs * SUB

    def one(g, total):
        real_part, imag_part = mixed[g, :half], mixed[g, half:]
        powers = real_part * real_part + imag_part * imag_part
        base = pl.multiple_of(g * SUB, SUB)
        grads = jnp.concatenate(
            [grad_feat[pl.ds(base, SUB), k * filters : (k + 1) * filters] for k in range(freqs)],
            axis=0,
        )
        share = 2.0 * grads / (1.0 + powers)
        grad_mixed = jnp.concatenate([real_part * share, imag_part * share], axis=0).astype(BF16)
        return total + mm_tn(grad_mixed, spec[g])

    total = lax.fori_loop(0, groups, one, jnp.zeros((filters, spec.shape[2]), F32), unroll=4)
    g_mix_ref[...] = total.T


def lower(grad_raw, w_out, piece, normed, rscale, w_in, mixed, spec, freqs, columns):
    count, feats = normed.shape
    _, _, filters = mixed.shape
    lanes = spec.shape[2]
    return pl.pallas_call(
        functools.partial(lower_kernel, freqs, columns),
        in_specs=[VMEM] + [ANY] * 3 + [VMEM] + [ANY] * 3,
        out_shape=shape((lanes, filters), F32),
        out_specs=VMEM,
        scratch_shapes=[
            pltpu.VMEM(w_out.shape, BF16),
            pltpu.VMEM((count, columns[1]), BF16),
            pltpu.VMEM(w_in.shape, BF16),
            pltpu.VMEM((count, feats), BF16),
            pltpu.VMEM(mixed.shape, F32),
            pltpu.VMEM(spec.shape, BF16),
            pltpu.VMEM((count, feats), F32),
            pltpu.SemaphoreType.DMA((6,)),
        ],
        compiler_params=params(20),
        cost_estimate=cost(1e9, 7e6),
    )(grad_raw, *map(hbm, (w_out, piece, normed)), rscale, *map(hbm, (w_in, mixed, spec)))


def up_to(rows, unit):
    return -(-rows // unit) * unit


class Layout:
    def __init__(self, lanes, filters, feats, width, embed, size, peers):
        self.size, self.peers = size, peers
        self.in_rows = feats // size // peers
        self.out_rows = width // size // peers
        self.mix_rows = lanes // peers
        self.top = up_to(self.in_rows, 16)
        self.strip = max(16, up_to(self.out_rows, 16))
        self.mix_blocks = -(-self.mix_rows // self.strip)
        self.rows = self.top + self.strip
        self.width = width
        assert embed == 128 and filters == 128 and (1 + self.mix_blocks) * 128 <= width

    def mix_parts(self):
        for block in range(self.mix_blocks):
            start = block * self.strip
            yield start, min(self.strip, self.mix_rows - start), slice(128 * (block + 1), 128 * (block + 2))


def weights_kernel(lay, columns, *refs):
    size, peers = lay.size, lay.peers
    pieces, raws, rest = refs[:size], refs[size : 2 * size], refs[2 * size :]
    out_w_ref, mix_ref, keep_ref, away_ref, g_in, g_out = rest
    deep, width, wide = columns
    share = width // size
    for i in range(size):
        raw = raws[i][...]
        grad_pre = pre_grads(raw, out_w_ref[...], pieces[i][:, deep : deep + width])
        term_in = mm_tn(pieces[i][:, :deep], grad_pre)
        term_out = mm_tn(pieces[i][:, deep + width :], raw)
        if i == 0:
            g_in[...] = term_in
            g_out[...] = term_out
        else:
            g_in[...] += term_in
            g_out[...] += term_out
    me = lax.axis_index("dp")
    first = 0 if wide == share else lax.axis_index("blk") * share
    keep_ref[...] = jnp.zeros(keep_ref.shape, F32)
    away_ref[...] = jnp.zeros(away_ref.shape, BF16)
    for slot in range(peers):
        owner = me ^ slot
        target = away_ref if slot & 1 else keep_ref
        at = slot >> 1
        target[at, : lay.in_rows, :] = g_in[pl.ds(owner * lay.in_rows, lay.in_rows), :].astype(target.dtype)
        target[at, lay.top : lay.top + lay.out_rows, :128] = g_out[
            pl.ds(first + owner * lay.out_rows, lay.out_rows), :
        ].astype(target.dtype)
        for start, rows, cols in lay.mix_parts():
            target[at, lay.top : lay.top + rows, cols] = mix_ref[
                pl.ds(owner * lay.mix_rows + start, rows), :
            ].astype(target.dtype)


def weight_grads(lay, columns, pieces, raws, w_out, g_mix):
    deep, width, wide = columns
    block = (lay.peers // 2, lay.rows, lay.width)
    args = [*pieces, *raws, w_out, g_mix]
    return pl.pallas_call(
        functools.partial(weights_kernel, lay, columns),
        in_specs=[VMEM] * len(args),
        out_shape=[shape(block, F32), shape(block, BF16)],
        out_specs=[VMEM] * 2,
        scratch_shapes=[pltpu.VMEM((deep, width), F32), pltpu.VMEM((wide, 128), F32)],
        compiler_params=params(16),
        cost_estimate=cost(6e8, 4e6),
    )(*args)


def pair_kernel(keep_ref, got_ref, own_ref, *out_refs):
    own_ref[...] = keep_ref[0] + got_ref[0].astype(F32)
    for i, out_ref in enumerate(out_refs):
        out_ref[...] = (keep_ref[i + 1] + got_ref[i + 1].astype(F32)).astype(BF16)


def pair_sum(keep, got):
    slots, rows, width = keep.shape
    return pl.pallas_call(
        pair_kernel,
        in_specs=[VMEM] * 2,
        out_shape=[shape((rows, width), F32)] + [shape((rows, width), BF16)] * (slots - 1),
        out_specs=[VMEM] * slots,
        compiler_params=params(8),
        cost_estimate=cost(1e6, 2e6),
    )(keep, got)


def total_kernel(own_ref, *refs):
    total = own_ref[...]
    for each in refs[:-1]:
        total = total + each[...].astype(F32)
    refs[-1][...] = total.astype(BF16)


def total_sum(own, got):
    return pl.pallas_call(
        total_kernel,
        in_specs=[VMEM] * (1 + len(got)),
        out_shape=shape(own.shape, BF16),
        out_specs=VMEM,
        compiler_params=params(8),
        cost_estimate=cost(1e6, 1e6),
    )(own, *got)


def finish_kernel(lay, *refs):
    size, slots = lay.size, lay.peers // 2
    evens, odds = refs[:size], refs[size : 2 * size]
    g_mix_ref, g_in_hbm, g_out_ref, stage, sems = refs[2 * size :]
    me_blk, me_dp = lax.axis_index("blk"), lax.axis_index("dp")
    copies = []
    for i in range(size):
        for core, source in enumerate((evens[i], odds[i])):
            for z in range(slots):
                at = z * lay.rows
                owner = me_dp ^ (2 * z + core)
                slot = (i * 2 + core) * slots + z
                stage[slot] = source[at : at + lay.in_rows, :].astype(F32)
                row = ((me_blk ^ i) * lay.peers + owner) * lay.in_rows
                copy = pltpu.make_async_copy(
                    stage.at[slot], g_in_hbm.at[pl.ds(row, lay.in_rows), :], sems.at[slot]
                )
                copy.start()
                copies.append(copy)
                row = ((me_blk ^ i) * lay.peers + owner) * lay.out_rows
                strip = at + lay.top
                g_out_ref[pl.ds(row, lay.out_rows), :] = source[
                    strip : strip + lay.out_rows, :128
                ].astype(F32)
    for core in range(2):
        for z in range(slots):
            strip = z * lay.rows + lay.top
            owner = me_dp ^ (2 * z + core)
            for start, rows, cols in lay.mix_parts():
                blocks = {0: evens, 1: odds}[core]
                terms = [blocks[i][strip : strip + rows, cols].astype(F32) for i in range(size)]
                while len(terms) > 1:
                    terms = [terms[t] + terms[t + 1] for t in range(0, len(terms), 2)]
                g_mix_ref[pl.ds(owner * lay.mix_rows + start, rows), :] = terms[0]
    for copy in copies:
        copy.wait()


def finish(lay, evens, odds, lanes, feats, width):
    slots = lay.size * lay.peers
    return pl.pallas_call(
        functools.partial(finish_kernel, lay),
        in_specs=[VMEM] * (2 * lay.size),
        out_shape=[shape((lanes, 128), F32), shape((feats, width), F32), shape((width, 128), F32)],
        out_specs=[VMEM, ANY, VMEM],
        scratch_shapes=[
            pltpu.VMEM((slots, lay.in_rows, lay.width), F32),
            pltpu.SemaphoreType.DMA((slots,)),
        ],
        compiler_params=params(24),
        cost_estimate=cost(1e6, 8e6),
    )(*evens, *odds)


def stack_kernel(*refs):
    rows = refs[0].shape[0]
    for i, each in enumerate(refs[:-1]):
        refs[-1][i * rows : (i + 1) * rows, :] = each[...]


def stack(blocks):
    rows, width = blocks[0].shape
    return pl.pallas_call(
        stack_kernel,
        in_specs=[VMEM] * len(blocks),
        out_shape=shape((len(blocks) * rows, width), blocks[0].dtype),
        out_specs=VMEM,
        compiler_params=params(8),
        cost_estimate=cost(1e3, 1e5),
    )(*blocks)


def swap(block, axis, bit):
    size = lax.axis_size(axis)
    return lax.ppermute(block, axis, [(src, src ^ bit) for src in range(size)])


def spread(block, axis, hops):
    return [block] + [swap(block, axis, hop) for hop in hops]


def on_device(patches, w_mix, w_in, w_out, partner_dev, partner_row):
    count, _, lanes = patches.shape
    filters = w_mix.shape[1]
    feats, width = w_in.shape
    embed = w_out.shape[1]
    freqs = feats // filters
    size, peers = lax.axis_size("blk"), lax.axis_size("dp")
    assert size & (size - 1) == 0 and peers & (peers - 1) == 0 and peers > 1
    across, along = range(1, size), range(2, peers, 2)
    columns = piece_columns(feats, width, size)
    lay = Layout(lanes, filters, feats, width, embed, size, peers)

    spec, mixed, normed, *rest = encode(patches, w_mix, w_in, w_out, size)
    early, (units, unit32, norms, rscale) = rest[:size], rest[size:]
    stacked = spread(units, "dp", along)
    pieces = spread(units, "blk", across)
    pieces[1:], stacked[1:] = lax.optimization_barrier((pieces[1:], stacked[1:]))
    zneg, numer, even = negatives(pieces, stacked[1:])
    odd = swap(even, "dp", 1)
    local, stats, loss = positives(partner_dev, partner_row, even, odd, zneg, numer)
    dp_stats = spread(stats, "dp", along)
    group_stats = spread(stats, "blk", across)
    dp_stats[1:], group_stats[1:] = lax.optimization_barrier((dp_stats[1:], group_stats[1:]))
    factors = [early[0]] + [swap(early[hop], "blk", hop) for hop in across]
    even_stats = stack(dp_stats)
    odd_stats = swap(even_stats, "dp", 1)
    grad_raw = upper(pieces, group_stats, even, odd, even_stats, odd_stats, local, unit32, norms)
    raws = spread(grad_raw, "blk", across)
    g_mix = lower(grad_raw, w_out, early[0], normed, rscale, w_in, mixed, spec, freqs, columns)
    keep, away = weight_grads(lay, columns, factors, raws, w_out, g_mix)
    got = swap(away, "dp", 1)
    own, *sends = pair_sum(keep, got)
    got = [swap(block, "dp", hop) for block, hop in zip(sends, along)]
    share = total_sum(own, got)
    plane = stack(spread(share, "dp", along))
    evens = spread(plane, "blk", across)
    odds = [swap(block, "dp", 1) for block in evens]
    g_mix, g_in, g_out = finish(lay, evens, odds, lanes, feats, width)
    return (loss.reshape(count), g_mix, g_in, g_out)


def solution(mesh):
    placed = (P(("blk", "dp"), None, None), P(), P(), P(), P(("blk", "dp")), P(("blk", "dp")))
    return jax.shard_map(
        on_device,
        mesh=mesh,
        in_specs=placed,
        out_specs=(P(("blk", "dp")), P(), P(), P()),
        check_vma=False,
    )
```

profile of v0, /device:TPU:0, one launch (start us, length us, event | category | flops | bytes accessed | tf_op | source)
XLA Modules:
  0.0 104.4 jit_solution(13271904432719609839)
XLA Ops:
  0.7 7.5 %shard_map.102 = (bf16[16,256,256]{2,1,0:T(8,128)(2,1)}, f32[16,256,128]{2,1,0:T(8,128)}, bf16[128,2048]{1,0:T(8,128)(2,1)}, bf16[128,1152]{1,0:T(8,128)(2,1)}, ...) custom-call(bf16[128,64,256]{2,1,0:T(8,128)(2,1)} %patch_hbm.1, ...), custom_call_target="tpu_custom_call" | custom-call | flops 3000000000 | bytes 14000000 | tf_op jit(solution)/shard_map/pallas_call | solution.py:207
  8.2 5.1 %collective-permute-start.5 = (bf16[128,128]{1,0:T(8,128)(2,1)S(1)}, bf16[128,128]{1,0:T(8,128)(2,1)S(1)}, u32[]{:S(2)}, u32[]{:S(2)}) collective-permute-start(bf16[128,128]{1,0:T(8,128)(2,1)S(1)} %get-tuple-element.42.refs_0_), channel_id=1, source_target_pairs={{0,6},{1,7},{2,4},{3,5},{4,2},{5,3},{6,0},{7,1},{8,14},{9,15},{10,... | collective-permute-start | bytes 98312 | tf_op jit(solution)/shard_map/ppermute | solution.py:653
  13.9 2.6 %collective-permute-start.2 = (bf16[128,128]{1,0:T(8,128)(2,1)S(1)}, bf16[128,128]{1,0:T(8,128)(2,1)S(1)}, u32[]{:S(2)}, u32[]{:S(2)}) collective-permute-start(bf16[128,128]{1,0:T(8,128)(2,1)S(1)} %get-tuple-element.42.refs_0_), channel_id=1, source_target_pairs={{0,24},{8,16},{16,8},{24,0},{1,25},{9,17},{17,9},{25,1},{2,26},{10... | collective-permute-start | bytes 98312 | tf_op jit(solution)/shard_map/ppermute | solution.py:653
  18.8 1.7 %collective-permute-done.1.refs_2_ = bf16[128,128]{1,0:T(8,128)(2,1)S(1)} collective-permute-done((bf16[128,128]{1,0:T(8,128)(2,1)S(1)}, bf16[128,128]{1,0:T(8,128)(2,1)S(1)}, u32[]{:S(2)}, u32[]{:S(2)}) %collective-permute-start.1) | collective-permute-done | bytes 32800 | tf_op jit(solution)/shard_map/ppermute | solution.py:653
  21.9 1.7 %collective-permute-start.8 = (bf16[128,1152]{1,0:T(8,128)(2,1)}, bf16[128,1152]{1,0:T(8,128)(2,1)S(1)}, u32[]{:S(2)}, u32[]{:S(2)}) collective-permute-start(bf16[128,1152]{1,0:T(8,128)(2,1)} %get-tuple-element.55), channel_id=1, source_target_pairs={{0,16},{8,24},{16,0},{24,8},{1,17},{9,25},{17,1},{25,9},{2,18},{10... | collective-permute-start | bytes 884744 | tf_op jit(solution)/shard_map/ppermute | solution.py:653
  23.5 1.4 %collective-permute-start.9 = (bf16[128,1152]{1,0:T(8,128)(2,1)}, bf16[128,1152]{1,0:T(8,128)(2,1)S(1)}, u32[]{:S(2)}, u32[]{:S(2)}) collective-permute-start(bf16[128,1152]{1,0:T(8,128)(2,1)} %get-tuple-element.56), channel_id=1, source_target_pairs={{0,24},{8,16},{16,8},{24,0},{1,25},{9,17},{17,9},{25,1},{2,26},{10... | collective-permute-start | bytes 884744 | tf_op jit(solution)/shard_map/ppermute | solution.py:653
  25.0 1.1 %shard_map.104 = (f32[128,128]{1,0:T(8,128)S(1)}, f32[8,128]{1,0:T(8,128)S(1)}, f32[1,128]{1,0:T(1,128)}) custom-call(s32[1,128]{1,0:T(1,128)S(1)} %bitcast.3, s32[1,128]{1,0:T(1,128)S(1)} %bitcast.4, bf16[512,128]{1,0:T(8,128)(2,1)S(1)} %get-tuple-element.49.even_ref.refs_8_, bf16[512,128]{1,0:T(8,128)(2,1)S(1)} %collective-permute-done.6.odd_ref.refs_9_, ...), custom_call_target="tpu_custom_call" | custom-call | flops 400000000 | bytes 1000000 | tf_op jit(solution)/shard_map/pallas_call | solution.py:317
  26.1 1.5 %collective-permute-start.15 = (f32[8,128]{1,0:T(8,128)S(1)}, f32[8,128]{1,0:T(8,128)S(1)}, u32[]{:S(2)}, u32[]{:S(2)}) collective-permute-start(f32[8,128]{1,0:T(8,128)S(1)} %get-tuple-element.57.refs_0_.refs_4_), channel_id=1, source_target_pairs={{0,24},{8,16},{16,8},{24,0},{1,25},{9,17},{17,9},{25,1},{2,26},{10... | collective-permute-start | bytes 12296 | tf_op jit(solution)/shard_map/ppermute | solution.py:653
  27.9 10.5 %collective-permute-done.15.refs_7_ = f32[8,128]{1,0:T(8,128)S(1)} collective-permute-done((f32[8,128]{1,0:T(8,128)S(1)}, f32[8,128]{1,0:T(8,128)S(1)}, u32[]{:S(2)}, u32[]{:S(2)}) %collective-permute-start.15) | collective-permute-done | bytes 4128 | tf_op jit(solution)/shard_map/ppermute | solution.py:653
  39.0 3.6 %collective-permute-start.12 = (f32[8,128]{1,0:T(8,128)S(1)}, f32[8,128]{1,0:T(8,128)S(1)}, u32[]{:S(2)}, u32[]{:S(2)}) collective-permute-start(f32[8,128]{1,0:T(8,128)S(1)} %get-tuple-element.57.refs_0_.refs_4_), channel_id=1, source_target_pairs={{0,6},{1,7},{2,4},{3,5},{4,2},{5,3},{6,0},{7,1},{8,14},{9,15},{10,... | collective-permute-start | bytes 12296 | tf_op jit(solution)/shard_map/ppermute | solution.py:653
  42.6 1.5 %collective-permute-start.11 = (f32[8,128]{1,0:T(8,128)S(1)}, f32[8,128]{1,0:T(8,128)S(1)}, u32[]{:S(2)}, u32[]{:S(2)}) collective-permute-start(f32[8,128]{1,0:T(8,128)S(1)} %get-tuple-element.57.refs_0_.refs_4_), channel_id=1, source_target_pairs={{0,4},{1,5},{2,6},{3,7},{4,0},{5,1},{6,2},{7,3},{8,12},{9,13},{10,... | collective-permute-start | bytes 12296 | tf_op jit(solution)/shard_map/ppermute | solution.py:653
  44.4 1.7 %collective-permute-start.10 = (f32[8,128]{1,0:T(8,128)S(1)}, f32[8,128]{1,0:T(8,128)S(1)}, u32[]{:S(2)}, u32[]{:S(2)}) collective-permute-start(f32[8,128]{1,0:T(8,128)S(1)} %get-tuple-element.57.refs_0_.refs_4_), channel_id=1, source_target_pairs={{0,2},{1,3},{2,0},{3,1},{4,6},{5,7},{6,4},{7,5},{8,10},{9,11},{10,... | collective-permute-start | bytes 12296 | tf_op jit(solution)/shard_map/ppermute | solution.py:653
  48.0 1.2 %collective-permute-done.16.refs_11_ = f32[32,128]{1,0:T(8,128)S(1)} collective-permute-done((f32[32,128]{1,0:T(8,128)S(1)}, f32[32,128]{1,0:T(8,128)S(1)}, u32[]{:S(2)}, u32[]{:S(2)}) %collective-permute-start.16) | collective-permute-done | bytes 16416 | tf_op jit(solution)/shard_map/ppermute | solution.py:653
  50.0 1.5 %collective-permute-start.19 = (bf16[128,128]{1,0:T(8,128)(2,1)S(1)}, bf16[128,128]{1,0:T(8,128)(2,1)S(1)}, u32[]{:S(2)}, u32[]{:S(2)}) collective-permute-start(bf16[128,128]{1,0:T(8,128)(2,1)S(1)} %shard_map.106.raw_ref.refs_4_), channel_id=1, source_target_pairs={{0,24},{8,16},{16,8},{24,0},{1,25},{9,17},{17,9},{25,1},{2,26},{10... | collective-permute-start | bytes 98312 | tf_op jit(solution)/shard_map/ppermute | solution.py:653
  51.5 1.4 %collective-permute-start.18 = (bf16[128,128]{1,0:T(8,128)(2,1)S(1)}, bf16[128,128]{1,0:T(8,128)(2,1)S(1)}, u32[]{:S(2)}, u32[]{:S(2)}) collective-permute-start(bf16[128,128]{1,0:T(8,128)(2,1)S(1)} %shard_map.106.raw_ref.refs_4_), channel_id=1, source_target_pairs={{0,16},{8,24},{16,0},{24,8},{1,17},{9,25},{17,1},{25,9},{2,18},{10... | collective-permute-start | bytes 98312 | tf_op jit(solution)/shard_map/ppermute | solution.py:653
  52.9 2.0 %collective-permute-done.19.refs_7_ = bf16[128,128]{1,0:T(8,128)(2,1)S(1)} collective-permute-done((bf16[128,128]{1,0:T(8,128)(2,1)S(1)}, bf16[128,128]{1,0:T(8,128)(2,1)S(1)}, u32[]{:S(2)}, u32[]{:S(2)}) %collective-permute-start.19) | collective-permute-done | bytes 32800 | tf_op jit(solution)/shard_map/ppermute | solution.py:653
  54.9 1.4 %collective-permute-start.17 = (bf16[128,128]{1,0:T(8,128)(2,1)S(1)}, bf16[128,128]{1,0:T(8,128)(2,1)S(1)}, u32[]{:S(2)}, u32[]{:S(2)}) collective-permute-start(bf16[128,128]{1,0:T(8,128)(2,1)S(1)} %shard_map.106.raw_ref.refs_4_), channel_id=1, source_target_pairs={{0,8},{8,0},{16,24},{24,16},{1,9},{9,1},{17,25},{25,17},{2,10},{10... | collective-permute-start | bytes 98312 | tf_op jit(solution)/shard_map/ppermute | solution.py:653
  56.3 4.5 %shard_map.107.refs_9_ = f32[256,128]{1,0:T(8,128)S(1)} custom-call(bf16[128,128]{1,0:T(8,128)(2,1)S(1)} %shard_map.106.raw_ref.refs_4_, bf16[512,128]{1,0:T(8,128)(2,1)} %refs_8_.1, bf16[128,1152]{1,0:T(8,128)(2,1)} %get-tuple-element.53.piece_hbm.refs_0_, bf16[128,2048]{1,0:T(8,128)(2,1)} %get-tuple-element.67.normed_hbm, ...), custom_call_target="tpu_custom_call" | custom-call | flops 1000000000 | bytes 7000000 | tf_op jit(solution)/shard_map/pallas_call | solution.py:450
  60.9 1.5 %shard_map.108 = (f32[4,80,512]{2,1,0:T(8,128)S(1)}, bf16[4,80,512]{2,1,0:T(8,128)(2,1)S(1)}) custom-call(bf16[128,1152]{1,0:T(8,128)(2,1)S(1)} %copy-done, bf16[128,1152]{1,0:T(8,128)(2,1)S(1)} %collective-permute-done.7.refs_1_, bf16[128,1152]{1,0:T(8,128)(2,1)S(1)} %collective-permute-done.8.refs_2_, ...), custom_call_target="tpu_custom_call" | custom-call | flops 600000000 | bytes 4000000 | tf_op jit(solution)/shard_map/pallas_call | solution.py:532
  62.5 1.6 %collective-permute-done.20.got_ref = bf16[4,80,512]{2,1,0:T(8,128)(2,1)S(1)} collective-permute-done((bf16[4,80,512]{2,1,0:T(8,128)(2,1)S(1)}, bf16[4,80,512]{2,1,0:T(8,128)(2,1)S(1)}, u32[]{:S(2)}, u32[]{:S(2)}) %collective-permute-start.20) | collective-permute-done | bytes 327712 | tf_op jit(solution)/shard_map/ppermute | solution.py:653
  65.2 3.2 %collective-permute-start.22 = (bf16[80,512]{1,0:T(8,128)(2,1)S(1)}, bf16[80,512]{1,0:T(8,128)(2,1)S(1)}, u32[]{:S(2)}, u32[]{:S(2)}) collective-permute-start(bf16[80,512]{1,0:T(8,128)(2,1)S(1)} %get-tuple-element.75), channel_id=1, source_target_pairs={{0,4},{1,5},{2,6},{3,7},{4,0},{5,1},{6,2},{7,3},{8,12},{9,13},{10,... | collective-permute-start | bytes 245768 | tf_op jit(solution)/shard_map/ppermute | solution.py:653
  68.7 6.4 %collective-permute-done.22.refs_1_ = bf16[80,512]{1,0:T(8,128)(2,1)S(1)} collective-permute-done((bf16[80,512]{1,0:T(8,128)(2,1)S(1)}, bf16[80,512]{1,0:T(8,128)(2,1)S(1)}, u32[]{:S(2)}, u32[]{:S(2)}) %collective-permute-start.22) | collective-permute-done | bytes 81952 | tf_op jit(solution)/shard_map/ppermute | solution.py:653
  75.1 2.7 %collective-permute-start.26 = (bf16[80,512]{1,0:T(8,128)(2,1)S(1)}, bf16[80,512]{1,0:T(8,128)(2,1)S(1)}, u32[]{:S(2)}, u32[]{:S(2)}) collective-permute-start(bf16[80,512]{1,0:T(8,128)(2,1)S(1)} %shard_map.110.refs_0_), channel_id=1, source_target_pairs={{0,6},{1,7},{2,4},{3,5},{4,2},{5,3},{6,0},{7,1},{8,14},{9,15},{10,... | collective-permute-start | bytes 245768 | tf_op jit(solution)/shard_map/ppermute | solution.py:653
  78.3 1.3 %collective-permute-start.24 = (bf16[80,512]{1,0:T(8,128)(2,1)S(1)}, bf16[80,512]{1,0:T(8,128)(2,1)S(1)}, u32[]{:S(2)}, u32[]{:S(2)}) collective-permute-start(bf16[80,512]{1,0:T(8,128)(2,1)S(1)} %shard_map.110.refs_0_), channel_id=1, source_target_pairs={{0,2},{1,3},{2,0},{3,1},{4,6},{5,7},{6,4},{7,5},{8,10},{9,11},{10,... | collective-permute-start | bytes 245768 | tf_op jit(solution)/shard_map/ppermute | solution.py:653
  79.5 2.8 %collective-permute-done.26.refs_3_ = bf16[80,512]{1,0:T(8,128)(2,1)S(1)} collective-permute-done((bf16[80,512]{1,0:T(8,128)(2,1)S(1)}, bf16[80,512]{1,0:T(8,128)(2,1)S(1)}, u32[]{:S(2)}, u32[]{:S(2)}) %collective-permute-start.26) | collective-permute-done | bytes 81952 | tf_op jit(solution)/shard_map/ppermute | solution.py:653
  82.3 2.3 %collective-permute-done.25.refs_2_ = bf16[80,512]{1,0:T(8,128)(2,1)S(1)} collective-permute-done((bf16[80,512]{1,0:T(8,128)(2,1)S(1)}, bf16[80,512]{1,0:T(8,128)(2,1)S(1)}, u32[]{:S(2)}, u32[]{:S(2)}) %collective-permute-start.25) | collective-permute-done | bytes 81952 | tf_op jit(solution)/shard_map/ppermute | solution.py:653
  85.3 1.5 %collective-permute-start.28 = (bf16[320,512]{1,0:T(8,128)(2,1)S(1)}, bf16[320,512]{1,0:T(8,128)(2,1)S(1)}, u32[]{:S(2)}, u32[]{:S(2)}) collective-permute-start(bf16[320,512]{1,0:T(8,128)(2,1)S(1)} %shard_map.111.refs_0_), channel_id=1, source_target_pairs={{0,16},{8,24},{16,0},{24,8},{1,17},{9,25},{17,1},{25,9},{2,18},{10... | collective-permute-start | bytes 983048 | tf_op jit(solution)/shard_map/ppermute | solution.py:653
  86.8 1.4 %collective-permute-start.27 = (bf16[320,512]{1,0:T(8,128)(2,1)S(1)}, bf16[320,512]{1,0:T(8,128)(2,1)S(1)}, u32[]{:S(2)}, u32[]{:S(2)}) collective-permute-start(bf16[320,512]{1,0:T(8,128)(2,1)S(1)} %shard_map.111.refs_0_), channel_id=1, source_target_pairs={{0,8},{8,0},{16,24},{24,16},{1,9},{9,1},{17,25},{25,17},{2,10},{10... | collective-permute-start | bytes 983048 | tf_op jit(solution)/shard_map/ppermute | solution.py:653
  88.3 8.0 %collective-permute-done.29.refs_3_ = bf16[320,512]{1,0:T(8,128)(2,1)S(1)} collective-permute-done((bf16[320,512]{1,0:T(8,128)(2,1)S(1)}, bf16[320,512]{1,0:T(8,128)(2,1)S(1)}, u32[]{:S(2)}, u32[]{:S(2)}) %collective-permute-start.29) | collective-permute-done | bytes 327712 | tf_op jit(solution)/shard_map/ppermute | solution.py:653
  96.2 3.1 %collective-permute-done.28.refs_2_ = bf16[320,512]{1,0:T(8,128)(2,1)S(1)} collective-permute-done((bf16[320,512]{1,0:T(8,128)(2,1)S(1)}, bf16[320,512]{1,0:T(8,128)(2,1)S(1)}, u32[]{:S(2)}, u32[]{:S(2)}) %collective-permute-start.28) | collective-permute-done | bytes 327712 | tf_op jit(solution)/shard_map/ppermute | solution.py:653
  99.8 1.1 %collective-permute-done.32.refs_6_ = bf16[320,512]{1,0:T(8,128)(2,1)S(1)} collective-permute-done((bf16[320,512]{1,0:T(8,128)(2,1)S(1)}, bf16[320,512]{1,0:T(8,128)(2,1)S(1)}, u32[]{:S(2)}, u32[]{:S(2)}) %collective-permute-start.32) | collective-permute-done | bytes 327712 | tf_op jit(solution)/shard_map/ppermute | solution.py:653
  101.4 3.0 %shard_map.112 = (f32[256,128]{1,0:T(8,128)}, f32[2048,512]{1,0:T(8,128)}, f32[512,128]{1,0:T(8,128)}) custom-call(bf16[320,512]{1,0:T(8,128)(2,1)S(1)} %shard_map.111.refs_0_, bf16[320,512]{1,0:T(8,128)(2,1)S(1)} %collective-permute-done.27.refs_1_, bf16[320,512]{1,0:T(8,128)(2,1)S(1)} %collective-permute-done.28.refs_2_, ...), custom_call_target="tpu_custom_call" | custom-call | flops 1000000 | bytes 8000000 | tf_op jit(solution)/shard_map/pallas_call | solution.py:619
  (55 shorter events, 11.9 us)
Async XLA Ops:
  8.2 8.9 %collective-permute-start.5 = (bf16[128,128]{1,0:T(8,128)(2,1)S(1)}, bf16[128,128]{1,0:T(8,128)(2,1)S(1)}, u32[]{:S(2)}, u32[]{:S(2)}) collective-permute-start(bf16[128,128]{1,0:T(8,128)(2,1)S(1)} %get-tuple-element.42.refs_0_), channel_id=1, source_target_pairs={{0,6},{1,7},{2,4},{3,5},{4,2},{5,3},{6,0},{7,1},{8,14},{9,15},{10,... | collective-permute-start | bytes 98312 | tf_op jit(solution)/shard_map/ppermute | solution.py:653
  13.3 4.8 %collective-permute-start.4 = (bf16[128,128]{1,0:T(8,128)(2,1)S(1)}, bf16[128,128]{1,0:T(8,128)(2,1)S(1)}, u32[]{:S(2)}, u32[]{:S(2)}) collective-permute-start(bf16[128,128]{1,0:T(8,128)(2,1)S(1)} %get-tuple-element.42.refs_0_), channel_id=1, source_target_pairs={{0,4},{1,5},{2,6},{3,7},{4,0},{5,1},{6,2},{7,3},{8,12},{9,13},{10,... | collective-permute-start | bytes 98312 | tf_op jit(solution)/shard_map/ppermute | solution.py:653
  13.3 4.8 %collective-permute-start.3 = (bf16[128,128]{1,0:T(8,128)(2,1)S(1)}, bf16[128,128]{1,0:T(8,128)(2,1)S(1)}, u32[]{:S(2)}, u32[]{:S(2)}) collective-permute-start(bf16[128,128]{1,0:T(8,128)(2,1)S(1)} %get-tuple-element.42.refs_0_), channel_id=1, source_target_pairs={{0,2},{1,3},{2,0},{3,1},{4,6},{5,7},{6,4},{7,5},{8,10},{9,11},{10,... | collective-permute-start | bytes 98312 | tf_op jit(solution)/shard_map/ppermute | solution.py:653
  13.9 4.8 %collective-permute-start.2 = (bf16[128,128]{1,0:T(8,128)(2,1)S(1)}, bf16[128,128]{1,0:T(8,128)(2,1)S(1)}, u32[]{:S(2)}, u32[]{:S(2)}) collective-permute-start(bf16[128,128]{1,0:T(8,128)(2,1)S(1)} %get-tuple-element.42.refs_0_), channel_id=1, source_target_pairs={{0,24},{8,16},{16,8},{24,0},{1,25},{9,17},{17,9},{25,1},{2,26},{10... | collective-permute-start | bytes 98312 | tf_op jit(solution)/shard_map/ppermute | solution.py:653
  16.5 3.9 %collective-permute-start.1 = (bf16[128,128]{1,0:T(8,128)(2,1)S(1)}, bf16[128,128]{1,0:T(8,128)(2,1)S(1)}, u32[]{:S(2)}, u32[]{:S(2)}) collective-permute-start(bf16[128,128]{1,0:T(8,128)(2,1)S(1)} %get-tuple-element.42.refs_0_), channel_id=1, source_target_pairs={{0,16},{8,24},{16,0},{24,8},{1,17},{9,25},{17,1},{25,9},{2,18},{10... | collective-permute-start | bytes 98312 | tf_op jit(solution)/shard_map/ppermute | solution.py:653
  17.0 3.9 %collective-permute-start = (bf16[128,128]{1,0:T(8,128)(2,1)S(1)}, bf16[128,128]{1,0:T(8,128)(2,1)S(1)}, u32[]{:S(2)}, u32[]{:S(2)}) collective-permute-start(bf16[128,128]{1,0:T(8,128)(2,1)S(1)} %get-tuple-element.42.refs_0_), channel_id=1, source_target_pairs={{0,8},{8,0},{16,24},{24,16},{1,9},{9,1},{17,25},{25,17},{2,10},{10... | collective-permute-start | bytes 98312 | tf_op jit(solution)/shard_map/ppermute | solution.py:653
  21.3 3.6 %collective-permute-start.6 = (bf16[512,128]{1,0:T(8,128)(2,1)S(1)}, bf16[512,128]{1,0:T(8,128)(2,1)S(1)}, u32[]{:S(2)}, u32[]{:S(2)}) collective-permute-start(bf16[512,128]{1,0:T(8,128)(2,1)S(1)} %get-tuple-element.49.even_ref.refs_8_), channel_id=1, source_target_pairs={{0,1},{1,0},{2,3},{3,2},{4,5},{5,4},{6,7},{7,6},{8,9},{9,8},{10,11... | collective-permute-start | bytes 393224 | tf_op jit(solution)/shard_map/ppermute | solution.py:653
  21.4 39.4 %collective-permute-start.7 = (bf16[128,1152]{1,0:T(8,128)(2,1)}, bf16[128,1152]{1,0:T(8,128)(2,1)S(1)}, u32[]{:S(2)}, u32[]{:S(2)}) collective-permute-start(bf16[128,1152]{1,0:T(8,128)(2,1)} %get-tuple-element.54), channel_id=1, source_target_pairs={{0,8},{8,0},{16,24},{24,16},{1,9},{9,1},{17,25},{25,17},{2,10},{10... | collective-permute-start | bytes 884744 | tf_op jit(solution)/shard_map/ppermute | solution.py:653
  21.9 39.0 %collective-permute-start.8 = (bf16[128,1152]{1,0:T(8,128)(2,1)}, bf16[128,1152]{1,0:T(8,128)(2,1)S(1)}, u32[]{:S(2)}, u32[]{:S(2)}) collective-permute-start(bf16[128,1152]{1,0:T(8,128)(2,1)} %get-tuple-element.55), channel_id=1, source_target_pairs={{0,16},{8,24},{16,0},{24,8},{1,17},{9,25},{17,1},{25,9},{2,18},{10... | collective-permute-start | bytes 884744 | tf_op jit(solution)/shard_map/ppermute | solution.py:653
  23.5 37.3 %collective-permute-start.9 = (bf16[128,1152]{1,0:T(8,128)(2,1)}, bf16[128,1152]{1,0:T(8,128)(2,1)S(1)}, u32[]{:S(2)}, u32[]{:S(2)}) collective-permute-start(bf16[128,1152]{1,0:T(8,128)(2,1)} %get-tuple-element.56), channel_id=1, source_target_pairs={{0,24},{8,16},{16,8},{24,0},{1,25},{9,17},{17,9},{25,1},{2,26},{10... | collective-permute-start | bytes 884744 | tf_op jit(solution)/shard_map/ppermute | solution.py:653
  26.1 12.3 %collective-permute-start.15 = (f32[8,128]{1,0:T(8,128)S(1)}, f32[8,128]{1,0:T(8,128)S(1)}, u32[]{:S(2)}, u32[]{:S(2)}) collective-permute-start(f32[8,128]{1,0:T(8,128)S(1)} %get-tuple-element.57.refs_0_.refs_4_), channel_id=1, source_target_pairs={{0,24},{8,16},{16,8},{24,0},{1,25},{9,17},{17,9},{25,1},{2,26},{10... | collective-permute-start | bytes 12296 | tf_op jit(solution)/shard_map/ppermute | solution.py:653
  27.6 11.5 %collective-permute-start.14 = (f32[8,128]{1,0:T(8,128)S(1)}, f32[8,128]{1,0:T(8,128)S(1)}, u32[]{:S(2)}, u32[]{:S(2)}) collective-permute-start(f32[8,128]{1,0:T(8,128)S(1)} %get-tuple-element.57.refs_0_.refs_4_), channel_id=1, source_target_pairs={{0,16},{8,24},{16,0},{24,8},{1,17},{9,25},{17,1},{25,9},{2,18},{10... | collective-permute-start | bytes 12296 | tf_op jit(solution)/shard_map/ppermute | solution.py:653
  38.4 4.2 %collective-permute-start.13 = (f32[8,128]{1,0:T(8,128)S(1)}, f32[8,128]{1,0:T(8,128)S(1)}, u32[]{:S(2)}, u32[]{:S(2)}) collective-permute-start(f32[8,128]{1,0:T(8,128)S(1)} %get-tuple-element.57.refs_0_.refs_4_), channel_id=1, source_target_pairs={{0,8},{8,0},{16,24},{24,16},{1,9},{9,1},{17,25},{25,17},{2,10},{10... | collective-permute-start | bytes 12296 | tf_op jit(solution)/shard_map/ppermute | solution.py:653
  39.0 5.4 %collective-permute-start.12 = (f32[8,128]{1,0:T(8,128)S(1)}, f32[8,128]{1,0:T(8,128)S(1)}, u32[]{:S(2)}, u32[]{:S(2)}) collective-permute-start(f32[8,128]{1,0:T(8,128)S(1)} %get-tuple-element.57.refs_0_.refs_4_), channel_id=1, source_target_pairs={{0,6},{1,7},{2,4},{3,5},{4,2},{5,3},{6,0},{7,1},{8,14},{9,15},{10,... | collective-permute-start | bytes 12296 | tf_op jit(solution)/shard_map/ppermute | solution.py:653
  42.6 4.5 %collective-permute-start.11 = (f32[8,128]{1,0:T(8,128)S(1)}, f32[8,128]{1,0:T(8,128)S(1)}, u32[]{:S(2)}, u32[]{:S(2)}) collective-permute-start(f32[8,128]{1,0:T(8,128)S(1)} %get-tuple-element.57.refs_0_.refs_4_), channel_id=1, source_target_pairs={{0,4},{1,5},{2,6},{3,7},{4,0},{5,1},{6,2},{7,3},{8,12},{9,13},{10,... | collective-permute-start | bytes 12296 | tf_op jit(solution)/shard_map/ppermute | solution.py:653
  44.4 3.6 %collective-permute-start.10 = (f32[8,128]{1,0:T(8,128)S(1)}, f32[8,128]{1,0:T(8,128)S(1)}, u32[]{:S(2)}, u32[]{:S(2)}) collective-permute-start(f32[8,128]{1,0:T(8,128)S(1)} %get-tuple-element.57.refs_0_.refs_4_), channel_id=1, source_target_pairs={{0,2},{1,3},{2,0},{3,1},{4,6},{5,7},{6,4},{7,5},{8,10},{9,11},{10,... | collective-permute-start | bytes 12296 | tf_op jit(solution)/shard_map/ppermute | solution.py:653
  50.0 4.9 %collective-permute-start.19 = (bf16[128,128]{1,0:T(8,128)(2,1)S(1)}, bf16[128,128]{1,0:T(8,128)(2,1)S(1)}, u32[]{:S(2)}, u32[]{:S(2)}) collective-permute-start(bf16[128,128]{1,0:T(8,128)(2,1)S(1)} %shard_map.106.raw_ref.refs_4_), channel_id=1, source_target_pairs={{0,24},{8,16},{16,8},{24,0},{1,25},{9,17},{17,9},{25,1},{2,26},{10... | collective-permute-start | bytes 98312 | tf_op jit(solution)/shard_map/ppermute | solution.py:653
  51.5 9.3 %collective-permute-start.18 = (bf16[128,128]{1,0:T(8,128)(2,1)S(1)}, bf16[128,128]{1,0:T(8,128)(2,1)S(1)}, u32[]{:S(2)}, u32[]{:S(2)}) collective-permute-start(bf16[128,128]{1,0:T(8,128)(2,1)S(1)} %shard_map.106.raw_ref.refs_4_), channel_id=1, source_target_pairs={{0,16},{8,24},{16,0},{24,8},{1,17},{9,25},{17,1},{25,9},{2,18},{10... | collective-permute-start | bytes 98312 | tf_op jit(solution)/shard_map/ppermute | solution.py:653
  54.9 5.9 %collective-permute-start.17 = (bf16[128,128]{1,0:T(8,128)(2,1)S(1)}, bf16[128,128]{1,0:T(8,128)(2,1)S(1)}, u32[]{:S(2)}, u32[]{:S(2)}) collective-permute-start(bf16[128,128]{1,0:T(8,128)(2,1)S(1)} %shard_map.106.raw_ref.refs_4_), channel_id=1, source_target_pairs={{0,8},{8,0},{16,24},{24,16},{1,9},{9,1},{17,25},{25,17},{2,10},{10... | collective-permute-start | bytes 98312 | tf_op jit(solution)/shard_map/ppermute | solution.py:653
  62.4 1.7 %collective-permute-start.20 = (bf16[4,80,512]{2,1,0:T(8,128)(2,1)S(1)}, bf16[4,80,512]{2,1,0:T(8,128)(2,1)S(1)}, u32[]{:S(2)}, u32[]{:S(2)}) collective-permute-start(bf16[4,80,512]{2,1,0:T(8,128)(2,1)S(1)} %get-tuple-element.72), channel_id=1, source_target_pairs={{0,1},{1,0},{2,3},{3,2},{4,5},{5,4},{6,7},{7,6},{8,9},{9,8},{10,11... | collective-permute-start | bytes 983048 | tf_op jit(solution)/shard_map/ppermute | solution.py:653
  64.1 4.6 %collective-permute-start.21 = (bf16[80,512]{1,0:T(8,128)(2,1)S(1)}, bf16[80,512]{1,0:T(8,128)(2,1)S(1)}, u32[]{:S(2)}, u32[]{:S(2)}) collective-permute-start(bf16[80,512]{1,0:T(8,128)(2,1)S(1)} %get-tuple-element.74), channel_id=1, source_target_pairs={{0,2},{1,3},{2,0},{3,1},{4,6},{5,7},{6,4},{7,5},{8,10},{9,11},{10,... | collective-permute-start | bytes 245768 | tf_op jit(solution)/shard_map/ppermute | solution.py:653
  65.2 9.9 %collective-permute-start.22 = (bf16[80,512]{1,0:T(8,128)(2,1)S(1)}, bf16[80,512]{1,0:T(8,128)(2,1)S(1)}, u32[]{:S(2)}, u32[]{:S(2)}) collective-permute-start(bf16[80,512]{1,0:T(8,128)(2,1)S(1)} %get-tuple-element.75), channel_id=1, source_target_pairs={{0,4},{1,5},{2,6},{3,7},{4,0},{5,1},{6,2},{7,3},{8,12},{9,13},{10,... | collective-permute-start | bytes 245768 | tf_op jit(solution)/shard_map/ppermute | solution.py:653
  68.4 6.6 %collective-permute-start.23 = (bf16[80,512]{1,0:T(8,128)(2,1)S(1)}, bf16[80,512]{1,0:T(8,128)(2,1)S(1)}, u32[]{:S(2)}, u32[]{:S(2)}) collective-permute-start(bf16[80,512]{1,0:T(8,128)(2,1)S(1)} %get-tuple-element.76), channel_id=1, source_target_pairs={{0,6},{1,7},{2,4},{3,5},{4,2},{5,3},{6,0},{7,1},{8,14},{9,15},{10,... | collective-permute-start | bytes 245768 | tf_op jit(solution)/shard_map/ppermute | solution.py:653
  75.1 7.2 %collective-permute-start.26 = (bf16[80,512]{1,0:T(8,128)(2,1)S(1)}, bf16[80,512]{1,0:T(8,128)(2,1)S(1)}, u32[]{:S(2)}, u32[]{:S(2)}) collective-permute-start(bf16[80,512]{1,0:T(8,128)(2,1)S(1)} %shard_map.110.refs_0_), channel_id=1, source_target_pairs={{0,6},{1,7},{2,4},{3,5},{4,2},{5,3},{6,0},{7,1},{8,14},{9,15},{10,... | collective-permute-start | bytes 245768 | tf_op jit(solution)/shard_map/ppermute | solution.py:653
  77.8 6.9 %collective-permute-start.25 = (bf16[80,512]{1,0:T(8,128)(2,1)S(1)}, bf16[80,512]{1,0:T(8,128)(2,1)S(1)}, u32[]{:S(2)}, u32[]{:S(2)}) collective-permute-start(bf16[80,512]{1,0:T(8,128)(2,1)S(1)} %shard_map.110.refs_0_), channel_id=1, source_target_pairs={{0,4},{1,5},{2,6},{3,7},{4,0},{5,1},{6,2},{7,3},{8,12},{9,13},{10,... | collective-permute-start | bytes 245768 | tf_op jit(solution)/shard_map/ppermute | solution.py:653
  78.3 6.4 %collective-permute-start.24 = (bf16[80,512]{1,0:T(8,128)(2,1)S(1)}, bf16[80,512]{1,0:T(8,128)(2,1)S(1)}, u32[]{:S(2)}, u32[]{:S(2)}) collective-permute-start(bf16[80,512]{1,0:T(8,128)(2,1)S(1)} %shard_map.110.refs_0_), channel_id=1, source_target_pairs={{0,2},{1,3},{2,0},{3,1},{4,6},{5,7},{6,4},{7,5},{8,10},{9,11},{10,... | collective-permute-start | bytes 245768 | tf_op jit(solution)/shard_map/ppermute | solution.py:653
  84.7 11.5 %collective-permute-start.29 = (bf16[320,512]{1,0:T(8,128)(2,1)S(1)}, bf16[320,512]{1,0:T(8,128)(2,1)S(1)}, u32[]{:S(2)}, u32[]{:S(2)}) collective-permute-start(bf16[320,512]{1,0:T(8,128)(2,1)S(1)} %shard_map.111.refs_0_), channel_id=1, source_target_pairs={{0,24},{8,16},{16,8},{24,0},{1,25},{9,17},{17,9},{25,1},{2,26},{10... | collective-permute-start | bytes 983048 | tf_op jit(solution)/shard_map/ppermute | solution.py:653
  85.3 14.0 %collective-permute-start.28 = (bf16[320,512]{1,0:T(8,128)(2,1)S(1)}, bf16[320,512]{1,0:T(8,128)(2,1)S(1)}, u32[]{:S(2)}, u32[]{:S(2)}) collective-permute-start(bf16[320,512]{1,0:T(8,128)(2,1)S(1)} %shard_map.111.refs_0_), channel_id=1, source_target_pairs={{0,16},{8,24},{16,0},{24,8},{1,17},{9,25},{17,1},{25,9},{2,18},{10... | collective-permute-start | bytes 983048 | tf_op jit(solution)/shard_map/ppermute | solution.py:653
  86.8 12.5 %collective-permute-start.27 = (bf16[320,512]{1,0:T(8,128)(2,1)S(1)}, bf16[320,512]{1,0:T(8,128)(2,1)S(1)}, u32[]{:S(2)}, u32[]{:S(2)}) collective-permute-start(bf16[320,512]{1,0:T(8,128)(2,1)S(1)} %shard_map.111.refs_0_), channel_id=1, source_target_pairs={{0,8},{8,0},{16,24},{24,16},{1,9},{9,1},{17,25},{25,17},{2,10},{10... | collective-permute-start | bytes 983048 | tf_op jit(solution)/shard_map/ppermute | solution.py:653
  88.3 11.6 %collective-permute-start.30 = (bf16[320,512]{1,0:T(8,128)(2,1)S(1)}, bf16[320,512]{1,0:T(8,128)(2,1)S(1)}, u32[]{:S(2)}, u32[]{:S(2)}) collective-permute-start(bf16[320,512]{1,0:T(8,128)(2,1)S(1)} %shard_map.111.refs_0_), channel_id=1, source_target_pairs={{0,1},{1,0},{2,3},{3,2},{4,5},{5,4},{6,7},{7,6},{8,9},{9,8},{10,11... | collective-permute-start | bytes 983048 | tf_op jit(solution)/shard_map/ppermute | solution.py:653
  96.2 3.6 %collective-permute-start.33 = (bf16[320,512]{1,0:T(8,128)(2,1)S(1)}, bf16[320,512]{1,0:T(8,128)(2,1)S(1)}, u32[]{:S(2)}, u32[]{:S(2)}) collective-permute-start(bf16[320,512]{1,0:T(8,128)(2,1)S(1)} %collective-permute-done.29.refs_3_), channel_id=1, source_target_pairs={{0,1},{1,0},{2,3},{3,2},{4,5},{5,4},{6,7},{7,6},{8,9},{9,8},{10,11... | collective-permute-start | bytes 983048 | tf_op jit(solution)/shard_map/ppermute | solution.py:653
  99.3 2.1 %collective-permute-start.31 = (bf16[320,512]{1,0:T(8,128)(2,1)S(1)}, bf16[320,512]{1,0:T(8,128)(2,1)S(1)}, u32[]{:S(2)}, u32[]{:S(2)}) collective-permute-start(bf16[320,512]{1,0:T(8,128)(2,1)S(1)} %collective-permute-done.27.refs_1_), channel_id=1, source_target_pairs={{0,1},{1,0},{2,3},{3,2},{4,5},{5,4},{6,7},{7,6},{8,9},{9,8},{10,11... | collective-permute-start | bytes 983048 | tf_op jit(solution)/shard_map/ppermute | solution.py:653
  (6 other events, 60.6 us)
where the time goes:
time: 105 us; the launch traced here: 104 us
  waiting for transfers between devices  45.1 us (43%)
  starting transfers between devices  39.6 us (38%)
  Pallas kernels  18.9 us (18%)
    ppermute x34, waiting for transfers between devices, swap(): return lax.ppermute(block, axis, [(src, src ^ bit) for src in range(size)])  45.1 us
    ppermute x34, starting transfers between devices, swap(): return lax.ppermute(block, axis, [(src, src ^ bit) for src in range(size)])  39.6 us
    pallas_call x1, Pallas kernels, encode(): pl.pallas_call(functools.partial(encode_kernel, freqs, size, rounds), in_...  7.49 us
    pallas_call x1, Pallas kernels, lower(): pl.pallas_call(functools.partial(lower_kernel, freqs, columns), in_specs=...  4.51 us
    pallas_call x1, Pallas kernels, finish(): pl.pallas_call(functools.partial(finish_kernel, lay), in_specs=[VMEM] * (...  3.02 us
  transfers between devices with their start and end apart: 34, of which 19 were waited for; matrix products, arithmetic and copies ran while one was open for 0% of the time, Pallas kernels for 6%

commit v1 on v0

--- a/solution.py
+++ b/solution.py
@@ -54,24 +54,11 @@
     return jnp.asarray(basis.reshape(2 * freqs * SUB, SUB * length), BF16)
 
 
-def encode_kernel(
-    freqs,
-    size,
-    rounds,
-    patch_hbm,
-    basis_hbm,
-    mix_hbm,
-    out_hbm,
-    in_hbm,
-    spec_hbm,
-    mixed_hbm,
-    normed_hbm,
-    *rest,
-):
+def encode_kernel(freqs, size, rounds, patch_hbm, basis_hbm, mix_hbm, out_hbm, in_hbm, *rest):
     piece_hbms, rest = rest[:size], rest[size:]
-    units_ref, unit32_ref, norm_ref, rscale_ref, *rest = rest
-    patches, basis, mix, out_w, in_w, spec, mixed, feat, normed, slope, hidden, *sems = rest
-    table_sems, patch_sems, spec_sems, mixed_sems, out_sems = sems
+    spec, mixed, normed, in_w, units_ref, unit32_ref, norm_ref, rscale_ref, *rest = rest
+    patches, basis, mix, out_w, feat, slope, hidden, *sems = rest
+    table_sems, patch_sems, out_sems = sems
     count, length, lanes = patches.shape
     filters = mix.shape[1]
     half = freqs * SUB
@@ -91,13 +78,6 @@
     def fetch(r):
         rows = pl.ds(r * per, per)
         return pltpu.make_async_copy(patch_hbm.at[rows], patches.at[rows], patch_sems.at[r])
-
-    def keep(r):
-        rows = pl.ds(r * groups, groups)
-        return (
-            pltpu.make_async_copy(spec.at[rows], spec_hbm.at[rows], spec_sems.at[r]),
-            pltpu.make_async_copy(mixed.at[rows], mixed_hbm.at[rows], mixed_sems.at[r]),
-        )
 
     tables[0].start()
     fetch(0).start()
@@ -125,8 +105,6 @@
                 feat[pl.ds(base, SUB), k * filters : (k + 1) * filters] = piece[
                     k * SUB : (k + 1) * SUB
                 ]
-        for each in keep(r):
-            each.start()
         return carry
 
     lax.fori_loop(0, rounds, one, 0)
@@ -137,7 +115,7 @@
     rscale_ref[...] = jnp.broadcast_to(rscale, rscale_ref.shape)
     deep, width, wide = piece_columns(normed.shape[1], hidden.shape[1], size)
     me = lax.axis_index("blk")
-    outs = [pltpu.make_async_copy(normed, normed_hbm, out_sems.at[0])]
+    outs = []
     for i, piece_hbm in enumerate(piece_hbms):
         columns = pl.ds(pl.multiple_of((me ^ i) * deep, 128), deep)
         outs.append(
@@ -174,9 +152,6 @@
     unit32 = raw / norms
     unit32_ref[...] = unit32
     units_ref[...] = unit32.astype(BF16)
-    for r in range(rounds):
-        for each in keep(r):
-            each.wait()
     for each in outs + late:
         each.wait()
 
@@ -197,13 +172,17 @@
     groups = count // SUB
     rows = 2 * freqs * SUB
     piece = (count, sum(piece_columns(feats, width, size)))
-    HBM = pltpu.MemorySpace.HBM
-    kept = [
-        HBM((groups, rows, lanes), BF16),
-        HBM((groups, rows, filters), F32),
-        HBM((count, feats), BF16),
-    ] + [HBM(piece, BF16)] * size
-    near = [shape((count, embed), BF16), shape((count, embed), F32)] + [shape((count, 128), F32)] * 2
+    kept = [pltpu.MemorySpace.HBM(piece, BF16)] * size
+    near = [
+        shape((groups, rows, lanes), BF16),
+        shape((groups, rows, filters), F32),
+        shape((count, feats), BF16),
+        shape(w_in.shape, BF16),
+        shape((count, embed), BF16),
+        shape((count, embed), F32),
+        shape((count, 128), F32),
+        shape((count, 128), F32),
+    ]
     return pl.pallas_call(
         functools.partial(encode_kernel, freqs, size, rounds),
         in_specs=[ANY] * 5,
@@ -214,18 +193,12 @@
             pltpu.VMEM((rows, SUB * length), BF16),
             pltpu.VMEM(w_mix.shape, BF16),
             pltpu.VMEM(w_out.shape, BF16),
-            pltpu.VMEM(w_in.shape, BF16),
-            pltpu.VMEM((groups, rows, lanes), BF16),
-            pltpu.VMEM((groups, rows, filters), F32),
             pltpu.VMEM((count, feats), F32),
-            pltpu.VMEM((count, feats), BF16),
             pltpu.VMEM((count, width), BF16),
             pltpu.VMEM((count, width), BF16),
             pltpu.SemaphoreType.DMA((4,)),
             pltpu.SemaphoreType.DMA((rounds,)),
-            pltpu.SemaphoreType.DMA((rounds,)),
-            pltpu.SemaphoreType.DMA((rounds,)),
-            pltpu.SemaphoreType.DMA((1 + 3 * size,)),
+            pltpu.SemaphoreType.DMA((3 * size,)),
         ],
         compiler_params=params(24),
         cost_estimate=cost(3e9, 14e6),
@@ -379,51 +352,34 @@
     freqs,
     columns,
     raw_ref,
-    out_w_hbm,
-    piece_hbm,
-    normed_hbm,
     rscale_ref,
-    in_hbm,
-    mixed_hbm,
-    spec_hbm,
-    g_mix_ref,
-    out_w,
-    slope,
     in_w,
     normed,
     mixed,
     spec,
+    out_w_hbm,
+    piece_hbm,
+    g_mix_ref,
+    out_w,
+    slope,
     grad_feat,
     sems,
 ):
     deep, width, _ = columns
-    sources = [
-        out_w_hbm,
-        piece_hbm.at[:, deep : deep + width],
-        in_hbm,
-        normed_hbm,
-        mixed_hbm,
-        spec_hbm,
-    ]
-    targets = [out_w, slope, in_w, normed, mixed, spec]
     loads = [
-        pltpu.make_async_copy(source, target, sems.at[i])
-        for i, (source, target) in enumerate(zip(sources, targets))
+        pltpu.make_async_copy(out_w_hbm, out_w, sems.at[0]),
+        pltpu.make_async_copy(piece_hbm.at[:, deep : deep + width], slope, sems.at[1]),
     ]
     for each in loads:
         each.start()
-    loads[0].wait()
-    loads[1].wait()
+    for each in loads:
+        each.wait()
     grad_pre = pre_grads(raw_ref[...], out_w[...], slope[...])
-    loads[2].wait()
     grad_norm = mm_nt(grad_pre, in_w[...])
-    loads[3].wait()
     xhat = normed[...].astype(F32)
     mean = jnp.mean(grad_norm, axis=1, keepdims=True)
     tilt = jnp.mean(grad_norm * xhat, axis=1, keepdims=True)
     grad_feat[...] = rscale_ref[:, :1] * (grad_norm - mean - xhat * tilt)
-    loads[4].wait()
-    loads[5].wait()
     groups, _, filters = mixed.shape
     half = freqs * SUB
 
@@ -443,28 +399,24 @@
     g_mix_ref[...] = total.T
 
 
-def lower(grad_raw, w_out, piece, normed, rscale, w_in, mixed, spec, freqs, columns):
+def lower(grad_raw, w_out, piece, normed, rscale, in_w, mixed, spec, freqs, columns):
     count, feats = normed.shape
     _, _, filters = mixed.shape
     lanes = spec.shape[2]
     return pl.pallas_call(
         functools.partial(lower_kernel, freqs, columns),
-        in_specs=[VMEM] + [ANY] * 3 + [VMEM] + [ANY] * 3,
+        in_specs=[VMEM] * 6 + [ANY] * 2,
         out_shape=shape((lanes, filters), F32),
         out_specs=VMEM,
         scratch_shapes=[
             pltpu.VMEM(w_out.shape, BF16),
             pltpu.VMEM((count, columns[1]), BF16),
-            pltpu.VMEM(w_in.shape, BF16),
-            pltpu.VMEM((count, feats), BF16),
-            pltpu.VMEM(mixed.shape, F32),
-            pltpu.VMEM(spec.shape, BF16),
             pltpu.VMEM((count, feats), F32),
-            pltpu.SemaphoreType.DMA((6,)),
+            pltpu.SemaphoreType.DMA((2,)),
         ],
         compiler_params=params(20),
         cost_estimate=cost(1e9, 7e6),
-    )(grad_raw, *map(hbm, (w_out, piece, normed)), rscale, *map(hbm, (w_in, mixed, spec)))
+    )(grad_raw, rscale, in_w, normed, mixed, spec, hbm(w_out), hbm(piece))
 
 
 def up_to(rows, unit):
@@ -576,58 +528,77 @@
     )(own, *got)
 
 
-def finish_kernel(lay, *refs):
-    size, slots = lay.size, lay.peers // 2
-    evens, odds = refs[:size], refs[size : 2 * size]
-    g_mix_ref, g_in_hbm, g_out_ref, stage, sems = refs[2 * size :]
+def finish_kernel(lay, parts, done, closing, *refs):
+    slots = lay.peers // 2
+    part_refs, refs = dict(zip(parts, refs)), refs[len(parts) :]
+    if done:
+        refs = refs[2:]
+    g_in_hbm, g_out_hbm, *refs = refs
+    if closing:
+        g_mix_ref, *refs = refs
+    stage, strip_stage, sems, strip_sems = refs
     me_blk, me_dp = lax.axis_index("blk"), lax.axis_index("dp")
     copies = []
-    for i in range(size):
-        for core, source in enumerate((evens[i], odds[i])):
-            for z in range(slots):
-                at = z * lay.rows
-                owner = me_dp ^ (2 * z + core)
-                slot = (i * 2 + core) * slots + z
-                stage[slot] = source[at : at + lay.in_rows, :].astype(F32)
-                row = ((me_blk ^ i) * lay.peers + owner) * lay.in_rows
+    slot = 0
+    for (hop, core, half), source in part_refs.items():
+        if closing and (hop, core, half) not in closing:
+            continue
+        for z in range(slots // 2):
+            at = z * lay.rows
+            owner = (me_blk ^ hop) * lay.peers + (me_dp ^ (half * slots + 2 * z + core))
+            stage[slot] = source[at : at + lay.in_rows, :].astype(F32)
+            strip = at + lay.top
+            strip_stage[slot] = source[strip : strip + lay.out_rows, :128].astype(F32)
+            for kept, target, rows, sem in (
+                (stage, g_in_hbm, lay.in_rows, sems),
+                (strip_stage, g_out_hbm, lay.out_rows, strip_sems),
+            ):
                 copy = pltpu.make_async_copy(
-                    stage.at[slot], g_in_hbm.at[pl.ds(row, lay.in_rows), :], sems.at[slot]
+                    kept.at[slot], target.at[pl.ds(owner * rows, rows), :], sem.at[slot]
                 )
                 copy.start()
                 copies.append(copy)
-                row = ((me_blk ^ i) * lay.peers + owner) * lay.out_rows
-                strip = at + lay.top
-                g_out_ref[pl.ds(row, lay.out_rows), :] = source[
-                    strip : strip + lay.out_rows, :128
-                ].astype(F32)
-    for core in range(2):
-        for z in range(slots):
-            strip = z * lay.rows + lay.top
-            owner = me_dp ^ (2 * z + core)
-            for start, rows, cols in lay.mix_parts():
-                blocks = {0: evens, 1: odds}[core]
-                terms = [blocks[i][strip : strip + rows, cols].astype(F32) for i in range(size)]
-                while len(terms) > 1:
-                    terms = [terms[t] + terms[t + 1] for t in range(0, len(terms), 2)]
-                g_mix_ref[pl.ds(owner * lay.mix_rows + start, rows), :] = terms[0]
+            slot += 1
+    if closing:
+        for core in range(2):
+            for half in range(2):
+                for z in range(slots // 2):
+                    strip = z * lay.rows + lay.top
+                    owner = me_dp ^ (half * slots + 2 * z + core)
+                    for start, rows, cols in lay.mix_parts():
+                        terms = [
+                            part_refs[hop, core, half][strip : strip + rows, cols].astype(F32)
+                            for hop in range(lay.size)
+                        ]
+                        while len(terms) > 1:
+                            terms = [terms[t] + terms[t + 1] for t in range(0, len(terms), 2)]
+                        g_mix_ref[pl.ds(owner * lay.mix_rows + start, rows), :] = terms[0]
     for copy in copies:
         copy.wait()
 
 
-def finish(lay, evens, odds, lanes, feats, width):
-    slots = lay.size * lay.peers
-    return pl.pallas_call(
-        functools.partial(finish_kernel, lay),
-        in_specs=[VMEM] * (2 * lay.size),
-        out_shape=[shape((lanes, 128), F32), shape((feats, width), F32), shape((width, 128), F32)],
-        out_specs=[VMEM, ANY, VMEM],
+def finish(lay, parts, done, closing, lanes, feats, width):
+    slots = (len(closing) if closing else len(parts)) * lay.peers // 4
+    outs = [shape((feats, width), F32), shape((width, 128), F32)]
+    specs = [ANY, ANY]
+    if closing:
+        outs.append(shape((lanes, 128), F32))
+        specs.append(VMEM)
+    return pl.pallas_call(
+        functools.partial(finish_kernel, lay, tuple(parts), bool(done), closing),
+        in_specs=[VMEM] * len(parts) + [ANY] * len(done),
+        out_shape=outs,
+        out_specs=specs,
         scratch_shapes=[
             pltpu.VMEM((slots, lay.in_rows, lay.width), F32),
+            pltpu.VMEM((slots, lay.out_rows, 128), F32),
+            pltpu.SemaphoreType.DMA((slots,)),
             pltpu.SemaphoreType.DMA((slots,)),
         ],
+        input_output_aliases={len(parts) + i: i for i in range(len(done))},
         compiler_params=params(24),
         cost_estimate=cost(1e6, 8e6),
-    )(*evens, *odds)
+    )(*parts.values(), *done)
 
 
 def stack_kernel(*refs):
@@ -669,8 +640,9 @@
     columns = piece_columns(feats, width, size)
     lay = Layout(lanes, filters, feats, width, embed, size, peers)
 
-    spec, mixed, normed, *rest = encode(patches, w_mix, w_in, w_out, size)
-    early, (units, unit32, norms, rscale) = rest[:size], rest[size:]
+    *early, spec, mixed, normed, in_w, units, unit32, norms, rscale = encode(
+        patches, w_mix, w_in, w_out, size
+    )
     stacked = spread(units, "dp", along)
     pieces = spread(units, "blk", across)
     pieces[1:], stacked[1:] = lax.optimization_barrier((pieces[1:], stacked[1:]))
@@ -685,16 +657,39 @@
     odd_stats = swap(even_stats, "dp", 1)
     grad_raw = upper(pieces, group_stats, even, odd, even_stats, odd_stats, local, unit32, norms)
     raws = spread(grad_raw, "blk", across)
-    g_mix = lower(grad_raw, w_out, early[0], normed, rscale, w_in, mixed, spec, freqs, columns)
+    g_mix = lower(grad_raw, w_out, early[0], normed, rscale, in_w, mixed, spec, freqs, columns)
     keep, away = weight_grads(lay, columns, factors, raws, w_out, g_mix)
     got = swap(away, "dp", 1)
     own, *sends = pair_sum(keep, got)
     got = [swap(block, "dp", hop) for block, hop in zip(sends, along)]
     share = total_sum(own, got)
-    plane = stack(spread(share, "dp", along))
-    evens = spread(plane, "blk", across)
-    odds = [swap(block, "dp", 1) for block in evens]
-    g_mix, g_in, g_out = finish(lay, evens, odds, lanes, feats, width)
+    shares = spread(share, "dp", along)
+    middle = len(shares) // 2
+    planes = {(0, 0): stack(shares[:middle]), (0, 1): stack(shares[middle:])}
+    single = [hop for hop in across if hop & (hop - 1) == 0]
+    several = [hop for hop in across if hop & (hop - 1)]
+    for turn in range(2):
+        for k, hop in enumerate(single):
+            half = (k + turn) % 2
+            planes[hop, half] = swap(planes[0, half], "blk", hop)
+    for hop in several:
+        low, high = hop & -hop, 1 << (hop.bit_length() - 1)
+        planes[hop, 0] = swap(planes[hop ^ high, 0], "blk", high)
+        planes[hop, 1] = swap(planes[hop ^ low, 1], "blk", low)
+    parts, done = {}, []
+    groups = [group for group in ([0], single, several) if group]
+    for order, group in enumerate(groups):
+        fresh = {}
+        for hop in group:
+            for half in range(2):
+                fresh[hop, 0, half] = planes[hop, half]
+                fresh[hop, 1, half] = swap(planes[hop, half], "dp", 1)
+        parts.update(fresh)
+        last = order == len(groups) - 1
+        done = finish(
+            lay, parts if last else fresh, done, tuple(fresh) if last else (), lanes, feats, width
+        )
+    g_in, g_out, g_mix = done
     return (loss.reshape(count), g_mix, g_in, g_out)
 
 

time: 105 us -> 103 us (0.981)
  waiting for transfers between devices: 45.1 us -> 41.5 us
    ppermute x34 -> x41, waiting for transfers between devices: 45.1 us -> 41.5 us  [swap(): return lax.ppermute(block, axis, [(src, src ^ bit) for src in range(size)])]
    pallas_call x1 -> x3, Pallas kernels: 3.02 us -> 4.6 us  [finish(): pl.pallas_call(functools.partial(finish_kernel, lay, tuple(parts), bool(d...]
    pallas_call x1, Pallas kernels: 4.51 us -> 3.36 us  [lower(): pl.pallas_call(functools.partial(lower_kernel, freqs, columns), in_specs=...]
    ppermute x34 -> x41, starting transfers between devices: 39.6 us -> 40.6 us  [swap(): return lax.ppermute(block, axis, [(src, src ^ bit) for src in range(size)])]
  transfers between devices with their start and end apart: 34 -> 41, of which waited for: 19 -> 19; matrix products, arithmetic and copies ran while one was open for 0% -> 0% of each run, Pallas kernels for 6% -> 8%
where the time goes in v1:
time: 103 us
  waiting for transfers between devices  41.5 us (40%)
  starting transfers between devices  40.6 us (39%)
  Pallas kernels  19.6 us (19%)
    ppermute x41, waiting for transfers between devices, swap(): return lax.ppermute(block, axis, [(src, src ^ bit) for src in range(size)])  41.5 us
    ppermute x41, starting transfers between devices, swap(): return lax.ppermute(block, axis, [(src, src ^ bit) for src in range(size)])  40.6 us
    pallas_call x1, Pallas kernels, encode(): pl.pallas_call(functools.partial(encode_kernel, freqs, size, rounds), in_...  7.72 us
    pallas_call x3, Pallas kernels, finish(): pl.pallas_call(functools.partial(finish_kernel, lay, tuple(parts), bool(d...  4.6 us
    pallas_call x1, Pallas kernels, lower(): pl.pallas_call(functools.partial(lower_kernel, freqs, columns), in_specs=...  3.36 us
  transfers between devices with their start and end apart: 41, of which 19 were waited for; matrix products, arithmetic and copies ran while one was open for 0% of the time, Pallas kernels for 8%

profile of v1, /device:TPU:0, one launch (start us, length us, event | category | flops | bytes accessed | tf_op | source)
XLA Modules:
  0.0 102.6 jit_solution(12494302912542275650)
XLA Ops:
  0.7 7.7 %shard_map.102 = (bf16[128,1152]{1,0:T(8,128)(2,1)}, bf16[128,1152]{1,0:T(8,128)(2,1)}, bf16[128,1152]{1,0:T(8,128)(2,1)}, bf16[128,1152]{1,0:T(8,128)(2,1)}, bf...) custom-call(bf16[128,64,256]{2,1,0:T(8,128)(2,1)} %patch_hbm.1, ...), custom_call_target="tpu_custom_call" | custom-call | flops 3000000000 | bytes 14000000 | tf_op jit(solution)/shard_map/pallas_call | solution.py:186
  8.4 5.1 %collective-permute-start.5 = (bf16[128,128]{1,0:T(8,128)(2,1)S(1)}, bf16[128,128]{1,0:T(8,128)(2,1)S(1)}, u32[]{:S(2)}, u32[]{:S(2)}) collective-permute-start(bf16[128,128]{1,0:T(8,128)(2,1)S(1)} %get-tuple-element.47.refs_0_), channel_id=1, source_target_pairs={{0,6},{1,7},{2,4},{3,5},{4,2},{5,3},{6,0},{7,1},{8,14},{9,15},{10,... | collective-permute-start | bytes 98312 | tf_op jit(solution)/shard_map/ppermute | solution.py:624
  14.2 2.6 %collective-permute-start.2 = (bf16[128,128]{1,0:T(8,128)(2,1)S(1)}, bf16[128,128]{1,0:T(8,128)(2,1)S(1)}, u32[]{:S(2)}, u32[]{:S(2)}) collective-permute-start(bf16[128,128]{1,0:T(8,128)(2,1)S(1)} %get-tuple-element.47.refs_0_), channel_id=1, source_target_pairs={{0,24},{8,16},{16,8},{24,0},{1,25},{9,17},{17,9},{25,1},{2,26},{10... | collective-permute-start | bytes 98312 | tf_op jit(solution)/shard_map/ppermute | solution.py:624
  19.0 1.7 %collective-permute-done.1.refs_2_ = bf16[128,128]{1,0:T(8,128)(2,1)S(1)} collective-permute-done((bf16[128,128]{1,0:T(8,128)(2,1)S(1)}, bf16[128,128]{1,0:T(8,128)(2,1)S(1)}, u32[]{:S(2)}, u32[]{:S(2)}) %collective-permute-start.1) | collective-permute-done | bytes 32800 | tf_op jit(solution)/shard_map/ppermute | solution.py:624
  22.1 1.7 %collective-permute-start.8 = (bf16[128,1152]{1,0:T(8,128)(2,1)}, bf16[128,1152]{1,0:T(8,128)(2,1)S(1)}, u32[]{:S(2)}, u32[]{:S(2)}) collective-permute-start(bf16[128,1152]{1,0:T(8,128)(2,1)} %get-tuple-element.60), channel_id=1, source_target_pairs={{0,16},{8,24},{16,0},{24,8},{1,17},{9,25},{17,1},{25,9},{2,18},{10... | collective-permute-start | bytes 884744 | tf_op jit(solution)/shard_map/ppermute | solution.py:624
  23.7 1.4 %collective-permute-start.9 = (bf16[128,1152]{1,0:T(8,128)(2,1)}, bf16[128,1152]{1,0:T(8,128)(2,1)S(1)}, u32[]{:S(2)}, u32[]{:S(2)}) collective-permute-start(bf16[128,1152]{1,0:T(8,128)(2,1)} %get-tuple-element.61), channel_id=1, source_target_pairs={{0,24},{8,16},{16,8},{24,0},{1,25},{9,17},{17,9},{25,1},{2,26},{10... | collective-permute-start | bytes 884744 | tf_op jit(solution)/shard_map/ppermute | solution.py:624
  26.3 1.5 %collective-permute-start.15 = (f32[8,128]{1,0:T(8,128)S(1)}, f32[8,128]{1,0:T(8,128)S(1)}, u32[]{:S(2)}, u32[]{:S(2)}) collective-permute-start(f32[8,128]{1,0:T(8,128)S(1)} %get-tuple-element.62.refs_0_.refs_4_), channel_id=1, source_target_pairs={{0,24},{8,16},{16,8},{24,0},{1,25},{9,17},{17,9},{25,1},{2,26},{10... | collective-permute-start | bytes 12296 | tf_op jit(solution)/shard_map/ppermute | solution.py:624
  28.2 10.5 %collective-permute-done.15.refs_7_ = f32[8,128]{1,0:T(8,128)S(1)} collective-permute-done((f32[8,128]{1,0:T(8,128)S(1)}, f32[8,128]{1,0:T(8,128)S(1)}, u32[]{:S(2)}, u32[]{:S(2)}) %collective-permute-start.15) | collective-permute-done | bytes 4128 | tf_op jit(solution)/shard_map/ppermute | solution.py:624
  39.2 3.6 %collective-permute-start.12 = (f32[8,128]{1,0:T(8,128)S(1)}, f32[8,128]{1,0:T(8,128)S(1)}, u32[]{:S(2)}, u32[]{:S(2)}) collective-permute-start(f32[8,128]{1,0:T(8,128)S(1)} %get-tuple-element.62.refs_0_.refs_4_), channel_id=1, source_target_pairs={{0,6},{1,7},{2,4},{3,5},{4,2},{5,3},{6,0},{7,1},{8,14},{9,15},{10,... | collective-permute-start | bytes 12296 | tf_op jit(solution)/shard_map/ppermute | solution.py:624
  42.9 1.5 %collective-permute-start.11 = (f32[8,128]{1,0:T(8,128)S(1)}, f32[8,128]{1,0:T(8,128)S(1)}, u32[]{:S(2)}, u32[]{:S(2)}) collective-permute-start(f32[8,128]{1,0:T(8,128)S(1)} %get-tuple-element.62.refs_0_.refs_4_), channel_id=1, source_target_pairs={{0,4},{1,5},{2,6},{3,7},{4,0},{5,1},{6,2},{7,3},{8,12},{9,13},{10,... | collective-permute-start | bytes 12296 | tf_op jit(solution)/shard_map/ppermute | solution.py:624
  44.7 1.7 %collective-permute-start.10 = (f32[8,128]{1,0:T(8,128)S(1)}, f32[8,128]{1,0:T(8,128)S(1)}, u32[]{:S(2)}, u32[]{:S(2)}) collective-permute-start(f32[8,128]{1,0:T(8,128)S(1)} %get-tuple-element.62.refs_0_.refs_4_), channel_id=1, source_target_pairs={{0,2},{1,3},{2,0},{3,1},{4,6},{5,7},{6,4},{7,5},{8,10},{9,11},{10,... | collective-permute-start | bytes 12296 | tf_op jit(solution)/shard_map/ppermute | solution.py:624
  48.3 1.2 %collective-permute-done.16.refs_11_ = f32[32,128]{1,0:T(8,128)S(1)} collective-permute-done((f32[32,128]{1,0:T(8,128)S(1)}, f32[32,128]{1,0:T(8,128)S(1)}, u32[]{:S(2)}, u32[]{:S(2)}) %collective-permute-start.16) | collective-permute-done | bytes 16416 | tf_op jit(solution)/shard_map/ppermute | solution.py:624
  50.3 1.5 %collective-permute-start.19 = (bf16[128,128]{1,0:T(8,128)(2,1)S(1)}, bf16[128,128]{1,0:T(8,128)(2,1)S(1)}, u32[]{:S(2)}, u32[]{:S(2)}) collective-permute-start(bf16[128,128]{1,0:T(8,128)(2,1)S(1)} %shard_map.106.raw_ref.refs_4_), channel_id=1, source_target_pairs={{0,24},{8,16},{16,8},{24,0},{1,25},{9,17},{17,9},{25,1},{2,26},{10... | collective-permute-start | bytes 98312 | tf_op jit(solution)/shard_map/ppermute | solution.py:624
  51.8 1.4 %collective-permute-start.18 = (bf16[128,128]{1,0:T(8,128)(2,1)S(1)}, bf16[128,128]{1,0:T(8,128)(2,1)S(1)}, u32[]{:S(2)}, u32[]{:S(2)}) collective-permute-start(bf16[128,128]{1,0:T(8,128)(2,1)S(1)} %shard_map.106.raw_ref.refs_4_), channel_id=1, source_target_pairs={{0,16},{8,24},{16,0},{24,8},{1,17},{9,25},{17,1},{25,9},{2,18},{10... | collective-permute-start | bytes 98312 | tf_op jit(solution)/shard_map/ppermute | solution.py:624
  53.2 2.0 %collective-permute-done.19.refs_7_ = bf16[128,128]{1,0:T(8,128)(2,1)S(1)} collective-permute-done((bf16[128,128]{1,0:T(8,128)(2,1)S(1)}, bf16[128,128]{1,0:T(8,128)(2,1)S(1)}, u32[]{:S(2)}, u32[]{:S(2)}) %collective-permute-start.19) | collective-permute-done | bytes 32800 | tf_op jit(solution)/shard_map/ppermute | solution.py:624
  55.1 1.4 %collective-permute-start.17 = (bf16[128,128]{1,0:T(8,128)(2,1)S(1)}, bf16[128,128]{1,0:T(8,128)(2,1)S(1)}, u32[]{:S(2)}, u32[]{:S(2)}) collective-permute-start(bf16[128,128]{1,0:T(8,128)(2,1)S(1)} %shard_map.106.raw_ref.refs_4_), channel_id=1, source_target_pairs={{0,8},{8,0},{16,24},{24,16},{1,9},{9,1},{17,25},{25,17},{2,10},{10... | collective-permute-start | bytes 98312 | tf_op jit(solution)/shard_map/ppermute | solution.py:624
  56.5 3.4 %shard_map.107.refs_9_ = f32[256,128]{1,0:T(8,128)S(1)} custom-call(bf16[128,128]{1,0:T(8,128)(2,1)S(1)} %shard_map.106.raw_ref.refs_4_, f32[128,128]{1,0:T(8,128)S(1)} %get-tuple-element.72.rscale_ref, bf16[2048,512]{1,0:T(8,128)(2,1)S(1)} %get-tuple-element.73.in_w, bf16[128,2048]{1,0:T(8,128)(2,1)S(1)} %get-tuple-element.74.normed, ...), custom_call_target="tpu_custom_call" | custom-call | flops 1000000000 | bytes 7000000 | tf_op jit(solution)/shard_map/pallas_call | solution.py:406
  60.0 1.5 %shard_map.108 = (f32[4,80,512]{2,1,0:T(8,128)S(1)}, bf16[4,80,512]{2,1,0:T(8,128)(2,1)S(1)}) custom-call(bf16[128,1152]{1,0:T(8,128)(2,1)S(1)} %copy-done, bf16[128,1152]{1,0:T(8,128)(2,1)S(1)} %collective-permute-done.7.refs_1_, bf16[128,1152]{1,0:T(8,128)(2,1)S(1)} %collective-permute-done.8.refs_2_, ...), custom_call_target="tpu_custom_call" | custom-call | flops 600000000 | bytes 4000000 | tf_op jit(solution)/shard_map/pallas_call | solution.py:484
  61.5 1.6 %collective-permute-done.20.got_ref = bf16[4,80,512]{2,1,0:T(8,128)(2,1)S(1)} collective-permute-done((bf16[4,80,512]{2,1,0:T(8,128)(2,1)S(1)}, bf16[4,80,512]{2,1,0:T(8,128)(2,1)S(1)}, u32[]{:S(2)}, u32[]{:S(2)}) %collective-permute-start.20) | collective-permute-done | bytes 327712 | tf_op jit(solution)/shard_map/ppermute | solution.py:624
  64.3 3.2 %collective-permute-start.22 = (bf16[80,512]{1,0:T(8,128)(2,1)S(1)}, bf16[80,512]{1,0:T(8,128)(2,1)S(1)}, u32[]{:S(2)}, u32[]{:S(2)}) collective-permute-start(bf16[80,512]{1,0:T(8,128)(2,1)S(1)} %get-tuple-element.81), channel_id=1, source_target_pairs={{0,4},{1,5},{2,6},{3,7},{4,0},{5,1},{6,2},{7,3},{8,12},{9,13},{10,... | collective-permute-start | bytes 245768 | tf_op jit(solution)/shard_map/ppermute | solution.py:624
  67.8 6.4 %collective-permute-done.22.refs_1_ = bf16[80,512]{1,0:T(8,128)(2,1)S(1)} collective-permute-done((bf16[80,512]{1,0:T(8,128)(2,1)S(1)}, bf16[80,512]{1,0:T(8,128)(2,1)S(1)}, u32[]{:S(2)}, u32[]{:S(2)}) %collective-permute-start.22) | collective-permute-done | bytes 81952 | tf_op jit(solution)/shard_map/ppermute | solution.py:624
  74.2 1.7 %collective-permute-start.24 = (bf16[80,512]{1,0:T(8,128)(2,1)S(1)}, bf16[80,512]{1,0:T(8,128)(2,1)S(1)}, u32[]{:S(2)}, u32[]{:S(2)}) collective-permute-start(bf16[80,512]{1,0:T(8,128)(2,1)S(1)} %shard_map.110.refs_0_), channel_id=1, source_target_pairs={{0,2},{1,3},{2,0},{3,1},{4,6},{5,7},{6,4},{7,5},{8,10},{9,11},{10,... | collective-permute-start | bytes 245768 | tf_op jit(solution)/shard_map/ppermute | solution.py:624
  75.9 2.4 %collective-permute-start.27 = (bf16[80,512]{1,0:T(8,128)(2,1)S(1)}, bf16[80,512]{1,0:T(8,128)(2,1)S(1)}, u32[]{:S(2)}, u32[]{:S(2)}) collective-permute-start(bf16[80,512]{1,0:T(8,128)(2,1)S(1)} %shard_map.110.refs_0_), channel_id=1, source_target_pairs={{0,6},{1,7},{2,4},{3,5},{4,2},{5,3},{6,0},{7,1},{8,14},{9,15},{10,... | collective-permute-start | bytes 245768 | tf_op jit(solution)/shard_map/ppermute | solution.py:624
  80.4 2.6 %collective-permute-done.27.refs_1_ = bf16[80,512]{1,0:T(8,128)(2,1)S(1)} collective-permute-done((bf16[80,512]{1,0:T(8,128)(2,1)S(1)}, bf16[80,512]{1,0:T(8,128)(2,1)S(1)}, u32[]{:S(2)}, u32[]{:S(2)}) %collective-permute-start.27) | collective-permute-done | bytes 81952 | tf_op jit(solution)/shard_map/ppermute | solution.py:624
  83.0 2.4 %collective-permute-done.26.refs_0_ = bf16[80,512]{1,0:T(8,128)(2,1)S(1)} collective-permute-done((bf16[80,512]{1,0:T(8,128)(2,1)S(1)}, bf16[80,512]{1,0:T(8,128)(2,1)S(1)}, u32[]{:S(2)}, u32[]{:S(2)}) %collective-permute-start.26) | collective-permute-done | bytes 81952 | tf_op jit(solution)/shard_map/ppermute | solution.py:624
  87.4 1.1 %collective-permute-start.37 = (bf16[160,512]{1,0:T(8,128)(2,1)S(1)}, bf16[160,512]{1,0:T(8,128)(2,1)S(1)}, u32[]{:S(2)}, u32[]{:S(2)}) collective-permute-start(bf16[160,512]{1,0:T(8,128)(2,1)S(1)} %collective-permute-done.29.refs_0_.refs_4_), channel_id=1, source_target_pairs={{0,16},{8,24},{16,0},{24,8},{1,17},{9,25},{17,1},{25,9},{2,18},{10... | collective-permute-start | bytes 491528 | tf_op jit(solution)/shard_map/ppermute | solution.py:624
  88.5 4.0 %collective-permute-done.35.refs_6_.refs_10_ = bf16[160,512]{1,0:T(8,128)(2,1)S(1)} collective-permute-done((bf16[160,512]{1,0:T(8,128)(2,1)S(1)}, bf16[160,512]{1,0:T(8,128)(2,1)S(1)}, u32[]{:S(2)}, u32[]{:S(2)}) %collective-permute-start.35) | collective-permute-done | bytes 163872 | tf_op jit(solution)/shard_map/ppermute | solution.py:624
  93.2 1.7 %collective-permute-done.37.refs_12_ = bf16[160,512]{1,0:T(8,128)(2,1)S(1)} collective-permute-done((bf16[160,512]{1,0:T(8,128)(2,1)S(1)}, bf16[160,512]{1,0:T(8,128)(2,1)S(1)}, u32[]{:S(2)}, u32[]{:S(2)}) %collective-permute-start.37) | collective-permute-done | bytes 163872 | tf_op jit(solution)/shard_map/ppermute | solution.py:624
  94.9 3.0 %collective-permute-done.39.refs_14_ = bf16[160,512]{1,0:T(8,128)(2,1)S(1)} collective-permute-done((bf16[160,512]{1,0:T(8,128)(2,1)S(1)}, bf16[160,512]{1,0:T(8,128)(2,1)S(1)}, u32[]{:S(2)}, u32[]{:S(2)}) %collective-permute-start.39) | collective-permute-done | bytes 163872 | tf_op jit(solution)/shard_map/ppermute | solution.py:624
  97.9 1.1 %shard_map.113 = (f32[2048,512]{1,0:T(8,128)}, f32[512,128]{1,0:T(8,128)}) custom-call(bf16[160,512]{1,0:T(8,128)(2,1)S(1)} %shard_map.111.refs_0_, bf16[160,512]{1,0:T(8,128)(2,1)S(1)} %collective-permute-done.25.refs_1_, bf16[160,512]{1,0:T(8,128)(2,1)S(1)} %shard_map.112.refs_2_, bf16[160,512]{1,0:T(8,128)(2,1)S(1)} %collective-permute-done.28.refs_3_), custom_call_target="tpu_custom_call" | custom-call | flops 1000000 | bytes 8000000 | tf_op jit(solution)/shard_map/pallas_call | solution.py:587
  99.1 1.7 %shard_map.114 = (f32[2048,512]{1,0:T(8,128)}, f32[512,128]{1,0:T(8,128)}) custom-call(bf16[160,512]{1,0:T(8,128)(2,1)S(1)} %collective-permute-done.29.refs_0_.refs_4_, bf16[160,512]{1,0:T(8,128)(2,1)S(1)} %collective-permute-done.30.refs_1_.refs_5_, ...), custom_call_target="tpu_custom_call", output_to_operand_aliasing={{0}: (8, {}), {1}: (9, {})} | custom-call | flops 1000000 | bytes 8000000 | tf_op jit(solution)/shard_map/pallas_call | solution.py:587
  100.7 1.8 %shard_map.115 = (f32[2048,512]{1,0:T(8,128)}, f32[512,128]{1,0:T(8,128)}, f32[256,128]{1,0:T(8,128)}) custom-call(bf16[160,512]{1,0:T(8,128)(2,1)S(1)} %shard_map.111.refs_0_, bf16[160,512]{1,0:T(8,128)(2,1)S(1)} %collective-permute-done.25.refs_1_, bf16[160,512]{1,0:T(8,128)(2,1)S(1)} %shard_map.112.refs_2_, ...), custom_call_target="tpu_custom_call", output_to_operand_aliasing={{0}: (16, {}), {1}: (17, {})} | custom-call | flops 1000000 | bytes 8000000 | tf_op jit(solution)/shard_map/pallas_call | solution.py:587
  (72 shorter events, 15.5 us)
Async XLA Ops:
  8.4 8.9 %collective-permute-start.5 = (bf16[128,128]{1,0:T(8,128)(2,1)S(1)}, bf16[128,128]{1,0:T(8,128)(2,1)S(1)}, u32[]{:S(2)}, u32[]{:S(2)}) collective-permute-start(bf16[128,128]{1,0:T(8,128)(2,1)S(1)} %get-tuple-element.47.refs_0_), channel_id=1, source_target_pairs={{0,6},{1,7},{2,4},{3,5},{4,2},{5,3},{6,0},{7,1},{8,14},{9,15},{10,... | collective-permute-start | bytes 98312 | tf_op jit(solution)/shard_map/ppermute | solution.py:624
  13.5 4.8 %collective-permute-start.4 = (bf16[128,128]{1,0:T(8,128)(2,1)S(1)}, bf16[128,128]{1,0:T(8,128)(2,1)S(1)}, u32[]{:S(2)}, u32[]{:S(2)}) collective-permute-start(bf16[128,128]{1,0:T(8,128)(2,1)S(1)} %get-tuple-element.47.refs_0_), channel_id=1, source_target_pairs={{0,4},{1,5},{2,6},{3,7},{4,0},{5,1},{6,2},{7,3},{8,12},{9,13},{10,... | collective-permute-start | bytes 98312 | tf_op jit(solution)/shard_map/ppermute | solution.py:624
  13.5 4.8 %collective-permute-start.3 = (bf16[128,128]{1,0:T(8,128)(2,1)S(1)}, bf16[128,128]{1,0:T(8,128)(2,1)S(1)}, u32[]{:S(2)}, u32[]{:S(2)}) collective-permute-start(bf16[128,128]{1,0:T(8,128)(2,1)S(1)} %get-tuple-element.47.refs_0_), channel_id=1, source_target_pairs={{0,2},{1,3},{2,0},{3,1},{4,6},{5,7},{6,4},{7,5},{8,10},{9,11},{10,... | collective-permute-start | bytes 98312 | tf_op jit(solution)/shard_map/ppermute | solution.py:624
  14.2 4.8 %collective-permute-start.2 = (bf16[128,128]{1,0:T(8,128)(2,1)S(1)}, bf16[128,128]{1,0:T(8,128)(2,1)S(1)}, u32[]{:S(2)}, u32[]{:S(2)}) collective-permute-start(bf16[128,128]{1,0:T(8,128)(2,1)S(1)} %get-tuple-element.47.refs_0_), channel_id=1, source_target_pairs={{0,24},{8,16},{16,8},{24,0},{1,25},{9,17},{17,9},{25,1},{2,26},{10... | collective-permute-start | bytes 98312 | tf_op jit(solution)/shard_map/ppermute | solution.py:624
  21.6 38.3 %collective-permute-start.7 = (bf16[128,1152]{1,0:T(8,128)(2,1)}, bf16[128,1152]{1,0:T(8,128)(2,1)S(1)}, u32[]{:S(2)}, u32[]{:S(2)}) collective-permute-start(bf16[128,1152]{1,0:T(8,128)(2,1)} %get-tuple-element.59), channel_id=1, source_target_pairs={{0,8},{8,0},{16,24},{24,16},{1,9},{9,1},{17,25},{25,17},{2,10},{10... | collective-permute-start | bytes 884744 | tf_op jit(solution)/shard_map/ppermute | solution.py:624
  22.1 37.8 %collective-permute-start.8 = (bf16[128,1152]{1,0:T(8,128)(2,1)}, bf16[128,1152]{1,0:T(8,128)(2,1)S(1)}, u32[]{:S(2)}, u32[]{:S(2)}) collective-permute-start(bf16[128,1152]{1,0:T(8,128)(2,1)} %get-tuple-element.60), channel_id=1, source_target_pairs={{0,16},{8,24},{16,0},{24,8},{1,17},{9,25},{17,1},{25,9},{2,18},{10... | collective-permute-start | bytes 884744 | tf_op jit(solution)/shard_map/ppermute | solution.py:624
  23.7 36.2 %collective-permute-start.9 = (bf16[128,1152]{1,0:T(8,128)(2,1)}, bf16[128,1152]{1,0:T(8,128)(2,1)S(1)}, u32[]{:S(2)}, u32[]{:S(2)}) collective-permute-start(bf16[128,1152]{1,0:T(8,128)(2,1)} %get-tuple-element.61), channel_id=1, source_target_pairs={{0,24},{8,16},{16,8},{24,0},{1,25},{9,17},{17,9},{25,1},{2,26},{10... | collective-permute-start | bytes 884744 | tf_op jit(solution)/shard_map/ppermute | solution.py:624
  26.3 12.3 %collective-permute-start.15 = (f32[8,128]{1,0:T(8,128)S(1)}, f32[8,128]{1,0:T(8,128)S(1)}, u32[]{:S(2)}, u32[]{:S(2)}) collective-permute-start(f32[8,128]{1,0:T(8,128)S(1)} %get-tuple-element.62.refs_0_.refs_4_), channel_id=1, source_target_pairs={{0,24},{8,16},{16,8},{24,0},{1,25},{9,17},{17,9},{25,1},{2,26},{10... | collective-permute-start | bytes 12296 | tf_op jit(solution)/shard_map/ppermute | solution.py:624
  27.8 11.5 %collective-permute-start.14 = (f32[8,128]{1,0:T(8,128)S(1)}, f32[8,128]{1,0:T(8,128)S(1)}, u32[]{:S(2)}, u32[]{:S(2)}) collective-permute-start(f32[8,128]{1,0:T(8,128)S(1)} %get-tuple-element.62.refs_0_.refs_4_), channel_id=1, source_target_pairs={{0,16},{8,24},{16,0},{24,8},{1,17},{9,25},{17,1},{25,9},{2,18},{10... | collective-permute-start | bytes 12296 | tf_op jit(solution)/shard_map/ppermute | solution.py:624
  39.2 5.4 %collective-permute-start.12 = (f32[8,128]{1,0:T(8,128)S(1)}, f32[8,128]{1,0:T(8,128)S(1)}, u32[]{:S(2)}, u32[]{:S(2)}) collective-permute-start(f32[8,128]{1,0:T(8,128)S(1)} %get-tuple-element.62.refs_0_.refs_4_), channel_id=1, source_target_pairs={{0,6},{1,7},{2,4},{3,5},{4,2},{5,3},{6,0},{7,1},{8,14},{9,15},{10,... | collective-permute-start | bytes 12296 | tf_op jit(solution)/shard_map/ppermute | solution.py:624
  42.9 4.5 %collective-permute-start.11 = (f32[8,128]{1,0:T(8,128)S(1)}, f32[8,128]{1,0:T(8,128)S(1)}, u32[]{:S(2)}, u32[]{:S(2)}) collective-permute-start(f32[8,128]{1,0:T(8,128)S(1)} %get-tuple-element.62.refs_0_.refs_4_), channel_id=1, source_target_pairs={{0,4},{1,5},{2,6},{3,7},{4,0},{5,1},{6,2},{7,3},{8,12},{9,13},{10,... | collective-permute-start | bytes 12296 | tf_op jit(solution)/shard_map/ppermute | solution.py:624
  50.3 4.9 %collective-permute-start.19 = (bf16[128,128]{1,0:T(8,128)(2,1)S(1)}, bf16[128,128]{1,0:T(8,128)(2,1)S(1)}, u32[]{:S(2)}, u32[]{:S(2)}) collective-permute-start(bf16[128,128]{1,0:T(8,128)(2,1)S(1)} %shard_map.106.raw_ref.refs_4_), channel_id=1, source_target_pairs={{0,24},{8,16},{16,8},{24,0},{1,25},{9,17},{17,9},{25,1},{2,26},{10... | collective-permute-start | bytes 98312 | tf_op jit(solution)/shard_map/ppermute | solution.py:624
  51.8 8.1 %collective-permute-start.18 = (bf16[128,128]{1,0:T(8,128)(2,1)S(1)}, bf16[128,128]{1,0:T(8,128)(2,1)S(1)}, u32[]{:S(2)}, u32[]{:S(2)}) collective-permute-start(bf16[128,128]{1,0:T(8,128)(2,1)S(1)} %shard_map.106.raw_ref.refs_4_), channel_id=1, source_target_pairs={{0,16},{8,24},{16,0},{24,8},{1,17},{9,25},{17,1},{25,9},{2,18},{10... | collective-permute-start | bytes 98312 | tf_op jit(solution)/shard_map/ppermute | solution.py:624
  55.1 4.8 %collective-permute-start.17 = (bf16[128,128]{1,0:T(8,128)(2,1)S(1)}, bf16[128,128]{1,0:T(8,128)(2,1)S(1)}, u32[]{:S(2)}, u32[]{:S(2)}) collective-permute-start(bf16[128,128]{1,0:T(8,128)(2,1)S(1)} %shard_map.106.raw_ref.refs_4_), channel_id=1, source_target_pairs={{0,8},{8,0},{16,24},{24,16},{1,9},{9,1},{17,25},{25,17},{2,10},{10... | collective-permute-start | bytes 98312 | tf_op jit(solution)/shard_map/ppermute | solution.py:624
  63.2 4.6 %collective-permute-start.21 = (bf16[80,512]{1,0:T(8,128)(2,1)S(1)}, bf16[80,512]{1,0:T(8,128)(2,1)S(1)}, u32[]{:S(2)}, u32[]{:S(2)}) collective-permute-start(bf16[80,512]{1,0:T(8,128)(2,1)S(1)} %get-tuple-element.80), channel_id=1, source_target_pairs={{0,2},{1,3},{2,0},{3,1},{4,6},{5,7},{6,4},{7,5},{8,10},{9,11},{10,... | collective-permute-start | bytes 245768 | tf_op jit(solution)/shard_map/ppermute | solution.py:624
  64.3 9.9 %collective-permute-start.22 = (bf16[80,512]{1,0:T(8,128)(2,1)S(1)}, bf16[80,512]{1,0:T(8,128)(2,1)S(1)}, u32[]{:S(2)}, u32[]{:S(2)}) collective-permute-start(bf16[80,512]{1,0:T(8,128)(2,1)S(1)} %get-tuple-element.81), channel_id=1, source_target_pairs={{0,4},{1,5},{2,6},{3,7},{4,0},{5,1},{6,2},{7,3},{8,12},{9,13},{10,... | collective-permute-start | bytes 245768 | tf_op jit(solution)/shard_map/ppermute | solution.py:624
  67.5 6.6 %collective-permute-start.23 = (bf16[80,512]{1,0:T(8,128)(2,1)S(1)}, bf16[80,512]{1,0:T(8,128)(2,1)S(1)}, u32[]{:S(2)}, u32[]{:S(2)}) collective-permute-start(bf16[80,512]{1,0:T(8,128)(2,1)S(1)} %get-tuple-element.82), channel_id=1, source_target_pairs={{0,6},{1,7},{2,4},{3,5},{4,2},{5,3},{6,0},{7,1},{8,14},{9,15},{10,... | collective-permute-start | bytes 245768 | tf_op jit(solution)/shard_map/ppermute | solution.py:624
  75.9 7.1 %collective-permute-start.27 = (bf16[80,512]{1,0:T(8,128)(2,1)S(1)}, bf16[80,512]{1,0:T(8,128)(2,1)S(1)}, u32[]{:S(2)}, u32[]{:S(2)}) collective-permute-start(bf16[80,512]{1,0:T(8,128)(2,1)S(1)} %shard_map.110.refs_0_), channel_id=1, source_target_pairs={{0,6},{1,7},{2,4},{3,5},{4,2},{5,3},{6,0},{7,1},{8,14},{9,15},{10,... | collective-permute-start | bytes 245768 | tf_op jit(solution)/shard_map/ppermute | solution.py:624
  78.3 7.1 %collective-permute-start.26 = (bf16[80,512]{1,0:T(8,128)(2,1)S(1)}, bf16[80,512]{1,0:T(8,128)(2,1)S(1)}, u32[]{:S(2)}, u32[]{:S(2)}) collective-permute-start(bf16[80,512]{1,0:T(8,128)(2,1)S(1)} %shard_map.110.refs_0_), channel_id=1, source_target_pairs={{0,4},{1,5},{2,6},{3,7},{4,0},{5,1},{6,2},{7,3},{8,12},{9,13},{10,... | collective-permute-start | bytes 245768 | tf_op jit(solution)/shard_map/ppermute | solution.py:624
  78.7 8.2 %collective-permute-start.33 = (bf16[160,512]{1,0:T(8,128)(2,1)S(1)}, bf16[160,512]{1,0:T(8,128)(2,1)S(1)}, u32[]{:S(2)}, u32[]{:S(2)}) collective-permute-start(bf16[160,512]{1,0:T(8,128)(2,1)S(1)} %shard_map.111.refs_0_), channel_id=1, source_target_pairs={{0,16},{8,24},{16,0},{24,8},{1,17},{9,25},{17,1},{25,9},{2,18},{10... | collective-permute-start | bytes 491528 | tf_op jit(solution)/shard_map/ppermute | solution.py:624
  79.3 7.6 %collective-permute-start.29 = (bf16[160,512]{1,0:T(8,128)(2,1)S(1)}, bf16[160,512]{1,0:T(8,128)(2,1)S(1)}, u32[]{:S(2)}, u32[]{:S(2)}) collective-permute-start(bf16[160,512]{1,0:T(8,128)(2,1)S(1)} %shard_map.111.refs_0_), channel_id=1, source_target_pairs={{0,8},{8,0},{16,24},{24,16},{1,9},{9,1},{17,25},{25,17},{2,10},{10... | collective-permute-start | bytes 491528 | tf_op jit(solution)/shard_map/ppermute | solution.py:624
  80.4 7.0 %collective-permute-start.25 = (bf16[160,512]{1,0:T(8,128)(2,1)S(1)}, bf16[160,512]{1,0:T(8,128)(2,1)S(1)}, u32[]{:S(2)}, u32[]{:S(2)}) collective-permute-start(bf16[160,512]{1,0:T(8,128)(2,1)S(1)} %shard_map.111.refs_0_), channel_id=1, source_target_pairs={{0,1},{1,0},{2,3},{3,2},{4,5},{5,4},{6,7},{7,6},{8,9},{9,8},{10,11... | collective-permute-start | bytes 491528 | tf_op jit(solution)/shard_map/ppermute | solution.py:624
  85.4 7.1 %collective-permute-start.35 = (bf16[160,512]{1,0:T(8,128)(2,1)S(1)}, bf16[160,512]{1,0:T(8,128)(2,1)S(1)}, u32[]{:S(2)}, u32[]{:S(2)}) collective-permute-start(bf16[160,512]{1,0:T(8,128)(2,1)S(1)} %shard_map.112.refs_2_), channel_id=1, source_target_pairs={{0,16},{8,24},{16,0},{24,8},{1,17},{9,25},{17,1},{25,9},{2,18},{10... | collective-permute-start | bytes 491528 | tf_op jit(solution)/shard_map/ppermute | solution.py:624
  86.1 6.5 %collective-permute-start.31 = (bf16[160,512]{1,0:T(8,128)(2,1)S(1)}, bf16[160,512]{1,0:T(8,128)(2,1)S(1)}, u32[]{:S(2)}, u32[]{:S(2)}) collective-permute-start(bf16[160,512]{1,0:T(8,128)(2,1)S(1)} %shard_map.112.refs_2_), channel_id=1, source_target_pairs={{0,8},{8,0},{16,24},{24,16},{1,9},{9,1},{17,25},{25,17},{2,10},{10... | collective-permute-start | bytes 491528 | tf_op jit(solution)/shard_map/ppermute | solution.py:624
  86.9 5.7 %collective-permute-start.28 = (bf16[160,512]{1,0:T(8,128)(2,1)S(1)}, bf16[160,512]{1,0:T(8,128)(2,1)S(1)}, u32[]{:S(2)}, u32[]{:S(2)}) collective-permute-start(bf16[160,512]{1,0:T(8,128)(2,1)S(1)} %shard_map.112.refs_2_), channel_id=1, source_target_pairs={{0,1},{1,0},{2,3},{3,2},{4,5},{5,4},{6,7},{7,6},{8,9},{9,8},{10,11... | collective-permute-start | bytes 491528 | tf_op jit(solution)/shard_map/ppermute | solution.py:624
  86.9 6.2 %collective-permute-start.34 = (bf16[160,512]{1,0:T(8,128)(2,1)S(1)}, bf16[160,512]{1,0:T(8,128)(2,1)S(1)}, u32[]{:S(2)}, u32[]{:S(2)}) collective-permute-start(bf16[160,512]{1,0:T(8,128)(2,1)S(1)} %collective-permute-done.33.refs_4_.refs_8_), channel_id=1, source_target_pairs={{0,1},{1,0},{2,3},{3,2},{4,5},{5,4},{6,7},{7,6},{8,9},{9,8},{10,11... | collective-permute-start | bytes 491528 | tf_op jit(solution)/shard_map/ppermute | solution.py:624
  87.4 7.5 %collective-permute-start.37 = (bf16[160,512]{1,0:T(8,128)(2,1)S(1)}, bf16[160,512]{1,0:T(8,128)(2,1)S(1)}, u32[]{:S(2)}, u32[]{:S(2)}) collective-permute-start(bf16[160,512]{1,0:T(8,128)(2,1)S(1)} %collective-permute-done.29.refs_0_.refs_4_), channel_id=1, source_target_pairs={{0,16},{8,24},{16,0},{24,8},{1,17},{9,25},{17,1},{25,9},{2,18},{10... | collective-permute-start | bytes 491528 | tf_op jit(solution)/shard_map/ppermute | solution.py:624
  92.6 5.3 %collective-permute-start.39 = (bf16[160,512]{1,0:T(8,128)(2,1)S(1)}, bf16[160,512]{1,0:T(8,128)(2,1)S(1)}, u32[]{:S(2)}, u32[]{:S(2)}) collective-permute-start(bf16[160,512]{1,0:T(8,128)(2,1)S(1)} %collective-permute-done.35.refs_6_.refs_10_), channel_id=1, source_target_pairs={{0,8},{8,0},{16,24},{24,16},{1,9},{9,1},{17,25},{25,17},{2,10},{10... | collective-permute-start | bytes 491528 | tf_op jit(solution)/shard_map/ppermute | solution.py:624
  92.6 6.5 %collective-permute-start.30 = (bf16[160,512]{1,0:T(8,128)(2,1)S(1)}, bf16[160,512]{1,0:T(8,128)(2,1)S(1)}, u32[]{:S(2)}, u32[]{:S(2)}) collective-permute-start(bf16[160,512]{1,0:T(8,128)(2,1)S(1)} %collective-permute-done.29.refs_0_.refs_4_), channel_id=1, source_target_pairs={{0,1},{1,0},{2,3},{3,2},{4,5},{5,4},{6,7},{7,6},{8,9},{9,8},{10,11... | collective-permute-start | bytes 491528 | tf_op jit(solution)/shard_map/ppermute | solution.py:624
  92.6 6.5 %collective-permute-start.36 = (bf16[160,512]{1,0:T(8,128)(2,1)S(1)}, bf16[160,512]{1,0:T(8,128)(2,1)S(1)}, u32[]{:S(2)}, u32[]{:S(2)}) collective-permute-start(bf16[160,512]{1,0:T(8,128)(2,1)S(1)} %collective-permute-done.35.refs_6_.refs_10_), channel_id=1, source_target_pairs={{0,1},{1,0},{2,3},{3,2},{4,5},{5,4},{6,7},{7,6},{8,9},{9,8},{10,11... | collective-permute-start | bytes 491528 | tf_op jit(solution)/shard_map/ppermute | solution.py:624
  93.1 6.0 %collective-permute-start.32 = (bf16[160,512]{1,0:T(8,128)(2,1)S(1)}, bf16[160,512]{1,0:T(8,128)(2,1)S(1)}, u32[]{:S(2)}, u32[]{:S(2)}) collective-permute-start(bf16[160,512]{1,0:T(8,128)(2,1)S(1)} %collective-permute-done.31.refs_2_.refs_6_), channel_id=1, source_target_pairs={{0,1},{1,0},{2,3},{3,2},{4,5},{5,4},{6,7},{7,6},{8,9},{9,8},{10,11... | collective-permute-start | bytes 491528 | tf_op jit(solution)/shard_map/ppermute | solution.py:624
  94.9 5.9 %collective-permute-start.38 = (bf16[160,512]{1,0:T(8,128)(2,1)S(1)}, bf16[160,512]{1,0:T(8,128)(2,1)S(1)}, u32[]{:S(2)}, u32[]{:S(2)}) collective-permute-start(bf16[160,512]{1,0:T(8,128)(2,1)S(1)} %collective-permute-done.37.refs_12_), channel_id=1, source_target_pairs={{0,1},{1,0},{2,3},{3,2},{4,5},{5,4},{6,7},{7,6},{8,9},{9,8},{10,11... | collective-permute-start | bytes 491528 | tf_op jit(solution)/shard_map/ppermute | solution.py:624
  (13 other events, 99.7 us)

commit v2 on v1

--- a/solution.py
+++ b/solution.py
@@ -214,132 +214,183 @@
     return expo
 
 
-def negative_kernel(size, *refs):
-    pieces, stacked, (zneg_ref, numer_ref, even_ref) = refs[:size], refs[size:-3], refs[-3:]
-    units = pieces[0][...]
+def pair_up_kernel(own_ref, other_ref, out_ref):
+    rows = own_ref.shape[0]
+    own, other = own_ref[...], other_ref[...]
+    first = lax.axis_index("dp") % 2 == 0
+    out_ref[:rows, :] = jnp.where(first, own, other)
+    out_ref[rows:, :] = jnp.where(first, other, own)
+
+
+def pair_up(own, other):
+    rows, width = own.shape
+    return pl.pallas_call(
+        pair_up_kernel,
+        in_specs=[VMEM] * 2,
+        out_shape=shape((2 * rows, width), own.dtype),
+        out_specs=VMEM,
+        compiler_params=params(8),
+        cost_estimate=cost(1e3, 1e5),
+    )(own, other)
+
+
+def cross(pair):
+    size, peers = lax.axis_size("blk"), lax.axis_size("dp")
+    got = []
+    for k in range(1, max(size, peers // 2)):
+        routes = []
+        for blk in range(size):
+            for dp in range(peers):
+                if dp % 2 == 0 and 2 * k < peers:
+                    routes.append((blk * peers + dp, blk * peers + (dp ^ (2 * k))))
+                if dp % 2 == 1 and k < size:
+                    routes.append((blk * peers + dp, (blk ^ k) * peers + dp))
+        got.append(lax.ppermute(pair, ("blk", "dp"), routes))
+    return got
+
+
+def crossed(got_ref, swapped_ref, rows):
+    first = lax.axis_index("dp") % 2 == 0
+
+    def along(k, core):
+        at = (2 * (k - 1) + core) * rows
+        return jnp.where(first, got_ref[at : at + rows, :], swapped_ref[at : at + rows, :])
+
+    def across(k):
+        at = 2 * (k - 1) * rows
+        low = jnp.where(first, swapped_ref[at : at + rows, :], got_ref[at + rows : at + 2 * rows, :])
+        return low
+
+    return along, across
+
+
+def as_rows(column, count):
+    return jnp.broadcast_to(column, (column.shape[0], count)).T
+
+
+def scores_kernel(
+    size,
+    peers,
+    dev_ref,
+    row_ref,
+    units_ref,
+    pair_ref,
+    got_ref,
+    swapped_ref,
+    local_ref,
+    stats_ref,
+    loss_ref,
+    group_ref,
+    around_ref,
+):
+    units = units_ref[...]
     count = units.shape[0]
-    even_ref[:count, :] = units
-    for i, each in enumerate(stacked):
-        even_ref[(i + 1) * count : (i + 2) * count, :] = each[...]
+    along, across = crossed(got_ref, swapped_ref, count)
     zneg = numer = None
-    for i, piece in enumerate(pieces):
-        keys = piece[...]
+    for i in range(size):
+        keys = across(i) if i else units
+        group_ref[i * count : (i + 1) * count, :] = keys
         expo = exponentials(units, keys, i == 0)
         total = jnp.sum(expo, axis=1, keepdims=True)
         term = mm(expo.astype(BF16), keys)
         zneg = total if zneg is None else zneg + total
         numer = term if numer is None else numer + term
-    zneg_ref[...] = jnp.broadcast_to(zneg, zneg_ref.shape)
-    numer_ref[...] = numer
-
-
-def negatives(pieces, stacked):
-    count, embed = pieces[0].shape
-    size = len(pieces)
-    return pl.pallas_call(
-        functools.partial(negative_kernel, size),
-        in_specs=[VMEM] * (size + len(stacked)),
-        out_shape=[
-            shape((count, 128), F32),
-            shape((count, embed), F32),
-            shape(((len(stacked) + 1) * count, embed), BF16),
-        ],
-        out_specs=[VMEM] * 3,
-        compiler_params=params(8),
-        cost_estimate=cost(4e8, 1e6),
-    )(*pieces, *stacked)
-
-
-def as_rows(column, count):
-    return jnp.broadcast_to(column, (column.shape[0], count)).T
-
-
-def positive_kernel(
-    dev_ref, row_ref, even_ref, odd_ref, zneg_ref, numer_ref, local_ref, stats_ref, loss_ref
-):
-    count = dev_ref.shape[1]
     me = lax.axis_index("dp")
-    step = dev_ref[...] ^ me
-    place = ((step & 1) * even_ref.shape[0] + (step >> 1) * count + row_ref[...]).astype(F32)
-    place = jnp.broadcast_to(place, (count, count)).T
+    dev = dev_ref[...]
+    place = (2 * ((dev ^ me) >> 1) + (dev & 1)) * count + row_ref[...]
+    place = jnp.broadcast_to(place.astype(F32), (count, count)).T
     lane = lax.broadcasted_iota(jnp.int32, (count, count), 1).astype(F32)
     positive = None
-    blocks = even_ref.shape[0] // count
-    for i in range(2 * blocks):
-        source = even_ref if i < blocks else odd_ref
-        at = (i % blocks) * count
+    for i in range(peers):
+        k, core = i // 2, i % 2
+        source = along(k, core) if k else pair_ref[core * count : (core + 1) * count, :]
+        around_ref[i * count : (i + 1) * count, :] = source
         hit = jnp.where(place - float(i * count) == lane, 1.0, 0.0).astype(BF16)
-        term = mm(hit, source[at : at + count, :])
+        term = mm(hit, source)
         positive = term if positive is None else positive + term
-    units = even_ref[:count, :].astype(F32)
-    spos = SCALE * jnp.sum(units * positive, axis=1, keepdims=True)
+    spos = SCALE * jnp.sum(units.astype(F32) * positive, axis=1, keepdims=True)
     top = jnp.exp(spos)
-    totals = top + zneg_ref[:, :1]
+    totals = top + zneg
     less = top / totals - 1.0
     coef = SCALE / count
-    local_ref[...] = coef * (less * positive + numer_ref[...] / totals)
+    local_ref[...] = coef * (less * positive + numer / totals)
     loss_ref[...] = as_rows(jnp.log(totals) - spos, count)[:1]
     stats_ref[...] = jnp.zeros(stats_ref.shape, F32)
     stats_ref[0:1, :] = as_rows(totals, count)[:1]
     stats_ref[1:2, :] = as_rows(coef * less, count)[:1]
-    stats_ref[2:3, :] = (dev_ref[...] * count + row_ref[...]).astype(F32)
-
-
-def positives(partner_dev, partner_row, even, odd, zneg, numer):
-    count, embed = numer.shape
-    return pl.pallas_call(
-        positive_kernel,
+    stats_ref[2:3, :] = (dev * count + row_ref[...]).astype(F32)
+
+
+def scores(partner_dev, partner_row, units, pair, got, swapped, size, peers):
+    count, embed = units.shape
+    return pl.pallas_call(
+        functools.partial(scores_kernel, size, peers),
         in_specs=[VMEM] * 6,
-        out_shape=[shape((count, embed), F32), shape((SUB, count), F32), shape((1, count), F32)],
-        out_specs=[VMEM] * 3,
-        compiler_params=params(8),
+        out_shape=[
+            shape((count, embed), F32),
+            shape((SUB, count), F32),
+            shape((1, count), F32),
+            shape((size * count, embed), BF16),
+            shape((peers * count, embed), BF16),
+        ],
+        out_specs=[VMEM] * 5,
+        compiler_params=params(16),
         cost_estimate=cost(4e8, 1e6),
-    )(partner_dev.reshape(1, count), partner_row.reshape(1, count), even, odd, zneg, numer)
-
-
-def upper_kernel(size, *refs):
-    pieces, rest = refs[:size], refs[size:]
-    stats, rest = rest[:size], rest[size:]
-    (even_ref, odd_ref, even_stats, odd_stats, local_ref, unit32_ref, norm_ref, out_ref) = rest
+    )(partner_dev.reshape(1, count), partner_row.reshape(1, count), units, pair, got, swapped)
+
+
+def upper_kernel(
+    size,
+    peers,
+    group_ref,
+    around_ref,
+    stats_ref,
+    pair_ref,
+    got_ref,
+    swapped_ref,
+    local_ref,
+    unit32_ref,
+    norm_ref,
+    out_ref,
+):
     count, _ = local_ref.shape
     coef = SCALE / count
-    units = pieces[0][...]
+    along, across = crossed(got_ref, swapped_ref, SUB)
+    units = group_ref[:count, :]
     keyterm = None
     for i in range(size):
-        keys = pieces[i][...]
+        keys = group_ref[i * count : (i + 1) * count, :]
         expo = exponentials(units, keys, i == 0)
-        weights = (expo / stats[i][0:1, :]).astype(BF16)
-        term = mm(weights, keys)
+        totals = (across(i) if i else stats_ref[...])[0:1, :]
+        term = mm((expo / totals).astype(BF16), keys)
         keyterm = term if keyterm is None else keyterm + term
     mine = lax.axis_index("dp") * count + lax.broadcasted_iota(jnp.int32, (count, count), 0)
     mine = mine.astype(F32)
-    blocks = even_ref.shape[0] // count
     chosen = amount = None
-    for i in range(2 * blocks):
-        source, table = (even_ref, even_stats) if i < blocks else (odd_ref, odd_stats)
-        j = i % blocks
-        hit = table[j * SUB + 2 : j * SUB + 3, :] == mine
-        share = jnp.where(hit, table[j * SUB + 1 : j * SUB + 2, :], 0.0)
-        term = mm(jnp.where(hit, 1.0, 0.0).astype(BF16), source[j * count : (j + 1) * count, :])
+    for i in range(peers):
+        k, core = i // 2, i % 2
+        table = along(k, core) if k else pair_ref[core * SUB : (core + 1) * SUB, :]
+        hit = table[2:3, :] == mine
+        share = jnp.where(hit, table[1:2, :], 0.0)
+        term = mm(jnp.where(hit, 1.0, 0.0).astype(BF16), around_ref[i * count : (i + 1) * count, :])
         chosen = term if chosen is None else chosen + term
         amount = share if amount is None else amount + share
     back = jnp.sum(amount, axis=1, keepdims=True) * chosen
     grad_units = local_ref[...] + coef * keyterm + back
     unit32 = unit32_ref[...]
-    along = jnp.sum(unit32 * grad_units, axis=1, keepdims=True)
-    out_ref[...] = ((grad_units - unit32 * along) / norm_ref[:, :1]).astype(BF16)
-
-
-def upper(pieces, stats, even, odd, even_stats, odd_stats, local, unit32, norms):
+    tilt = jnp.sum(unit32 * grad_units, axis=1, keepdims=True)
+    out_ref[...] = ((grad_units - unit32 * tilt) / norm_ref[:, :1]).astype(BF16)
+
+
+def upper(group, around, stats, pair, got, swapped, local, unit32, norms, size, peers):
     count, embed = local.shape
-    size = len(pieces)
-    args = [*pieces, *stats, even, odd, even_stats, odd_stats, local, unit32, norms]
-    return pl.pallas_call(
-        functools.partial(upper_kernel, size),
+    args = [group, around, stats, pair, got, swapped, local, unit32, norms]
+    return pl.pallas_call(
+        functools.partial(upper_kernel, size, peers),
         in_specs=[VMEM] * len(args),
         out_shape=shape((count, embed), BF16),
         out_specs=VMEM,
-        compiler_params=params(8),
+        compiler_params=params(16),
         cost_estimate=cost(4e8, 2e6),
     )(*args)
 
@@ -643,19 +694,19 @@
     *early, spec, mixed, normed, in_w, units, unit32, norms, rscale = encode(
         patches, w_mix, w_in, w_out, size
     )
-    stacked = spread(units, "dp", along)
-    pieces = spread(units, "blk", across)
-    pieces[1:], stacked[1:] = lax.optimization_barrier((pieces[1:], stacked[1:]))
-    zneg, numer, even = negatives(pieces, stacked[1:])
-    odd = swap(even, "dp", 1)
-    local, stats, loss = positives(partner_dev, partner_row, even, odd, zneg, numer)
-    dp_stats = spread(stats, "dp", along)
-    group_stats = spread(stats, "blk", across)
-    dp_stats[1:], group_stats[1:] = lax.optimization_barrier((dp_stats[1:], group_stats[1:]))
+    other = swap(units, "dp", 1)
+    pair = pair_up(units, other)
+    got = stack(lax.optimization_barrier(cross(pair)))
     factors = [early[0]] + [swap(early[hop], "blk", hop) for hop in across]
-    even_stats = stack(dp_stats)
-    odd_stats = swap(even_stats, "dp", 1)
-    grad_raw = upper(pieces, group_stats, even, odd, even_stats, odd_stats, local, unit32, norms)
+    swapped = swap(got, "dp", 1)
+    local, stats, loss, group, around = scores(
+        partner_dev, partner_row, units, pair, got, swapped, size, peers
+    )
+    other = swap(stats, "dp", 1)
+    pair = pair_up(stats, other)
+    got = stack(lax.optimization_barrier(cross(pair)))
+    swapped = swap(got, "dp", 1)
+    grad_raw = upper(group, around, stats, pair, got, swapped, local, unit32, norms, size, peers)
     raws = spread(grad_raw, "blk", across)
     g_mix = lower(grad_raw, w_out, early[0], normed, rscale, in_w, mixed, spec, freqs, columns)
     keep, away = weight_grads(lay, columns, factors, raws, w_out, g_mix)

time: 103 us -> 89.9 us (0.87)
  waiting for transfers between devices: 41.5 us -> 32.2 us
  starting transfers between devices: 40.6 us -> 37.2 us
    ppermute x41 -> x31, waiting for transfers between devices: 41.5 us -> 20.7 us  [swap(): return lax.ppermute(block, axis, [(src, src ^ bit) for src in range(size)])]
    ppermute x0 -> x6, waiting for transfers between devices: none -> 11.5 us  [cross(): got.append(lax.ppermute(pair, ('blk', 'dp'), routes))]
    ppermute x41 -> x31, starting transfers between devices: 40.6 us -> 29.5 us  [swap(): return lax.ppermute(block, axis, [(src, src ^ bit) for src in range(size)])]
    ppermute x0 -> x6, starting transfers between devices: none -> 7.73 us  [cross(): got.append(lax.ppermute(pair, ('blk', 'dp'), routes))]
    pallas_call x3 -> x4, Pallas kernels: 2.27 us -> 2.17 us  [the longest x1 1.35 us: scores(): pl.pallas_call(functools.partial(scores_kernel, size, peers), in_specs=[V...]
  transfers between devices with their start and end apart: 41 -> 37, of which waited for: 19 -> 16; matrix products, arithmetic and copies ran while one was open for 0% -> 0% of each run, Pallas kernels for 8% -> 9%
where the time goes in v2:
time: 89.9 us; the launch traced here: 89.7 us
  starting transfers between devices  37.2 us (41%)
  waiting for transfers between devices  32.2 us (36%)
  Pallas kernels  19.4 us (22%)
    ppermute x31, starting transfers between devices, swap(): return lax.ppermute(block, axis, [(src, src ^ bit) for src in range(size)])  29.5 us
    ppermute x31, waiting for transfers between devices, swap(): return lax.ppermute(block, axis, [(src, src ^ bit) for src in range(size)])  20.7 us
    ppermute x6, waiting for transfers between devices, cross(): got.append(lax.ppermute(pair, ('blk', 'dp'), routes))  11.5 us
    ppermute x6, starting transfers between devices, cross(): got.append(lax.ppermute(pair, ('blk', 'dp'), routes))  7.73 us
    pallas_call x1, Pallas kernels, encode(): pl.pallas_call(functools.partial(encode_kernel, freqs, size, rounds), in_...  7.69 us
    pallas_call x3, Pallas kernels, finish(): pl.pallas_call(functools.partial(finish_kernel, lay, tuple(parts), bool(d...  4.6 us
    pallas_call x1, Pallas kernels, lower(): pl.pallas_call(functools.partial(lower_kernel, freqs, columns), in_specs=...  3.36 us
  transfers between devices with their start and end apart: 37, of which 16 were waited for; matrix products, arithmetic and copies ran while one was open for 0% of the time, Pallas kernels for 9%

profile of v2, /device:TPU:0, one launch (start us, length us, event | category | flops | bytes accessed | tf_op | source)
XLA Modules:
  0.0 89.7 jit_solution(4129927535086061839)
XLA Ops:
  0.7 7.7 %shard_map.102 = (bf16[128,1152]{1,0:T(8,128)(2,1)}, bf16[128,1152]{1,0:T(8,128)(2,1)}, bf16[128,1152]{1,0:T(8,128)(2,1)}, bf16[128,1152]{1,0:T(8,128)(2,1)}, bf...) custom-call(bf16[128,64,256]{2,1,0:T(8,128)(2,1)} %patch_hbm.1, ...), custom_call_target="tpu_custom_call" | custom-call | flops 3000000000 | bytes 14000000 | tf_op jit(solution)/shard_map/pallas_call | solution.py:186
  9.8 5.0 %collective-permute-start.3 = (bf16[256,128]{1,0:T(8,128)(2,1)S(1)}, bf16[256,128]{1,0:T(8,128)(2,1)S(1)}, u32[]{:S(2)}, u32[]{:S(2)}) collective-permute-start(bf16[256,128]{1,0:T(8,128)(2,1)S(1)} %shard_map.103.pair_ref), channel_id=1, source_target_pairs={{0,6},{1,25},{2,4},{3,27},{4,2},{5,29},{6,0},{7,31},{8,14},{9,17},... | collective-permute-start | bytes 196616 | tf_op jit(solution)/shard_map/ppermute | solution.py:248
  15.4 1.7 %collective-permute-done.3.refs_2_ = bf16[256,128]{1,0:T(8,128)(2,1)S(1)} collective-permute-done((bf16[256,128]{1,0:T(8,128)(2,1)S(1)}, bf16[256,128]{1,0:T(8,128)(2,1)S(1)}, u32[]{:S(2)}, u32[]{:S(2)}) %collective-permute-start.3) | collective-permute-done | bytes 65568 | tf_op jit(solution)/shard_map/ppermute | solution.py:248
  17.1 2.8 %collective-permute-done.2.refs_1_ = bf16[256,128]{1,0:T(8,128)(2,1)S(1)} collective-permute-done((bf16[256,128]{1,0:T(8,128)(2,1)S(1)}, bf16[256,128]{1,0:T(8,128)(2,1)S(1)}, u32[]{:S(2)}, u32[]{:S(2)}) %collective-permute-start.2) | collective-permute-done | bytes 65568 | tf_op jit(solution)/shard_map/ppermute | solution.py:248
  20.1 1.6 %collective-permute-start.5 = (bf16[128,1152]{1,0:T(8,128)(2,1)}, bf16[128,1152]{1,0:T(8,128)(2,1)S(1)}, u32[]{:S(2)}, u32[]{:S(2)}) collective-permute-start(bf16[128,1152]{1,0:T(8,128)(2,1)} %get-tuple-element.46), channel_id=1, source_target_pairs={{0,8},{8,0},{16,24},{24,16},{1,9},{9,1},{17,25},{25,17},{2,10},{10... | collective-permute-start | bytes 884744 | tf_op jit(solution)/shard_map/ppermute | solution.py:675
  21.6 1.5 %collective-permute-start.6 = (bf16[128,1152]{1,0:T(8,128)(2,1)}, bf16[128,1152]{1,0:T(8,128)(2,1)S(1)}, u32[]{:S(2)}, u32[]{:S(2)}) collective-permute-start(bf16[128,1152]{1,0:T(8,128)(2,1)} %get-tuple-element.47), channel_id=1, source_target_pairs={{0,16},{8,24},{16,0},{24,8},{1,17},{9,25},{17,1},{25,9},{2,18},{10... | collective-permute-start | bytes 884744 | tf_op jit(solution)/shard_map/ppermute | solution.py:675
  23.6 1.3 %shard_map.105 = (f32[128,128]{1,0:T(8,128)S(1)}, f32[8,128]{1,0:T(8,128)S(1)}, f32[1,128]{1,0:T(1,128)}, bf16[512,128]{1,0:T(8,128)(2,1)S(1)}, bf16[1024,128]{1,0:T(8,128)(2,1)S(1)}) custom-call(s32[1,128]{1,0:T(1,128)S(1)} %bitcast.3, s32[1,128]{1,0:T(1,128)S(1)} %bitcast.4, bf16[128,128]{1,0:T(8,128)(2,1)S(1)} %get-tuple-element.40.own_ref.units_ref, ...), custom_call_target="tpu_custom_call" | custom-call | flops 400000000 | bytes 1000000 | tf_op jit(solution)/shard_map/pallas_call | solution.py:326
  26.1 1.6 %collective-permute-start.11 = (f32[16,128]{1,0:T(8,128)S(1)}, f32[16,128]{1,0:T(8,128)S(1)}, u32[]{:S(2)}, u32[]{:S(2)}) collective-permute-start(f32[16,128]{1,0:T(8,128)S(1)} %shard_map.106.pair_ref), channel_id=1, source_target_pairs={{0,6},{1,25},{2,4},{3,27},{4,2},{5,29},{6,0},{7,31},{8,14},{9,17},... | collective-permute-start | bytes 24584 | tf_op jit(solution)/shard_map/ppermute | solution.py:248
  28.2 3.4 %collective-permute-done.11.refs_2_ = f32[16,128]{1,0:T(8,128)S(1)} collective-permute-done((f32[16,128]{1,0:T(8,128)S(1)}, f32[16,128]{1,0:T(8,128)S(1)}, u32[]{:S(2)}, u32[]{:S(2)}) %collective-permute-start.11) | collective-permute-done | bytes 8224 | tf_op jit(solution)/shard_map/ppermute | solution.py:248
  32.3 3.0 %collective-permute-done.9.refs_0_ = f32[16,128]{1,0:T(8,128)S(1)} collective-permute-done((f32[16,128]{1,0:T(8,128)S(1)}, f32[16,128]{1,0:T(8,128)S(1)}, u32[]{:S(2)}, u32[]{:S(2)}) %collective-permute-start.9) | collective-permute-done | bytes 8224 | tf_op jit(solution)/shard_map/ppermute | solution.py:248
  35.2 4.0 %collective-permute-start.12 = (f32[48,128]{1,0:T(8,128)S(1)}, f32[48,128]{1,0:T(8,128)S(1)}, u32[]{:S(2)}, u32[]{:S(2)}) collective-permute-start(f32[48,128]{1,0:T(8,128)S(1)} %shard_map.107.got_ref), channel_id=1, source_target_pairs={{0,1},{1,0},{2,3},{3,2},{4,5},{5,4},{6,7},{7,6},{8,9},{9,8},{10,11... | collective-permute-start | bytes 73736 | tf_op jit(solution)/shard_map/ppermute | solution.py:675
  40.9 1.5 %collective-permute-start.15 = (bf16[128,128]{1,0:T(8,128)(2,1)S(1)}, bf16[128,128]{1,0:T(8,128)(2,1)S(1)}, u32[]{:S(2)}, u32[]{:S(2)}) collective-permute-start(bf16[128,128]{1,0:T(8,128)(2,1)S(1)} %shard_map.108.raw_ref.refs_4_), channel_id=1, source_target_pairs={{0,24},{8,16},{16,8},{24,0},{1,25},{9,17},{17,9},{25,1},{2,26},{10... | collective-permute-start | bytes 98312 | tf_op jit(solution)/shard_map/ppermute | solution.py:675
  42.4 1.5 %collective-permute-start.14 = (bf16[128,128]{1,0:T(8,128)(2,1)S(1)}, bf16[128,128]{1,0:T(8,128)(2,1)S(1)}, u32[]{:S(2)}, u32[]{:S(2)}) collective-permute-start(bf16[128,128]{1,0:T(8,128)(2,1)S(1)} %shard_map.108.raw_ref.refs_4_), channel_id=1, source_target_pairs={{0,16},{8,24},{16,0},{24,8},{1,17},{9,25},{17,1},{25,9},{2,18},{10... | collective-permute-start | bytes 98312 | tf_op jit(solution)/shard_map/ppermute | solution.py:675
  44.5 3.4 %shard_map.109.refs_9_ = f32[256,128]{1,0:T(8,128)S(1)} custom-call(bf16[128,128]{1,0:T(8,128)(2,1)S(1)} %shard_map.108.raw_ref.refs_4_, f32[128,128]{1,0:T(8,128)S(1)} %get-tuple-element.58.rscale_ref, bf16[2048,512]{1,0:T(8,128)(2,1)S(1)} %get-tuple-element.59.in_w, bf16[128,2048]{1,0:T(8,128)(2,1)S(1)} %get-tuple-element.60.normed, ...), custom_call_target="tpu_custom_call" | custom-call | flops 1000000000 | bytes 7000000 | tf_op jit(solution)/shard_map/pallas_call | solution.py:457
  47.9 1.5 %shard_map.110 = (f32[4,80,512]{2,1,0:T(8,128)S(1)}, bf16[4,80,512]{2,1,0:T(8,128)(2,1)S(1)}) custom-call(bf16[128,1152]{1,0:T(8,128)(2,1)S(1)} %copy-done, bf16[128,1152]{1,0:T(8,128)(2,1)S(1)} %collective-permute-done.5.refs_1_, bf16[128,1152]{1,0:T(8,128)(2,1)S(1)} %collective-permute-done.6.refs_2_, ...), custom_call_target="tpu_custom_call" | custom-call | flops 600000000 | bytes 4000000 | tf_op jit(solution)/shard_map/pallas_call | solution.py:535
  49.5 1.6 %collective-permute-done.16.got_ref = bf16[4,80,512]{2,1,0:T(8,128)(2,1)S(1)} collective-permute-done((bf16[4,80,512]{2,1,0:T(8,128)(2,1)S(1)}, bf16[4,80,512]{2,1,0:T(8,128)(2,1)S(1)}, u32[]{:S(2)}, u32[]{:S(2)}) %collective-permute-start.16) | collective-permute-done | bytes 327712 | tf_op jit(solution)/shard_map/ppermute | solution.py:675
  51.7 1.7 %collective-permute-start.18 = (bf16[80,512]{1,0:T(8,128)(2,1)S(1)}, bf16[80,512]{1,0:T(8,128)(2,1)S(1)}, u32[]{:S(2)}, u32[]{:S(2)}) collective-permute-start(bf16[80,512]{1,0:T(8,128)(2,1)S(1)} %get-tuple-element.67), channel_id=1, source_target_pairs={{0,4},{1,5},{2,6},{3,7},{4,0},{5,1},{6,2},{7,3},{8,12},{9,13},{10,... | collective-permute-start | bytes 245768 | tf_op jit(solution)/shard_map/ppermute | solution.py:675
  53.4 2.2 %collective-permute-start.19 = (bf16[80,512]{1,0:T(8,128)(2,1)S(1)}, bf16[80,512]{1,0:T(8,128)(2,1)S(1)}, u32[]{:S(2)}, u32[]{:S(2)}) collective-permute-start(bf16[80,512]{1,0:T(8,128)(2,1)S(1)} %get-tuple-element.68), channel_id=1, source_target_pairs={{0,6},{1,7},{2,4},{3,5},{4,2},{5,3},{6,0},{7,1},{8,14},{9,15},{10,... | collective-permute-start | bytes 245768 | tf_op jit(solution)/shard_map/ppermute | solution.py:675
  55.6 1.4 %collective-permute-done.17.refs_0_ = bf16[80,512]{1,0:T(8,128)(2,1)S(1)} collective-permute-done((bf16[80,512]{1,0:T(8,128)(2,1)S(1)}, bf16[80,512]{1,0:T(8,128)(2,1)S(1)}, u32[]{:S(2)}, u32[]{:S(2)}) %collective-permute-start.17) | collective-permute-done | bytes 81952 | tf_op jit(solution)/shard_map/ppermute | solution.py:675
  57.1 4.0 %collective-permute-done.18.refs_1_ = bf16[80,512]{1,0:T(8,128)(2,1)S(1)} collective-permute-done((bf16[80,512]{1,0:T(8,128)(2,1)S(1)}, bf16[80,512]{1,0:T(8,128)(2,1)S(1)}, u32[]{:S(2)}, u32[]{:S(2)}) %collective-permute-start.18) | collective-permute-done | bytes 81952 | tf_op jit(solution)/shard_map/ppermute | solution.py:675
  61.1 1.9 %collective-permute-start.20 = (bf16[80,512]{1,0:T(8,128)(2,1)S(1)}, bf16[80,512]{1,0:T(8,128)(2,1)S(1)}, u32[]{:S(2)}, u32[]{:S(2)}) collective-permute-start(bf16[80,512]{1,0:T(8,128)(2,1)S(1)} %shard_map.112.refs_0_), channel_id=1, source_target_pairs={{0,2},{1,3},{2,0},{3,1},{4,6},{5,7},{6,4},{7,5},{8,10},{9,11},{10,... | collective-permute-start | bytes 245768 | tf_op jit(solution)/shard_map/ppermute | solution.py:675
  63.0 2.6 %collective-permute-start.23 = (bf16[80,512]{1,0:T(8,128)(2,1)S(1)}, bf16[80,512]{1,0:T(8,128)(2,1)S(1)}, u32[]{:S(2)}, u32[]{:S(2)}) collective-permute-start(bf16[80,512]{1,0:T(8,128)(2,1)S(1)} %shard_map.112.refs_0_), channel_id=1, source_target_pairs={{0,6},{1,7},{2,4},{3,5},{4,2},{5,3},{6,0},{7,1},{8,14},{9,15},{10,... | collective-permute-start | bytes 245768 | tf_op jit(solution)/shard_map/ppermute | solution.py:675
  66.2 1.5 %collective-permute-start.25 = (bf16[160,512]{1,0:T(8,128)(2,1)S(1)}, bf16[160,512]{1,0:T(8,128)(2,1)S(1)}, u32[]{:S(2)}, u32[]{:S(2)}) collective-permute-start(bf16[160,512]{1,0:T(8,128)(2,1)S(1)} %shard_map.113.refs_0_), channel_id=1, source_target_pairs={{0,8},{8,0},{16,24},{24,16},{1,9},{9,1},{17,25},{25,17},{2,10},{10... | collective-permute-start | bytes 491528 | tf_op jit(solution)/shard_map/ppermute | solution.py:675
  67.7 2.9 %collective-permute-done.23.refs_1_ = bf16[80,512]{1,0:T(8,128)(2,1)S(1)} collective-permute-done((bf16[80,512]{1,0:T(8,128)(2,1)S(1)}, bf16[80,512]{1,0:T(8,128)(2,1)S(1)}, u32[]{:S(2)}, u32[]{:S(2)}) %collective-permute-start.23) | collective-permute-done | bytes 81952 | tf_op jit(solution)/shard_map/ppermute | solution.py:675
  70.7 2.3 %collective-permute-done.22.refs_0_ = bf16[80,512]{1,0:T(8,128)(2,1)S(1)} collective-permute-done((bf16[80,512]{1,0:T(8,128)(2,1)S(1)}, bf16[80,512]{1,0:T(8,128)(2,1)S(1)}, u32[]{:S(2)}, u32[]{:S(2)}) %collective-permute-start.22) | collective-permute-done | bytes 81952 | tf_op jit(solution)/shard_map/ppermute | solution.py:675
  73.6 1.5 %collective-permute-start.27 = (bf16[160,512]{1,0:T(8,128)(2,1)S(1)}, bf16[160,512]{1,0:T(8,128)(2,1)S(1)}, u32[]{:S(2)}, u32[]{:S(2)}) collective-permute-start(bf16[160,512]{1,0:T(8,128)(2,1)S(1)} %shard_map.114.refs_2_), channel_id=1, source_target_pairs={{0,8},{8,0},{16,24},{24,16},{1,9},{9,1},{17,25},{25,17},{2,10},{10... | collective-permute-start | bytes 491528 | tf_op jit(solution)/shard_map/ppermute | solution.py:675
  75.6 1.5 %collective-permute-start.33 = (bf16[160,512]{1,0:T(8,128)(2,1)S(1)}, bf16[160,512]{1,0:T(8,128)(2,1)S(1)}, u32[]{:S(2)}, u32[]{:S(2)}) collective-permute-start(bf16[160,512]{1,0:T(8,128)(2,1)S(1)} %collective-permute-done.25.refs_0_.refs_4_), channel_id=1, source_target_pairs={{0,16},{8,24},{16,0},{24,8},{1,17},{9,25},{17,1},{25,9},{2,18},{10... | collective-permute-start | bytes 491528 | tf_op jit(solution)/shard_map/ppermute | solution.py:675
  77.1 2.7 %collective-permute-done.31.refs_6_.refs_10_ = bf16[160,512]{1,0:T(8,128)(2,1)S(1)} collective-permute-done((bf16[160,512]{1,0:T(8,128)(2,1)S(1)}, bf16[160,512]{1,0:T(8,128)(2,1)S(1)}, u32[]{:S(2)}, u32[]{:S(2)}) %collective-permute-start.31) | collective-permute-done | bytes 163872 | tf_op jit(solution)/shard_map/ppermute | solution.py:675
  79.8 1.8 %collective-permute-start.35 = (bf16[160,512]{1,0:T(8,128)(2,1)S(1)}, bf16[160,512]{1,0:T(8,128)(2,1)S(1)}, u32[]{:S(2)}, u32[]{:S(2)}) collective-permute-start(bf16[160,512]{1,0:T(8,128)(2,1)S(1)} %collective-permute-done.31.refs_6_.refs_10_), channel_id=1, source_target_pairs={{0,8},{8,0},{16,24},{24,16},{1,9},{9,1},{17,25},{25,17},{2,10},{10... | collective-permute-start | bytes 491528 | tf_op jit(solution)/shard_map/ppermute | solution.py:675
  82.6 2.4 %collective-permute-done.35.refs_14_ = bf16[160,512]{1,0:T(8,128)(2,1)S(1)} collective-permute-done((bf16[160,512]{1,0:T(8,128)(2,1)S(1)}, bf16[160,512]{1,0:T(8,128)(2,1)S(1)}, u32[]{:S(2)}, u32[]{:S(2)}) %collective-permute-start.35) | collective-permute-done | bytes 163872 | tf_op jit(solution)/shard_map/ppermute | solution.py:675
  86.3 1.7 %shard_map.116 = (f32[2048,512]{1,0:T(8,128)}, f32[512,128]{1,0:T(8,128)}) custom-call(bf16[160,512]{1,0:T(8,128)(2,1)S(1)} %collective-permute-done.25.refs_0_.refs_4_, bf16[160,512]{1,0:T(8,128)(2,1)S(1)} %collective-permute-done.26.refs_1_.refs_5_, ...), custom_call_target="tpu_custom_call", output_to_operand_aliasing={{0}: (8, {}), {1}: (9, {})} | custom-call | flops 1000000 | bytes 8000000 | tf_op jit(solution)/shard_map/pallas_call | solution.py:638
  87.9 1.8 %shard_map.117 = (f32[2048,512]{1,0:T(8,128)}, f32[512,128]{1,0:T(8,128)}, f32[256,128]{1,0:T(8,128)}) custom-call(bf16[160,512]{1,0:T(8,128)(2,1)S(1)} %shard_map.113.refs_0_, bf16[160,512]{1,0:T(8,128)(2,1)S(1)} %collective-permute-done.21.refs_1_, bf16[160,512]{1,0:T(8,128)(2,1)S(1)} %shard_map.114.refs_2_, ...), custom_call_target="tpu_custom_call", output_to_operand_aliasing={{0}: (16, {}), {1}: (17, {})} | custom-call | flops 1000000 | bytes 8000000 | tf_op jit(solution)/shard_map/pallas_call | solution.py:638
  (66 shorter events, 11.9 us)
Async XLA Ops:
  9.8 7.3 %collective-permute-start.3 = (bf16[256,128]{1,0:T(8,128)(2,1)S(1)}, bf16[256,128]{1,0:T(8,128)(2,1)S(1)}, u32[]{:S(2)}, u32[]{:S(2)}) collective-permute-start(bf16[256,128]{1,0:T(8,128)(2,1)S(1)} %shard_map.103.pair_ref), channel_id=1, source_target_pairs={{0,6},{1,25},{2,4},{3,27},{4,2},{5,29},{6,0},{7,31},{8,14},{9,17},... | collective-permute-start | bytes 196616 | tf_op jit(solution)/shard_map/ppermute | solution.py:248
  14.8 5.2 %collective-permute-start.2 = (bf16[256,128]{1,0:T(8,128)(2,1)S(1)}, bf16[256,128]{1,0:T(8,128)(2,1)S(1)}, u32[]{:S(2)}, u32[]{:S(2)}) collective-permute-start(bf16[256,128]{1,0:T(8,128)(2,1)S(1)} %shard_map.103.pair_ref), channel_id=1, source_target_pairs={{0,4},{1,17},{2,6},{3,19},{4,0},{5,21},{6,2},{7,23},{8,12},{9,25},... | collective-permute-start | bytes 196616 | tf_op jit(solution)/shard_map/ppermute | solution.py:248
  14.8 5.2 %collective-permute-start.1 = (bf16[256,128]{1,0:T(8,128)(2,1)S(1)}, bf16[256,128]{1,0:T(8,128)(2,1)S(1)}, u32[]{:S(2)}, u32[]{:S(2)}) collective-permute-start(bf16[256,128]{1,0:T(8,128)(2,1)S(1)} %shard_map.103.pair_ref), channel_id=1, source_target_pairs={{0,2},{1,9},{2,0},{3,11},{4,6},{5,13},{6,4},{7,15},{8,10},{9,1},{1... | collective-permute-start | bytes 196616 | tf_op jit(solution)/shard_map/ppermute | solution.py:248
  20.1 23.8 %collective-permute-start.5 = (bf16[128,1152]{1,0:T(8,128)(2,1)}, bf16[128,1152]{1,0:T(8,128)(2,1)S(1)}, u32[]{:S(2)}, u32[]{:S(2)}) collective-permute-start(bf16[128,1152]{1,0:T(8,128)(2,1)} %get-tuple-element.46), channel_id=1, source_target_pairs={{0,8},{8,0},{16,24},{24,16},{1,9},{9,1},{17,25},{25,17},{2,10},{10... | collective-permute-start | bytes 884744 | tf_op jit(solution)/shard_map/ppermute | solution.py:675
  21.6 26.2 %collective-permute-start.6 = (bf16[128,1152]{1,0:T(8,128)(2,1)}, bf16[128,1152]{1,0:T(8,128)(2,1)S(1)}, u32[]{:S(2)}, u32[]{:S(2)}) collective-permute-start(bf16[128,1152]{1,0:T(8,128)(2,1)} %get-tuple-element.47), channel_id=1, source_target_pairs={{0,16},{8,24},{16,0},{24,8},{1,17},{9,25},{17,1},{25,9},{2,18},{10... | collective-permute-start | bytes 884744 | tf_op jit(solution)/shard_map/ppermute | solution.py:675
  23.1 24.7 %collective-permute-start.7 = (bf16[128,1152]{1,0:T(8,128)(2,1)}, bf16[128,1152]{1,0:T(8,128)(2,1)S(1)}, u32[]{:S(2)}, u32[]{:S(2)}) collective-permute-start(bf16[128,1152]{1,0:T(8,128)(2,1)} %get-tuple-element.48), channel_id=1, source_target_pairs={{0,24},{8,16},{16,8},{24,0},{1,25},{9,17},{17,9},{25,1},{2,26},{10... | collective-permute-start | bytes 884744 | tf_op jit(solution)/shard_map/ppermute | solution.py:675
  26.1 5.4 %collective-permute-start.11 = (f32[16,128]{1,0:T(8,128)S(1)}, f32[16,128]{1,0:T(8,128)S(1)}, u32[]{:S(2)}, u32[]{:S(2)}) collective-permute-start(f32[16,128]{1,0:T(8,128)S(1)} %shard_map.106.pair_ref), channel_id=1, source_target_pairs={{0,6},{1,25},{2,4},{3,27},{4,2},{5,29},{6,0},{7,31},{8,14},{9,17},... | collective-permute-start | bytes 24584 | tf_op jit(solution)/shard_map/ppermute | solution.py:248
  27.7 4.5 %collective-permute-start.10 = (f32[16,128]{1,0:T(8,128)S(1)}, f32[16,128]{1,0:T(8,128)S(1)}, u32[]{:S(2)}, u32[]{:S(2)}) collective-permute-start(f32[16,128]{1,0:T(8,128)S(1)} %shard_map.106.pair_ref), channel_id=1, source_target_pairs={{0,4},{1,17},{2,6},{3,19},{4,0},{5,21},{6,2},{7,23},{8,12},{9,25},... | collective-permute-start | bytes 24584 | tf_op jit(solution)/shard_map/ppermute | solution.py:248
  31.6 3.7 %collective-permute-start.9 = (f32[16,128]{1,0:T(8,128)S(1)}, f32[16,128]{1,0:T(8,128)S(1)}, u32[]{:S(2)}, u32[]{:S(2)}) collective-permute-start(f32[16,128]{1,0:T(8,128)S(1)} %shard_map.106.pair_ref), channel_id=1, source_target_pairs={{0,2},{1,9},{2,0},{3,11},{4,6},{5,13},{6,4},{7,15},{8,10},{9,1},{1... | collective-permute-start | bytes 24584 | tf_op jit(solution)/shard_map/ppermute | solution.py:248
  35.2 4.9 %collective-permute-start.12 = (f32[48,128]{1,0:T(8,128)S(1)}, f32[48,128]{1,0:T(8,128)S(1)}, u32[]{:S(2)}, u32[]{:S(2)}) collective-permute-start(f32[48,128]{1,0:T(8,128)S(1)} %shard_map.107.got_ref), channel_id=1, source_target_pairs={{0,1},{1,0},{2,3},{3,2},{4,5},{5,4},{6,7},{7,6},{8,9},{9,8},{10,11... | collective-permute-start | bytes 73736 | tf_op jit(solution)/shard_map/ppermute | solution.py:675
  40.9 7.0 %collective-permute-start.15 = (bf16[128,128]{1,0:T(8,128)(2,1)S(1)}, bf16[128,128]{1,0:T(8,128)(2,1)S(1)}, u32[]{:S(2)}, u32[]{:S(2)}) collective-permute-start(bf16[128,128]{1,0:T(8,128)(2,1)S(1)} %shard_map.108.raw_ref.refs_4_), channel_id=1, source_target_pairs={{0,24},{8,16},{16,8},{24,0},{1,25},{9,17},{17,9},{25,1},{2,26},{10... | collective-permute-start | bytes 98312 | tf_op jit(solution)/shard_map/ppermute | solution.py:675
  42.4 5.5 %collective-permute-start.14 = (bf16[128,128]{1,0:T(8,128)(2,1)S(1)}, bf16[128,128]{1,0:T(8,128)(2,1)S(1)}, u32[]{:S(2)}, u32[]{:S(2)}) collective-permute-start(bf16[128,128]{1,0:T(8,128)(2,1)S(1)} %shard_map.108.raw_ref.refs_4_), channel_id=1, source_target_pairs={{0,16},{8,24},{16,0},{24,8},{1,17},{9,25},{17,1},{25,9},{2,18},{10... | collective-permute-start | bytes 98312 | tf_op jit(solution)/shard_map/ppermute | solution.py:675
  43.9 4.0 %collective-permute-start.13 = (bf16[128,128]{1,0:T(8,128)(2,1)S(1)}, bf16[128,128]{1,0:T(8,128)(2,1)S(1)}, u32[]{:S(2)}, u32[]{:S(2)}) collective-permute-start(bf16[128,128]{1,0:T(8,128)(2,1)S(1)} %shard_map.108.raw_ref.refs_4_), channel_id=1, source_target_pairs={{0,8},{8,0},{16,24},{24,16},{1,9},{9,1},{17,25},{25,17},{2,10},{10... | collective-permute-start | bytes 98312 | tf_op jit(solution)/shard_map/ppermute | solution.py:675
  51.2 5.9 %collective-permute-start.17 = (bf16[80,512]{1,0:T(8,128)(2,1)S(1)}, bf16[80,512]{1,0:T(8,128)(2,1)S(1)}, u32[]{:S(2)}, u32[]{:S(2)}) collective-permute-start(bf16[80,512]{1,0:T(8,128)(2,1)S(1)} %get-tuple-element.66), channel_id=1, source_target_pairs={{0,2},{1,3},{2,0},{3,1},{4,6},{5,7},{6,4},{7,5},{8,10},{9,11},{10,... | collective-permute-start | bytes 245768 | tf_op jit(solution)/shard_map/ppermute | solution.py:675
  51.7 9.3 %collective-permute-start.18 = (bf16[80,512]{1,0:T(8,128)(2,1)S(1)}, bf16[80,512]{1,0:T(8,128)(2,1)S(1)}, u32[]{:S(2)}, u32[]{:S(2)}) collective-permute-start(bf16[80,512]{1,0:T(8,128)(2,1)S(1)} %get-tuple-element.67), channel_id=1, source_target_pairs={{0,4},{1,5},{2,6},{3,7},{4,0},{5,1},{6,2},{7,3},{8,12},{9,13},{10,... | collective-permute-start | bytes 245768 | tf_op jit(solution)/shard_map/ppermute | solution.py:675
  53.4 7.6 %collective-permute-start.19 = (bf16[80,512]{1,0:T(8,128)(2,1)S(1)}, bf16[80,512]{1,0:T(8,128)(2,1)S(1)}, u32[]{:S(2)}, u32[]{:S(2)}) collective-permute-start(bf16[80,512]{1,0:T(8,128)(2,1)S(1)} %get-tuple-element.68), channel_id=1, source_target_pairs={{0,6},{1,7},{2,4},{3,5},{4,2},{5,3},{6,0},{7,1},{8,14},{9,15},{10,... | collective-permute-start | bytes 245768 | tf_op jit(solution)/shard_map/ppermute | solution.py:675
  61.1 4.6 %collective-permute-start.20 = (bf16[80,512]{1,0:T(8,128)(2,1)S(1)}, bf16[80,512]{1,0:T(8,128)(2,1)S(1)}, u32[]{:S(2)}, u32[]{:S(2)}) collective-permute-start(bf16[80,512]{1,0:T(8,128)(2,1)S(1)} %shard_map.112.refs_0_), channel_id=1, source_target_pairs={{0,2},{1,3},{2,0},{3,1},{4,6},{5,7},{6,4},{7,5},{8,10},{9,11},{10,... | collective-permute-start | bytes 245768 | tf_op jit(solution)/shard_map/ppermute | solution.py:675
  63.0 7.7 %collective-permute-start.23 = (bf16[80,512]{1,0:T(8,128)(2,1)S(1)}, bf16[80,512]{1,0:T(8,128)(2,1)S(1)}, u32[]{:S(2)}, u32[]{:S(2)}) collective-permute-start(bf16[80,512]{1,0:T(8,128)(2,1)S(1)} %shard_map.112.refs_0_), channel_id=1, source_target_pairs={{0,6},{1,7},{2,4},{3,5},{4,2},{5,3},{6,0},{7,1},{8,14},{9,15},{10,... | collective-permute-start | bytes 245768 | tf_op jit(solution)/shard_map/ppermute | solution.py:675
  65.7 7.4 %collective-permute-start.22 = (bf16[80,512]{1,0:T(8,128)(2,1)S(1)}, bf16[80,512]{1,0:T(8,128)(2,1)S(1)}, u32[]{:S(2)}, u32[]{:S(2)}) collective-permute-start(bf16[80,512]{1,0:T(8,128)(2,1)S(1)} %shard_map.112.refs_0_), channel_id=1, source_target_pairs={{0,4},{1,5},{2,6},{3,7},{4,0},{5,1},{6,2},{7,3},{8,12},{9,13},{10,... | collective-permute-start | bytes 245768 | tf_op jit(solution)/shard_map/ppermute | solution.py:675
  65.7 9.4 %collective-permute-start.29 = (bf16[160,512]{1,0:T(8,128)(2,1)S(1)}, bf16[160,512]{1,0:T(8,128)(2,1)S(1)}, u32[]{:S(2)}, u32[]{:S(2)}) collective-permute-start(bf16[160,512]{1,0:T(8,128)(2,1)S(1)} %shard_map.113.refs_0_), channel_id=1, source_target_pairs={{0,16},{8,24},{16,0},{24,8},{1,17},{9,25},{17,1},{25,9},{2,18},{10... | collective-permute-start | bytes 491528 | tf_op jit(solution)/shard_map/ppermute | solution.py:675
  66.2 8.8 %collective-permute-start.25 = (bf16[160,512]{1,0:T(8,128)(2,1)S(1)}, bf16[160,512]{1,0:T(8,128)(2,1)S(1)}, u32[]{:S(2)}, u32[]{:S(2)}) collective-permute-start(bf16[160,512]{1,0:T(8,128)(2,1)S(1)} %shard_map.113.refs_0_), channel_id=1, source_target_pairs={{0,8},{8,0},{16,24},{24,16},{1,9},{9,1},{17,25},{25,17},{2,10},{10... | collective-permute-start | bytes 491528 | tf_op jit(solution)/shard_map/ppermute | solution.py:675
  67.7 7.9 %collective-permute-start.21 = (bf16[160,512]{1,0:T(8,128)(2,1)S(1)}, bf16[160,512]{1,0:T(8,128)(2,1)S(1)}, u32[]{:S(2)}, u32[]{:S(2)}) collective-permute-start(bf16[160,512]{1,0:T(8,128)(2,1)S(1)} %shard_map.113.refs_0_), channel_id=1, source_target_pairs={{0,1},{1,0},{2,3},{3,2},{4,5},{5,4},{6,7},{7,6},{8,9},{9,8},{10,11... | collective-permute-start | bytes 491528 | tf_op jit(solution)/shard_map/ppermute | solution.py:675
  73.0 6.7 %collective-permute-start.31 = (bf16[160,512]{1,0:T(8,128)(2,1)S(1)}, bf16[160,512]{1,0:T(8,128)(2,1)S(1)}, u32[]{:S(2)}, u32[]{:S(2)}) collective-permute-start(bf16[160,512]{1,0:T(8,128)(2,1)S(1)} %shard_map.114.refs_2_), channel_id=1, source_target_pairs={{0,16},{8,24},{16,0},{24,8},{1,17},{9,25},{17,1},{25,9},{2,18},{10... | collective-permute-start | bytes 491528 | tf_op jit(solution)/shard_map/ppermute | solution.py:675
  73.6 8.0 %collective-permute-start.27 = (bf16[160,512]{1,0:T(8,128)(2,1)S(1)}, bf16[160,512]{1,0:T(8,128)(2,1)S(1)}, u32[]{:S(2)}, u32[]{:S(2)}) collective-permute-start(bf16[160,512]{1,0:T(8,128)(2,1)S(1)} %shard_map.114.refs_2_), channel_id=1, source_target_pairs={{0,8},{8,0},{16,24},{24,16},{1,9},{9,1},{17,25},{25,17},{2,10},{10... | collective-permute-start | bytes 491528 | tf_op jit(solution)/shard_map/ppermute | solution.py:675
  75.1 6.5 %collective-permute-start.24 = (bf16[160,512]{1,0:T(8,128)(2,1)S(1)}, bf16[160,512]{1,0:T(8,128)(2,1)S(1)}, u32[]{:S(2)}, u32[]{:S(2)}) collective-permute-start(bf16[160,512]{1,0:T(8,128)(2,1)S(1)} %shard_map.114.refs_2_), channel_id=1, source_target_pairs={{0,1},{1,0},{2,3},{3,2},{4,5},{5,4},{6,7},{7,6},{8,9},{9,8},{10,11... | collective-permute-start | bytes 491528 | tf_op jit(solution)/shard_map/ppermute | solution.py:675
  75.1 7.0 %collective-permute-start.30 = (bf16[160,512]{1,0:T(8,128)(2,1)S(1)}, bf16[160,512]{1,0:T(8,128)(2,1)S(1)}, u32[]{:S(2)}, u32[]{:S(2)}) collective-permute-start(bf16[160,512]{1,0:T(8,128)(2,1)S(1)} %collective-permute-done.29.refs_4_.refs_8_), channel_id=1, source_target_pairs={{0,1},{1,0},{2,3},{3,2},{4,5},{5,4},{6,7},{7,6},{8,9},{9,8},{10,11... | collective-permute-start | bytes 491528 | tf_op jit(solution)/shard_map/ppermute | solution.py:675
  75.6 6.9 %collective-permute-start.33 = (bf16[160,512]{1,0:T(8,128)(2,1)S(1)}, bf16[160,512]{1,0:T(8,128)(2,1)S(1)}, u32[]{:S(2)}, u32[]{:S(2)}) collective-permute-start(bf16[160,512]{1,0:T(8,128)(2,1)S(1)} %collective-permute-done.25.refs_0_.refs_4_), channel_id=1, source_target_pairs={{0,16},{8,24},{16,0},{24,8},{1,17},{9,25},{17,1},{25,9},{2,18},{10... | collective-permute-start | bytes 491528 | tf_op jit(solution)/shard_map/ppermute | solution.py:675
  79.8 5.3 %collective-permute-start.35 = (bf16[160,512]{1,0:T(8,128)(2,1)S(1)}, bf16[160,512]{1,0:T(8,128)(2,1)S(1)}, u32[]{:S(2)}, u32[]{:S(2)}) collective-permute-start(bf16[160,512]{1,0:T(8,128)(2,1)S(1)} %collective-permute-done.31.refs_6_.refs_10_), channel_id=1, source_target_pairs={{0,8},{8,0},{16,24},{24,16},{1,9},{9,1},{17,25},{25,17},{2,10},{10... | collective-permute-start | bytes 491528 | tf_op jit(solution)/shard_map/ppermute | solution.py:675
  81.6 4.6 %collective-permute-start.26 = (bf16[160,512]{1,0:T(8,128)(2,1)S(1)}, bf16[160,512]{1,0:T(8,128)(2,1)S(1)}, u32[]{:S(2)}, u32[]{:S(2)}) collective-permute-start(bf16[160,512]{1,0:T(8,128)(2,1)S(1)} %collective-permute-done.25.refs_0_.refs_4_), channel_id=1, source_target_pairs={{0,1},{1,0},{2,3},{3,2},{4,5},{5,4},{6,7},{7,6},{8,9},{9,8},{10,11... | collective-permute-start | bytes 491528 | tf_op jit(solution)/shard_map/ppermute | solution.py:675
  81.6 4.6 %collective-permute-start.32 = (bf16[160,512]{1,0:T(8,128)(2,1)S(1)}, bf16[160,512]{1,0:T(8,128)(2,1)S(1)}, u32[]{:S(2)}, u32[]{:S(2)}) collective-permute-start(bf16[160,512]{1,0:T(8,128)(2,1)S(1)} %collective-permute-done.31.refs_6_.refs_10_), channel_id=1, source_target_pairs={{0,1},{1,0},{2,3},{3,2},{4,5},{5,4},{6,7},{7,6},{8,9},{9,8},{10,11... | collective-permute-start | bytes 491528 | tf_op jit(solution)/shard_map/ppermute | solution.py:675
  82.1 4.1 %collective-permute-start.28 = (bf16[160,512]{1,0:T(8,128)(2,1)S(1)}, bf16[160,512]{1,0:T(8,128)(2,1)S(1)}, u32[]{:S(2)}, u32[]{:S(2)}) collective-permute-start(bf16[160,512]{1,0:T(8,128)(2,1)S(1)} %collective-permute-done.27.refs_2_.refs_6_), channel_id=1, source_target_pairs={{0,1},{1,0},{2,3},{3,2},{4,5},{5,4},{6,7},{7,6},{8,9},{9,8},{10,11... | collective-permute-start | bytes 491528 | tf_op jit(solution)/shard_map/ppermute | solution.py:675
  82.5 5.4 %collective-permute-start.34 = (bf16[160,512]{1,0:T(8,128)(2,1)S(1)}, bf16[160,512]{1,0:T(8,128)(2,1)S(1)}, u32[]{:S(2)}, u32[]{:S(2)}) collective-permute-start(bf16[160,512]{1,0:T(8,128)(2,1)S(1)} %collective-permute-done.33.refs_12_), channel_id=1, source_target_pairs={{0,1},{1,0},{2,3},{3,2},{4,5},{5,4},{6,7},{7,6},{8,9},{9,8},{10,11... | collective-permute-start | bytes 491528 | tf_op jit(solution)/shard_map/ppermute | solution.py:675
  (9 other events, 72.3 us)

commit v3 on v2

--- a/solution.py
+++ b/solution.py
@@ -98,9 +98,12 @@
             part = mm(basis[...], block).astype(BF16)
             spec[g] = part
             both = mm(part, mix[...])
-            mixed[g] = both
             real_part, imag_part = both[:half], both[half:]
-            piece = jnp.log1p(real_part * real_part + imag_part * imag_part)
+            powers = real_part * real_part + imag_part * imag_part
+            share = 2.0 / (1.0 + powers)
+            mixed[g, :half] = real_part * share
+            mixed[g, half:] = imag_part * share
+            piece = jnp.log1p(powers)
             for k in range(freqs):
                 feat[pl.ds(base, SUB), k * filters : (k + 1) * filters] = piece[
                     k * SUB : (k + 1) * SUB
@@ -435,15 +438,14 @@
     half = freqs * SUB
 
     def one(g, total):
-        real_part, imag_part = mixed[g, :half], mixed[g, half:]
-        powers = real_part * real_part + imag_part * imag_part
         base = pl.multiple_of(g * SUB, SUB)
         grads = jnp.concatenate(
             [grad_feat[pl.ds(base, SUB), k * filters : (k + 1) * filters] for k in range(freqs)],
             axis=0,
         )
-        share = 2.0 * grads / (1.0 + powers)
-        grad_mixed = jnp.concatenate([real_part * share, imag_part * share], axis=0).astype(BF16)
+        grad_mixed = jnp.concatenate(
+            [mixed[g, :half] * grads, mixed[g, half:] * grads], axis=0
+        ).astype(BF16)
         return total + mm_tn(grad_mixed, spec[g])
 
     total = lax.fori_loop(0, groups, one, jnp.zeros((filters, spec.shape[2]), F32), unroll=4)
@@ -719,14 +721,12 @@
     planes = {(0, 0): stack(shares[:middle]), (0, 1): stack(shares[middle:])}
     single = [hop for hop in across if hop & (hop - 1) == 0]
     several = [hop for hop in across if hop & (hop - 1)]
-    for turn in range(2):
-        for k, hop in enumerate(single):
-            half = (k + turn) % 2
+    for half in range(2):
+        for hop in single:
             planes[hop, half] = swap(planes[0, half], "blk", hop)
-    for hop in several:
-        low, high = hop & -hop, 1 << (hop.bit_length() - 1)
-        planes[hop, 0] = swap(planes[hop ^ high, 0], "blk", high)
-        planes[hop, 1] = swap(planes[hop ^ low, 1], "blk", low)
+        for hop in several:
+            bit = hop & -hop if half else 1 << (hop.bit_length() - 1)
+            planes[hop, half] = swap(planes[hop ^ bit, half], "blk", bit)
     parts, done = {}, []
     groups = [group for group in ([0], single, several) if group]
     for order, group in enumerate(groups):

time: 89.9 us -> 89.8 us (level)
  no operation moved by 1% of the time
where the time goes in v3:
time: 89.8 us; the launch traced here: 89.7 us
  starting transfers between devices  37.2 us (41%)
  waiting for transfers between devices  32.2 us (36%)
  Pallas kernels  19.4 us (22%)
    ppermute x31, starting transfers between devices, swap(): return lax.ppermute(block, axis, [(src, src ^ bit) for src in range(size)])  29.5 us
    ppermute x31, waiting for transfers between devices, swap(): return lax.ppermute(block, axis, [(src, src ^ bit) for src in range(size)])  20.7 us
    ppermute x6, waiting for transfers between devices, cross(): got.append(lax.ppermute(pair, ('blk', 'dp'), routes))  11.5 us
    ppermute x6, starting transfers between devices, cross(): got.append(lax.ppermute(pair, ('blk', 'dp'), routes))  7.73 us
    pallas_call x1, Pallas kernels, encode(): pl.pallas_call(functools.partial(encode_kernel, freqs, size, rounds), in_...  7.7 us
    pallas_call x3, Pallas kernels, finish(): pl.pallas_call(functools.partial(finish_kernel, lay, tuple(parts), bool(d...  4.6 us
    pallas_call x1, Pallas kernels, lower(): pl.pallas_call(functools.partial(lower_kernel, freqs, columns), in_specs=...  3.3 us
  transfers between devices with their start and end apart: 37, of which 16 were waited for; matrix products, arithmetic and copies ran while one was open for 0% of the time, Pallas kernels for 9%

profile of v3, /device:TPU:0, one launch (start us, length us, event | category | flops | bytes accessed | tf_op | source)
XLA Modules:
  0.0 89.7 jit_solution(11598083997163313415)
XLA Ops:
  0.7 7.7 %shard_map.102 = (bf16[128,1152]{1,0:T(8,128)(2,1)}, bf16[128,1152]{1,0:T(8,128)(2,1)}, bf16[128,1152]{1,0:T(8,128)(2,1)}, bf16[128,1152]{1,0:T(8,128)(2,1)}, bf...) custom-call(bf16[128,64,256]{2,1,0:T(8,128)(2,1)} %patch_hbm.1, ...), custom_call_target="tpu_custom_call" | custom-call | flops 3000000000 | bytes 14000000 | tf_op jit(solution)/shard_map/pallas_call | solution.py:189
  9.8 5.0 %collective-permute-start.3 = (bf16[256,128]{1,0:T(8,128)(2,1)S(1)}, bf16[256,128]{1,0:T(8,128)(2,1)S(1)}, u32[]{:S(2)}, u32[]{:S(2)}) collective-permute-start(bf16[256,128]{1,0:T(8,128)(2,1)S(1)} %shard_map.103.pair_ref), channel_id=1, source_target_pairs={{0,6},{1,25},{2,4},{3,27},{4,2},{5,29},{6,0},{7,31},{8,14},{9,17},... | collective-permute-start | bytes 196616 | tf_op jit(solution)/shard_map/ppermute | solution.py:251
  15.4 1.7 %collective-permute-done.3.refs_2_ = bf16[256,128]{1,0:T(8,128)(2,1)S(1)} collective-permute-done((bf16[256,128]{1,0:T(8,128)(2,1)S(1)}, bf16[256,128]{1,0:T(8,128)(2,1)S(1)}, u32[]{:S(2)}, u32[]{:S(2)}) %collective-permute-start.3) | collective-permute-done | bytes 65568 | tf_op jit(solution)/shard_map/ppermute | solution.py:251
  17.1 2.8 %collective-permute-done.2.refs_1_ = bf16[256,128]{1,0:T(8,128)(2,1)S(1)} collective-permute-done((bf16[256,128]{1,0:T(8,128)(2,1)S(1)}, bf16[256,128]{1,0:T(8,128)(2,1)S(1)}, u32[]{:S(2)}, u32[]{:S(2)}) %collective-permute-start.2) | collective-permute-done | bytes 65568 | tf_op jit(solution)/shard_map/ppermute | solution.py:251
  20.1 1.6 %collective-permute-start.5 = (bf16[128,1152]{1,0:T(8,128)(2,1)}, bf16[128,1152]{1,0:T(8,128)(2,1)S(1)}, u32[]{:S(2)}, u32[]{:S(2)}) collective-permute-start(bf16[128,1152]{1,0:T(8,128)(2,1)} %get-tuple-element.46), channel_id=1, source_target_pairs={{0,8},{8,0},{16,24},{24,16},{1,9},{9,1},{17,25},{25,17},{2,10},{10... | collective-permute-start | bytes 884744 | tf_op jit(solution)/shard_map/ppermute | solution.py:677
  21.6 1.5 %collective-permute-start.6 = (bf16[128,1152]{1,0:T(8,128)(2,1)}, bf16[128,1152]{1,0:T(8,128)(2,1)S(1)}, u32[]{:S(2)}, u32[]{:S(2)}) collective-permute-start(bf16[128,1152]{1,0:T(8,128)(2,1)} %get-tuple-element.47), channel_id=1, source_target_pairs={{0,16},{8,24},{16,0},{24,8},{1,17},{9,25},{17,1},{25,9},{2,18},{10... | collective-permute-start | bytes 884744 | tf_op jit(solution)/shard_map/ppermute | solution.py:677
  23.6 1.3 %shard_map.105 = (f32[128,128]{1,0:T(8,128)S(1)}, f32[8,128]{1,0:T(8,128)S(1)}, f32[1,128]{1,0:T(1,128)}, bf16[512,128]{1,0:T(8,128)(2,1)S(1)}, bf16[1024,128]{1,0:T(8,128)(2,1)S(1)}) custom-call(s32[1,128]{1,0:T(1,128)S(1)} %bitcast.3, s32[1,128]{1,0:T(1,128)S(1)} %bitcast.4, bf16[128,128]{1,0:T(8,128)(2,1)S(1)} %get-tuple-element.40.own_ref.units_ref, ...), custom_call_target="tpu_custom_call" | custom-call | flops 400000000 | bytes 1000000 | tf_op jit(solution)/shard_map/pallas_call | solution.py:329
  26.1 1.6 %collective-permute-start.11 = (f32[16,128]{1,0:T(8,128)S(1)}, f32[16,128]{1,0:T(8,128)S(1)}, u32[]{:S(2)}, u32[]{:S(2)}) collective-permute-start(f32[16,128]{1,0:T(8,128)S(1)} %shard_map.106.pair_ref), channel_id=1, source_target_pairs={{0,6},{1,25},{2,4},{3,27},{4,2},{5,29},{6,0},{7,31},{8,14},{9,17},... | collective-permute-start | bytes 24584 | tf_op jit(solution)/shard_map/ppermute | solution.py:251
  28.2 3.4 %collective-permute-done.11.refs_2_ = f32[16,128]{1,0:T(8,128)S(1)} collective-permute-done((f32[16,128]{1,0:T(8,128)S(1)}, f32[16,128]{1,0:T(8,128)S(1)}, u32[]{:S(2)}, u32[]{:S(2)}) %collective-permute-start.11) | collective-permute-done | bytes 8224 | tf_op jit(solution)/shard_map/ppermute | solution.py:251
  32.3 3.0 %collective-permute-done.9.refs_0_ = f32[16,128]{1,0:T(8,128)S(1)} collective-permute-done((f32[16,128]{1,0:T(8,128)S(1)}, f32[16,128]{1,0:T(8,128)S(1)}, u32[]{:S(2)}, u32[]{:S(2)}) %collective-permute-start.9) | collective-permute-done | bytes 8224 | tf_op jit(solution)/shard_map/ppermute | solution.py:251
  35.2 4.0 %collective-permute-start.12 = (f32[48,128]{1,0:T(8,128)S(1)}, f32[48,128]{1,0:T(8,128)S(1)}, u32[]{:S(2)}, u32[]{:S(2)}) collective-permute-start(f32[48,128]{1,0:T(8,128)S(1)} %shard_map.107.got_ref), channel_id=1, source_target_pairs={{0,1},{1,0},{2,3},{3,2},{4,5},{5,4},{6,7},{7,6},{8,9},{9,8},{10,11... | collective-permute-start | bytes 73736 | tf_op jit(solution)/shard_map/ppermute | solution.py:677
  40.9 1.5 %collective-permute-start.15 = (bf16[128,128]{1,0:T(8,128)(2,1)S(1)}, bf16[128,128]{1,0:T(8,128)(2,1)S(1)}, u32[]{:S(2)}, u32[]{:S(2)}) collective-permute-start(bf16[128,128]{1,0:T(8,128)(2,1)S(1)} %shard_map.108.raw_ref.refs_4_), channel_id=1, source_target_pairs={{0,24},{8,16},{16,8},{24,0},{1,25},{9,17},{17,9},{25,1},{2,26},{10... | collective-permute-start | bytes 98312 | tf_op jit(solution)/shard_map/ppermute | solution.py:677
  42.4 1.5 %collective-permute-start.14 = (bf16[128,128]{1,0:T(8,128)(2,1)S(1)}, bf16[128,128]{1,0:T(8,128)(2,1)S(1)}, u32[]{:S(2)}, u32[]{:S(2)}) collective-permute-start(bf16[128,128]{1,0:T(8,128)(2,1)S(1)} %shard_map.108.raw_ref.refs_4_), channel_id=1, source_target_pairs={{0,16},{8,24},{16,0},{24,8},{1,17},{9,25},{17,1},{25,9},{2,18},{10... | collective-permute-start | bytes 98312 | tf_op jit(solution)/shard_map/ppermute | solution.py:677
  44.5 3.3 %shard_map.109.refs_9_ = f32[256,128]{1,0:T(8,128)S(1)} custom-call(bf16[128,128]{1,0:T(8,128)(2,1)S(1)} %shard_map.108.raw_ref.refs_4_, f32[128,128]{1,0:T(8,128)S(1)} %get-tuple-element.58.rscale_ref, bf16[2048,512]{1,0:T(8,128)(2,1)S(1)} %get-tuple-element.59.in_w, bf16[128,2048]{1,0:T(8,128)(2,1)S(1)} %get-tuple-element.60.normed, ...), custom_call_target="tpu_custom_call" | custom-call | flops 1000000000 | bytes 7000000 | tf_op jit(solution)/shard_map/pallas_call | solution.py:459
  47.9 1.5 %shard_map.110 = (f32[4,80,512]{2,1,0:T(8,128)S(1)}, bf16[4,80,512]{2,1,0:T(8,128)(2,1)S(1)}) custom-call(bf16[128,1152]{1,0:T(8,128)(2,1)S(1)} %copy-done, bf16[128,1152]{1,0:T(8,128)(2,1)S(1)} %collective-permute-done.5.refs_1_, bf16[128,1152]{1,0:T(8,128)(2,1)S(1)} %collective-permute-done.6.refs_2_, ...), custom_call_target="tpu_custom_call" | custom-call | flops 600000000 | bytes 4000000 | tf_op jit(solution)/shard_map/pallas_call | solution.py:537
  49.4 1.6 %collective-permute-done.16.got_ref = bf16[4,80,512]{2,1,0:T(8,128)(2,1)S(1)} collective-permute-done((bf16[4,80,512]{2,1,0:T(8,128)(2,1)S(1)}, bf16[4,80,512]{2,1,0:T(8,128)(2,1)S(1)}, u32[]{:S(2)}, u32[]{:S(2)}) %collective-permute-start.16) | collective-permute-done | bytes 327712 | tf_op jit(solution)/shard_map/ppermute | solution.py:677
  51.7 1.7 %collective-permute-start.18 = (bf16[80,512]{1,0:T(8,128)(2,1)S(1)}, bf16[80,512]{1,0:T(8,128)(2,1)S(1)}, u32[]{:S(2)}, u32[]{:S(2)}) collective-permute-start(bf16[80,512]{1,0:T(8,128)(2,1)S(1)} %get-tuple-element.67), channel_id=1, source_target_pairs={{0,4},{1,5},{2,6},{3,7},{4,0},{5,1},{6,2},{7,3},{8,12},{9,13},{10,... | collective-permute-start | bytes 245768 | tf_op jit(solution)/shard_map/ppermute | solution.py:677
  53.4 2.2 %collective-permute-start.19 = (bf16[80,512]{1,0:T(8,128)(2,1)S(1)}, bf16[80,512]{1,0:T(8,128)(2,1)S(1)}, u32[]{:S(2)}, u32[]{:S(2)}) collective-permute-start(bf16[80,512]{1,0:T(8,128)(2,1)S(1)} %get-tuple-element.68), channel_id=1, source_target_pairs={{0,6},{1,7},{2,4},{3,5},{4,2},{5,3},{6,0},{7,1},{8,14},{9,15},{10,... | collective-permute-start | bytes 245768 | tf_op jit(solution)/shard_map/ppermute | solution.py:677
  55.6 1.4 %collective-permute-done.17.refs_0_ = bf16[80,512]{1,0:T(8,128)(2,1)S(1)} collective-permute-done((bf16[80,512]{1,0:T(8,128)(2,1)S(1)}, bf16[80,512]{1,0:T(8,128)(2,1)S(1)}, u32[]{:S(2)}, u32[]{:S(2)}) %collective-permute-start.17) | collective-permute-done | bytes 81952 | tf_op jit(solution)/shard_map/ppermute | solution.py:677
  57.0 4.0 %collective-permute-done.18.refs_1_ = bf16[80,512]{1,0:T(8,128)(2,1)S(1)} collective-permute-done((bf16[80,512]{1,0:T(8,128)(2,1)S(1)}, bf16[80,512]{1,0:T(8,128)(2,1)S(1)}, u32[]{:S(2)}, u32[]{:S(2)}) %collective-permute-start.18) | collective-permute-done | bytes 81952 | tf_op jit(solution)/shard_map/ppermute | solution.py:677
  61.0 1.9 %collective-permute-start.20 = (bf16[80,512]{1,0:T(8,128)(2,1)S(1)}, bf16[80,512]{1,0:T(8,128)(2,1)S(1)}, u32[]{:S(2)}, u32[]{:S(2)}) collective-permute-start(bf16[80,512]{1,0:T(8,128)(2,1)S(1)} %shard_map.112.refs_0_), channel_id=1, source_target_pairs={{0,2},{1,3},{2,0},{3,1},{4,6},{5,7},{6,4},{7,5},{8,10},{9,11},{10,... | collective-permute-start | bytes 245768 | tf_op jit(solution)/shard_map/ppermute | solution.py:677
  63.0 2.6 %collective-permute-start.23 = (bf16[80,512]{1,0:T(8,128)(2,1)S(1)}, bf16[80,512]{1,0:T(8,128)(2,1)S(1)}, u32[]{:S(2)}, u32[]{:S(2)}) collective-permute-start(bf16[80,512]{1,0:T(8,128)(2,1)S(1)} %shard_map.112.refs_0_), channel_id=1, source_target_pairs={{0,6},{1,7},{2,4},{3,5},{4,2},{5,3},{6,0},{7,1},{8,14},{9,15},{10,... | collective-permute-start | bytes 245768 | tf_op jit(solution)/shard_map/ppermute | solution.py:677
  66.2 1.5 %collective-permute-start.25 = (bf16[160,512]{1,0:T(8,128)(2,1)S(1)}, bf16[160,512]{1,0:T(8,128)(2,1)S(1)}, u32[]{:S(2)}, u32[]{:S(2)}) collective-permute-start(bf16[160,512]{1,0:T(8,128)(2,1)S(1)} %shard_map.113.refs_0_), channel_id=1, source_target_pairs={{0,8},{8,0},{16,24},{24,16},{1,9},{9,1},{17,25},{25,17},{2,10},{10... | collective-permute-start | bytes 491528 | tf_op jit(solution)/shard_map/ppermute | solution.py:677
  67.7 2.9 %collective-permute-done.23.refs_1_ = bf16[80,512]{1,0:T(8,128)(2,1)S(1)} collective-permute-done((bf16[80,512]{1,0:T(8,128)(2,1)S(1)}, bf16[80,512]{1,0:T(8,128)(2,1)S(1)}, u32[]{:S(2)}, u32[]{:S(2)}) %collective-permute-start.23) | collective-permute-done | bytes 81952 | tf_op jit(solution)/shard_map/ppermute | solution.py:677
  70.6 2.3 %collective-permute-done.22.refs_0_ = bf16[80,512]{1,0:T(8,128)(2,1)S(1)} collective-permute-done((bf16[80,512]{1,0:T(8,128)(2,1)S(1)}, bf16[80,512]{1,0:T(8,128)(2,1)S(1)}, u32[]{:S(2)}, u32[]{:S(2)}) %collective-permute-start.22) | collective-permute-done | bytes 81952 | tf_op jit(solution)/shard_map/ppermute | solution.py:677
  73.5 1.5 %collective-permute-start.27 = (bf16[160,512]{1,0:T(8,128)(2,1)S(1)}, bf16[160,512]{1,0:T(8,128)(2,1)S(1)}, u32[]{:S(2)}, u32[]{:S(2)}) collective-permute-start(bf16[160,512]{1,0:T(8,128)(2,1)S(1)} %shard_map.114.refs_2_), channel_id=1, source_target_pairs={{0,8},{8,0},{16,24},{24,16},{1,9},{9,1},{17,25},{25,17},{2,10},{10... | collective-permute-start | bytes 491528 | tf_op jit(solution)/shard_map/ppermute | solution.py:677
  75.5 1.5 %collective-permute-start.33 = (bf16[160,512]{1,0:T(8,128)(2,1)S(1)}, bf16[160,512]{1,0:T(8,128)(2,1)S(1)}, u32[]{:S(2)}, u32[]{:S(2)}) collective-permute-start(bf16[160,512]{1,0:T(8,128)(2,1)S(1)} %collective-permute-done.25.refs_0_.refs_4_), channel_id=1, source_target_pairs={{0,16},{8,24},{16,0},{24,8},{1,17},{9,25},{17,1},{25,9},{2,18},{10... | collective-permute-start | bytes 491528 | tf_op jit(solution)/shard_map/ppermute | solution.py:677
  77.0 2.7 %collective-permute-done.31.refs_6_.refs_10_ = bf16[160,512]{1,0:T(8,128)(2,1)S(1)} collective-permute-done((bf16[160,512]{1,0:T(8,128)(2,1)S(1)}, bf16[160,512]{1,0:T(8,128)(2,1)S(1)}, u32[]{:S(2)}, u32[]{:S(2)}) %collective-permute-start.31) | collective-permute-done | bytes 163872 | tf_op jit(solution)/shard_map/ppermute | solution.py:677
  79.7 1.8 %collective-permute-start.35 = (bf16[160,512]{1,0:T(8,128)(2,1)S(1)}, bf16[160,512]{1,0:T(8,128)(2,1)S(1)}, u32[]{:S(2)}, u32[]{:S(2)}) collective-permute-start(bf16[160,512]{1,0:T(8,128)(2,1)S(1)} %collective-permute-done.31.refs_6_.refs_10_), channel_id=1, source_target_pairs={{0,8},{8,0},{16,24},{24,16},{1,9},{9,1},{17,25},{25,17},{2,10},{10... | collective-permute-start | bytes 491528 | tf_op jit(solution)/shard_map/ppermute | solution.py:677
  82.6 2.4 %collective-permute-done.35.refs_14_ = bf16[160,512]{1,0:T(8,128)(2,1)S(1)} collective-permute-done((bf16[160,512]{1,0:T(8,128)(2,1)S(1)}, bf16[160,512]{1,0:T(8,128)(2,1)S(1)}, u32[]{:S(2)}, u32[]{:S(2)}) %collective-permute-start.35) | collective-permute-done | bytes 163872 | tf_op jit(solution)/shard_map/ppermute | solution.py:677
  86.2 1.7 %shard_map.116 = (f32[2048,512]{1,0:T(8,128)}, f32[512,128]{1,0:T(8,128)}) custom-call(bf16[160,512]{1,0:T(8,128)(2,1)S(1)} %collective-permute-done.25.refs_0_.refs_4_, bf16[160,512]{1,0:T(8,128)(2,1)S(1)} %collective-permute-done.26.refs_1_.refs_5_, ...), custom_call_target="tpu_custom_call", output_to_operand_aliasing={{0}: (8, {}), {1}: (9, {})} | custom-call | flops 1000000 | bytes 8000000 | tf_op jit(solution)/shard_map/pallas_call | solution.py:640
  87.9 1.8 %shard_map.117 = (f32[2048,512]{1,0:T(8,128)}, f32[512,128]{1,0:T(8,128)}, f32[256,128]{1,0:T(8,128)}) custom-call(bf16[160,512]{1,0:T(8,128)(2,1)S(1)} %shard_map.113.refs_0_, bf16[160,512]{1,0:T(8,128)(2,1)S(1)} %collective-permute-done.21.refs_1_, bf16[160,512]{1,0:T(8,128)(2,1)S(1)} %shard_map.114.refs_2_, ...), custom_call_target="tpu_custom_call", output_to_operand_aliasing={{0}: (16, {}), {1}: (17, {})} | custom-call | flops 1000000 | bytes 8000000 | tf_op jit(solution)/shard_map/pallas_call | solution.py:640
  (66 shorter events, 11.9 us)
Async XLA Ops:
  9.8 7.3 %collective-permute-start.3 = (bf16[256,128]{1,0:T(8,128)(2,1)S(1)}, bf16[256,128]{1,0:T(8,128)(2,1)S(1)}, u32[]{:S(2)}, u32[]{:S(2)}) collective-permute-start(bf16[256,128]{1,0:T(8,128)(2,1)S(1)} %shard_map.103.pair_ref), channel_id=1, source_target_pairs={{0,6},{1,25},{2,4},{3,27},{4,2},{5,29},{6,0},{7,31},{8,14},{9,17},... | collective-permute-start | bytes 196616 | tf_op jit(solution)/shard_map/ppermute | solution.py:251
  14.8 5.2 %collective-permute-start.2 = (bf16[256,128]{1,0:T(8,128)(2,1)S(1)}, bf16[256,128]{1,0:T(8,128)(2,1)S(1)}, u32[]{:S(2)}, u32[]{:S(2)}) collective-permute-start(bf16[256,128]{1,0:T(8,128)(2,1)S(1)} %shard_map.103.pair_ref), channel_id=1, source_target_pairs={{0,4},{1,17},{2,6},{3,19},{4,0},{5,21},{6,2},{7,23},{8,12},{9,25},... | collective-permute-start | bytes 196616 | tf_op jit(solution)/shard_map/ppermute | solution.py:251
  14.8 5.2 %collective-permute-start.1 = (bf16[256,128]{1,0:T(8,128)(2,1)S(1)}, bf16[256,128]{1,0:T(8,128)(2,1)S(1)}, u32[]{:S(2)}, u32[]{:S(2)}) collective-permute-start(bf16[256,128]{1,0:T(8,128)(2,1)S(1)} %shard_map.103.pair_ref), channel_id=1, source_target_pairs={{0,2},{1,9},{2,0},{3,11},{4,6},{5,13},{6,4},{7,15},{8,10},{9,1},{1... | collective-permute-start | bytes 196616 | tf_op jit(solution)/shard_map/ppermute | solution.py:251
  20.1 23.8 %collective-permute-start.5 = (bf16[128,1152]{1,0:T(8,128)(2,1)}, bf16[128,1152]{1,0:T(8,128)(2,1)S(1)}, u32[]{:S(2)}, u32[]{:S(2)}) collective-permute-start(bf16[128,1152]{1,0:T(8,128)(2,1)} %get-tuple-element.46), channel_id=1, source_target_pairs={{0,8},{8,0},{16,24},{24,16},{1,9},{9,1},{17,25},{25,17},{2,10},{10... | collective-permute-start | bytes 884744 | tf_op jit(solution)/shard_map/ppermute | solution.py:677
  21.6 26.2 %collective-permute-start.6 = (bf16[128,1152]{1,0:T(8,128)(2,1)}, bf16[128,1152]{1,0:T(8,128)(2,1)S(1)}, u32[]{:S(2)}, u32[]{:S(2)}) collective-permute-start(bf16[128,1152]{1,0:T(8,128)(2,1)} %get-tuple-element.47), channel_id=1, source_target_pairs={{0,16},{8,24},{16,0},{24,8},{1,17},{9,25},{17,1},{25,9},{2,18},{10... | collective-permute-start | bytes 884744 | tf_op jit(solution)/shard_map/ppermute | solution.py:677
  23.1 24.7 %collective-permute-start.7 = (bf16[128,1152]{1,0:T(8,128)(2,1)}, bf16[128,1152]{1,0:T(8,128)(2,1)S(1)}, u32[]{:S(2)}, u32[]{:S(2)}) collective-permute-start(bf16[128,1152]{1,0:T(8,128)(2,1)} %get-tuple-element.48), channel_id=1, source_target_pairs={{0,24},{8,16},{16,8},{24,0},{1,25},{9,17},{17,9},{25,1},{2,26},{10... | collective-permute-start | bytes 884744 | tf_op jit(solution)/shard_map/ppermute | solution.py:677
  26.1 5.4 %collective-permute-start.11 = (f32[16,128]{1,0:T(8,128)S(1)}, f32[16,128]{1,0:T(8,128)S(1)}, u32[]{:S(2)}, u32[]{:S(2)}) collective-permute-start(f32[16,128]{1,0:T(8,128)S(1)} %shard_map.106.pair_ref), channel_id=1, source_target_pairs={{0,6},{1,25},{2,4},{3,27},{4,2},{5,29},{6,0},{7,31},{8,14},{9,17},... | collective-permute-start | bytes 24584 | tf_op jit(solution)/shard_map/ppermute | solution.py:251
  27.7 4.5 %collective-permute-start.10 = (f32[16,128]{1,0:T(8,128)S(1)}, f32[16,128]{1,0:T(8,128)S(1)}, u32[]{:S(2)}, u32[]{:S(2)}) collective-permute-start(f32[16,128]{1,0:T(8,128)S(1)} %shard_map.106.pair_ref), channel_id=1, source_target_pairs={{0,4},{1,17},{2,6},{3,19},{4,0},{5,21},{6,2},{7,23},{8,12},{9,25},... | collective-permute-start | bytes 24584 | tf_op jit(solution)/shard_map/ppermute | solution.py:251
  31.6 3.7 %collective-permute-start.9 = (f32[16,128]{1,0:T(8,128)S(1)}, f32[16,128]{1,0:T(8,128)S(1)}, u32[]{:S(2)}, u32[]{:S(2)}) collective-permute-start(f32[16,128]{1,0:T(8,128)S(1)} %shard_map.106.pair_ref), channel_id=1, source_target_pairs={{0,2},{1,9},{2,0},{3,11},{4,6},{5,13},{6,4},{7,15},{8,10},{9,1},{1... | collective-permute-start | bytes 24584 | tf_op jit(solution)/shard_map/ppermute | solution.py:251
  35.2 4.9 %collective-permute-start.12 = (f32[48,128]{1,0:T(8,128)S(1)}, f32[48,128]{1,0:T(8,128)S(1)}, u32[]{:S(2)}, u32[]{:S(2)}) collective-permute-start(f32[48,128]{1,0:T(8,128)S(1)} %shard_map.107.got_ref), channel_id=1, source_target_pairs={{0,1},{1,0},{2,3},{3,2},{4,5},{5,4},{6,7},{7,6},{8,9},{9,8},{10,11... | collective-permute-start | bytes 73736 | tf_op jit(solution)/shard_map/ppermute | solution.py:677
  40.9 6.9 %collective-permute-start.15 = (bf16[128,128]{1,0:T(8,128)(2,1)S(1)}, bf16[128,128]{1,0:T(8,128)(2,1)S(1)}, u32[]{:S(2)}, u32[]{:S(2)}) collective-permute-start(bf16[128,128]{1,0:T(8,128)(2,1)S(1)} %shard_map.108.raw_ref.refs_4_), channel_id=1, source_target_pairs={{0,24},{8,16},{16,8},{24,0},{1,25},{9,17},{17,9},{25,1},{2,26},{10... | collective-permute-start | bytes 98312 | tf_op jit(solution)/shard_map/ppermute | solution.py:677
  42.4 5.4 %collective-permute-start.14 = (bf16[128,128]{1,0:T(8,128)(2,1)S(1)}, bf16[128,128]{1,0:T(8,128)(2,1)S(1)}, u32[]{:S(2)}, u32[]{:S(2)}) collective-permute-start(bf16[128,128]{1,0:T(8,128)(2,1)S(1)} %shard_map.108.raw_ref.refs_4_), channel_id=1, source_target_pairs={{0,16},{8,24},{16,0},{24,8},{1,17},{9,25},{17,1},{25,9},{2,18},{10... | collective-permute-start | bytes 98312 | tf_op jit(solution)/shard_map/ppermute | solution.py:677
  43.9 3.9 %collective-permute-start.13 = (bf16[128,128]{1,0:T(8,128)(2,1)S(1)}, bf16[128,128]{1,0:T(8,128)(2,1)S(1)}, u32[]{:S(2)}, u32[]{:S(2)}) collective-permute-start(bf16[128,128]{1,0:T(8,128)(2,1)S(1)} %shard_map.108.raw_ref.refs_4_), channel_id=1, source_target_pairs={{0,8},{8,0},{16,24},{24,16},{1,9},{9,1},{17,25},{25,17},{2,10},{10... | collective-permute-start | bytes 98312 | tf_op jit(solution)/shard_map/ppermute | solution.py:677
  51.1 5.9 %collective-permute-start.17 = (bf16[80,512]{1,0:T(8,128)(2,1)S(1)}, bf16[80,512]{1,0:T(8,128)(2,1)S(1)}, u32[]{:S(2)}, u32[]{:S(2)}) collective-permute-start(bf16[80,512]{1,0:T(8,128)(2,1)S(1)} %get-tuple-element.66), channel_id=1, source_target_pairs={{0,2},{1,3},{2,0},{3,1},{4,6},{5,7},{6,4},{7,5},{8,10},{9,11},{10,... | collective-permute-start | bytes 245768 | tf_op jit(solution)/shard_map/ppermute | solution.py:677
  51.7 9.3 %collective-permute-start.18 = (bf16[80,512]{1,0:T(8,128)(2,1)S(1)}, bf16[80,512]{1,0:T(8,128)(2,1)S(1)}, u32[]{:S(2)}, u32[]{:S(2)}) collective-permute-start(bf16[80,512]{1,0:T(8,128)(2,1)S(1)} %get-tuple-element.67), channel_id=1, source_target_pairs={{0,4},{1,5},{2,6},{3,7},{4,0},{5,1},{6,2},{7,3},{8,12},{9,13},{10,... | collective-permute-start | bytes 245768 | tf_op jit(solution)/shard_map/ppermute | solution.py:677
  53.4 7.6 %collective-permute-start.19 = (bf16[80,512]{1,0:T(8,128)(2,1)S(1)}, bf16[80,512]{1,0:T(8,128)(2,1)S(1)}, u32[]{:S(2)}, u32[]{:S(2)}) collective-permute-start(bf16[80,512]{1,0:T(8,128)(2,1)S(1)} %get-tuple-element.68), channel_id=1, source_target_pairs={{0,6},{1,7},{2,4},{3,5},{4,2},{5,3},{6,0},{7,1},{8,14},{9,15},{10,... | collective-permute-start | bytes 245768 | tf_op jit(solution)/shard_map/ppermute | solution.py:677
  61.0 4.6 %collective-permute-start.20 = (bf16[80,512]{1,0:T(8,128)(2,1)S(1)}, bf16[80,512]{1,0:T(8,128)(2,1)S(1)}, u32[]{:S(2)}, u32[]{:S(2)}) collective-permute-start(bf16[80,512]{1,0:T(8,128)(2,1)S(1)} %shard_map.112.refs_0_), channel_id=1, source_target_pairs={{0,2},{1,3},{2,0},{3,1},{4,6},{5,7},{6,4},{7,5},{8,10},{9,11},{10,... | collective-permute-start | bytes 245768 | tf_op jit(solution)/shard_map/ppermute | solution.py:677
  63.0 7.7 %collective-permute-start.23 = (bf16[80,512]{1,0:T(8,128)(2,1)S(1)}, bf16[80,512]{1,0:T(8,128)(2,1)S(1)}, u32[]{:S(2)}, u32[]{:S(2)}) collective-permute-start(bf16[80,512]{1,0:T(8,128)(2,1)S(1)} %shard_map.112.refs_0_), channel_id=1, source_target_pairs={{0,6},{1,7},{2,4},{3,5},{4,2},{5,3},{6,0},{7,1},{8,14},{9,15},{10,... | collective-permute-start | bytes 245768 | tf_op jit(solution)/shard_map/ppermute | solution.py:677
  65.6 7.4 %collective-permute-start.22 = (bf16[80,512]{1,0:T(8,128)(2,1)S(1)}, bf16[80,512]{1,0:T(8,128)(2,1)S(1)}, u32[]{:S(2)}, u32[]{:S(2)}) collective-permute-start(bf16[80,512]{1,0:T(8,128)(2,1)S(1)} %shard_map.112.refs_0_), channel_id=1, source_target_pairs={{0,4},{1,5},{2,6},{3,7},{4,0},{5,1},{6,2},{7,3},{8,12},{9,13},{10,... | collective-permute-start | bytes 245768 | tf_op jit(solution)/shard_map/ppermute | solution.py:677
  65.6 9.4 %collective-permute-start.29 = (bf16[160,512]{1,0:T(8,128)(2,1)S(1)}, bf16[160,512]{1,0:T(8,128)(2,1)S(1)}, u32[]{:S(2)}, u32[]{:S(2)}) collective-permute-start(bf16[160,512]{1,0:T(8,128)(2,1)S(1)} %shard_map.113.refs_0_), channel_id=1, source_target_pairs={{0,16},{8,24},{16,0},{24,8},{1,17},{9,25},{17,1},{25,9},{2,18},{10... | collective-permute-start | bytes 491528 | tf_op jit(solution)/shard_map/ppermute | solution.py:677
  66.2 8.8 %collective-permute-start.25 = (bf16[160,512]{1,0:T(8,128)(2,1)S(1)}, bf16[160,512]{1,0:T(8,128)(2,1)S(1)}, u32[]{:S(2)}, u32[]{:S(2)}) collective-permute-start(bf16[160,512]{1,0:T(8,128)(2,1)S(1)} %shard_map.113.refs_0_), channel_id=1, source_target_pairs={{0,8},{8,0},{16,24},{24,16},{1,9},{9,1},{17,25},{25,17},{2,10},{10... | collective-permute-start | bytes 491528 | tf_op jit(solution)/shard_map/ppermute | solution.py:677
  67.7 7.9 %collective-permute-start.21 = (bf16[160,512]{1,0:T(8,128)(2,1)S(1)}, bf16[160,512]{1,0:T(8,128)(2,1)S(1)}, u32[]{:S(2)}, u32[]{:S(2)}) collective-permute-start(bf16[160,512]{1,0:T(8,128)(2,1)S(1)} %shard_map.113.refs_0_), channel_id=1, source_target_pairs={{0,1},{1,0},{2,3},{3,2},{4,5},{5,4},{6,7},{7,6},{8,9},{9,8},{10,11... | collective-permute-start | bytes 491528 | tf_op jit(solution)/shard_map/ppermute | solution.py:677
  73.0 6.7 %collective-permute-start.31 = (bf16[160,512]{1,0:T(8,128)(2,1)S(1)}, bf16[160,512]{1,0:T(8,128)(2,1)S(1)}, u32[]{:S(2)}, u32[]{:S(2)}) collective-permute-start(bf16[160,512]{1,0:T(8,128)(2,1)S(1)} %shard_map.114.refs_2_), channel_id=1, source_target_pairs={{0,16},{8,24},{16,0},{24,8},{1,17},{9,25},{17,1},{25,9},{2,18},{10... | collective-permute-start | bytes 491528 | tf_op jit(solution)/shard_map/ppermute | solution.py:677
  73.5 8.0 %collective-permute-start.27 = (bf16[160,512]{1,0:T(8,128)(2,1)S(1)}, bf16[160,512]{1,0:T(8,128)(2,1)S(1)}, u32[]{:S(2)}, u32[]{:S(2)}) collective-permute-start(bf16[160,512]{1,0:T(8,128)(2,1)S(1)} %shard_map.114.refs_2_), channel_id=1, source_target_pairs={{0,8},{8,0},{16,24},{24,16},{1,9},{9,1},{17,25},{25,17},{2,10},{10... | collective-permute-start | bytes 491528 | tf_op jit(solution)/shard_map/ppermute | solution.py:677
  75.0 6.5 %collective-permute-start.24 = (bf16[160,512]{1,0:T(8,128)(2,1)S(1)}, bf16[160,512]{1,0:T(8,128)(2,1)S(1)}, u32[]{:S(2)}, u32[]{:S(2)}) collective-permute-start(bf16[160,512]{1,0:T(8,128)(2,1)S(1)} %shard_map.114.refs_2_), channel_id=1, source_target_pairs={{0,1},{1,0},{2,3},{3,2},{4,5},{5,4},{6,7},{7,6},{8,9},{9,8},{10,11... | collective-permute-start | bytes 491528 | tf_op jit(solution)/shard_map/ppermute | solution.py:677
  75.0 7.0 %collective-permute-start.30 = (bf16[160,512]{1,0:T(8,128)(2,1)S(1)}, bf16[160,512]{1,0:T(8,128)(2,1)S(1)}, u32[]{:S(2)}, u32[]{:S(2)}) collective-permute-start(bf16[160,512]{1,0:T(8,128)(2,1)S(1)} %collective-permute-done.29.refs_4_.refs_8_), channel_id=1, source_target_pairs={{0,1},{1,0},{2,3},{3,2},{4,5},{5,4},{6,7},{7,6},{8,9},{9,8},{10,11... | collective-permute-start | bytes 491528 | tf_op jit(solution)/shard_map/ppermute | solution.py:677
  75.5 6.9 %collective-permute-start.33 = (bf16[160,512]{1,0:T(8,128)(2,1)S(1)}, bf16[160,512]{1,0:T(8,128)(2,1)S(1)}, u32[]{:S(2)}, u32[]{:S(2)}) collective-permute-start(bf16[160,512]{1,0:T(8,128)(2,1)S(1)} %collective-permute-done.25.refs_0_.refs_4_), channel_id=1, source_target_pairs={{0,16},{8,24},{16,0},{24,8},{1,17},{9,25},{17,1},{25,9},{2,18},{10... | collective-permute-start | bytes 491528 | tf_op jit(solution)/shard_map/ppermute | solution.py:677
  79.7 5.3 %collective-permute-start.35 = (bf16[160,512]{1,0:T(8,128)(2,1)S(1)}, bf16[160,512]{1,0:T(8,128)(2,1)S(1)}, u32[]{:S(2)}, u32[]{:S(2)}) collective-permute-start(bf16[160,512]{1,0:T(8,128)(2,1)S(1)} %collective-permute-done.31.refs_6_.refs_10_), channel_id=1, source_target_pairs={{0,8},{8,0},{16,24},{24,16},{1,9},{9,1},{17,25},{25,17},{2,10},{10... | collective-permute-start | bytes 491528 | tf_op jit(solution)/shard_map/ppermute | solution.py:677
  81.5 4.6 %collective-permute-start.26 = (bf16[160,512]{1,0:T(8,128)(2,1)S(1)}, bf16[160,512]{1,0:T(8,128)(2,1)S(1)}, u32[]{:S(2)}, u32[]{:S(2)}) collective-permute-start(bf16[160,512]{1,0:T(8,128)(2,1)S(1)} %collective-permute-done.25.refs_0_.refs_4_), channel_id=1, source_target_pairs={{0,1},{1,0},{2,3},{3,2},{4,5},{5,4},{6,7},{7,6},{8,9},{9,8},{10,11... | collective-permute-start | bytes 491528 | tf_op jit(solution)/shard_map/ppermute | solution.py:677
  81.5 4.6 %collective-permute-start.32 = (bf16[160,512]{1,0:T(8,128)(2,1)S(1)}, bf16[160,512]{1,0:T(8,128)(2,1)S(1)}, u32[]{:S(2)}, u32[]{:S(2)}) collective-permute-start(bf16[160,512]{1,0:T(8,128)(2,1)S(1)} %collective-permute-done.31.refs_6_.refs_10_), channel_id=1, source_target_pairs={{0,1},{1,0},{2,3},{3,2},{4,5},{5,4},{6,7},{7,6},{8,9},{9,8},{10,11... | collective-permute-start | bytes 491528 | tf_op jit(solution)/shard_map/ppermute | solution.py:677
  82.1 4.1 %collective-permute-start.28 = (bf16[160,512]{1,0:T(8,128)(2,1)S(1)}, bf16[160,512]{1,0:T(8,128)(2,1)S(1)}, u32[]{:S(2)}, u32[]{:S(2)}) collective-permute-start(bf16[160,512]{1,0:T(8,128)(2,1)S(1)} %collective-permute-done.27.refs_2_.refs_6_), channel_id=1, source_target_pairs={{0,1},{1,0},{2,3},{3,2},{4,5},{5,4},{6,7},{7,6},{8,9},{9,8},{10,11... | collective-permute-start | bytes 491528 | tf_op jit(solution)/shard_map/ppermute | solution.py:677
  82.5 5.4 %collective-permute-start.34 = (bf16[160,512]{1,0:T(8,128)(2,1)S(1)}, bf16[160,512]{1,0:T(8,128)(2,1)S(1)}, u32[]{:S(2)}, u32[]{:S(2)}) collective-permute-start(bf16[160,512]{1,0:T(8,128)(2,1)S(1)} %collective-permute-done.33.refs_12_), channel_id=1, source_target_pairs={{0,1},{1,0},{2,3},{3,2},{4,5},{5,4},{6,7},{7,6},{8,9},{9,8},{10,11... | collective-permute-start | bytes 491528 | tf_op jit(solution)/shard_map/ppermute | solution.py:677
  (9 other events, 72.2 us)

commit v4 on v3

--- a/solution.py
+++ b/solution.py
@@ -56,8 +56,8 @@
 
 def encode_kernel(freqs, size, rounds, patch_hbm, basis_hbm, mix_hbm, out_hbm, in_hbm, *rest):
     piece_hbms, rest = rest[:size], rest[size:]
-    spec, mixed, normed, in_w, units_ref, unit32_ref, norm_ref, rscale_ref, *rest = rest
-    patches, basis, mix, out_w, feat, slope, hidden, *sems = rest
+    spec, mixed, normed, in_w, out_w, slope, units_ref, unit32_ref, norm_ref, rscale_ref, *rest = rest
+    patches, basis, mix, feat, hidden, *sems = rest
     table_sems, patch_sems, out_sems = sems
     count, length, lanes = patches.shape
     filters = mix.shape[1]
@@ -181,6 +181,8 @@
         shape((groups, rows, filters), F32),
         shape((count, feats), BF16),
         shape(w_in.shape, BF16),
+        shape(w_out.shape, BF16),
+        shape((count, width), BF16),
         shape((count, embed), BF16),
         shape((count, embed), F32),
         shape((count, 128), F32),
@@ -195,9 +197,7 @@
             pltpu.VMEM(patches.shape, BF16),
             pltpu.VMEM((rows, SUB * length), BF16),
             pltpu.VMEM(w_mix.shape, BF16),
-            pltpu.VMEM(w_out.shape, BF16),
             pltpu.VMEM((count, feats), F32),
-            pltpu.VMEM((count, width), BF16),
             pltpu.VMEM((count, width), BF16),
             pltpu.SemaphoreType.DMA((4,)),
             pltpu.SemaphoreType.DMA((rounds,)),
@@ -403,31 +403,8 @@
 
 
 def lower_kernel(
-    freqs,
-    columns,
-    raw_ref,
-    rscale_ref,
-    in_w,
-    normed,
-    mixed,
-    spec,
-    out_w_hbm,
-    piece_hbm,
-    g_mix_ref,
-    out_w,
-    slope,
-    grad_feat,
-    sems,
+    freqs, raw_ref, rscale_ref, in_w, out_w, slope, normed, mixed, spec, g_mix_ref, grad_feat
 ):
-    deep, width, _ = columns
-    loads = [
-        pltpu.make_async_copy(out_w_hbm, out_w, sems.at[0]),
-        pltpu.make_async_copy(piece_hbm.at[:, deep : deep + width], slope, sems.at[1]),
-    ]
-    for each in loads:
-        each.start()
-    for each in loads:
-        each.wait()
     grad_pre = pre_grads(raw_ref[...], out_w[...], slope[...])
     grad_norm = mm_nt(grad_pre, in_w[...])
     xhat = normed[...].astype(F32)
@@ -448,28 +425,21 @@
         ).astype(BF16)
         return total + mm_tn(grad_mixed, spec[g])
 
-    total = lax.fori_loop(0, groups, one, jnp.zeros((filters, spec.shape[2]), F32), unroll=4)
+    total = lax.fori_loop(0, groups, one, jnp.zeros((filters, spec.shape[2]), F32), unroll=16)
     g_mix_ref[...] = total.T
 
 
-def lower(grad_raw, w_out, piece, normed, rscale, in_w, mixed, spec, freqs, columns):
-    count, feats = normed.shape
-    _, _, filters = mixed.shape
-    lanes = spec.shape[2]
-    return pl.pallas_call(
-        functools.partial(lower_kernel, freqs, columns),
-        in_specs=[VMEM] * 6 + [ANY] * 2,
+def lower(grad_raw, rscale, in_w, out_w, slope, normed, mixed, spec, freqs):
+    filters, lanes = mixed.shape[2], spec.shape[2]
+    return pl.pallas_call(
+        functools.partial(lower_kernel, freqs),
+        in_specs=[VMEM] * 8,
         out_shape=shape((lanes, filters), F32),
         out_specs=VMEM,
-        scratch_shapes=[
-            pltpu.VMEM(w_out.shape, BF16),
-            pltpu.VMEM((count, columns[1]), BF16),
-            pltpu.VMEM((count, feats), F32),
-            pltpu.SemaphoreType.DMA((2,)),
-        ],
+        scratch_shapes=[pltpu.VMEM(normed.shape, F32)],
         compiler_params=params(20),
         cost_estimate=cost(1e9, 7e6),
-    )(grad_raw, rscale, in_w, normed, mixed, spec, hbm(w_out), hbm(piece))
+    )(grad_raw, rscale, in_w, out_w, slope, normed, mixed, spec)
 
 
 def up_to(rows, unit):
@@ -690,16 +660,18 @@
     size, peers = lax.axis_size("blk"), lax.axis_size("dp")
     assert size & (size - 1) == 0 and peers & (peers - 1) == 0 and peers > 1
     across, along = range(1, size), range(2, peers, 2)
+    single = [hop for hop in across if hop & (hop - 1) == 0]
+    several = [hop for hop in across if hop & (hop - 1)]
     columns = piece_columns(feats, width, size)
     lay = Layout(lanes, filters, feats, width, embed, size, peers)
 
-    *early, spec, mixed, normed, in_w, units, unit32, norms, rscale = encode(
+    *early, spec, mixed, normed, in_w, out_w, slope, units, unit32, norms, rscale = encode(
         patches, w_mix, w_in, w_out, size
     )
     other = swap(units, "dp", 1)
     pair = pair_up(units, other)
     got = stack(lax.optimization_barrier(cross(pair)))
-    factors = [early[0]] + [swap(early[hop], "blk", hop) for hop in across]
+    factors = {hop: swap(early[hop], "blk", hop) for hop in single}
     swapped = swap(got, "dp", 1)
     local, stats, loss, group, around = scores(
         partner_dev, partner_row, units, pair, got, swapped, size, peers
@@ -707,11 +679,13 @@
     other = swap(stats, "dp", 1)
     pair = pair_up(stats, other)
     got = stack(lax.optimization_barrier(cross(pair)))
+    factors.update({hop: swap(early[hop], "blk", hop) for hop in several})
+    factors = [early[0]] + [factors[hop] for hop in across]
     swapped = swap(got, "dp", 1)
     grad_raw = upper(group, around, stats, pair, got, swapped, local, unit32, norms, size, peers)
     raws = spread(grad_raw, "blk", across)
-    g_mix = lower(grad_raw, w_out, early[0], normed, rscale, in_w, mixed, spec, freqs, columns)
-    keep, away = weight_grads(lay, columns, factors, raws, w_out, g_mix)
+    g_mix = lower(grad_raw, rscale, in_w, out_w, slope, normed, mixed, spec, freqs)
+    keep, away = weight_grads(lay, columns, factors, raws, out_w, g_mix)
     got = swap(away, "dp", 1)
     own, *sends = pair_sum(keep, got)
     got = [swap(block, "dp", hop) for block, hop in zip(sends, along)]
@@ -719,8 +693,6 @@
     shares = spread(share, "dp", along)
     middle = len(shares) // 2
     planes = {(0, 0): stack(shares[:middle]), (0, 1): stack(shares[middle:])}
-    single = [hop for hop in across if hop & (hop - 1) == 0]
-    several = [hop for hop in across if hop & (hop - 1)]
     for half in range(2):
         for hop in single:
             planes[hop, half] = swap(planes[0, half], "blk", hop)

time: 89.8 us -> 89.9 us (level)
  waiting for transfers between devices: 32.2 us -> 37.4 us
  starting transfers between devices: 37.2 us -> 33.7 us
  Pallas kernels: 19.4 us -> 17.9 us
    ppermute x31, waiting for transfers between devices: 20.7 us -> 25.8 us  [swap(): return lax.ppermute(block, axis, [(src, src ^ bit) for src in range(size)])]
    ppermute x31, starting transfers between devices: 29.5 us -> 25.9 us  [swap(): return lax.ppermute(block, axis, [(src, src ^ bit) for src in range(size)])]
    pallas_call x1, Pallas kernels: 3.3 us -> 2.07 us  [lower(): pl.pallas_call(functools.partial(lower_kernel, freqs), in_specs=[VMEM] *...]
  transfers between devices with their start and end apart: 37 -> 37, of which waited for: 16 -> 17; matrix products, arithmetic and copies ran while one was open for 0% -> 0% of each run, Pallas kernels for 9% -> 8%
where the time goes in v4:
time: 89.9 us; the launch traced here: 89.7 us
  waiting for transfers between devices  37.4 us (42%)
  starting transfers between devices  33.7 us (37%)
  Pallas kernels  17.9 us (20%)
    ppermute x31, starting transfers between devices, swap(): return lax.ppermute(block, axis, [(src, src ^ bit) for src in range(size)])  25.9 us
    ppermute x31, waiting for transfers between devices, swap(): return lax.ppermute(block, axis, [(src, src ^ bit) for src in range(size)])  25.8 us
    ppermute x6, waiting for transfers between devices, cross(): got.append(lax.ppermute(pair, ('blk', 'dp'), routes))  11.5 us
    ppermute x6, starting transfers between devices, cross(): got.append(lax.ppermute(pair, ('blk', 'dp'), routes))  7.73 us
    pallas_call x1, Pallas kernels, encode(): pl.pallas_call(functools.partial(encode_kernel, freqs, size, rounds), in_...  7.41 us
    pallas_call x3, Pallas kernels, finish(): pl.pallas_call(functools.partial(finish_kernel, lay, tuple(parts), bool(d...  4.6 us
    pallas_call x1, Pallas kernels, lower(): pl.pallas_call(functools.partial(lower_kernel, freqs), in_specs=[VMEM] *...  2.07 us
  transfers between devices with their start and end apart: 37, of which 17 were waited for; matrix products, arithmetic and copies ran while one was open for 0% of the time, Pallas kernels for 8%

profile of v4, /device:TPU:0, one launch (start us, length us, event | category | flops | bytes accessed | tf_op | source)
XLA Modules:
  0.0 89.7 jit_solution(8769125569202052508)
XLA Ops:
  0.7 7.4 %shard_map.102 = (bf16[128,1152]{1,0:T(8,128)(2,1)}, bf16[128,1152]{1,0:T(8,128)(2,1)}, bf16[128,1152]{1,0:T(8,128)(2,1)}, bf16[128,1152]{1,0:T(8,128)(2,1)}, bf...) custom-call(bf16[128,64,256]{2,1,0:T(8,128)(2,1)} %patch_hbm.1, ...), custom_call_target="tpu_custom_call" | custom-call | flops 3000000000 | bytes 14000000 | tf_op jit(solution)/shard_map/pallas_call | solution.py:191
  9.5 5.0 %collective-permute-start.3 = (bf16[256,128]{1,0:T(8,128)(2,1)S(1)}, bf16[256,128]{1,0:T(8,128)(2,1)S(1)}, u32[]{:S(2)}, u32[]{:S(2)}) collective-permute-start(bf16[256,128]{1,0:T(8,128)(2,1)S(1)} %shard_map.103.pair_ref), channel_id=1, source_target_pairs={{0,6},{1,25},{2,4},{3,27},{4,2},{5,29},{6,0},{7,31},{8,14},{9,17},... | collective-permute-start | bytes 196616 | tf_op jit(solution)/shard_map/ppermute | solution.py:251
  15.1 1.7 %collective-permute-done.3.refs_2_ = bf16[256,128]{1,0:T(8,128)(2,1)S(1)} collective-permute-done((bf16[256,128]{1,0:T(8,128)(2,1)S(1)}, bf16[256,128]{1,0:T(8,128)(2,1)S(1)}, u32[]{:S(2)}, u32[]{:S(2)}) %collective-permute-start.3) | collective-permute-done | bytes 65568 | tf_op jit(solution)/shard_map/ppermute | solution.py:251
  16.9 2.8 %collective-permute-done.2.refs_1_ = bf16[256,128]{1,0:T(8,128)(2,1)S(1)} collective-permute-done((bf16[256,128]{1,0:T(8,128)(2,1)S(1)}, bf16[256,128]{1,0:T(8,128)(2,1)S(1)}, u32[]{:S(2)}, u32[]{:S(2)}) %collective-permute-start.2) | collective-permute-done | bytes 65568 | tf_op jit(solution)/shard_map/ppermute | solution.py:251
  19.8 1.6 %collective-permute-start.5 = (bf16[128,1152]{1,0:T(8,128)(2,1)}, bf16[128,1152]{1,0:T(8,128)(2,1)S(1)}, u32[]{:S(2)}, u32[]{:S(2)}) collective-permute-start(bf16[128,1152]{1,0:T(8,128)(2,1)} %get-tuple-element.48), channel_id=1, source_target_pairs={{0,8},{8,0},{16,24},{24,16},{1,9},{9,1},{17,25},{25,17},{2,10},{10... | collective-permute-start | bytes 884744 | tf_op jit(solution)/shard_map/ppermute | solution.py:647
  21.3 1.5 %collective-permute-start.6 = (bf16[128,1152]{1,0:T(8,128)(2,1)}, bf16[128,1152]{1,0:T(8,128)(2,1)S(1)}, u32[]{:S(2)}, u32[]{:S(2)}) collective-permute-start(bf16[128,1152]{1,0:T(8,128)(2,1)} %get-tuple-element.49), channel_id=1, source_target_pairs={{0,16},{8,24},{16,0},{24,8},{1,17},{9,25},{17,1},{25,9},{2,18},{10... | collective-permute-start | bytes 884744 | tf_op jit(solution)/shard_map/ppermute | solution.py:647
  23.3 1.3 %shard_map.105 = (f32[128,128]{1,0:T(8,128)S(1)}, f32[8,128]{1,0:T(8,128)S(1)}, f32[1,128]{1,0:T(1,128)}, bf16[512,128]{1,0:T(8,128)(2,1)S(1)}, bf16[1024,128]{1,0:T(8,128)(2,1)S(1)}) custom-call(s32[1,128]{1,0:T(1,128)S(1)} %bitcast.3, s32[1,128]{1,0:T(1,128)S(1)} %bitcast.4, bf16[128,128]{1,0:T(8,128)(2,1)S(1)} %get-tuple-element.42.own_ref.units_ref, ...), custom_call_target="tpu_custom_call" | custom-call | flops 400000000 | bytes 1000000 | tf_op jit(solution)/shard_map/pallas_call | solution.py:329
  24.7 1.2 %collective-permute-done.8.other_ref = f32[8,128]{1,0:T(8,128)S(1)} collective-permute-done((f32[8,128]{1,0:T(8,128)S(1)}, f32[8,128]{1,0:T(8,128)S(1)}, u32[]{:S(2)}, u32[]{:S(2)}) %collective-permute-start.8) | collective-permute-done | bytes 4128 | tf_op jit(solution)/shard_map/ppermute | solution.py:647
  25.9 1.6 %collective-permute-start.11 = (f32[16,128]{1,0:T(8,128)S(1)}, f32[16,128]{1,0:T(8,128)S(1)}, u32[]{:S(2)}, u32[]{:S(2)}) collective-permute-start(f32[16,128]{1,0:T(8,128)S(1)} %shard_map.106.pair_ref), channel_id=1, source_target_pairs={{0,6},{1,25},{2,4},{3,27},{4,2},{5,29},{6,0},{7,31},{8,14},{9,17},... | collective-permute-start | bytes 24584 | tf_op jit(solution)/shard_map/ppermute | solution.py:251
  27.9 3.4 %collective-permute-done.11.refs_2_ = f32[16,128]{1,0:T(8,128)S(1)} collective-permute-done((f32[16,128]{1,0:T(8,128)S(1)}, f32[16,128]{1,0:T(8,128)S(1)}, u32[]{:S(2)}, u32[]{:S(2)}) %collective-permute-start.11) | collective-permute-done | bytes 8224 | tf_op jit(solution)/shard_map/ppermute | solution.py:251
  32.0 3.0 %collective-permute-done.9.refs_0_ = f32[16,128]{1,0:T(8,128)S(1)} collective-permute-done((f32[16,128]{1,0:T(8,128)S(1)}, f32[16,128]{1,0:T(8,128)S(1)}, u32[]{:S(2)}, u32[]{:S(2)}) %collective-permute-start.9) | collective-permute-done | bytes 8224 | tf_op jit(solution)/shard_map/ppermute | solution.py:251
  35.0 4.0 %collective-permute-start.12 = (f32[48,128]{1,0:T(8,128)S(1)}, f32[48,128]{1,0:T(8,128)S(1)}, u32[]{:S(2)}, u32[]{:S(2)}) collective-permute-start(f32[48,128]{1,0:T(8,128)S(1)} %shard_map.107.got_ref), channel_id=1, source_target_pairs={{0,1},{1,0},{2,3},{3,2},{4,5},{5,4},{6,7},{7,6},{8,9},{9,8},{10,11... | collective-permute-start | bytes 73736 | tf_op jit(solution)/shard_map/ppermute | solution.py:647
  40.6 1.5 %collective-permute-start.15 = (bf16[128,128]{1,0:T(8,128)(2,1)S(1)}, bf16[128,128]{1,0:T(8,128)(2,1)S(1)}, u32[]{:S(2)}, u32[]{:S(2)}) collective-permute-start(bf16[128,128]{1,0:T(8,128)(2,1)S(1)} %shard_map.108.raw_ref.refs_4_), channel_id=1, source_target_pairs={{0,24},{8,16},{16,8},{24,0},{1,25},{9,17},{17,9},{25,1},{2,26},{10... | collective-permute-start | bytes 98312 | tf_op jit(solution)/shard_map/ppermute | solution.py:647
  42.1 1.5 %collective-permute-start.14 = (bf16[128,128]{1,0:T(8,128)(2,1)S(1)}, bf16[128,128]{1,0:T(8,128)(2,1)S(1)}, u32[]{:S(2)}, u32[]{:S(2)}) collective-permute-start(bf16[128,128]{1,0:T(8,128)(2,1)S(1)} %shard_map.108.raw_ref.refs_4_), channel_id=1, source_target_pairs={{0,16},{8,24},{16,0},{24,8},{1,17},{9,25},{17,1},{25,9},{2,18},{10... | collective-permute-start | bytes 98312 | tf_op jit(solution)/shard_map/ppermute | solution.py:647
  44.2 2.1 %shard_map.109.refs_9_ = f32[256,128]{1,0:T(8,128)S(1)} custom-call(bf16[128,128]{1,0:T(8,128)(2,1)S(1)} %shard_map.108.raw_ref.refs_4_, f32[128,128]{1,0:T(8,128)S(1)} %get-tuple-element.61.rscale_ref, bf16[2048,512]{1,0:T(8,128)(2,1)S(1)} %get-tuple-element.62.in_w, bf16[512,128]{1,0:T(8,128)(2,1)S(1)} %get-tuple-element.60.out_w.refs_8_, ...), custom_call_target="tpu_custom_call" | custom-call | flops 1000000000 | bytes 7000000 | tf_op jit(solution)/shard_map/pallas_call | solution.py:434
  46.3 1.2 %collective-permute-done.13.refs_5_ = bf16[128,128]{1,0:T(8,128)(2,1)S(1)} collective-permute-done((bf16[128,128]{1,0:T(8,128)(2,1)S(1)}, bf16[128,128]{1,0:T(8,128)(2,1)S(1)}, u32[]{:S(2)}, u32[]{:S(2)}) %collective-permute-start.13) | collective-permute-done | bytes 32800 | tf_op jit(solution)/shard_map/ppermute | solution.py:647
  47.5 1.5 %shard_map.110 = (f32[4,80,512]{2,1,0:T(8,128)S(1)}, bf16[4,80,512]{2,1,0:T(8,128)(2,1)S(1)}) custom-call(bf16[128,1152]{1,0:T(8,128)(2,1)S(1)} %copy-done.2, bf16[128,1152]{1,0:T(8,128)(2,1)S(1)} %collective-permute-done.5.refs_1_, bf16[128,1152]{1,0:T(8,128)(2,1)S(1)} %collective-permute-done.6.refs_2_, ...), custom_call_target="tpu_custom_call" | custom-call | flops 600000000 | bytes 4000000 | tf_op jit(solution)/shard_map/pallas_call | solution.py:507
  49.1 1.6 %collective-permute-done.16.got_ref = bf16[4,80,512]{2,1,0:T(8,128)(2,1)S(1)} collective-permute-done((bf16[4,80,512]{2,1,0:T(8,128)(2,1)S(1)}, bf16[4,80,512]{2,1,0:T(8,128)(2,1)S(1)}, u32[]{:S(2)}, u32[]{:S(2)}) %collective-permute-start.16) | collective-permute-done | bytes 327712 | tf_op jit(solution)/shard_map/ppermute | solution.py:647
  51.3 1.7 %collective-permute-start.18 = (bf16[80,512]{1,0:T(8,128)(2,1)S(1)}, bf16[80,512]{1,0:T(8,128)(2,1)S(1)}, u32[]{:S(2)}, u32[]{:S(2)}) collective-permute-start(bf16[80,512]{1,0:T(8,128)(2,1)S(1)} %get-tuple-element.71), channel_id=1, source_target_pairs={{0,4},{1,5},{2,6},{3,7},{4,0},{5,1},{6,2},{7,3},{8,12},{9,13},{10,... | collective-permute-start | bytes 245768 | tf_op jit(solution)/shard_map/ppermute | solution.py:647
  53.0 2.2 %collective-permute-start.19 = (bf16[80,512]{1,0:T(8,128)(2,1)S(1)}, bf16[80,512]{1,0:T(8,128)(2,1)S(1)}, u32[]{:S(2)}, u32[]{:S(2)}) collective-permute-start(bf16[80,512]{1,0:T(8,128)(2,1)S(1)} %get-tuple-element.72), channel_id=1, source_target_pairs={{0,6},{1,7},{2,4},{3,5},{4,2},{5,3},{6,0},{7,1},{8,14},{9,15},{10,... | collective-permute-start | bytes 245768 | tf_op jit(solution)/shard_map/ppermute | solution.py:647
  55.2 1.4 %collective-permute-done.17.refs_0_ = bf16[80,512]{1,0:T(8,128)(2,1)S(1)} collective-permute-done((bf16[80,512]{1,0:T(8,128)(2,1)S(1)}, bf16[80,512]{1,0:T(8,128)(2,1)S(1)}, u32[]{:S(2)}, u32[]{:S(2)}) %collective-permute-start.17) | collective-permute-done | bytes 81952 | tf_op jit(solution)/shard_map/ppermute | solution.py:647
  56.7 4.0 %collective-permute-done.18.refs_1_ = bf16[80,512]{1,0:T(8,128)(2,1)S(1)} collective-permute-done((bf16[80,512]{1,0:T(8,128)(2,1)S(1)}, bf16[80,512]{1,0:T(8,128)(2,1)S(1)}, u32[]{:S(2)}, u32[]{:S(2)}) %collective-permute-start.18) | collective-permute-done | bytes 81952 | tf_op jit(solution)/shard_map/ppermute | solution.py:647
  60.7 1.9 %collective-permute-start.20 = (bf16[80,512]{1,0:T(8,128)(2,1)S(1)}, bf16[80,512]{1,0:T(8,128)(2,1)S(1)}, u32[]{:S(2)}, u32[]{:S(2)}) collective-permute-start(bf16[80,512]{1,0:T(8,128)(2,1)S(1)} %shard_map.112.refs_0_), channel_id=1, source_target_pairs={{0,2},{1,3},{2,0},{3,1},{4,6},{5,7},{6,4},{7,5},{8,10},{9,11},{10,... | collective-permute-start | bytes 245768 | tf_op jit(solution)/shard_map/ppermute | solution.py:647
  62.6 2.6 %collective-permute-start.23 = (bf16[80,512]{1,0:T(8,128)(2,1)S(1)}, bf16[80,512]{1,0:T(8,128)(2,1)S(1)}, u32[]{:S(2)}, u32[]{:S(2)}) collective-permute-start(bf16[80,512]{1,0:T(8,128)(2,1)S(1)} %shard_map.112.refs_0_), channel_id=1, source_target_pairs={{0,6},{1,7},{2,4},{3,5},{4,2},{5,3},{6,0},{7,1},{8,14},{9,15},{10,... | collective-permute-start | bytes 245768 | tf_op jit(solution)/shard_map/ppermute | solution.py:647
  66.4 3.8 %collective-permute-done.23.refs_1_ = bf16[80,512]{1,0:T(8,128)(2,1)S(1)} collective-permute-done((bf16[80,512]{1,0:T(8,128)(2,1)S(1)}, bf16[80,512]{1,0:T(8,128)(2,1)S(1)}, u32[]{:S(2)}, u32[]{:S(2)}) %collective-permute-start.23) | collective-permute-done | bytes 81952 | tf_op jit(solution)/shard_map/ppermute | solution.py:647
  70.3 2.3 %collective-permute-done.22.refs_0_ = bf16[80,512]{1,0:T(8,128)(2,1)S(1)} collective-permute-done((bf16[80,512]{1,0:T(8,128)(2,1)S(1)}, bf16[80,512]{1,0:T(8,128)(2,1)S(1)}, u32[]{:S(2)}, u32[]{:S(2)}) %collective-permute-start.22) | collective-permute-done | bytes 81952 | tf_op jit(solution)/shard_map/ppermute | solution.py:647
  74.3 1.5 %collective-permute-start.33 = (bf16[160,512]{1,0:T(8,128)(2,1)S(1)}, bf16[160,512]{1,0:T(8,128)(2,1)S(1)}, u32[]{:S(2)}, u32[]{:S(2)}) collective-permute-start(bf16[160,512]{1,0:T(8,128)(2,1)S(1)} %collective-permute-done.25.refs_0_.refs_4_), channel_id=1, source_target_pairs={{0,16},{8,24},{16,0},{24,8},{1,17},{9,25},{17,1},{25,9},{2,18},{10... | collective-permute-start | bytes 491528 | tf_op jit(solution)/shard_map/ppermute | solution.py:647
  75.8 3.9 %collective-permute-done.31.refs_6_.refs_10_ = bf16[160,512]{1,0:T(8,128)(2,1)S(1)} collective-permute-done((bf16[160,512]{1,0:T(8,128)(2,1)S(1)}, bf16[160,512]{1,0:T(8,128)(2,1)S(1)}, u32[]{:S(2)}, u32[]{:S(2)}) %collective-permute-start.31) | collective-permute-done | bytes 163872 | tf_op jit(solution)/shard_map/ppermute | solution.py:647
  80.5 1.6 %collective-permute-done.33.refs_12_ = bf16[160,512]{1,0:T(8,128)(2,1)S(1)} collective-permute-done((bf16[160,512]{1,0:T(8,128)(2,1)S(1)}, bf16[160,512]{1,0:T(8,128)(2,1)S(1)}, u32[]{:S(2)}, u32[]{:S(2)}) %collective-permute-start.33) | collective-permute-done | bytes 163872 | tf_op jit(solution)/shard_map/ppermute | solution.py:647
  82.1 3.0 %collective-permute-done.35.refs_14_ = bf16[160,512]{1,0:T(8,128)(2,1)S(1)} collective-permute-done((bf16[160,512]{1,0:T(8,128)(2,1)S(1)}, bf16[160,512]{1,0:T(8,128)(2,1)S(1)}, u32[]{:S(2)}, u32[]{:S(2)}) %collective-permute-start.35) | collective-permute-done | bytes 163872 | tf_op jit(solution)/shard_map/ppermute | solution.py:647
  86.3 1.7 %shard_map.116 = (f32[2048,512]{1,0:T(8,128)}, f32[512,128]{1,0:T(8,128)}) custom-call(bf16[160,512]{1,0:T(8,128)(2,1)S(1)} %collective-permute-done.25.refs_0_.refs_4_, bf16[160,512]{1,0:T(8,128)(2,1)S(1)} %collective-permute-done.26.refs_1_.refs_5_, ...), custom_call_target="tpu_custom_call", output_to_operand_aliasing={{0}: (8, {}), {1}: (9, {})} | custom-call | flops 1000000 | bytes 8000000 | tf_op jit(solution)/shard_map/pallas_call | solution.py:610
  87.9 1.8 %shard_map.117 = (f32[2048,512]{1,0:T(8,128)}, f32[512,128]{1,0:T(8,128)}, f32[256,128]{1,0:T(8,128)}) custom-call(bf16[160,512]{1,0:T(8,128)(2,1)S(1)} %shard_map.113.refs_0_, bf16[160,512]{1,0:T(8,128)(2,1)S(1)} %collective-permute-done.21.refs_1_, bf16[160,512]{1,0:T(8,128)(2,1)S(1)} %shard_map.114.refs_2_, ...), custom_call_target="tpu_custom_call", output_to_operand_aliasing={{0}: (16, {}), {1}: (17, {})} | custom-call | flops 1000000 | bytes 8000000 | tf_op jit(solution)/shard_map/pallas_call | solution.py:610
  (64 shorter events, 11.6 us)
Async XLA Ops:
  9.5 7.3 %collective-permute-start.3 = (bf16[256,128]{1,0:T(8,128)(2,1)S(1)}, bf16[256,128]{1,0:T(8,128)(2,1)S(1)}, u32[]{:S(2)}, u32[]{:S(2)}) collective-permute-start(bf16[256,128]{1,0:T(8,128)(2,1)S(1)} %shard_map.103.pair_ref), channel_id=1, source_target_pairs={{0,6},{1,25},{2,4},{3,27},{4,2},{5,29},{6,0},{7,31},{8,14},{9,17},... | collective-permute-start | bytes 196616 | tf_op jit(solution)/shard_map/ppermute | solution.py:251
  14.5 5.2 %collective-permute-start.2 = (bf16[256,128]{1,0:T(8,128)(2,1)S(1)}, bf16[256,128]{1,0:T(8,128)(2,1)S(1)}, u32[]{:S(2)}, u32[]{:S(2)}) collective-permute-start(bf16[256,128]{1,0:T(8,128)(2,1)S(1)} %shard_map.103.pair_ref), channel_id=1, source_target_pairs={{0,4},{1,17},{2,6},{3,19},{4,0},{5,21},{6,2},{7,23},{8,12},{9,25},... | collective-permute-start | bytes 196616 | tf_op jit(solution)/shard_map/ppermute | solution.py:251
  14.5 5.2 %collective-permute-start.1 = (bf16[256,128]{1,0:T(8,128)(2,1)S(1)}, bf16[256,128]{1,0:T(8,128)(2,1)S(1)}, u32[]{:S(2)}, u32[]{:S(2)}) collective-permute-start(bf16[256,128]{1,0:T(8,128)(2,1)S(1)} %shard_map.103.pair_ref), channel_id=1, source_target_pairs={{0,2},{1,9},{2,0},{3,11},{4,6},{5,13},{6,4},{7,15},{8,10},{9,1},{1... | collective-permute-start | bytes 196616 | tf_op jit(solution)/shard_map/ppermute | solution.py:251
  19.8 23.8 %collective-permute-start.5 = (bf16[128,1152]{1,0:T(8,128)(2,1)}, bf16[128,1152]{1,0:T(8,128)(2,1)S(1)}, u32[]{:S(2)}, u32[]{:S(2)}) collective-permute-start(bf16[128,1152]{1,0:T(8,128)(2,1)} %get-tuple-element.48), channel_id=1, source_target_pairs={{0,8},{8,0},{16,24},{24,16},{1,9},{9,1},{17,25},{25,17},{2,10},{10... | collective-permute-start | bytes 884744 | tf_op jit(solution)/shard_map/ppermute | solution.py:647
  21.3 24.9 %collective-permute-start.6 = (bf16[128,1152]{1,0:T(8,128)(2,1)}, bf16[128,1152]{1,0:T(8,128)(2,1)S(1)}, u32[]{:S(2)}, u32[]{:S(2)}) collective-permute-start(bf16[128,1152]{1,0:T(8,128)(2,1)} %get-tuple-element.49), channel_id=1, source_target_pairs={{0,16},{8,24},{16,0},{24,8},{1,17},{9,25},{17,1},{25,9},{2,18},{10... | collective-permute-start | bytes 884744 | tf_op jit(solution)/shard_map/ppermute | solution.py:647
  22.8 23.4 %collective-permute-start.7 = (bf16[128,1152]{1,0:T(8,128)(2,1)}, bf16[128,1152]{1,0:T(8,128)(2,1)S(1)}, u32[]{:S(2)}, u32[]{:S(2)}) collective-permute-start(bf16[128,1152]{1,0:T(8,128)(2,1)} %get-tuple-element.50), channel_id=1, source_target_pairs={{0,24},{8,16},{16,8},{24,0},{1,25},{9,17},{17,9},{25,1},{2,26},{10... | collective-permute-start | bytes 884744 | tf_op jit(solution)/shard_map/ppermute | solution.py:647
  25.9 5.4 %collective-permute-start.11 = (f32[16,128]{1,0:T(8,128)S(1)}, f32[16,128]{1,0:T(8,128)S(1)}, u32[]{:S(2)}, u32[]{:S(2)}) collective-permute-start(f32[16,128]{1,0:T(8,128)S(1)} %shard_map.106.pair_ref), channel_id=1, source_target_pairs={{0,6},{1,25},{2,4},{3,27},{4,2},{5,29},{6,0},{7,31},{8,14},{9,17},... | collective-permute-start | bytes 24584 | tf_op jit(solution)/shard_map/ppermute | solution.py:251
  27.4 4.5 %collective-permute-start.10 = (f32[16,128]{1,0:T(8,128)S(1)}, f32[16,128]{1,0:T(8,128)S(1)}, u32[]{:S(2)}, u32[]{:S(2)}) collective-permute-start(f32[16,128]{1,0:T(8,128)S(1)} %shard_map.106.pair_ref), channel_id=1, source_target_pairs={{0,4},{1,17},{2,6},{3,19},{4,0},{5,21},{6,2},{7,23},{8,12},{9,25},... | collective-permute-start | bytes 24584 | tf_op jit(solution)/shard_map/ppermute | solution.py:251
  31.3 3.7 %collective-permute-start.9 = (f32[16,128]{1,0:T(8,128)S(1)}, f32[16,128]{1,0:T(8,128)S(1)}, u32[]{:S(2)}, u32[]{:S(2)}) collective-permute-start(f32[16,128]{1,0:T(8,128)S(1)} %shard_map.106.pair_ref), channel_id=1, source_target_pairs={{0,2},{1,9},{2,0},{3,11},{4,6},{5,13},{6,4},{7,15},{8,10},{9,1},{1... | collective-permute-start | bytes 24584 | tf_op jit(solution)/shard_map/ppermute | solution.py:251
  35.0 4.9 %collective-permute-start.12 = (f32[48,128]{1,0:T(8,128)S(1)}, f32[48,128]{1,0:T(8,128)S(1)}, u32[]{:S(2)}, u32[]{:S(2)}) collective-permute-start(f32[48,128]{1,0:T(8,128)S(1)} %shard_map.107.got_ref), channel_id=1, source_target_pairs={{0,1},{1,0},{2,3},{3,2},{4,5},{5,4},{6,7},{7,6},{8,9},{9,8},{10,11... | collective-permute-start | bytes 73736 | tf_op jit(solution)/shard_map/ppermute | solution.py:647
  40.6 5.7 %collective-permute-start.15 = (bf16[128,128]{1,0:T(8,128)(2,1)S(1)}, bf16[128,128]{1,0:T(8,128)(2,1)S(1)}, u32[]{:S(2)}, u32[]{:S(2)}) collective-permute-start(bf16[128,128]{1,0:T(8,128)(2,1)S(1)} %shard_map.108.raw_ref.refs_4_), channel_id=1, source_target_pairs={{0,24},{8,16},{16,8},{24,0},{1,25},{9,17},{17,9},{25,1},{2,26},{10... | collective-permute-start | bytes 98312 | tf_op jit(solution)/shard_map/ppermute | solution.py:647
  42.1 4.2 %collective-permute-start.14 = (bf16[128,128]{1,0:T(8,128)(2,1)S(1)}, bf16[128,128]{1,0:T(8,128)(2,1)S(1)}, u32[]{:S(2)}, u32[]{:S(2)}) collective-permute-start(bf16[128,128]{1,0:T(8,128)(2,1)S(1)} %shard_map.108.raw_ref.refs_4_), channel_id=1, source_target_pairs={{0,16},{8,24},{16,0},{24,8},{1,17},{9,25},{17,1},{25,9},{2,18},{10... | collective-permute-start | bytes 98312 | tf_op jit(solution)/shard_map/ppermute | solution.py:647
  43.6 3.9 %collective-permute-start.13 = (bf16[128,128]{1,0:T(8,128)(2,1)S(1)}, bf16[128,128]{1,0:T(8,128)(2,1)S(1)}, u32[]{:S(2)}, u32[]{:S(2)}) collective-permute-start(bf16[128,128]{1,0:T(8,128)(2,1)S(1)} %shard_map.108.raw_ref.refs_4_), channel_id=1, source_target_pairs={{0,8},{8,0},{16,24},{24,16},{1,9},{9,1},{17,25},{25,17},{2,10},{10... | collective-permute-start | bytes 98312 | tf_op jit(solution)/shard_map/ppermute | solution.py:647
  50.8 5.9 %collective-permute-start.17 = (bf16[80,512]{1,0:T(8,128)(2,1)S(1)}, bf16[80,512]{1,0:T(8,128)(2,1)S(1)}, u32[]{:S(2)}, u32[]{:S(2)}) collective-permute-start(bf16[80,512]{1,0:T(8,128)(2,1)S(1)} %get-tuple-element.70), channel_id=1, source_target_pairs={{0,2},{1,3},{2,0},{3,1},{4,6},{5,7},{6,4},{7,5},{8,10},{9,11},{10,... | collective-permute-start | bytes 245768 | tf_op jit(solution)/shard_map/ppermute | solution.py:647
  51.3 9.3 %collective-permute-start.18 = (bf16[80,512]{1,0:T(8,128)(2,1)S(1)}, bf16[80,512]{1,0:T(8,128)(2,1)S(1)}, u32[]{:S(2)}, u32[]{:S(2)}) collective-permute-start(bf16[80,512]{1,0:T(8,128)(2,1)S(1)} %get-tuple-element.71), channel_id=1, source_target_pairs={{0,4},{1,5},{2,6},{3,7},{4,0},{5,1},{6,2},{7,3},{8,12},{9,13},{10,... | collective-permute-start | bytes 245768 | tf_op jit(solution)/shard_map/ppermute | solution.py:647
  53.0 7.6 %collective-permute-start.19 = (bf16[80,512]{1,0:T(8,128)(2,1)S(1)}, bf16[80,512]{1,0:T(8,128)(2,1)S(1)}, u32[]{:S(2)}, u32[]{:S(2)}) collective-permute-start(bf16[80,512]{1,0:T(8,128)(2,1)S(1)} %get-tuple-element.72), channel_id=1, source_target_pairs={{0,6},{1,7},{2,4},{3,5},{4,2},{5,3},{6,0},{7,1},{8,14},{9,15},{10,... | collective-permute-start | bytes 245768 | tf_op jit(solution)/shard_map/ppermute | solution.py:647
  60.7 4.6 %collective-permute-start.20 = (bf16[80,512]{1,0:T(8,128)(2,1)S(1)}, bf16[80,512]{1,0:T(8,128)(2,1)S(1)}, u32[]{:S(2)}, u32[]{:S(2)}) collective-permute-start(bf16[80,512]{1,0:T(8,128)(2,1)S(1)} %shard_map.112.refs_0_), channel_id=1, source_target_pairs={{0,2},{1,3},{2,0},{3,1},{4,6},{5,7},{6,4},{7,5},{8,10},{9,11},{10,... | collective-permute-start | bytes 245768 | tf_op jit(solution)/shard_map/ppermute | solution.py:647
  62.6 7.7 %collective-permute-start.23 = (bf16[80,512]{1,0:T(8,128)(2,1)S(1)}, bf16[80,512]{1,0:T(8,128)(2,1)S(1)}, u32[]{:S(2)}, u32[]{:S(2)}) collective-permute-start(bf16[80,512]{1,0:T(8,128)(2,1)S(1)} %shard_map.112.refs_0_), channel_id=1, source_target_pairs={{0,6},{1,7},{2,4},{3,5},{4,2},{5,3},{6,0},{7,1},{8,14},{9,15},{10,... | collective-permute-start | bytes 245768 | tf_op jit(solution)/shard_map/ppermute | solution.py:647
  65.3 7.4 %collective-permute-start.22 = (bf16[80,512]{1,0:T(8,128)(2,1)S(1)}, bf16[80,512]{1,0:T(8,128)(2,1)S(1)}, u32[]{:S(2)}, u32[]{:S(2)}) collective-permute-start(bf16[80,512]{1,0:T(8,128)(2,1)S(1)} %shard_map.112.refs_0_), channel_id=1, source_target_pairs={{0,4},{1,5},{2,6},{3,7},{4,0},{5,1},{6,2},{7,3},{8,12},{9,13},{10,... | collective-permute-start | bytes 245768 | tf_op jit(solution)/shard_map/ppermute | solution.py:647
  65.3 8.5 %collective-permute-start.29 = (bf16[160,512]{1,0:T(8,128)(2,1)S(1)}, bf16[160,512]{1,0:T(8,128)(2,1)S(1)}, u32[]{:S(2)}, u32[]{:S(2)}) collective-permute-start(bf16[160,512]{1,0:T(8,128)(2,1)S(1)} %shard_map.113.refs_0_), channel_id=1, source_target_pairs={{0,16},{8,24},{16,0},{24,8},{1,17},{9,25},{17,1},{25,9},{2,18},{10... | collective-permute-start | bytes 491528 | tf_op jit(solution)/shard_map/ppermute | solution.py:647
  65.9 7.9 %collective-permute-start.25 = (bf16[160,512]{1,0:T(8,128)(2,1)S(1)}, bf16[160,512]{1,0:T(8,128)(2,1)S(1)}, u32[]{:S(2)}, u32[]{:S(2)}) collective-permute-start(bf16[160,512]{1,0:T(8,128)(2,1)S(1)} %shard_map.113.refs_0_), channel_id=1, source_target_pairs={{0,8},{8,0},{16,24},{24,16},{1,9},{9,1},{17,25},{25,17},{2,10},{10... | collective-permute-start | bytes 491528 | tf_op jit(solution)/shard_map/ppermute | solution.py:647
  66.4 7.9 %collective-permute-start.21 = (bf16[160,512]{1,0:T(8,128)(2,1)S(1)}, bf16[160,512]{1,0:T(8,128)(2,1)S(1)}, u32[]{:S(2)}, u32[]{:S(2)}) collective-permute-start(bf16[160,512]{1,0:T(8,128)(2,1)S(1)} %shard_map.113.refs_0_), channel_id=1, source_target_pairs={{0,1},{1,0},{2,3},{3,2},{4,5},{5,4},{6,7},{7,6},{8,9},{9,8},{10,11... | collective-permute-start | bytes 491528 | tf_op jit(solution)/shard_map/ppermute | solution.py:647
  72.6 7.1 %collective-permute-start.31 = (bf16[160,512]{1,0:T(8,128)(2,1)S(1)}, bf16[160,512]{1,0:T(8,128)(2,1)S(1)}, u32[]{:S(2)}, u32[]{:S(2)}) collective-permute-start(bf16[160,512]{1,0:T(8,128)(2,1)S(1)} %shard_map.114.refs_2_), channel_id=1, source_target_pairs={{0,16},{8,24},{16,0},{24,8},{1,17},{9,25},{17,1},{25,9},{2,18},{10... | collective-permute-start | bytes 491528 | tf_op jit(solution)/shard_map/ppermute | solution.py:647
  73.2 6.7 %collective-permute-start.27 = (bf16[160,512]{1,0:T(8,128)(2,1)S(1)}, bf16[160,512]{1,0:T(8,128)(2,1)S(1)}, u32[]{:S(2)}, u32[]{:S(2)}) collective-permute-start(bf16[160,512]{1,0:T(8,128)(2,1)S(1)} %shard_map.114.refs_2_), channel_id=1, source_target_pairs={{0,8},{8,0},{16,24},{24,16},{1,9},{9,1},{17,25},{25,17},{2,10},{10... | collective-permute-start | bytes 491528 | tf_op jit(solution)/shard_map/ppermute | solution.py:647
  73.8 6.2 %collective-permute-start.24 = (bf16[160,512]{1,0:T(8,128)(2,1)S(1)}, bf16[160,512]{1,0:T(8,128)(2,1)S(1)}, u32[]{:S(2)}, u32[]{:S(2)}) collective-permute-start(bf16[160,512]{1,0:T(8,128)(2,1)S(1)} %shard_map.114.refs_2_), channel_id=1, source_target_pairs={{0,1},{1,0},{2,3},{3,2},{4,5},{5,4},{6,7},{7,6},{8,9},{9,8},{10,11... | collective-permute-start | bytes 491528 | tf_op jit(solution)/shard_map/ppermute | solution.py:647
  73.8 6.7 %collective-permute-start.30 = (bf16[160,512]{1,0:T(8,128)(2,1)S(1)}, bf16[160,512]{1,0:T(8,128)(2,1)S(1)}, u32[]{:S(2)}, u32[]{:S(2)}) collective-permute-start(bf16[160,512]{1,0:T(8,128)(2,1)S(1)} %collective-permute-done.29.refs_4_.refs_8_), channel_id=1, source_target_pairs={{0,1},{1,0},{2,3},{3,2},{4,5},{5,4},{6,7},{7,6},{8,9},{9,8},{10,11... | collective-permute-start | bytes 491528 | tf_op jit(solution)/shard_map/ppermute | solution.py:647
  74.3 7.8 %collective-permute-start.33 = (bf16[160,512]{1,0:T(8,128)(2,1)S(1)}, bf16[160,512]{1,0:T(8,128)(2,1)S(1)}, u32[]{:S(2)}, u32[]{:S(2)}) collective-permute-start(bf16[160,512]{1,0:T(8,128)(2,1)S(1)} %collective-permute-done.25.refs_0_.refs_4_), channel_id=1, source_target_pairs={{0,16},{8,24},{16,0},{24,8},{1,17},{9,25},{17,1},{25,9},{2,18},{10... | collective-permute-start | bytes 491528 | tf_op jit(solution)/shard_map/ppermute | solution.py:647
  79.8 5.3 %collective-permute-start.35 = (bf16[160,512]{1,0:T(8,128)(2,1)S(1)}, bf16[160,512]{1,0:T(8,128)(2,1)S(1)}, u32[]{:S(2)}, u32[]{:S(2)}) collective-permute-start(bf16[160,512]{1,0:T(8,128)(2,1)S(1)} %collective-permute-done.31.refs_6_.refs_10_), channel_id=1, source_target_pairs={{0,8},{8,0},{16,24},{24,16},{1,9},{9,1},{17,25},{25,17},{2,10},{10... | collective-permute-start | bytes 491528 | tf_op jit(solution)/shard_map/ppermute | solution.py:647
  79.9 6.3 %collective-permute-start.26 = (bf16[160,512]{1,0:T(8,128)(2,1)S(1)}, bf16[160,512]{1,0:T(8,128)(2,1)S(1)}, u32[]{:S(2)}, u32[]{:S(2)}) collective-permute-start(bf16[160,512]{1,0:T(8,128)(2,1)S(1)} %collective-permute-done.25.refs_0_.refs_4_), channel_id=1, source_target_pairs={{0,1},{1,0},{2,3},{3,2},{4,5},{5,4},{6,7},{7,6},{8,9},{9,8},{10,11... | collective-permute-start | bytes 491528 | tf_op jit(solution)/shard_map/ppermute | solution.py:647
  79.9 6.3 %collective-permute-start.32 = (bf16[160,512]{1,0:T(8,128)(2,1)S(1)}, bf16[160,512]{1,0:T(8,128)(2,1)S(1)}, u32[]{:S(2)}, u32[]{:S(2)}) collective-permute-start(bf16[160,512]{1,0:T(8,128)(2,1)S(1)} %collective-permute-done.31.refs_6_.refs_10_), channel_id=1, source_target_pairs={{0,1},{1,0},{2,3},{3,2},{4,5},{5,4},{6,7},{7,6},{8,9},{9,8},{10,11... | collective-permute-start | bytes 491528 | tf_op jit(solution)/shard_map/ppermute | solution.py:647
  80.5 5.8 %collective-permute-start.28 = (bf16[160,512]{1,0:T(8,128)(2,1)S(1)}, bf16[160,512]{1,0:T(8,128)(2,1)S(1)}, u32[]{:S(2)}, u32[]{:S(2)}) collective-permute-start(bf16[160,512]{1,0:T(8,128)(2,1)S(1)} %collective-permute-done.27.refs_2_.refs_6_), channel_id=1, source_target_pairs={{0,1},{1,0},{2,3},{3,2},{4,5},{5,4},{6,7},{7,6},{8,9},{9,8},{10,11... | collective-permute-start | bytes 491528 | tf_op jit(solution)/shard_map/ppermute | solution.py:647
  82.1 5.8 %collective-permute-start.34 = (bf16[160,512]{1,0:T(8,128)(2,1)S(1)}, bf16[160,512]{1,0:T(8,128)(2,1)S(1)}, u32[]{:S(2)}, u32[]{:S(2)}) collective-permute-start(bf16[160,512]{1,0:T(8,128)(2,1)S(1)} %collective-permute-done.33.refs_12_), channel_id=1, source_target_pairs={{0,1},{1,0},{2,3},{3,2},{4,5},{5,4},{6,7},{7,6},{8,9},{9,8},{10,11... | collective-permute-start | bytes 491528 | tf_op jit(solution)/shard_map/ppermute | solution.py:647
  (8 other events, 63.9 us)

commit v5 on v4

--- a/solution.py
+++ b/solution.py
@@ -484,8 +484,11 @@
             g_out[...] += term_out
     me = lax.axis_index("dp")
     first = 0 if wide == share else lax.axis_index("blk") * share
-    keep_ref[...] = jnp.zeros(keep_ref.shape, F32)
-    away_ref[...] = jnp.zeros(away_ref.shape, BF16)
+    keep_ref[:, lay.top :, :] = jnp.zeros((peers // 2, lay.strip, width), F32)
+    away_ref[:, lay.top :, :] = jnp.zeros((peers // 2, lay.strip, width), BF16)
+    if lay.top > lay.in_rows:
+        keep_ref[:, : lay.top, :] = jnp.zeros((peers // 2, lay.top, width), F32)
+        away_ref[:, : lay.top, :] = jnp.zeros((peers // 2, lay.top, width), BF16)
     for slot in range(peers):
         owner = me ^ slot
         target = away_ref if slot & 1 else keep_ref
@@ -515,22 +518,33 @@
     )(*args)
 
 
-def pair_kernel(keep_ref, got_ref, own_ref, *out_refs):
-    own_ref[...] = keep_ref[0] + got_ref[0].astype(F32)
-    for i, out_ref in enumerate(out_refs):
-        out_ref[...] = (keep_ref[i + 1] + got_ref[i + 1].astype(F32)).astype(BF16)
+HALVES = 2
+
+
+def pair_kernel(keep_ref, got_ref, *out_refs):
+    slots, _, width = keep_ref.shape
+    part = width // HALVES
+    for half in range(HALVES):
+        cols = slice(half * part, (half + 1) * part)
+        for i in range(slots):
+            out_ref = out_refs[half * slots + i]
+            total = keep_ref[i, :, cols] + got_ref[i, :, cols].astype(F32)
+            out_ref[...] = total.astype(out_ref.dtype)
 
 
 def pair_sum(keep, got):
     slots, rows, width = keep.shape
-    return pl.pallas_call(
+    part = (rows, width // HALVES)
+    outs = [shape(part, F32)] + [shape(part, BF16)] * (slots - 1)
+    sums = pl.pallas_call(
         pair_kernel,
         in_specs=[VMEM] * 2,
-        out_shape=[shape((rows, width), F32)] + [shape((rows, width), BF16)] * (slots - 1),
-        out_specs=[VMEM] * slots,
+        out_shape=outs * HALVES,
+        out_specs=[VMEM] * (slots * HALVES),
         compiler_params=params(8),
         cost_estimate=cost(1e6, 2e6),
     )(keep, got)
+    return [sums[half * slots : (half + 1) * slots] for half in range(HALVES)]
 
 
 def total_kernel(own_ref, *refs):
@@ -551,8 +565,9 @@
     )(own, *got)
 
 
-def finish_kernel(lay, parts, done, closing, *refs):
+def finish_kernel(lay, parts, done, fresh, closing, *refs):
     slots = lay.peers // 2
+    part_cols = lay.width // HALVES
     part_refs, refs = dict(zip(parts, refs)), refs[len(parts) :]
     if done:
         refs = refs[2:]
@@ -562,58 +577,62 @@
     stage, strip_stage, sems, strip_sems = refs
     me_blk, me_dp = lax.axis_index("blk"), lax.axis_index("dp")
     copies = []
-    slot = 0
-    for (hop, core, half), source in part_refs.items():
-        if closing and (hop, core, half) not in closing:
-            continue
-        for z in range(slots // 2):
+
+    def send(kept, slot, target, sem):
+        copy = pltpu.make_async_copy(kept.at[slot], target, sem.at[slot])
+        copy.start()
+        copies.append(copy)
+
+    for n, (hop, core, half) in enumerate(fresh):
+        source = part_refs[hop, core, half]
+        cols = slice(half * part_cols, (half + 1) * part_cols)
+        for z in range(slots):
+            slot = n * slots + z
             at = z * lay.rows
-            owner = (me_blk ^ hop) * lay.peers + (me_dp ^ (half * slots + 2 * z + core))
+            owner = (me_blk ^ hop) * lay.peers + (me_dp ^ (2 * z + core))
             stage[slot] = source[at : at + lay.in_rows, :].astype(F32)
-            strip = at + lay.top
-            strip_stage[slot] = source[strip : strip + lay.out_rows, :128].astype(F32)
-            for kept, target, rows, sem in (
-                (stage, g_in_hbm, lay.in_rows, sems),
-                (strip_stage, g_out_hbm, lay.out_rows, strip_sems),
-            ):
-                copy = pltpu.make_async_copy(
-                    kept.at[slot], target.at[pl.ds(owner * rows, rows), :], sem.at[slot]
+            send(stage, slot, g_in_hbm.at[pl.ds(owner * lay.in_rows, lay.in_rows), cols], sems)
+            if half == 0:
+                strip = at + lay.top
+                strip_stage[slot] = source[strip : strip + lay.out_rows, :128].astype(F32)
+                send(
+                    strip_stage,
+                    slot,
+                    g_out_hbm.at[pl.ds(owner * lay.out_rows, lay.out_rows), :],
+                    strip_sems,
                 )
-                copy.start()
-                copies.append(copy)
-            slot += 1
     if closing:
         for core in range(2):
-            for half in range(2):
-                for z in range(slots // 2):
-                    strip = z * lay.rows + lay.top
-                    owner = me_dp ^ (half * slots + 2 * z + core)
-                    for start, rows, cols in lay.mix_parts():
-                        terms = [
-                            part_refs[hop, core, half][strip : strip + rows, cols].astype(F32)
-                            for hop in range(lay.size)
-                        ]
-                        while len(terms) > 1:
-                            terms = [terms[t] + terms[t + 1] for t in range(0, len(terms), 2)]
-                        g_mix_ref[pl.ds(owner * lay.mix_rows + start, rows), :] = terms[0]
+            for z in range(slots):
+                strip = z * lay.rows + lay.top
+                owner = me_dp ^ (2 * z + core)
+                for start, rows, cols in lay.mix_parts():
+                    half, first = divmod(cols.start, part_cols)
+                    terms = [
+                        part_refs[hop, core, half][strip : strip + rows, first : first + 128].astype(F32)
+                        for hop in range(lay.size)
+                    ]
+                    while len(terms) > 1:
+                        terms = [terms[t] + terms[t + 1] for t in range(0, len(terms), 2)]
+                    g_mix_ref[pl.ds(owner * lay.mix_rows + start, rows), :] = terms[0]
     for copy in copies:
         copy.wait()
 
 
-def finish(lay, parts, done, closing, lanes, feats, width):
-    slots = (len(closing) if closing else len(parts)) * lay.peers // 4
+def finish(lay, parts, done, fresh, closing, lanes, feats, width):
+    slots = len(fresh) * lay.peers // 2
     outs = [shape((feats, width), F32), shape((width, 128), F32)]
     specs = [ANY, ANY]
     if closing:
         outs.append(shape((lanes, 128), F32))
         specs.append(VMEM)
     return pl.pallas_call(
-        functools.partial(finish_kernel, lay, tuple(parts), bool(done), closing),
+        functools.partial(finish_kernel, lay, tuple(parts), bool(done), tuple(fresh), closing),
         in_specs=[VMEM] * len(parts) + [ANY] * len(done),
         out_shape=outs,
         out_specs=specs,
         scratch_shapes=[
-            pltpu.VMEM((slots, lay.in_rows, lay.width), F32),
+            pltpu.VMEM((slots, lay.in_rows, lay.width // HALVES), F32),
             pltpu.VMEM((slots, lay.out_rows, 128), F32),
             pltpu.SemaphoreType.DMA((slots,)),
             pltpu.SemaphoreType.DMA((slots,)),
@@ -687,30 +706,30 @@
     g_mix = lower(grad_raw, rscale, in_w, out_w, slope, normed, mixed, spec, freqs)
     keep, away = weight_grads(lay, columns, factors, raws, out_w, g_mix)
     got = swap(away, "dp", 1)
-    own, *sends = pair_sum(keep, got)
-    got = [swap(block, "dp", hop) for block, hop in zip(sends, along)]
-    share = total_sum(own, got)
-    shares = spread(share, "dp", along)
-    middle = len(shares) // 2
-    planes = {(0, 0): stack(shares[:middle]), (0, 1): stack(shares[middle:])}
-    for half in range(2):
+    planes = {}
+    for half, (own, *sends) in enumerate(pair_sum(keep, got)):
+        got = [swap(block, "dp", hop) for block, hop in zip(sends, along)]
+        share = total_sum(own, got)
+        shares = spread(share, "dp", along)
+        planes[0, half] = stack(shares)
         for hop in single:
             planes[hop, half] = swap(planes[0, half], "blk", hop)
         for hop in several:
             bit = hop & -hop if half else 1 << (hop.bit_length() - 1)
             planes[hop, half] = swap(planes[hop ^ bit, half], "blk", bit)
     parts, done = {}, []
-    groups = [group for group in ([0], single, several) if group]
-    for order, group in enumerate(groups):
+    stages = [[(0, 0), (0, 1)], [(hop, 0) for hop in single], [(hop, 1) for hop in single]]
+    stages += [[(hop, half) for hop in several] for half in range(HALVES)]
+    stages = [stage for stage in stages if stage]
+    for order, stage in enumerate(stages):
         fresh = {}
-        for hop in group:
-            for half in range(2):
-                fresh[hop, 0, half] = planes[hop, half]
-                fresh[hop, 1, half] = swap(planes[hop, half], "dp", 1)
+        for hop, half in stage:
+            fresh[hop, 0, half] = planes[hop, half]
+            fresh[hop, 1, half] = swap(planes[hop, half], "dp", 1)
         parts.update(fresh)
-        last = order == len(groups) - 1
+        last = order == len(stages) - 1
         done = finish(
-            lay, parts if last else fresh, done, tuple(fresh) if last else (), lanes, feats, width
+            lay, parts if last else fresh, done, fresh, last, lanes, feats, width
         )
     g_in, g_out, g_mix = done
     return (loss.reshape(count), g_mix, g_in, g_out)

time: 89.9 us -> 89.2 us (level)
  waiting for transfers between devices: 37.4 us -> 24.6 us
  starting transfers between devices: 33.7 us -> 43.9 us
  Pallas kernels: 17.9 us -> 19.6 us
    ppermute x31 -> x37, waiting for transfers between devices: 25.8 us -> 13.1 us  [swap(): return lax.ppermute(block, axis, [(src, src ^ bit) for src in range(size)])]
    ppermute x31 -> x37, starting transfers between devices: 25.9 us -> 36.2 us  [swap(): return lax.ppermute(block, axis, [(src, src ^ bit) for src in range(size)])]
    pallas_call x3 -> x5, Pallas kernels: 4.6 us -> 6.4 us  [finish(): pl.pallas_call(functools.partial(finish_kernel, lay, tuple(parts), bool(d...]
  transfers between devices with their start and end apart: 37 -> 43, of which waited for: 17 -> 17; matrix products, arithmetic and copies ran while one was open for 0% -> 0% of each run, Pallas kernels for 8% -> 10%
where the time goes in v5:
time: 89.2 us; the launch traced here: 89 us
  starting transfers between devices  43.9 us (49%)
  waiting for transfers between devices  24.6 us (28%)
  Pallas kernels  19.6 us (22%)
    ppermute x37, starting transfers between devices, swap(): return lax.ppermute(block, axis, [(src, src ^ bit) for src in range(size)])  36.2 us
    ppermute x37, waiting for transfers between devices, swap(): return lax.ppermute(block, axis, [(src, src ^ bit) for src in range(size)])  13.1 us
    ppermute x6, waiting for transfers between devices, cross(): got.append(lax.ppermute(pair, ('blk', 'dp'), routes))  11.5 us
    ppermute x6, starting transfers between devices, cross(): got.append(lax.ppermute(pair, ('blk', 'dp'), routes))  7.73 us
    pallas_call x1, Pallas kernels, encode(): pl.pallas_call(functools.partial(encode_kernel, freqs, size, rounds), in_...  7.38 us
    pallas_call x5, Pallas kernels, finish(): pl.pallas_call(functools.partial(finish_kernel, lay, tuple(parts), bool(d...  6.4 us
    pallas_call x1, Pallas kernels, lower(): pl.pallas_call(functools.partial(lower_kernel, freqs), in_specs=[VMEM] *...  2.07 us
  transfers between devices with their start and end apart: 43, of which 17 were waited for; matrix products, arithmetic and copies ran while one was open for 0% of the time, Pallas kernels for 10%

profile of v5, /device:TPU:0, one launch (start us, length us, event | category | flops | bytes accessed | tf_op | source)
XLA Modules:
  0.0 89.0 jit_solution(1271717495276766944)
XLA Ops:
  0.7 7.4 %shard_map.102 = (bf16[128,1152]{1,0:T(8,128)(2,1)}, bf16[128,1152]{1,0:T(8,128)(2,1)}, bf16[128,1152]{1,0:T(8,128)(2,1)}, bf16[128,1152]{1,0:T(8,128)(2,1)}, bf...) custom-call(bf16[128,64,256]{2,1,0:T(8,128)(2,1)} %patch_hbm.1, ...), custom_call_target="tpu_custom_call" | custom-call | flops 3000000000 | bytes 14000000 | tf_op jit(solution)/shard_map/pallas_call | solution.py:191
  9.5 5.0 %collective-permute-start.3 = (bf16[256,128]{1,0:T(8,128)(2,1)S(1)}, bf16[256,128]{1,0:T(8,128)(2,1)S(1)}, u32[]{:S(2)}, u32[]{:S(2)}) collective-permute-start(bf16[256,128]{1,0:T(8,128)(2,1)S(1)} %shard_map.103.pair_ref), channel_id=1, source_target_pairs={{0,6},{1,25},{2,4},{3,27},{4,2},{5,29},{6,0},{7,31},{8,14},{9,17},... | collective-permute-start | bytes 196616 | tf_op jit(solution)/shard_map/ppermute | solution.py:251
  15.1 1.7 %collective-permute-done.3.refs_2_ = bf16[256,128]{1,0:T(8,128)(2,1)S(1)} collective-permute-done((bf16[256,128]{1,0:T(8,128)(2,1)S(1)}, bf16[256,128]{1,0:T(8,128)(2,1)S(1)}, u32[]{:S(2)}, u32[]{:S(2)}) %collective-permute-start.3) | collective-permute-done | bytes 65568 | tf_op jit(solution)/shard_map/ppermute | solution.py:251
  16.8 2.8 %collective-permute-done.2.refs_1_ = bf16[256,128]{1,0:T(8,128)(2,1)S(1)} collective-permute-done((bf16[256,128]{1,0:T(8,128)(2,1)S(1)}, bf16[256,128]{1,0:T(8,128)(2,1)S(1)}, u32[]{:S(2)}, u32[]{:S(2)}) %collective-permute-start.2) | collective-permute-done | bytes 65568 | tf_op jit(solution)/shard_map/ppermute | solution.py:251
  19.7 1.6 %collective-permute-start.5 = (bf16[128,1152]{1,0:T(8,128)(2,1)}, bf16[128,1152]{1,0:T(8,128)(2,1)S(1)}, u32[]{:S(2)}, u32[]{:S(2)}) collective-permute-start(bf16[128,1152]{1,0:T(8,128)(2,1)} %get-tuple-element.56), channel_id=1, source_target_pairs={{0,8},{8,0},{16,24},{24,16},{1,9},{9,1},{17,25},{25,17},{2,10},{10... | collective-permute-start | bytes 884744 | tf_op jit(solution)/shard_map/ppermute | solution.py:666
  21.3 1.5 %collective-permute-start.6 = (bf16[128,1152]{1,0:T(8,128)(2,1)}, bf16[128,1152]{1,0:T(8,128)(2,1)S(1)}, u32[]{:S(2)}, u32[]{:S(2)}) collective-permute-start(bf16[128,1152]{1,0:T(8,128)(2,1)} %get-tuple-element.57), channel_id=1, source_target_pairs={{0,16},{8,24},{16,0},{24,8},{1,17},{9,25},{17,1},{25,9},{2,18},{10... | collective-permute-start | bytes 884744 | tf_op jit(solution)/shard_map/ppermute | solution.py:666
  23.3 1.3 %shard_map.105 = (f32[128,128]{1,0:T(8,128)S(1)}, f32[8,128]{1,0:T(8,128)S(1)}, f32[1,128]{1,0:T(1,128)}, bf16[512,128]{1,0:T(8,128)(2,1)S(1)}, bf16[1024,128]{1,0:T(8,128)(2,1)S(1)}) custom-call(s32[1,128]{1,0:T(1,128)S(1)} %bitcast.3, s32[1,128]{1,0:T(1,128)S(1)} %bitcast.4, bf16[128,128]{1,0:T(8,128)(2,1)S(1)} %get-tuple-element.50.own_ref.units_ref, ...), custom_call_target="tpu_custom_call" | custom-call | flops 400000000 | bytes 1000000 | tf_op jit(solution)/shard_map/pallas_call | solution.py:329
  25.8 1.6 %collective-permute-start.11 = (f32[16,128]{1,0:T(8,128)S(1)}, f32[16,128]{1,0:T(8,128)S(1)}, u32[]{:S(2)}, u32[]{:S(2)}) collective-permute-start(f32[16,128]{1,0:T(8,128)S(1)} %shard_map.106.pair_ref), channel_id=1, source_target_pairs={{0,6},{1,25},{2,4},{3,27},{4,2},{5,29},{6,0},{7,31},{8,14},{9,17},... | collective-permute-start | bytes 24584 | tf_op jit(solution)/shard_map/ppermute | solution.py:251
  27.9 3.4 %collective-permute-done.11.refs_2_ = f32[16,128]{1,0:T(8,128)S(1)} collective-permute-done((f32[16,128]{1,0:T(8,128)S(1)}, f32[16,128]{1,0:T(8,128)S(1)}, u32[]{:S(2)}, u32[]{:S(2)}) %collective-permute-start.11) | collective-permute-done | bytes 8224 | tf_op jit(solution)/shard_map/ppermute | solution.py:251
  32.0 3.0 %collective-permute-done.9.refs_0_ = f32[16,128]{1,0:T(8,128)S(1)} collective-permute-done((f32[16,128]{1,0:T(8,128)S(1)}, f32[16,128]{1,0:T(8,128)S(1)}, u32[]{:S(2)}, u32[]{:S(2)}) %collective-permute-start.9) | collective-permute-done | bytes 8224 | tf_op jit(solution)/shard_map/ppermute | solution.py:251
  34.9 4.0 %collective-permute-start.12 = (f32[48,128]{1,0:T(8,128)S(1)}, f32[48,128]{1,0:T(8,128)S(1)}, u32[]{:S(2)}, u32[]{:S(2)}) collective-permute-start(f32[48,128]{1,0:T(8,128)S(1)} %shard_map.107.got_ref), channel_id=1, source_target_pairs={{0,1},{1,0},{2,3},{3,2},{4,5},{5,4},{6,7},{7,6},{8,9},{9,8},{10,11... | collective-permute-start | bytes 73736 | tf_op jit(solution)/shard_map/ppermute | solution.py:666
  40.6 1.5 %collective-permute-start.15 = (bf16[128,128]{1,0:T(8,128)(2,1)S(1)}, bf16[128,128]{1,0:T(8,128)(2,1)S(1)}, u32[]{:S(2)}, u32[]{:S(2)}) collective-permute-start(bf16[128,128]{1,0:T(8,128)(2,1)S(1)} %shard_map.108.raw_ref.refs_4_), channel_id=1, source_target_pairs={{0,24},{8,16},{16,8},{24,0},{1,25},{9,17},{17,9},{25,1},{2,26},{10... | collective-permute-start | bytes 98312 | tf_op jit(solution)/shard_map/ppermute | solution.py:666
  42.1 1.5 %collective-permute-start.14 = (bf16[128,128]{1,0:T(8,128)(2,1)S(1)}, bf16[128,128]{1,0:T(8,128)(2,1)S(1)}, u32[]{:S(2)}, u32[]{:S(2)}) collective-permute-start(bf16[128,128]{1,0:T(8,128)(2,1)S(1)} %shard_map.108.raw_ref.refs_4_), channel_id=1, source_target_pairs={{0,16},{8,24},{16,0},{24,8},{1,17},{9,25},{17,1},{25,9},{2,18},{10... | collective-permute-start | bytes 98312 | tf_op jit(solution)/shard_map/ppermute | solution.py:666
  44.2 2.1 %shard_map.109.refs_9_ = f32[256,128]{1,0:T(8,128)S(1)} custom-call(bf16[128,128]{1,0:T(8,128)(2,1)S(1)} %shard_map.108.raw_ref.refs_4_, f32[128,128]{1,0:T(8,128)S(1)} %get-tuple-element.69.rscale_ref, bf16[2048,512]{1,0:T(8,128)(2,1)S(1)} %get-tuple-element.70.in_w, bf16[512,128]{1,0:T(8,128)(2,1)S(1)} %get-tuple-element.68.out_w.refs_8_, ...), custom_call_target="tpu_custom_call" | custom-call | flops 1000000000 | bytes 7000000 | tf_op jit(solution)/shard_map/pallas_call | solution.py:434
  46.3 1.2 %collective-permute-done.13.refs_5_ = bf16[128,128]{1,0:T(8,128)(2,1)S(1)} collective-permute-done((bf16[128,128]{1,0:T(8,128)(2,1)S(1)}, bf16[128,128]{1,0:T(8,128)(2,1)S(1)}, u32[]{:S(2)}, u32[]{:S(2)}) %collective-permute-start.13) | collective-permute-done | bytes 32800 | tf_op jit(solution)/shard_map/ppermute | solution.py:666
  47.5 1.5 %shard_map.110 = (f32[4,80,512]{2,1,0:T(8,128)S(1)}, bf16[4,80,512]{2,1,0:T(8,128)(2,1)S(1)}) custom-call(bf16[128,1152]{1,0:T(8,128)(2,1)S(1)} %copy-done.2, bf16[128,1152]{1,0:T(8,128)(2,1)S(1)} %collective-permute-done.5.refs_1_, bf16[128,1152]{1,0:T(8,128)(2,1)S(1)} %collective-permute-done.6.refs_2_, ...), custom_call_target="tpu_custom_call" | custom-call | flops 600000000 | bytes 4000000 | tf_op jit(solution)/shard_map/pallas_call | solution.py:510
  49.1 1.6 %collective-permute-done.16.got_ref = bf16[4,80,512]{2,1,0:T(8,128)(2,1)S(1)} collective-permute-done((bf16[4,80,512]{2,1,0:T(8,128)(2,1)S(1)}, bf16[4,80,512]{2,1,0:T(8,128)(2,1)S(1)}, u32[]{:S(2)}, u32[]{:S(2)}) %collective-permute-start.16) | collective-permute-done | bytes 327712 | tf_op jit(solution)/shard_map/ppermute | solution.py:666
  51.3 1.7 %collective-permute-start.25 = (bf16[80,256]{1,0:T(8,128)(2,1)S(1)}, bf16[80,256]{1,0:T(8,128)(2,1)S(1)}, u32[]{:S(2)}, u32[]{:S(2)}) collective-permute-start(bf16[80,256]{1,0:T(8,128)(2,1)S(1)} %get-tuple-element.83), channel_id=1, source_target_pairs={{0,4},{1,5},{2,6},{3,7},{4,0},{5,1},{6,2},{7,3},{8,12},{9,13},{10,... | collective-permute-start | bytes 122888 | tf_op jit(solution)/shard_map/ppermute | solution.py:666
  53.0 2.2 %collective-permute-start.26 = (bf16[80,256]{1,0:T(8,128)(2,1)S(1)}, bf16[80,256]{1,0:T(8,128)(2,1)S(1)}, u32[]{:S(2)}, u32[]{:S(2)}) collective-permute-start(bf16[80,256]{1,0:T(8,128)(2,1)S(1)} %get-tuple-element.84), channel_id=1, source_target_pairs={{0,6},{1,7},{2,4},{3,5},{4,2},{5,3},{6,0},{7,1},{8,14},{9,15},{10,... | collective-permute-start | bytes 122888 | tf_op jit(solution)/shard_map/ppermute | solution.py:666
  55.2 2.2 %collective-permute-start.18 = (bf16[80,256]{1,0:T(8,128)(2,1)S(1)}, bf16[80,256]{1,0:T(8,128)(2,1)S(1)}, u32[]{:S(2)}, u32[]{:S(2)}) collective-permute-start(bf16[80,256]{1,0:T(8,128)(2,1)S(1)} %get-tuple-element.79), channel_id=1, source_target_pairs={{0,4},{1,5},{2,6},{3,7},{4,0},{5,1},{6,2},{7,3},{8,12},{9,13},{10,... | collective-permute-start | bytes 122888 | tf_op jit(solution)/shard_map/ppermute | solution.py:666
  57.4 2.2 %collective-permute-start.19 = (bf16[80,256]{1,0:T(8,128)(2,1)S(1)}, bf16[80,256]{1,0:T(8,128)(2,1)S(1)}, u32[]{:S(2)}, u32[]{:S(2)}) collective-permute-start(bf16[80,256]{1,0:T(8,128)(2,1)S(1)} %get-tuple-element.80), channel_id=1, source_target_pairs={{0,6},{1,7},{2,4},{3,5},{4,2},{5,3},{6,0},{7,1},{8,14},{9,15},{10,... | collective-permute-start | bytes 122888 | tf_op jit(solution)/shard_map/ppermute | solution.py:666
  59.6 1.7 %collective-permute-start.29 = (bf16[80,256]{1,0:T(8,128)(2,1)S(1)}, bf16[80,256]{1,0:T(8,128)(2,1)S(1)}, u32[]{:S(2)}, u32[]{:S(2)}) collective-permute-start(bf16[80,256]{1,0:T(8,128)(2,1)S(1)} %shard_map.114.refs_0_), channel_id=1, source_target_pairs={{0,6},{1,7},{2,4},{3,5},{4,2},{5,3},{6,0},{7,1},{8,14},{9,15},{10,... | collective-permute-start | bytes 122888 | tf_op jit(solution)/shard_map/ppermute | solution.py:666
  61.3 2.8 %collective-permute-start.27 = (bf16[80,256]{1,0:T(8,128)(2,1)S(1)}, bf16[80,256]{1,0:T(8,128)(2,1)S(1)}, u32[]{:S(2)}, u32[]{:S(2)}) collective-permute-start(bf16[80,256]{1,0:T(8,128)(2,1)S(1)} %shard_map.114.refs_0_), channel_id=1, source_target_pairs={{0,2},{1,3},{2,0},{3,1},{4,6},{5,7},{6,4},{7,5},{8,10},{9,11},{10,... | collective-permute-start | bytes 122888 | tf_op jit(solution)/shard_map/ppermute | solution.py:666
  64.1 1.8 %collective-permute-start.22 = (bf16[80,256]{1,0:T(8,128)(2,1)S(1)}, bf16[80,256]{1,0:T(8,128)(2,1)S(1)}, u32[]{:S(2)}, u32[]{:S(2)}) collective-permute-start(bf16[80,256]{1,0:T(8,128)(2,1)S(1)} %shard_map.112.refs_0_), channel_id=1, source_target_pairs={{0,6},{1,7},{2,4},{3,5},{4,2},{5,3},{6,0},{7,1},{8,14},{9,15},{10,... | collective-permute-start | bytes 122888 | tf_op jit(solution)/shard_map/ppermute | solution.py:666
  65.9 2.7 %collective-permute-start.20 = (bf16[80,256]{1,0:T(8,128)(2,1)S(1)}, bf16[80,256]{1,0:T(8,128)(2,1)S(1)}, u32[]{:S(2)}, u32[]{:S(2)}) collective-permute-start(bf16[80,256]{1,0:T(8,128)(2,1)S(1)} %shard_map.112.refs_0_), channel_id=1, source_target_pairs={{0,2},{1,3},{2,0},{3,1},{4,6},{5,7},{6,4},{7,5},{8,10},{9,11},{10,... | collective-permute-start | bytes 122888 | tf_op jit(solution)/shard_map/ppermute | solution.py:666
  72.8 1.4 %collective-permute-done.37.refs_2_.refs_10_ = bf16[320,256]{1,0:T(8,128)(2,1)S(1)} collective-permute-done((bf16[320,256]{1,0:T(8,128)(2,1)S(1)}, bf16[320,256]{1,0:T(8,128)(2,1)S(1)}, u32[]{:S(2)}, u32[]{:S(2)}) %collective-permute-start.37) | collective-permute-done | bytes 163872 | tf_op jit(solution)/shard_map/ppermute | solution.py:666
  76.4 1.4 %collective-permute-start.39 = (bf16[320,256]{1,0:T(8,128)(2,1)S(1)}, bf16[320,256]{1,0:T(8,128)(2,1)S(1)}, u32[]{:S(2)}, u32[]{:S(2)}) collective-permute-start(bf16[320,256]{1,0:T(8,128)(2,1)S(1)} %collective-permute-done.31.refs_0_.refs_4_), channel_id=1, source_target_pairs={{0,16},{8,24},{16,0},{24,8},{1,17},{9,25},{17,1},{25,9},{2,18},{10... | collective-permute-start | bytes 491528 | tf_op jit(solution)/shard_map/ppermute | solution.py:666
  78.4 2.5 %collective-permute-done.41.refs_14_ = bf16[320,256]{1,0:T(8,128)(2,1)S(1)} collective-permute-done((bf16[320,256]{1,0:T(8,128)(2,1)S(1)}, bf16[320,256]{1,0:T(8,128)(2,1)S(1)}, u32[]{:S(2)}, u32[]{:S(2)}) %collective-permute-start.41) | collective-permute-done | bytes 163872 | tf_op jit(solution)/shard_map/ppermute | solution.py:666
  82.6 1.3 %shard_map.116 = (f32[2048,512]{1,0:T(8,128)}, f32[512,128]{1,0:T(8,128)}) custom-call(bf16[320,256]{1,0:T(8,128)(2,1)S(1)} %shard_map.113.refs_0_, bf16[320,256]{1,0:T(8,128)(2,1)S(1)} %collective-permute-done.23.refs_1_, bf16[320,256]{1,0:T(8,128)(2,1)S(1)} %shard_map.115.refs_2_, bf16[320,256]{1,0:T(8,128)(2,1)S(1)} %collective-permute-done.30.refs_3_), custom_call_target="tpu_custom_call" | custom-call | flops 1000000 | bytes 8000000 | tf_op jit(solution)/shard_map/pallas_call | solution.py:629
  83.9 1.3 %shard_map.117 = (f32[2048,512]{1,0:T(8,128)}, f32[512,128]{1,0:T(8,128)}) custom-call(bf16[320,256]{1,0:T(8,128)(2,1)S(1)} %collective-permute-done.31.refs_0_.refs_4_, bf16[320,256]{1,0:T(8,128)(2,1)S(1)} %collective-permute-done.32.refs_1_.refs_5_, ...), custom_call_target="tpu_custom_call", output_to_operand_aliasing={{0}: (4, {}), {1}: (5, {})} | custom-call | flops 1000000 | bytes 8000000 | tf_op jit(solution)/shard_map/pallas_call | solution.py:629
  85.2 1.3 %shard_map.118 = (f32[2048,512]{1,0:T(8,128)}, f32[512,128]{1,0:T(8,128)}) custom-call(bf16[320,256]{1,0:T(8,128)(2,1)S(1)} %collective-permute-done.35.refs_0_.refs_8_, bf16[320,256]{1,0:T(8,128)(2,1)S(1)} %collective-permute-done.36.refs_1_.refs_9_, ...), custom_call_target="tpu_custom_call", output_to_operand_aliasing={{0}: (4, {}), {1}: (5, {})} | custom-call | flops 1000000 | bytes 8000000 | tf_op jit(solution)/shard_map/pallas_call | solution.py:629
  87.4 1.6 %shard_map.120 = (f32[2048,512]{1,0:T(8,128)}, f32[512,128]{1,0:T(8,128)}, f32[256,128]{1,0:T(8,128)}) custom-call(bf16[320,256]{1,0:T(8,128)(2,1)S(1)} %shard_map.113.refs_0_, bf16[320,256]{1,0:T(8,128)(2,1)S(1)} %collective-permute-done.23.refs_1_, bf16[320,256]{1,0:T(8,128)(2,1)S(1)} %shard_map.115.refs_2_, ...), custom_call_target="tpu_custom_call", output_to_operand_aliasing={{0}: (16, {}), {1}: (17, {})} | custom-call | flops 1000000 | bytes 8000000 | tf_op jit(solution)/shard_map/pallas_call | solution.py:629
  (79 shorter events, 17.6 us)
Async XLA Ops:
  9.5 7.3 %collective-permute-start.3 = (bf16[256,128]{1,0:T(8,128)(2,1)S(1)}, bf16[256,128]{1,0:T(8,128)(2,1)S(1)}, u32[]{:S(2)}, u32[]{:S(2)}) collective-permute-start(bf16[256,128]{1,0:T(8,128)(2,1)S(1)} %shard_map.103.pair_ref), channel_id=1, source_target_pairs={{0,6},{1,25},{2,4},{3,27},{4,2},{5,29},{6,0},{7,31},{8,14},{9,17},... | collective-permute-start | bytes 196616 | tf_op jit(solution)/shard_map/ppermute | solution.py:251
  14.5 5.2 %collective-permute-start.2 = (bf16[256,128]{1,0:T(8,128)(2,1)S(1)}, bf16[256,128]{1,0:T(8,128)(2,1)S(1)}, u32[]{:S(2)}, u32[]{:S(2)}) collective-permute-start(bf16[256,128]{1,0:T(8,128)(2,1)S(1)} %shard_map.103.pair_ref), channel_id=1, source_target_pairs={{0,4},{1,17},{2,6},{3,19},{4,0},{5,21},{6,2},{7,23},{8,12},{9,25},... | collective-permute-start | bytes 196616 | tf_op jit(solution)/shard_map/ppermute | solution.py:251
  14.5 5.2 %collective-permute-start.1 = (bf16[256,128]{1,0:T(8,128)(2,1)S(1)}, bf16[256,128]{1,0:T(8,128)(2,1)S(1)}, u32[]{:S(2)}, u32[]{:S(2)}) collective-permute-start(bf16[256,128]{1,0:T(8,128)(2,1)S(1)} %shard_map.103.pair_ref), channel_id=1, source_target_pairs={{0,2},{1,9},{2,0},{3,11},{4,6},{5,13},{6,4},{7,15},{8,10},{9,1},{1... | collective-permute-start | bytes 196616 | tf_op jit(solution)/shard_map/ppermute | solution.py:251
  19.7 23.8 %collective-permute-start.5 = (bf16[128,1152]{1,0:T(8,128)(2,1)}, bf16[128,1152]{1,0:T(8,128)(2,1)S(1)}, u32[]{:S(2)}, u32[]{:S(2)}) collective-permute-start(bf16[128,1152]{1,0:T(8,128)(2,1)} %get-tuple-element.56), channel_id=1, source_target_pairs={{0,8},{8,0},{16,24},{24,16},{1,9},{9,1},{17,25},{25,17},{2,10},{10... | collective-permute-start | bytes 884744 | tf_op jit(solution)/shard_map/ppermute | solution.py:666
  21.3 24.9 %collective-permute-start.6 = (bf16[128,1152]{1,0:T(8,128)(2,1)}, bf16[128,1152]{1,0:T(8,128)(2,1)S(1)}, u32[]{:S(2)}, u32[]{:S(2)}) collective-permute-start(bf16[128,1152]{1,0:T(8,128)(2,1)} %get-tuple-element.57), channel_id=1, source_target_pairs={{0,16},{8,24},{16,0},{24,8},{1,17},{9,25},{17,1},{25,9},{2,18},{10... | collective-permute-start | bytes 884744 | tf_op jit(solution)/shard_map/ppermute | solution.py:666
  22.8 23.4 %collective-permute-start.7 = (bf16[128,1152]{1,0:T(8,128)(2,1)}, bf16[128,1152]{1,0:T(8,128)(2,1)S(1)}, u32[]{:S(2)}, u32[]{:S(2)}) collective-permute-start(bf16[128,1152]{1,0:T(8,128)(2,1)} %get-tuple-element.58), channel_id=1, source_target_pairs={{0,24},{8,16},{16,8},{24,0},{1,25},{9,17},{17,9},{25,1},{2,26},{10... | collective-permute-start | bytes 884744 | tf_op jit(solution)/shard_map/ppermute | solution.py:666
  25.8 5.4 %collective-permute-start.11 = (f32[16,128]{1,0:T(8,128)S(1)}, f32[16,128]{1,0:T(8,128)S(1)}, u32[]{:S(2)}, u32[]{:S(2)}) collective-permute-start(f32[16,128]{1,0:T(8,128)S(1)} %shard_map.106.pair_ref), channel_id=1, source_target_pairs={{0,6},{1,25},{2,4},{3,27},{4,2},{5,29},{6,0},{7,31},{8,14},{9,17},... | collective-permute-start | bytes 24584 | tf_op jit(solution)/shard_map/ppermute | solution.py:251
  27.4 4.5 %collective-permute-start.10 = (f32[16,128]{1,0:T(8,128)S(1)}, f32[16,128]{1,0:T(8,128)S(1)}, u32[]{:S(2)}, u32[]{:S(2)}) collective-permute-start(f32[16,128]{1,0:T(8,128)S(1)} %shard_map.106.pair_ref), channel_id=1, source_target_pairs={{0,4},{1,17},{2,6},{3,19},{4,0},{5,21},{6,2},{7,23},{8,12},{9,25},... | collective-permute-start | bytes 24584 | tf_op jit(solution)/shard_map/ppermute | solution.py:251
  34.9 4.9 %collective-permute-start.12 = (f32[48,128]{1,0:T(8,128)S(1)}, f32[48,128]{1,0:T(8,128)S(1)}, u32[]{:S(2)}, u32[]{:S(2)}) collective-permute-start(f32[48,128]{1,0:T(8,128)S(1)} %shard_map.107.got_ref), channel_id=1, source_target_pairs={{0,1},{1,0},{2,3},{3,2},{4,5},{5,4},{6,7},{7,6},{8,9},{9,8},{10,11... | collective-permute-start | bytes 73736 | tf_op jit(solution)/shard_map/ppermute | solution.py:666
  40.6 5.7 %collective-permute-start.15 = (bf16[128,128]{1,0:T(8,128)(2,1)S(1)}, bf16[128,128]{1,0:T(8,128)(2,1)S(1)}, u32[]{:S(2)}, u32[]{:S(2)}) collective-permute-start(bf16[128,128]{1,0:T(8,128)(2,1)S(1)} %shard_map.108.raw_ref.refs_4_), channel_id=1, source_target_pairs={{0,24},{8,16},{16,8},{24,0},{1,25},{9,17},{17,9},{25,1},{2,26},{10... | collective-permute-start | bytes 98312 | tf_op jit(solution)/shard_map/ppermute | solution.py:666
  50.7 6.6 %collective-permute-start.24 = (bf16[80,256]{1,0:T(8,128)(2,1)S(1)}, bf16[80,256]{1,0:T(8,128)(2,1)S(1)}, u32[]{:S(2)}, u32[]{:S(2)}) collective-permute-start(bf16[80,256]{1,0:T(8,128)(2,1)S(1)} %get-tuple-element.82), channel_id=1, source_target_pairs={{0,2},{1,3},{2,0},{3,1},{4,6},{5,7},{6,4},{7,5},{8,10},{9,11},{10,... | collective-permute-start | bytes 122888 | tf_op jit(solution)/shard_map/ppermute | solution.py:666
  51.3 8.3 %collective-permute-start.25 = (bf16[80,256]{1,0:T(8,128)(2,1)S(1)}, bf16[80,256]{1,0:T(8,128)(2,1)S(1)}, u32[]{:S(2)}, u32[]{:S(2)}) collective-permute-start(bf16[80,256]{1,0:T(8,128)(2,1)S(1)} %get-tuple-element.83), channel_id=1, source_target_pairs={{0,4},{1,5},{2,6},{3,7},{4,0},{5,1},{6,2},{7,3},{8,12},{9,13},{10,... | collective-permute-start | bytes 122888 | tf_op jit(solution)/shard_map/ppermute | solution.py:666
  53.0 6.6 %collective-permute-start.26 = (bf16[80,256]{1,0:T(8,128)(2,1)S(1)}, bf16[80,256]{1,0:T(8,128)(2,1)S(1)}, u32[]{:S(2)}, u32[]{:S(2)}) collective-permute-start(bf16[80,256]{1,0:T(8,128)(2,1)S(1)} %get-tuple-element.84), channel_id=1, source_target_pairs={{0,6},{1,7},{2,4},{3,5},{4,2},{5,3},{6,0},{7,1},{8,14},{9,15},{10,... | collective-permute-start | bytes 122888 | tf_op jit(solution)/shard_map/ppermute | solution.py:666
  55.2 6.1 %collective-permute-start.17 = (bf16[80,256]{1,0:T(8,128)(2,1)S(1)}, bf16[80,256]{1,0:T(8,128)(2,1)S(1)}, u32[]{:S(2)}, u32[]{:S(2)}) collective-permute-start(bf16[80,256]{1,0:T(8,128)(2,1)S(1)} %get-tuple-element.78), channel_id=1, source_target_pairs={{0,2},{1,3},{2,0},{3,1},{4,6},{5,7},{6,4},{7,5},{8,10},{9,11},{10,... | collective-permute-start | bytes 122888 | tf_op jit(solution)/shard_map/ppermute | solution.py:666
  55.2 8.9 %collective-permute-start.18 = (bf16[80,256]{1,0:T(8,128)(2,1)S(1)}, bf16[80,256]{1,0:T(8,128)(2,1)S(1)}, u32[]{:S(2)}, u32[]{:S(2)}) collective-permute-start(bf16[80,256]{1,0:T(8,128)(2,1)S(1)} %get-tuple-element.79), channel_id=1, source_target_pairs={{0,4},{1,5},{2,6},{3,7},{4,0},{5,1},{6,2},{7,3},{8,12},{9,13},{10,... | collective-permute-start | bytes 122888 | tf_op jit(solution)/shard_map/ppermute | solution.py:666
  57.4 6.7 %collective-permute-start.19 = (bf16[80,256]{1,0:T(8,128)(2,1)S(1)}, bf16[80,256]{1,0:T(8,128)(2,1)S(1)}, u32[]{:S(2)}, u32[]{:S(2)}) collective-permute-start(bf16[80,256]{1,0:T(8,128)(2,1)S(1)} %get-tuple-element.80), channel_id=1, source_target_pairs={{0,6},{1,7},{2,4},{3,5},{4,2},{5,3},{6,0},{7,1},{8,14},{9,15},{10,... | collective-permute-start | bytes 122888 | tf_op jit(solution)/shard_map/ppermute | solution.py:666
  59.6 6.3 %collective-permute-start.29 = (bf16[80,256]{1,0:T(8,128)(2,1)S(1)}, bf16[80,256]{1,0:T(8,128)(2,1)S(1)}, u32[]{:S(2)}, u32[]{:S(2)}) collective-permute-start(bf16[80,256]{1,0:T(8,128)(2,1)S(1)} %shard_map.114.refs_0_), channel_id=1, source_target_pairs={{0,6},{1,7},{2,4},{3,5},{4,2},{5,3},{6,0},{7,1},{8,14},{9,15},{10,... | collective-permute-start | bytes 122888 | tf_op jit(solution)/shard_map/ppermute | solution.py:666
  61.3 7.3 %collective-permute-start.28 = (bf16[80,256]{1,0:T(8,128)(2,1)S(1)}, bf16[80,256]{1,0:T(8,128)(2,1)S(1)}, u32[]{:S(2)}, u32[]{:S(2)}) collective-permute-start(bf16[80,256]{1,0:T(8,128)(2,1)S(1)} %shard_map.114.refs_0_), channel_id=1, source_target_pairs={{0,4},{1,5},{2,6},{3,7},{4,0},{5,1},{6,2},{7,3},{8,12},{9,13},{10,... | collective-permute-start | bytes 122888 | tf_op jit(solution)/shard_map/ppermute | solution.py:666
  61.3 7.3 %collective-permute-start.27 = (bf16[80,256]{1,0:T(8,128)(2,1)S(1)}, bf16[80,256]{1,0:T(8,128)(2,1)S(1)}, u32[]{:S(2)}, u32[]{:S(2)}) collective-permute-start(bf16[80,256]{1,0:T(8,128)(2,1)S(1)} %shard_map.114.refs_0_), channel_id=1, source_target_pairs={{0,2},{1,3},{2,0},{3,1},{4,6},{5,7},{6,4},{7,5},{8,10},{9,11},{10,... | collective-permute-start | bytes 122888 | tf_op jit(solution)/shard_map/ppermute | solution.py:666
  64.1 5.9 %collective-permute-start.22 = (bf16[80,256]{1,0:T(8,128)(2,1)S(1)}, bf16[80,256]{1,0:T(8,128)(2,1)S(1)}, u32[]{:S(2)}, u32[]{:S(2)}) collective-permute-start(bf16[80,256]{1,0:T(8,128)(2,1)S(1)} %shard_map.112.refs_0_), channel_id=1, source_target_pairs={{0,6},{1,7},{2,4},{3,5},{4,2},{5,3},{6,0},{7,1},{8,14},{9,15},{10,... | collective-permute-start | bytes 122888 | tf_op jit(solution)/shard_map/ppermute | solution.py:666
  65.9 5.1 %collective-permute-start.21 = (bf16[80,256]{1,0:T(8,128)(2,1)S(1)}, bf16[80,256]{1,0:T(8,128)(2,1)S(1)}, u32[]{:S(2)}, u32[]{:S(2)}) collective-permute-start(bf16[80,256]{1,0:T(8,128)(2,1)S(1)} %shard_map.112.refs_0_), channel_id=1, source_target_pairs={{0,4},{1,5},{2,6},{3,7},{4,0},{5,1},{6,2},{7,3},{8,12},{9,13},{10,... | collective-permute-start | bytes 122888 | tf_op jit(solution)/shard_map/ppermute | solution.py:666
  65.9 5.1 %collective-permute-start.20 = (bf16[80,256]{1,0:T(8,128)(2,1)S(1)}, bf16[80,256]{1,0:T(8,128)(2,1)S(1)}, u32[]{:S(2)}, u32[]{:S(2)}) collective-permute-start(bf16[80,256]{1,0:T(8,128)(2,1)S(1)} %shard_map.112.refs_0_), channel_id=1, source_target_pairs={{0,2},{1,3},{2,0},{3,1},{4,6},{5,7},{6,4},{7,5},{8,10},{9,11},{10,... | collective-permute-start | bytes 122888 | tf_op jit(solution)/shard_map/ppermute | solution.py:666
  68.6 5.7 %collective-permute-start.37 = (bf16[320,256]{1,0:T(8,128)(2,1)S(1)}, bf16[320,256]{1,0:T(8,128)(2,1)S(1)}, u32[]{:S(2)}, u32[]{:S(2)}) collective-permute-start(bf16[320,256]{1,0:T(8,128)(2,1)S(1)} %shard_map.115.refs_2_), channel_id=1, source_target_pairs={{0,16},{8,24},{16,0},{24,8},{1,17},{9,25},{17,1},{25,9},{2,18},{10... | collective-permute-start | bytes 491528 | tf_op jit(solution)/shard_map/ppermute | solution.py:666
  69.2 5.3 %collective-permute-start.35 = (bf16[320,256]{1,0:T(8,128)(2,1)S(1)}, bf16[320,256]{1,0:T(8,128)(2,1)S(1)}, u32[]{:S(2)}, u32[]{:S(2)}) collective-permute-start(bf16[320,256]{1,0:T(8,128)(2,1)S(1)} %shard_map.115.refs_2_), channel_id=1, source_target_pairs={{0,8},{8,0},{16,24},{24,16},{1,9},{9,1},{17,25},{25,17},{2,10},{10... | collective-permute-start | bytes 491528 | tf_op jit(solution)/shard_map/ppermute | solution.py:666
  71.0 5.4 %collective-permute-start.31 = (bf16[320,256]{1,0:T(8,128)(2,1)S(1)}, bf16[320,256]{1,0:T(8,128)(2,1)S(1)}, u32[]{:S(2)}, u32[]{:S(2)}) collective-permute-start(bf16[320,256]{1,0:T(8,128)(2,1)S(1)} %shard_map.113.refs_0_), channel_id=1, source_target_pairs={{0,8},{8,0},{16,24},{24,16},{1,9},{9,1},{17,25},{25,17},{2,10},{10... | collective-permute-start | bytes 491528 | tf_op jit(solution)/shard_map/ppermute | solution.py:666
  71.7 6.1 %collective-permute-start.33 = (bf16[320,256]{1,0:T(8,128)(2,1)S(1)}, bf16[320,256]{1,0:T(8,128)(2,1)S(1)}, u32[]{:S(2)}, u32[]{:S(2)}) collective-permute-start(bf16[320,256]{1,0:T(8,128)(2,1)S(1)} %shard_map.113.refs_0_), channel_id=1, source_target_pairs={{0,16},{8,24},{16,0},{24,8},{1,17},{9,25},{17,1},{25,9},{2,18},{10... | collective-permute-start | bytes 491528 | tf_op jit(solution)/shard_map/ppermute | solution.py:666
  72.8 5.0 %collective-permute-start.30 = (bf16[320,256]{1,0:T(8,128)(2,1)S(1)}, bf16[320,256]{1,0:T(8,128)(2,1)S(1)}, u32[]{:S(2)}, u32[]{:S(2)}) collective-permute-start(bf16[320,256]{1,0:T(8,128)(2,1)S(1)} %shard_map.115.refs_2_), channel_id=1, source_target_pairs={{0,1},{1,0},{2,3},{3,2},{4,5},{5,4},{6,7},{7,6},{8,9},{9,8},{10,11... | collective-permute-start | bytes 491528 | tf_op jit(solution)/shard_map/ppermute | solution.py:666
  74.5 6.3 %collective-permute-start.41 = (bf16[320,256]{1,0:T(8,128)(2,1)S(1)}, bf16[320,256]{1,0:T(8,128)(2,1)S(1)}, u32[]{:S(2)}, u32[]{:S(2)}) collective-permute-start(bf16[320,256]{1,0:T(8,128)(2,1)S(1)} %collective-permute-done.37.refs_2_.refs_10_), channel_id=1, source_target_pairs={{0,8},{8,0},{16,24},{24,16},{1,9},{9,1},{17,25},{25,17},{2,10},{10... | collective-permute-start | bytes 491528 | tf_op jit(solution)/shard_map/ppermute | solution.py:666
  76.4 5.7 %collective-permute-start.39 = (bf16[320,256]{1,0:T(8,128)(2,1)S(1)}, bf16[320,256]{1,0:T(8,128)(2,1)S(1)}, u32[]{:S(2)}, u32[]{:S(2)}) collective-permute-start(bf16[320,256]{1,0:T(8,128)(2,1)S(1)} %collective-permute-done.31.refs_0_.refs_4_), channel_id=1, source_target_pairs={{0,16},{8,24},{16,0},{24,8},{1,17},{9,25},{17,1},{25,9},{2,18},{10... | collective-permute-start | bytes 491528 | tf_op jit(solution)/shard_map/ppermute | solution.py:666
  77.8 6.1 %collective-permute-start.32 = (bf16[320,256]{1,0:T(8,128)(2,1)S(1)}, bf16[320,256]{1,0:T(8,128)(2,1)S(1)}, u32[]{:S(2)}, u32[]{:S(2)}) collective-permute-start(bf16[320,256]{1,0:T(8,128)(2,1)S(1)} %collective-permute-done.31.refs_0_.refs_4_), channel_id=1, source_target_pairs={{0,1},{1,0},{2,3},{3,2},{4,5},{5,4},{6,7},{7,6},{8,9},{9,8},{10,11... | collective-permute-start | bytes 491528 | tf_op jit(solution)/shard_map/ppermute | solution.py:666
  78.3 6.9 %collective-permute-start.38 = (bf16[320,256]{1,0:T(8,128)(2,1)S(1)}, bf16[320,256]{1,0:T(8,128)(2,1)S(1)}, u32[]{:S(2)}, u32[]{:S(2)}) collective-permute-start(bf16[320,256]{1,0:T(8,128)(2,1)S(1)} %collective-permute-done.37.refs_2_.refs_10_), channel_id=1, source_target_pairs={{0,1},{1,0},{2,3},{3,2},{4,5},{5,4},{6,7},{7,6},{8,9},{9,8},{10,11... | collective-permute-start | bytes 491528 | tf_op jit(solution)/shard_map/ppermute | solution.py:666
  82.1 5.4 %collective-permute-start.42 = (bf16[320,256]{1,0:T(8,128)(2,1)S(1)}, bf16[320,256]{1,0:T(8,128)(2,1)S(1)}, u32[]{:S(2)}, u32[]{:S(2)}) collective-permute-start(bf16[320,256]{1,0:T(8,128)(2,1)S(1)} %collective-permute-done.41.refs_14_), channel_id=1, source_target_pairs={{0,1},{1,0},{2,3},{3,2},{4,5},{5,4},{6,7},{7,6},{8,9},{9,8},{10,11... | collective-permute-start | bytes 491528 | tf_op jit(solution)/shard_map/ppermute | solution.py:666
  (14 other events, 89.7 us)

commit v6 on v5

--- a/solution.py
+++ b/solution.py
@@ -521,48 +521,45 @@
 HALVES = 2
 
 
-def pair_kernel(keep_ref, got_ref, *out_refs):
-    slots, _, width = keep_ref.shape
-    part = width // HALVES
-    for half in range(HALVES):
+def fold_kernel(halves, keep_ref, got_ref, *out_refs):
+    slots, rows, width = keep_ref.shape
+    part = width // halves
+    for half in range(halves):
         cols = slice(half * part, (half + 1) * part)
+        outs = out_refs[half * (len(out_refs) // halves) :]
         for i in range(slots):
-            out_ref = out_refs[half * slots + i]
-            total = keep_ref[i, :, cols] + got_ref[i, :, cols].astype(F32)
-            out_ref[...] = total.astype(out_ref.dtype)
-
-
-def pair_sum(keep, got):
+            total = keep_ref[i, :, cols] + got_ref[i * rows : (i + 1) * rows, cols].astype(F32)
+            if slots == 1:
+                outs[0][...] = total.astype(BF16)
+            elif i % 2 == 0:
+                outs[0][i // 2] = total
+            else:
+                outs[1][i // 2 * rows : (i // 2 + 1) * rows, :] = total.astype(BF16)
+
+
+def fold(keep, got, halves=1):
     slots, rows, width = keep.shape
-    part = (rows, width // HALVES)
-    outs = [shape(part, F32)] + [shape(part, BF16)] * (slots - 1)
-    sums = pl.pallas_call(
-        pair_kernel,
+    part = width // halves
+    outs = [shape((rows, part), BF16)]
+    if slots > 1:
+        outs = [shape((slots // 2, rows, part), F32), shape((slots // 2 * rows, part), BF16)]
+    outs = outs * halves
+    return pl.pallas_call(
+        functools.partial(fold_kernel, halves),
         in_specs=[VMEM] * 2,
-        out_shape=outs * HALVES,
-        out_specs=[VMEM] * (slots * HALVES),
+        out_shape=outs,
+        out_specs=[VMEM] * len(outs),
         compiler_params=params(8),
         cost_estimate=cost(1e6, 2e6),
     )(keep, got)
-    return [sums[half * slots : (half + 1) * slots] for half in range(HALVES)]
-
-
-def total_kernel(own_ref, *refs):
-    total = own_ref[...]
-    for each in refs[:-1]:
-        total = total + each[...].astype(F32)
-    refs[-1][...] = total.astype(BF16)
-
-
-def total_sum(own, got):
-    return pl.pallas_call(
-        total_kernel,
-        in_specs=[VMEM] * (1 + len(got)),
-        out_shape=shape(own.shape, BF16),
-        out_specs=VMEM,
-        compiler_params=params(8),
-        cost_estimate=cost(1e6, 1e6),
-    )(own, *got)
+
+
+def plane_order(slots):
+    order, step = [0], slots // 2
+    while step:
+        order += [z ^ step for z in order]
+        step //= 2
+    return order
 
 
 def finish_kernel(lay, parts, done, fresh, closing, *refs):
@@ -586,9 +583,9 @@
     for n, (hop, core, half) in enumerate(fresh):
         source = part_refs[hop, core, half]
         cols = slice(half * part_cols, (half + 1) * part_cols)
-        for z in range(slots):
-            slot = n * slots + z
-            at = z * lay.rows
+        for block, z in enumerate(plane_order(slots)):
+            slot = n * slots + block
+            at = block * lay.rows
             owner = (me_blk ^ hop) * lay.peers + (me_dp ^ (2 * z + core))
             stage[slot] = source[at : at + lay.in_rows, :].astype(F32)
             send(stage, slot, g_in_hbm.at[pl.ds(owner * lay.in_rows, lay.in_rows), cols], sems)
@@ -603,8 +600,8 @@
                 )
     if closing:
         for core in range(2):
-            for z in range(slots):
-                strip = z * lay.rows + lay.top
+            for block, z in enumerate(plane_order(slots)):
+                strip = block * lay.rows + lay.top
                 owner = me_dp ^ (2 * z + core)
                 for start, rows, cols in lay.mix_parts():
                     half, first = divmod(cols.start, part_cols)
@@ -677,8 +674,8 @@
     embed = w_out.shape[1]
     freqs = feats // filters
     size, peers = lax.axis_size("blk"), lax.axis_size("dp")
-    assert size & (size - 1) == 0 and peers & (peers - 1) == 0 and peers > 1
-    across, along = range(1, size), range(2, peers, 2)
+    assert size & (size - 1) == 0 and peers & (peers - 1) == 0 and peers > 2
+    across = range(1, size)
     single = [hop for hop in across if hop & (hop - 1) == 0]
     several = [hop for hop in across if hop & (hop - 1)]
     columns = piece_columns(feats, width, size)
@@ -705,13 +702,22 @@
     raws = spread(grad_raw, "blk", across)
     g_mix = lower(grad_raw, rscale, in_w, out_w, slope, normed, mixed, spec, freqs)
     keep, away = weight_grads(lay, columns, factors, raws, out_w, g_mix)
-    got = swap(away, "dp", 1)
-    planes = {}
-    for half, (own, *sends) in enumerate(pair_sum(keep, got)):
-        got = [swap(block, "dp", hop) for block, hop in zip(sends, along)]
-        share = total_sum(own, got)
-        shares = spread(share, "dp", along)
-        planes[0, half] = stack(shares)
+    got = swap(away.reshape(-1, away.shape[2]), "dp", 1)
+    planes, first = {}, fold(keep, got, HALVES)
+    turns = range((peers // 2).bit_length() - 1)
+    halves = range(HALVES)
+    kept = {half: first[2 * half : 2 * half + 2] for half in halves}
+    for turn in turns:
+        for half in halves:
+            got = swap(kept[half][1], "dp", 2 << turn)
+            kept[half] = fold(kept[half][0], got)
+    for half in halves:
+        planes[0, half] = kept[half][0]
+    for turn in reversed(turns):
+        for half in halves:
+            got = swap(planes[0, half], "dp", 2 << turn)
+            planes[0, half] = stack([planes[0, half], got])
+    for half in halves:
         for hop in single:
             planes[hop, half] = swap(planes[0, half], "blk", hop)
         for hop in several:

time: 89.2 us -> 91.4 us (1.025)
  waiting for transfers between devices: 24.6 us -> 36.3 us
  starting transfers between devices: 43.9 us -> 34.4 us
    ppermute x37 -> x33, waiting for transfers between devices: 13.1 us -> 24.7 us  [swap(): return lax.ppermute(block, axis, [(src, src ^ bit) for src in range(size)])]
    ppermute x37 -> x33, starting transfers between devices: 36.2 us -> 26.7 us  [swap(): return lax.ppermute(block, axis, [(src, src ^ bit) for src in range(size)])]
  transfers between devices with their start and end apart: 43 -> 39, of which waited for: 17 -> 22; matrix products, arithmetic and copies ran while one was open for 0% -> 0% of each run, Pallas kernels for 10% -> 10%
where the time goes in v6:
time: 91.4 us; the launch traced here: 91.3 us
  waiting for transfers between devices  36.3 us (40%)
  starting transfers between devices  34.4 us (38%)
  Pallas kernels  19.7 us (22%)
    ppermute x33, starting transfers between devices, swap(): return lax.ppermute(block, axis, [(src, src ^ bit) for src in range(size)])  26.7 us
    ppermute x33, waiting for transfers between devices, swap(): return lax.ppermute(block, axis, [(src, src ^ bit) for src in range(size)])  24.7 us
    ppermute x6, waiting for transfers between devices, cross(): got.append(lax.ppermute(pair, ('blk', 'dp'), routes))  11.5 us
    ppermute x6, starting transfers between devices, cross(): got.append(lax.ppermute(pair, ('blk', 'dp'), routes))  7.73 us
    pallas_call x1, Pallas kernels, encode(): pl.pallas_call(functools.partial(encode_kernel, freqs, size, rounds), in_...  7.41 us
    pallas_call x5, Pallas kernels, finish(): pl.pallas_call(functools.partial(finish_kernel, lay, tuple(parts), bool(d...  6.4 us
    pallas_call x1, Pallas kernels, lower(): pl.pallas_call(functools.partial(lower_kernel, freqs), in_specs=[VMEM] *...  2.06 us
  transfers between devices with their start and end apart: 39, of which 22 were waited for; matrix products, arithmetic and copies ran while one was open for 0% of the time, Pallas kernels for 10%

profile of v6, /device:TPU:0, one launch (start us, length us, event | category | flops | bytes accessed | tf_op | source)
XLA Modules:
  0.0 91.3 jit_solution(16356082777115519294)
XLA Ops:
  0.7 7.4 %shard_map.102 = (bf16[128,1152]{1,0:T(8,128)(2,1)}, bf16[128,1152]{1,0:T(8,128)(2,1)}, bf16[128,1152]{1,0:T(8,128)(2,1)}, bf16[128,1152]{1,0:T(8,128)(2,1)}, bf...) custom-call(bf16[128,64,256]{2,1,0:T(8,128)(2,1)} %patch_hbm.1, ...), custom_call_target="tpu_custom_call" | custom-call | flops 3000000000 | bytes 14000000 | tf_op jit(solution)/shard_map/pallas_call | solution.py:191
  9.5 5.0 %collective-permute-start.3 = (bf16[256,128]{1,0:T(8,128)(2,1)S(1)}, bf16[256,128]{1,0:T(8,128)(2,1)S(1)}, u32[]{:S(2)}, u32[]{:S(2)}) collective-permute-start(bf16[256,128]{1,0:T(8,128)(2,1)S(1)} %shard_map.103.pair_ref), channel_id=1, source_target_pairs={{0,6},{1,25},{2,4},{3,27},{4,2},{5,29},{6,0},{7,31},{8,14},{9,17},... | collective-permute-start | bytes 196616 | tf_op jit(solution)/shard_map/ppermute | solution.py:251
  15.1 1.7 %collective-permute-done.3.refs_2_ = bf16[256,128]{1,0:T(8,128)(2,1)S(1)} collective-permute-done((bf16[256,128]{1,0:T(8,128)(2,1)S(1)}, bf16[256,128]{1,0:T(8,128)(2,1)S(1)}, u32[]{:S(2)}, u32[]{:S(2)}) %collective-permute-start.3) | collective-permute-done | bytes 65568 | tf_op jit(solution)/shard_map/ppermute | solution.py:251
  16.9 2.8 %collective-permute-done.2.refs_1_ = bf16[256,128]{1,0:T(8,128)(2,1)S(1)} collective-permute-done((bf16[256,128]{1,0:T(8,128)(2,1)S(1)}, bf16[256,128]{1,0:T(8,128)(2,1)S(1)}, u32[]{:S(2)}, u32[]{:S(2)}) %collective-permute-start.2) | collective-permute-done | bytes 65568 | tf_op jit(solution)/shard_map/ppermute | solution.py:251
  19.8 1.6 %collective-permute-start.5 = (bf16[128,1152]{1,0:T(8,128)(2,1)}, bf16[128,1152]{1,0:T(8,128)(2,1)S(1)}, u32[]{:S(2)}, u32[]{:S(2)}) collective-permute-start(bf16[128,1152]{1,0:T(8,128)(2,1)} %get-tuple-element.56), channel_id=1, source_target_pairs={{0,8},{8,0},{16,24},{24,16},{1,9},{9,1},{17,25},{25,17},{2,10},{10... | collective-permute-start | bytes 884744 | tf_op jit(solution)/shard_map/ppermute | solution.py:663
  21.3 1.5 %collective-permute-start.6 = (bf16[128,1152]{1,0:T(8,128)(2,1)}, bf16[128,1152]{1,0:T(8,128)(2,1)S(1)}, u32[]{:S(2)}, u32[]{:S(2)}) collective-permute-start(bf16[128,1152]{1,0:T(8,128)(2,1)} %get-tuple-element.57), channel_id=1, source_target_pairs={{0,16},{8,24},{16,0},{24,8},{1,17},{9,25},{17,1},{25,9},{2,18},{10... | collective-permute-start | bytes 884744 | tf_op jit(solution)/shard_map/ppermute | solution.py:663
  23.3 1.3 %shard_map.105 = (f32[128,128]{1,0:T(8,128)S(1)}, f32[8,128]{1,0:T(8,128)S(1)}, f32[1,128]{1,0:T(1,128)}, bf16[512,128]{1,0:T(8,128)(2,1)S(1)}, bf16[1024,128]{1,0:T(8,128)(2,1)S(1)}) custom-call(s32[1,128]{1,0:T(1,128)S(1)} %bitcast.5, s32[1,128]{1,0:T(1,128)S(1)} %bitcast.6, bf16[128,128]{1,0:T(8,128)(2,1)S(1)} %get-tuple-element.50.own_ref.units_ref, ...), custom_call_target="tpu_custom_call" | custom-call | flops 400000000 | bytes 1000000 | tf_op jit(solution)/shard_map/pallas_call | solution.py:329
  25.9 1.6 %collective-permute-start.11 = (f32[16,128]{1,0:T(8,128)S(1)}, f32[16,128]{1,0:T(8,128)S(1)}, u32[]{:S(2)}, u32[]{:S(2)}) collective-permute-start(f32[16,128]{1,0:T(8,128)S(1)} %shard_map.106.pair_ref), channel_id=1, source_target_pairs={{0,6},{1,25},{2,4},{3,27},{4,2},{5,29},{6,0},{7,31},{8,14},{9,17},... | collective-permute-start | bytes 24584 | tf_op jit(solution)/shard_map/ppermute | solution.py:251
  27.9 3.4 %collective-permute-done.11.refs_2_ = f32[16,128]{1,0:T(8,128)S(1)} collective-permute-done((f32[16,128]{1,0:T(8,128)S(1)}, f32[16,128]{1,0:T(8,128)S(1)}, u32[]{:S(2)}, u32[]{:S(2)}) %collective-permute-start.11) | collective-permute-done | bytes 8224 | tf_op jit(solution)/shard_map/ppermute | solution.py:251
  32.0 3.0 %collective-permute-done.9.refs_0_ = f32[16,128]{1,0:T(8,128)S(1)} collective-permute-done((f32[16,128]{1,0:T(8,128)S(1)}, f32[16,128]{1,0:T(8,128)S(1)}, u32[]{:S(2)}, u32[]{:S(2)}) %collective-permute-start.9) | collective-permute-done | bytes 8224 | tf_op jit(solution)/shard_map/ppermute | solution.py:251
  35.0 4.0 %collective-permute-start.12 = (f32[48,128]{1,0:T(8,128)S(1)}, f32[48,128]{1,0:T(8,128)S(1)}, u32[]{:S(2)}, u32[]{:S(2)}) collective-permute-start(f32[48,128]{1,0:T(8,128)S(1)} %shard_map.107.got_ref), channel_id=1, source_target_pairs={{0,1},{1,0},{2,3},{3,2},{4,5},{5,4},{6,7},{7,6},{8,9},{9,8},{10,11... | collective-permute-start | bytes 73736 | tf_op jit(solution)/shard_map/ppermute | solution.py:663
  40.6 1.5 %collective-permute-start.15 = (bf16[128,128]{1,0:T(8,128)(2,1)S(1)}, bf16[128,128]{1,0:T(8,128)(2,1)S(1)}, u32[]{:S(2)}, u32[]{:S(2)}) collective-permute-start(bf16[128,128]{1,0:T(8,128)(2,1)S(1)} %shard_map.108.raw_ref.refs_4_), channel_id=1, source_target_pairs={{0,24},{8,16},{16,8},{24,0},{1,25},{9,17},{17,9},{25,1},{2,26},{10... | collective-permute-start | bytes 98312 | tf_op jit(solution)/shard_map/ppermute | solution.py:663
  42.1 1.5 %collective-permute-start.14 = (bf16[128,128]{1,0:T(8,128)(2,1)S(1)}, bf16[128,128]{1,0:T(8,128)(2,1)S(1)}, u32[]{:S(2)}, u32[]{:S(2)}) collective-permute-start(bf16[128,128]{1,0:T(8,128)(2,1)S(1)} %shard_map.108.raw_ref.refs_4_), channel_id=1, source_target_pairs={{0,16},{8,24},{16,0},{24,8},{1,17},{9,25},{17,1},{25,9},{2,18},{10... | collective-permute-start | bytes 98312 | tf_op jit(solution)/shard_map/ppermute | solution.py:663
  44.2 2.1 %shard_map.109.refs_9_ = f32[256,128]{1,0:T(8,128)S(1)} custom-call(bf16[128,128]{1,0:T(8,128)(2,1)S(1)} %shard_map.108.raw_ref.refs_4_, f32[128,128]{1,0:T(8,128)S(1)} %get-tuple-element.69.rscale_ref, bf16[2048,512]{1,0:T(8,128)(2,1)S(1)} %get-tuple-element.70.in_w, bf16[512,128]{1,0:T(8,128)(2,1)S(1)} %get-tuple-element.68.out_w.refs_8_, ...), custom_call_target="tpu_custom_call" | custom-call | flops 1000000000 | bytes 7000000 | tf_op jit(solution)/shard_map/pallas_call | solution.py:434
  47.5 1.5 %shard_map.110 = (f32[4,80,512]{2,1,0:T(8,128)S(1)}, bf16[4,80,512]{2,1,0:T(8,128)(2,1)S(1)}) custom-call(bf16[128,1152]{1,0:T(8,128)(2,1)S(1)} %copy-done.2, bf16[128,1152]{1,0:T(8,128)(2,1)S(1)} %collective-permute-done.5.refs_1_, bf16[128,1152]{1,0:T(8,128)(2,1)S(1)} %collective-permute-done.6.refs_2_, ...), custom_call_target="tpu_custom_call" | custom-call | flops 600000000 | bytes 4000000 | tf_op jit(solution)/shard_map/pallas_call | solution.py:510
  49.1 1.6 %collective-permute-done.16.got_ref = bf16[320,512]{1,0:T(8,128)(2,1)S(1)} collective-permute-done((bf16[320,512]{1,0:T(8,128)(2,1)S(1)}, bf16[320,512]{1,0:T(8,128)(2,1)S(1)}, u32[]{:S(2)}, u32[]{:S(2)}) %collective-permute-start.16) | collective-permute-done | bytes 327712 | tf_op jit(solution)/shard_map/ppermute | solution.py:663
  51.3 1.5 %collective-permute-start.17 = (bf16[160,256]{1,0:T(8,128)(2,1)S(1)}, bf16[160,256]{1,0:T(8,128)(2,1)S(1)}, u32[]{:S(2)}, u32[]{:S(2)}) collective-permute-start(bf16[160,256]{1,0:T(8,128)(2,1)S(1)} %get-tuple-element.78), channel_id=1, source_target_pairs={{0,2},{1,3},{2,0},{3,1},{4,6},{5,7},{6,4},{7,5},{8,10},{9,11},{10,... | collective-permute-start | bytes 245768 | tf_op jit(solution)/shard_map/ppermute | solution.py:663
  52.9 3.3 %collective-permute-done.22.got_ref = bf16[160,256]{1,0:T(8,128)(2,1)S(1)} collective-permute-done((bf16[160,256]{1,0:T(8,128)(2,1)S(1)}, bf16[160,256]{1,0:T(8,128)(2,1)S(1)}, u32[]{:S(2)}, u32[]{:S(2)}) %collective-permute-start.22) | collective-permute-done | bytes 81952 | tf_op jit(solution)/shard_map/ppermute | solution.py:663
  56.2 2.1 %collective-permute-start.23 = (bf16[80,256]{1,0:T(8,128)(2,1)S(1)}, bf16[80,256]{1,0:T(8,128)(2,1)S(1)}, u32[]{:S(2)}, u32[]{:S(2)}) collective-permute-start(bf16[80,256]{1,0:T(8,128)(2,1)S(1)} %get-tuple-element.84), channel_id=1, source_target_pairs={{0,4},{1,5},{2,6},{3,7},{4,0},{5,1},{6,2},{7,3},{8,12},{9,13},{10,... | collective-permute-start | bytes 122888 | tf_op jit(solution)/shard_map/ppermute | solution.py:663
  58.3 1.3 %collective-permute-start.18 = (bf16[80,256]{1,0:T(8,128)(2,1)S(1)}, bf16[80,256]{1,0:T(8,128)(2,1)S(1)}, u32[]{:S(2)}, u32[]{:S(2)}) collective-permute-start(bf16[80,256]{1,0:T(8,128)(2,1)S(1)} %get-tuple-element.80), channel_id=1, source_target_pairs={{0,4},{1,5},{2,6},{3,7},{4,0},{5,1},{6,2},{7,3},{8,12},{9,13},{10,... | collective-permute-start | bytes 122888 | tf_op jit(solution)/shard_map/ppermute | solution.py:663
  59.6 2.2 %collective-permute-done.23.got_ref = bf16[80,256]{1,0:T(8,128)(2,1)S(1)} collective-permute-done((bf16[80,256]{1,0:T(8,128)(2,1)S(1)}, bf16[80,256]{1,0:T(8,128)(2,1)S(1)}, u32[]{:S(2)}, u32[]{:S(2)}) %collective-permute-start.23) | collective-permute-done | bytes 40992 | tf_op jit(solution)/shard_map/ppermute | solution.py:663
  61.8 1.6 %collective-permute-start.24 = (bf16[80,256]{1,0:T(8,128)(2,1)S(1)}, bf16[80,256]{1,0:T(8,128)(2,1)S(1)}, u32[]{:S(2)}, u32[]{:S(2)}) collective-permute-start(bf16[80,256]{1,0:T(8,128)(2,1)S(1)} %shard_map.117.refs_0_), channel_id=1, source_target_pairs={{0,4},{1,5},{2,6},{3,7},{4,0},{5,1},{6,2},{7,3},{8,12},{9,13},{10,... | collective-permute-start | bytes 122888 | tf_op jit(solution)/shard_map/ppermute | solution.py:663
  65.0 1.8 %collective-permute-done.24.refs_1_ = bf16[80,256]{1,0:T(8,128)(2,1)S(1)} collective-permute-done((bf16[80,256]{1,0:T(8,128)(2,1)S(1)}, bf16[80,256]{1,0:T(8,128)(2,1)S(1)}, u32[]{:S(2)}, u32[]{:S(2)}) %collective-permute-start.24) | collective-permute-done | bytes 40992 | tf_op jit(solution)/shard_map/ppermute | solution.py:663
  66.8 2.0 %collective-permute-done.19.refs_1_ = bf16[80,256]{1,0:T(8,128)(2,1)S(1)} collective-permute-done((bf16[80,256]{1,0:T(8,128)(2,1)S(1)}, bf16[80,256]{1,0:T(8,128)(2,1)S(1)}, u32[]{:S(2)}, u32[]{:S(2)}) %collective-permute-start.19) | collective-permute-done | bytes 40992 | tf_op jit(solution)/shard_map/ppermute | solution.py:663
  68.9 2.3 %collective-permute-done.25.refs_1_ = bf16[160,256]{1,0:T(8,128)(2,1)S(1)} collective-permute-done((bf16[160,256]{1,0:T(8,128)(2,1)S(1)}, bf16[160,256]{1,0:T(8,128)(2,1)S(1)}, u32[]{:S(2)}, u32[]{:S(2)}) %collective-permute-start.25) | collective-permute-done | bytes 81952 | tf_op jit(solution)/shard_map/ppermute | solution.py:663
  74.0 1.5 %collective-permute-start.29 = (bf16[320,256]{1,0:T(8,128)(2,1)S(1)}, bf16[320,256]{1,0:T(8,128)(2,1)S(1)}, u32[]{:S(2)}, u32[]{:S(2)}) collective-permute-start(bf16[320,256]{1,0:T(8,128)(2,1)S(1)} %shard_map.115.refs_0_), channel_id=1, source_target_pairs={{0,16},{8,24},{16,0},{24,8},{1,17},{9,25},{17,1},{25,9},{2,18},{10... | collective-permute-start | bytes 491528 | tf_op jit(solution)/shard_map/ppermute | solution.py:663
  78.9 1.6 %collective-permute-start.35 = (bf16[320,256]{1,0:T(8,128)(2,1)S(1)}, bf16[320,256]{1,0:T(8,128)(2,1)S(1)}, u32[]{:S(2)}, u32[]{:S(2)}) collective-permute-start(bf16[320,256]{1,0:T(8,128)(2,1)S(1)} %collective-permute-done.27.refs_0_.refs_4_), channel_id=1, source_target_pairs={{0,16},{8,24},{16,0},{24,8},{1,17},{9,25},{17,1},{25,9},{2,18},{10... | collective-permute-start | bytes 491528 | tf_op jit(solution)/shard_map/ppermute | solution.py:663
  81.1 2.1 %collective-permute-done.37.refs_14_ = bf16[320,256]{1,0:T(8,128)(2,1)S(1)} collective-permute-done((bf16[320,256]{1,0:T(8,128)(2,1)S(1)}, bf16[320,256]{1,0:T(8,128)(2,1)S(1)}, u32[]{:S(2)}, u32[]{:S(2)}) %collective-permute-start.37) | collective-permute-done | bytes 163872 | tf_op jit(solution)/shard_map/ppermute | solution.py:663
  84.8 1.3 %shard_map.120 = (f32[2048,512]{1,0:T(8,128)}, f32[512,128]{1,0:T(8,128)}) custom-call(bf16[320,256]{1,0:T(8,128)(2,1)S(1)} %shard_map.115.refs_0_, bf16[320,256]{1,0:T(8,128)(2,1)S(1)} %collective-permute-done.21.refs_1_, bf16[320,256]{1,0:T(8,128)(2,1)S(1)} %shard_map.119.refs_2_, bf16[320,256]{1,0:T(8,128)(2,1)S(1)} %collective-permute-done.26.refs_3_), custom_call_target="tpu_custom_call" | custom-call | flops 1000000 | bytes 8000000 | tf_op jit(solution)/shard_map/pallas_call | solution.py:626
  86.1 1.3 %shard_map.121 = (f32[2048,512]{1,0:T(8,128)}, f32[512,128]{1,0:T(8,128)}) custom-call(bf16[320,256]{1,0:T(8,128)(2,1)S(1)} %collective-permute-done.27.refs_0_.refs_4_, bf16[320,256]{1,0:T(8,128)(2,1)S(1)} %collective-permute-done.28.refs_1_.refs_5_, ...), custom_call_target="tpu_custom_call", output_to_operand_aliasing={{0}: (4, {}), {1}: (5, {})} | custom-call | flops 1000000 | bytes 8000000 | tf_op jit(solution)/shard_map/pallas_call | solution.py:626
  87.4 1.3 %shard_map.122 = (f32[2048,512]{1,0:T(8,128)}, f32[512,128]{1,0:T(8,128)}) custom-call(bf16[320,256]{1,0:T(8,128)(2,1)S(1)} %collective-permute-done.31.refs_0_.refs_8_, bf16[320,256]{1,0:T(8,128)(2,1)S(1)} %collective-permute-done.32.refs_1_.refs_9_, ...), custom_call_target="tpu_custom_call", output_to_operand_aliasing={{0}: (4, {}), {1}: (5, {})} | custom-call | flops 1000000 | bytes 8000000 | tf_op jit(solution)/shard_map/pallas_call | solution.py:626
  89.7 1.6 %shard_map.124 = (f32[2048,512]{1,0:T(8,128)}, f32[512,128]{1,0:T(8,128)}, f32[256,128]{1,0:T(8,128)}) custom-call(bf16[320,256]{1,0:T(8,128)(2,1)S(1)} %shard_map.115.refs_0_, bf16[320,256]{1,0:T(8,128)(2,1)S(1)} %collective-permute-done.21.refs_1_, bf16[320,256]{1,0:T(8,128)(2,1)S(1)} %shard_map.119.refs_2_, ...), custom_call_target="tpu_custom_call", output_to_operand_aliasing={{0}: (16, {}), {1}: (17, {})} | custom-call | flops 1000000 | bytes 8000000 | tf_op jit(solution)/shard_map/pallas_call | solution.py:626
  (75 shorter events, 20.2 us)
Async XLA Ops:
  9.5 7.3 %collective-permute-start.3 = (bf16[256,128]{1,0:T(8,128)(2,1)S(1)}, bf16[256,128]{1,0:T(8,128)(2,1)S(1)}, u32[]{:S(2)}, u32[]{:S(2)}) collective-permute-start(bf16[256,128]{1,0:T(8,128)(2,1)S(1)} %shard_map.103.pair_ref), channel_id=1, source_target_pairs={{0,6},{1,25},{2,4},{3,27},{4,2},{5,29},{6,0},{7,31},{8,14},{9,17},... | collective-permute-start | bytes 196616 | tf_op jit(solution)/shard_map/ppermute | solution.py:251
  14.5 5.2 %collective-permute-start.2 = (bf16[256,128]{1,0:T(8,128)(2,1)S(1)}, bf16[256,128]{1,0:T(8,128)(2,1)S(1)}, u32[]{:S(2)}, u32[]{:S(2)}) collective-permute-start(bf16[256,128]{1,0:T(8,128)(2,1)S(1)} %shard_map.103.pair_ref), channel_id=1, source_target_pairs={{0,4},{1,17},{2,6},{3,19},{4,0},{5,21},{6,2},{7,23},{8,12},{9,25},... | collective-permute-start | bytes 196616 | tf_op jit(solution)/shard_map/ppermute | solution.py:251
  14.5 5.2 %collective-permute-start.1 = (bf16[256,128]{1,0:T(8,128)(2,1)S(1)}, bf16[256,128]{1,0:T(8,128)(2,1)S(1)}, u32[]{:S(2)}, u32[]{:S(2)}) collective-permute-start(bf16[256,128]{1,0:T(8,128)(2,1)S(1)} %shard_map.103.pair_ref), channel_id=1, source_target_pairs={{0,2},{1,9},{2,0},{3,11},{4,6},{5,13},{6,4},{7,15},{8,10},{9,1},{1... | collective-permute-start | bytes 196616 | tf_op jit(solution)/shard_map/ppermute | solution.py:251
  19.8 23.8 %collective-permute-start.5 = (bf16[128,1152]{1,0:T(8,128)(2,1)}, bf16[128,1152]{1,0:T(8,128)(2,1)S(1)}, u32[]{:S(2)}, u32[]{:S(2)}) collective-permute-start(bf16[128,1152]{1,0:T(8,128)(2,1)} %get-tuple-element.56), channel_id=1, source_target_pairs={{0,8},{8,0},{16,24},{24,16},{1,9},{9,1},{17,25},{25,17},{2,10},{10... | collective-permute-start | bytes 884744 | tf_op jit(solution)/shard_map/ppermute | solution.py:663
  21.3 24.9 %collective-permute-start.6 = (bf16[128,1152]{1,0:T(8,128)(2,1)}, bf16[128,1152]{1,0:T(8,128)(2,1)S(1)}, u32[]{:S(2)}, u32[]{:S(2)}) collective-permute-start(bf16[128,1152]{1,0:T(8,128)(2,1)} %get-tuple-element.57), channel_id=1, source_target_pairs={{0,16},{8,24},{16,0},{24,8},{1,17},{9,25},{17,1},{25,9},{2,18},{10... | collective-permute-start | bytes 884744 | tf_op jit(solution)/shard_map/ppermute | solution.py:663
  22.8 23.4 %collective-permute-start.7 = (bf16[128,1152]{1,0:T(8,128)(2,1)}, bf16[128,1152]{1,0:T(8,128)(2,1)S(1)}, u32[]{:S(2)}, u32[]{:S(2)}) collective-permute-start(bf16[128,1152]{1,0:T(8,128)(2,1)} %get-tuple-element.58), channel_id=1, source_target_pairs={{0,24},{8,16},{16,8},{24,0},{1,25},{9,17},{17,9},{25,1},{2,26},{10... | collective-permute-start | bytes 884744 | tf_op jit(solution)/shard_map/ppermute | solution.py:663
  25.9 5.4 %collective-permute-start.11 = (f32[16,128]{1,0:T(8,128)S(1)}, f32[16,128]{1,0:T(8,128)S(1)}, u32[]{:S(2)}, u32[]{:S(2)}) collective-permute-start(f32[16,128]{1,0:T(8,128)S(1)} %shard_map.106.pair_ref), channel_id=1, source_target_pairs={{0,6},{1,25},{2,4},{3,27},{4,2},{5,29},{6,0},{7,31},{8,14},{9,17},... | collective-permute-start | bytes 24584 | tf_op jit(solution)/shard_map/ppermute | solution.py:251
  27.4 4.5 %collective-permute-start.10 = (f32[16,128]{1,0:T(8,128)S(1)}, f32[16,128]{1,0:T(8,128)S(1)}, u32[]{:S(2)}, u32[]{:S(2)}) collective-permute-start(f32[16,128]{1,0:T(8,128)S(1)} %shard_map.106.pair_ref), channel_id=1, source_target_pairs={{0,4},{1,17},{2,6},{3,19},{4,0},{5,21},{6,2},{7,23},{8,12},{9,25},... | collective-permute-start | bytes 24584 | tf_op jit(solution)/shard_map/ppermute | solution.py:251
  35.0 4.9 %collective-permute-start.12 = (f32[48,128]{1,0:T(8,128)S(1)}, f32[48,128]{1,0:T(8,128)S(1)}, u32[]{:S(2)}, u32[]{:S(2)}) collective-permute-start(f32[48,128]{1,0:T(8,128)S(1)} %shard_map.107.got_ref), channel_id=1, source_target_pairs={{0,1},{1,0},{2,3},{3,2},{4,5},{5,4},{6,7},{7,6},{8,9},{9,8},{10,11... | collective-permute-start | bytes 73736 | tf_op jit(solution)/shard_map/ppermute | solution.py:663
  40.6 5.7 %collective-permute-start.15 = (bf16[128,128]{1,0:T(8,128)(2,1)S(1)}, bf16[128,128]{1,0:T(8,128)(2,1)S(1)}, u32[]{:S(2)}, u32[]{:S(2)}) collective-permute-start(bf16[128,128]{1,0:T(8,128)(2,1)S(1)} %shard_map.108.raw_ref.refs_4_), channel_id=1, source_target_pairs={{0,24},{8,16},{16,8},{24,0},{1,25},{9,17},{17,9},{25,1},{2,26},{10... | collective-permute-start | bytes 98312 | tf_op jit(solution)/shard_map/ppermute | solution.py:663
  42.1 4.2 %collective-permute-start.14 = (bf16[128,128]{1,0:T(8,128)(2,1)S(1)}, bf16[128,128]{1,0:T(8,128)(2,1)S(1)}, u32[]{:S(2)}, u32[]{:S(2)}) collective-permute-start(bf16[128,128]{1,0:T(8,128)(2,1)S(1)} %shard_map.108.raw_ref.refs_4_), channel_id=1, source_target_pairs={{0,16},{8,24},{16,0},{24,8},{1,17},{9,25},{17,1},{25,9},{2,18},{10... | collective-permute-start | bytes 98312 | tf_op jit(solution)/shard_map/ppermute | solution.py:663
  50.8 5.4 %collective-permute-start.22 = (bf16[160,256]{1,0:T(8,128)(2,1)S(1)}, bf16[160,256]{1,0:T(8,128)(2,1)S(1)}, u32[]{:S(2)}, u32[]{:S(2)}) collective-permute-start(bf16[160,256]{1,0:T(8,128)(2,1)S(1)} %get-tuple-element.82), channel_id=1, source_target_pairs={{0,2},{1,3},{2,0},{3,1},{4,6},{5,7},{6,4},{7,5},{8,10},{9,11},{10,... | collective-permute-start | bytes 245768 | tf_op jit(solution)/shard_map/ppermute | solution.py:663
  51.3 6.9 %collective-permute-start.17 = (bf16[160,256]{1,0:T(8,128)(2,1)S(1)}, bf16[160,256]{1,0:T(8,128)(2,1)S(1)}, u32[]{:S(2)}, u32[]{:S(2)}) collective-permute-start(bf16[160,256]{1,0:T(8,128)(2,1)S(1)} %get-tuple-element.78), channel_id=1, source_target_pairs={{0,2},{1,3},{2,0},{3,1},{4,6},{5,7},{6,4},{7,5},{8,10},{9,11},{10,... | collective-permute-start | bytes 245768 | tf_op jit(solution)/shard_map/ppermute | solution.py:663
  56.2 5.6 %collective-permute-start.23 = (bf16[80,256]{1,0:T(8,128)(2,1)S(1)}, bf16[80,256]{1,0:T(8,128)(2,1)S(1)}, u32[]{:S(2)}, u32[]{:S(2)}) collective-permute-start(bf16[80,256]{1,0:T(8,128)(2,1)S(1)} %get-tuple-element.84), channel_id=1, source_target_pairs={{0,4},{1,5},{2,6},{3,7},{4,0},{5,1},{6,2},{7,3},{8,12},{9,13},{10,... | collective-permute-start | bytes 122888 | tf_op jit(solution)/shard_map/ppermute | solution.py:663
  58.3 5.5 %collective-permute-start.18 = (bf16[80,256]{1,0:T(8,128)(2,1)S(1)}, bf16[80,256]{1,0:T(8,128)(2,1)S(1)}, u32[]{:S(2)}, u32[]{:S(2)}) collective-permute-start(bf16[80,256]{1,0:T(8,128)(2,1)S(1)} %get-tuple-element.80), channel_id=1, source_target_pairs={{0,4},{1,5},{2,6},{3,7},{4,0},{5,1},{6,2},{7,3},{8,12},{9,13},{10,... | collective-permute-start | bytes 122888 | tf_op jit(solution)/shard_map/ppermute | solution.py:663
  61.8 5.0 %collective-permute-start.24 = (bf16[80,256]{1,0:T(8,128)(2,1)S(1)}, bf16[80,256]{1,0:T(8,128)(2,1)S(1)}, u32[]{:S(2)}, u32[]{:S(2)}) collective-permute-start(bf16[80,256]{1,0:T(8,128)(2,1)S(1)} %shard_map.117.refs_0_), channel_id=1, source_target_pairs={{0,4},{1,5},{2,6},{3,7},{4,0},{5,1},{6,2},{7,3},{8,12},{9,13},{10,... | collective-permute-start | bytes 122888 | tf_op jit(solution)/shard_map/ppermute | solution.py:663
  63.8 5.1 %collective-permute-start.19 = (bf16[80,256]{1,0:T(8,128)(2,1)S(1)}, bf16[80,256]{1,0:T(8,128)(2,1)S(1)}, u32[]{:S(2)}, u32[]{:S(2)}) collective-permute-start(bf16[80,256]{1,0:T(8,128)(2,1)S(1)} %shard_map.113.refs_0_), channel_id=1, source_target_pairs={{0,4},{1,5},{2,6},{3,7},{4,0},{5,1},{6,2},{7,3},{8,12},{9,13},{10,... | collective-permute-start | bytes 122888 | tf_op jit(solution)/shard_map/ppermute | solution.py:663
  66.8 4.4 %collective-permute-start.25 = (bf16[160,256]{1,0:T(8,128)(2,1)S(1)}, bf16[160,256]{1,0:T(8,128)(2,1)S(1)}, u32[]{:S(2)}, u32[]{:S(2)}) collective-permute-start(bf16[160,256]{1,0:T(8,128)(2,1)S(1)} %shard_map.118.refs_0_), channel_id=1, source_target_pairs={{0,2},{1,3},{2,0},{3,1},{4,6},{5,7},{6,4},{7,5},{8,10},{9,11},{10,... | collective-permute-start | bytes 245768 | tf_op jit(solution)/shard_map/ppermute | solution.py:663
  68.8 4.4 %collective-permute-start.20 = (bf16[160,256]{1,0:T(8,128)(2,1)S(1)}, bf16[160,256]{1,0:T(8,128)(2,1)S(1)}, u32[]{:S(2)}, u32[]{:S(2)}) collective-permute-start(bf16[160,256]{1,0:T(8,128)(2,1)S(1)} %shard_map.114.refs_0_), channel_id=1, source_target_pairs={{0,2},{1,3},{2,0},{3,1},{4,6},{5,7},{6,4},{7,5},{8,10},{9,11},{10,... | collective-permute-start | bytes 245768 | tf_op jit(solution)/shard_map/ppermute | solution.py:663
  71.3 5.4 %collective-permute-start.33 = (bf16[320,256]{1,0:T(8,128)(2,1)S(1)}, bf16[320,256]{1,0:T(8,128)(2,1)S(1)}, u32[]{:S(2)}, u32[]{:S(2)}) collective-permute-start(bf16[320,256]{1,0:T(8,128)(2,1)S(1)} %shard_map.119.refs_2_), channel_id=1, source_target_pairs={{0,16},{8,24},{16,0},{24,8},{1,17},{9,25},{17,1},{25,9},{2,18},{10... | collective-permute-start | bytes 491528 | tf_op jit(solution)/shard_map/ppermute | solution.py:663
  71.9 5.3 %collective-permute-start.31 = (bf16[320,256]{1,0:T(8,128)(2,1)S(1)}, bf16[320,256]{1,0:T(8,128)(2,1)S(1)}, u32[]{:S(2)}, u32[]{:S(2)}) collective-permute-start(bf16[320,256]{1,0:T(8,128)(2,1)S(1)} %shard_map.119.refs_2_), channel_id=1, source_target_pairs={{0,8},{8,0},{16,24},{24,16},{1,9},{9,1},{17,25},{25,17},{2,10},{10... | collective-permute-start | bytes 491528 | tf_op jit(solution)/shard_map/ppermute | solution.py:663
  73.3 5.6 %collective-permute-start.27 = (bf16[320,256]{1,0:T(8,128)(2,1)S(1)}, bf16[320,256]{1,0:T(8,128)(2,1)S(1)}, u32[]{:S(2)}, u32[]{:S(2)}) collective-permute-start(bf16[320,256]{1,0:T(8,128)(2,1)S(1)} %shard_map.115.refs_0_), channel_id=1, source_target_pairs={{0,8},{8,0},{16,24},{24,16},{1,9},{9,1},{17,25},{25,17},{2,10},{10... | collective-permute-start | bytes 491528 | tf_op jit(solution)/shard_map/ppermute | solution.py:663
  74.0 6.6 %collective-permute-start.29 = (bf16[320,256]{1,0:T(8,128)(2,1)S(1)}, bf16[320,256]{1,0:T(8,128)(2,1)S(1)}, u32[]{:S(2)}, u32[]{:S(2)}) collective-permute-start(bf16[320,256]{1,0:T(8,128)(2,1)S(1)} %shard_map.115.refs_0_), channel_id=1, source_target_pairs={{0,16},{8,24},{16,0},{24,8},{1,17},{9,25},{17,1},{25,9},{2,18},{10... | collective-permute-start | bytes 491528 | tf_op jit(solution)/shard_map/ppermute | solution.py:663
  75.5 5.1 %collective-permute-start.26 = (bf16[320,256]{1,0:T(8,128)(2,1)S(1)}, bf16[320,256]{1,0:T(8,128)(2,1)S(1)}, u32[]{:S(2)}, u32[]{:S(2)}) collective-permute-start(bf16[320,256]{1,0:T(8,128)(2,1)S(1)} %shard_map.119.refs_2_), channel_id=1, source_target_pairs={{0,1},{1,0},{2,3},{3,2},{4,5},{5,4},{6,7},{7,6},{8,9},{9,8},{10,11... | collective-permute-start | bytes 491528 | tf_op jit(solution)/shard_map/ppermute | solution.py:663
  76.6 4.4 %collective-permute-start.21 = (bf16[320,256]{1,0:T(8,128)(2,1)S(1)}, bf16[320,256]{1,0:T(8,128)(2,1)S(1)}, u32[]{:S(2)}, u32[]{:S(2)}) collective-permute-start(bf16[320,256]{1,0:T(8,128)(2,1)S(1)} %shard_map.115.refs_0_), channel_id=1, source_target_pairs={{0,1},{1,0},{2,3},{3,2},{4,5},{5,4},{6,7},{7,6},{8,9},{9,8},{10,11... | collective-permute-start | bytes 491528 | tf_op jit(solution)/shard_map/ppermute | solution.py:663
  77.2 6.1 %collective-permute-start.37 = (bf16[320,256]{1,0:T(8,128)(2,1)S(1)}, bf16[320,256]{1,0:T(8,128)(2,1)S(1)}, u32[]{:S(2)}, u32[]{:S(2)}) collective-permute-start(bf16[320,256]{1,0:T(8,128)(2,1)S(1)} %collective-permute-done.33.refs_2_.refs_10_), channel_id=1, source_target_pairs={{0,8},{8,0},{16,24},{24,16},{1,9},{9,1},{17,25},{25,17},{2,10},{10... | collective-permute-start | bytes 491528 | tf_op jit(solution)/shard_map/ppermute | solution.py:663
  78.9 5.3 %collective-permute-start.35 = (bf16[320,256]{1,0:T(8,128)(2,1)S(1)}, bf16[320,256]{1,0:T(8,128)(2,1)S(1)}, u32[]{:S(2)}, u32[]{:S(2)}) collective-permute-start(bf16[320,256]{1,0:T(8,128)(2,1)S(1)} %collective-permute-done.27.refs_0_.refs_4_), channel_id=1, source_target_pairs={{0,16},{8,24},{16,0},{24,8},{1,17},{9,25},{17,1},{25,9},{2,18},{10... | collective-permute-start | bytes 491528 | tf_op jit(solution)/shard_map/ppermute | solution.py:663
  80.6 5.5 %collective-permute-start.28 = (bf16[320,256]{1,0:T(8,128)(2,1)S(1)}, bf16[320,256]{1,0:T(8,128)(2,1)S(1)}, u32[]{:S(2)}, u32[]{:S(2)}) collective-permute-start(bf16[320,256]{1,0:T(8,128)(2,1)S(1)} %collective-permute-done.27.refs_0_.refs_4_), channel_id=1, source_target_pairs={{0,1},{1,0},{2,3},{3,2},{4,5},{5,4},{6,7},{7,6},{8,9},{9,8},{10,11... | collective-permute-start | bytes 491528 | tf_op jit(solution)/shard_map/ppermute | solution.py:663
  81.1 6.3 %collective-permute-start.34 = (bf16[320,256]{1,0:T(8,128)(2,1)S(1)}, bf16[320,256]{1,0:T(8,128)(2,1)S(1)}, u32[]{:S(2)}, u32[]{:S(2)}) collective-permute-start(bf16[320,256]{1,0:T(8,128)(2,1)S(1)} %collective-permute-done.33.refs_2_.refs_10_), channel_id=1, source_target_pairs={{0,1},{1,0},{2,3},{3,2},{4,5},{5,4},{6,7},{7,6},{8,9},{9,8},{10,11... | collective-permute-start | bytes 491528 | tf_op jit(solution)/shard_map/ppermute | solution.py:663
  83.3 4.1 %collective-permute-start.32 = (bf16[320,256]{1,0:T(8,128)(2,1)S(1)}, bf16[320,256]{1,0:T(8,128)(2,1)S(1)}, u32[]{:S(2)}, u32[]{:S(2)}) collective-permute-start(bf16[320,256]{1,0:T(8,128)(2,1)S(1)} %collective-permute-done.31.refs_0_.refs_8_), channel_id=1, source_target_pairs={{0,1},{1,0},{2,3},{3,2},{4,5},{5,4},{6,7},{7,6},{8,9},{9,8},{10,11... | collective-permute-start | bytes 491528 | tf_op jit(solution)/shard_map/ppermute | solution.py:663
  84.3 4.4 %collective-permute-start.36 = (bf16[320,256]{1,0:T(8,128)(2,1)S(1)}, bf16[320,256]{1,0:T(8,128)(2,1)S(1)}, u32[]{:S(2)}, u32[]{:S(2)}) collective-permute-start(bf16[320,256]{1,0:T(8,128)(2,1)S(1)} %collective-permute-done.35.refs_0_.refs_12_), channel_id=1, source_target_pairs={{0,1},{1,0},{2,3},{3,2},{4,5},{5,4},{6,7},{7,6},{8,9},{9,8},{10,11... | collective-permute-start | bytes 491528 | tf_op jit(solution)/shard_map/ppermute | solution.py:663
  84.3 5.4 %collective-permute-start.38 = (bf16[320,256]{1,0:T(8,128)(2,1)S(1)}, bf16[320,256]{1,0:T(8,128)(2,1)S(1)}, u32[]{:S(2)}, u32[]{:S(2)}) collective-permute-start(bf16[320,256]{1,0:T(8,128)(2,1)S(1)} %collective-permute-done.37.refs_14_), channel_id=1, source_target_pairs={{0,1},{1,0},{2,3},{3,2},{4,5},{5,4},{6,7},{7,6},{8,9},{9,8},{10,11... | collective-permute-start | bytes 491528 | tf_op jit(solution)/shard_map/ppermute | solution.py:663
  (10 other events, 72.3 us)

commit v7 on v5

--- a/solution.py
+++ b/solution.py
@@ -569,10 +569,10 @@
     slots = lay.peers // 2
     part_cols = lay.width // HALVES
     part_refs, refs = dict(zip(parts, refs)), refs[len(parts) :]
-    if done:
-        refs = refs[2:]
-    g_in_hbm, g_out_hbm, *refs = refs
-    if closing:
+    if done > 2:
+        mix_ref = refs[2]
+    g_in_hbm, g_out_hbm, *refs = refs[done:]
+    if closing is not None:
         g_mix_ref, *refs = refs
     stage, strip_stage, sems, strip_sems = refs
     me_blk, me_dp = lax.axis_index("blk"), lax.axis_index("dp")
@@ -601,20 +601,25 @@
                     g_out_hbm.at[pl.ds(owner * lay.out_rows, lay.out_rows), :],
                     strip_sems,
                 )
-    if closing:
+    if closing is not None:
         for core in range(2):
             for z in range(slots):
                 strip = z * lay.rows + lay.top
                 owner = me_dp ^ (2 * z + core)
                 for start, rows, cols in lay.mix_parts():
                     half, first = divmod(cols.start, part_cols)
+                    at = pl.ds(owner * lay.mix_rows + start, rows)
+                    if half < closing:
+                        g_mix_ref[at, :] = mix_ref[at, :]
+                    if half != closing:
+                        continue
                     terms = [
                         part_refs[hop, core, half][strip : strip + rows, first : first + 128].astype(F32)
                         for hop in range(lay.size)
                     ]
                     while len(terms) > 1:
                         terms = [terms[t] + terms[t + 1] for t in range(0, len(terms), 2)]
-                    g_mix_ref[pl.ds(owner * lay.mix_rows + start, rows), :] = terms[0]
+                    g_mix_ref[at, :] = terms[0]
     for copy in copies:
         copy.wait()
 
@@ -623,12 +628,12 @@
     slots = len(fresh) * lay.peers // 2
     outs = [shape((feats, width), F32), shape((width, 128), F32)]
     specs = [ANY, ANY]
-    if closing:
+    if closing is not None:
         outs.append(shape((lanes, 128), F32))
         specs.append(VMEM)
     return pl.pallas_call(
-        functools.partial(finish_kernel, lay, tuple(parts), bool(done), tuple(fresh), closing),
-        in_specs=[VMEM] * len(parts) + [ANY] * len(done),
+        functools.partial(finish_kernel, lay, tuple(parts), len(done), tuple(fresh), closing),
+        in_specs=[VMEM] * len(parts) + [ANY, ANY, VMEM][: len(done)],
         out_shape=outs,
         out_specs=specs,
         scratch_shapes=[
@@ -637,7 +642,7 @@
             pltpu.SemaphoreType.DMA((slots,)),
             pltpu.SemaphoreType.DMA((slots,)),
         ],
-        input_output_aliases={len(parts) + i: i for i in range(len(done))},
+        input_output_aliases={len(parts) + i: i for i in range(min(2, len(done)))},
         compiler_params=params(24),
         cost_estimate=cost(1e6, 8e6),
     )(*parts.values(), *done)
@@ -727,9 +732,12 @@
             fresh[hop, 0, half] = planes[hop, half]
             fresh[hop, 1, half] = swap(planes[hop, half], "dp", 1)
         parts.update(fresh)
-        last = order == len(stages) - 1
+        closing = order - len(stages) + HALVES
+        taken = fresh
+        if closing >= 0:
+            taken = {part: block for part, block in parts.items() if part[2] == closing}
         done = finish(
-            lay, parts if last else fresh, done, fresh, last, lanes, feats, width
+            lay, taken, done, fresh, closing if closing >= 0 else None, lanes, feats, width
         )
     g_in, g_out, g_mix = done
     return (loss.reshape(count), g_mix, g_in, g_out)

time: 89.2 us -> 94.1 us (1.055)
  waiting for transfers between devices: 24.6 us -> 28.1 us
  starting transfers between devices: 43.9 us -> 45.3 us
    ppermute x37, starting transfers between devices: 36.2 us -> 38.7 us  [swap(): return lax.ppermute(block, axis, [(src, src ^ bit) for src in range(size)])]
    ppermute x37, waiting for transfers between devices: 13.1 us -> 14.8 us  [swap(): return lax.ppermute(block, axis, [(src, src ^ bit) for src in range(size)])]
    ppermute x6, waiting for transfers between devices: 11.5 us -> 13.2 us  [cross(): got.append(lax.ppermute(pair, ('blk', 'dp'), routes))]
    ppermute x6, starting transfers between devices: 7.73 us -> 6.58 us  [cross(): got.append(lax.ppermute(pair, ('blk', 'dp'), routes))]
  transfers between devices with their start and end apart: 43 -> 43, of which waited for: 17 -> 14; matrix products, arithmetic and copies ran while one was open for 0% -> 0% of each run, Pallas kernels for 10% -> 10%
where the time goes in v7:
time: 94.1 us; the launch traced here: 93.9 us
  starting transfers between devices  45.3 us (48%)
  waiting for transfers between devices  28.1 us (30%)
  Pallas kernels  19.6 us (21%)
    ppermute x37, starting transfers between devices, swap(): return lax.ppermute(block, axis, [(src, src ^ bit) for src in range(size)])  38.7 us
    ppermute x37, waiting for transfers between devices, swap(): return lax.ppermute(block, axis, [(src, src ^ bit) for src in range(size)])  14.8 us
    ppermute x6, waiting for transfers between devices, cross(): got.append(lax.ppermute(pair, ('blk', 'dp'), routes))  13.2 us
    pallas_call x1, Pallas kernels, encode(): pl.pallas_call(functools.partial(encode_kernel, freqs, size, rounds), in_...  7.38 us
    ppermute x6, starting transfers between devices, cross(): got.append(lax.ppermute(pair, ('blk', 'dp'), routes))  6.58 us
    pallas_call x5, Pallas kernels, finish(): pl.pallas_call(functools.partial(finish_kernel, lay, tuple(parts), len(do...  6.4 us
    pallas_call x1, Pallas kernels, lower(): pl.pallas_call(functools.partial(lower_kernel, freqs), in_specs=[VMEM] *...  2.06 us
  transfers between devices with their start and end apart: 43, of which 14 were waited for; matrix products, arithmetic and copies ran while one was open for 0% of the time, Pallas kernels for 10%

profile of v7, /device:TPU:0, one launch (start us, length us, event | category | flops | bytes accessed | tf_op | source)
XLA Modules:
  0.0 93.9 jit_solution(14330320757984187483)
XLA Ops:
  0.7 7.4 %shard_map.102 = (bf16[128,1152]{1,0:T(8,128)(2,1)}, bf16[128,1152]{1,0:T(8,128)(2,1)}, bf16[128,1152]{1,0:T(8,128)(2,1)}, bf16[128,1152]{1,0:T(8,128)(2,1)}, bf...) custom-call(bf16[128,64,256]{2,1,0:T(8,128)(2,1)} %patch_hbm.1, ...), custom_call_target="tpu_custom_call" | custom-call | flops 3000000000 | bytes 14000000 | tf_op jit(solution)/shard_map/pallas_call | solution.py:191
  9.5 3.0 %collective-permute-start.1 = (bf16[256,128]{1,0:T(8,128)(2,1)S(1)}, bf16[256,128]{1,0:T(8,128)(2,1)S(1)}, u32[]{:S(2)}, u32[]{:S(2)}) collective-permute-start(bf16[256,128]{1,0:T(8,128)(2,1)S(1)} %shard_map.103.pair_ref), channel_id=1, source_target_pairs={{0,2},{1,9},{2,0},{3,11},{4,6},{5,13},{6,4},{7,15},{8,10},{9,1},{1... | collective-permute-start | bytes 196616 | tf_op jit(solution)/shard_map/ppermute | solution.py:251
  12.5 2.6 %collective-permute-start.2 = (bf16[256,128]{1,0:T(8,128)(2,1)S(1)}, bf16[256,128]{1,0:T(8,128)(2,1)S(1)}, u32[]{:S(2)}, u32[]{:S(2)}) collective-permute-start(bf16[256,128]{1,0:T(8,128)(2,1)S(1)} %shard_map.103.pair_ref), channel_id=1, source_target_pairs={{0,4},{1,17},{2,6},{3,19},{4,0},{5,21},{6,2},{7,23},{8,12},{9,25},... | collective-permute-start | bytes 196616 | tf_op jit(solution)/shard_map/ppermute | solution.py:251
  15.0 3.3 %collective-permute-done.2.refs_1_ = bf16[256,128]{1,0:T(8,128)(2,1)S(1)} collective-permute-done((bf16[256,128]{1,0:T(8,128)(2,1)S(1)}, bf16[256,128]{1,0:T(8,128)(2,1)S(1)}, u32[]{:S(2)}, u32[]{:S(2)}) %collective-permute-start.2) | collective-permute-done | bytes 65568 | tf_op jit(solution)/shard_map/ppermute | solution.py:251
  18.3 2.8 %collective-permute-done.3.refs_2_ = bf16[256,128]{1,0:T(8,128)(2,1)S(1)} collective-permute-done((bf16[256,128]{1,0:T(8,128)(2,1)S(1)}, bf16[256,128]{1,0:T(8,128)(2,1)S(1)}, u32[]{:S(2)}, u32[]{:S(2)}) %collective-permute-start.3) | collective-permute-done | bytes 65568 | tf_op jit(solution)/shard_map/ppermute | solution.py:251
  21.2 1.6 %collective-permute-start.5 = (bf16[128,1152]{1,0:T(8,128)(2,1)}, bf16[128,1152]{1,0:T(8,128)(2,1)S(1)}, u32[]{:S(2)}, u32[]{:S(2)}) collective-permute-start(bf16[128,1152]{1,0:T(8,128)(2,1)} %get-tuple-element.57), channel_id=1, source_target_pairs={{0,8},{8,0},{16,24},{24,16},{1,9},{9,1},{17,25},{25,17},{2,10},{10... | collective-permute-start | bytes 884744 | tf_op jit(solution)/shard_map/ppermute | solution.py:671
  22.8 1.5 %collective-permute-start.6 = (bf16[128,1152]{1,0:T(8,128)(2,1)}, bf16[128,1152]{1,0:T(8,128)(2,1)S(1)}, u32[]{:S(2)}, u32[]{:S(2)}) collective-permute-start(bf16[128,1152]{1,0:T(8,128)(2,1)} %get-tuple-element.58), channel_id=1, source_target_pairs={{0,16},{8,24},{16,0},{24,8},{1,17},{9,25},{17,1},{25,9},{2,18},{10... | collective-permute-start | bytes 884744 | tf_op jit(solution)/shard_map/ppermute | solution.py:671
  28.3 3.5 %collective-permute-done.10.refs_1_ = f32[16,128]{1,0:T(8,128)S(1)} collective-permute-done((f32[16,128]{1,0:T(8,128)S(1)}, f32[16,128]{1,0:T(8,128)S(1)}, u32[]{:S(2)}, u32[]{:S(2)}) %collective-permute-start.10) | collective-permute-done | bytes 8224 | tf_op jit(solution)/shard_map/ppermute | solution.py:251
  32.9 2.6 %collective-permute-done.9.refs_0_ = f32[16,128]{1,0:T(8,128)S(1)} collective-permute-done((f32[16,128]{1,0:T(8,128)S(1)}, f32[16,128]{1,0:T(8,128)S(1)}, u32[]{:S(2)}, u32[]{:S(2)}) %collective-permute-start.9) | collective-permute-done | bytes 8224 | tf_op jit(solution)/shard_map/ppermute | solution.py:251
  35.5 3.8 %collective-permute-start.12 = (f32[48,128]{1,0:T(8,128)S(1)}, f32[48,128]{1,0:T(8,128)S(1)}, u32[]{:S(2)}, u32[]{:S(2)}) collective-permute-start(f32[48,128]{1,0:T(8,128)S(1)} %shard_map.107.got_ref), channel_id=1, source_target_pairs={{0,1},{1,0},{2,3},{3,2},{4,5},{5,4},{6,7},{7,6},{8,9},{9,8},{10,11... | collective-permute-start | bytes 73736 | tf_op jit(solution)/shard_map/ppermute | solution.py:671
  41.5 2.4 %collective-permute-start.14 = (bf16[128,128]{1,0:T(8,128)(2,1)S(1)}, bf16[128,128]{1,0:T(8,128)(2,1)S(1)}, u32[]{:S(2)}, u32[]{:S(2)}) collective-permute-start(bf16[128,128]{1,0:T(8,128)(2,1)S(1)} %shard_map.108.raw_ref.refs_4_), channel_id=1, source_target_pairs={{0,16},{8,24},{16,0},{24,8},{1,17},{9,25},{17,1},{25,9},{2,18},{10... | collective-permute-start | bytes 98312 | tf_op jit(solution)/shard_map/ppermute | solution.py:671
  45.1 2.1 %shard_map.109.refs_9_ = f32[256,128]{1,0:T(8,128)S(1)} custom-call(bf16[128,128]{1,0:T(8,128)(2,1)S(1)} %shard_map.108.raw_ref.refs_4_, f32[128,128]{1,0:T(8,128)S(1)} %get-tuple-element.70.rscale_ref, bf16[2048,512]{1,0:T(8,128)(2,1)S(1)} %get-tuple-element.71.in_w, bf16[512,128]{1,0:T(8,128)(2,1)S(1)} %get-tuple-element.69.out_w.refs_8_, ...), custom_call_target="tpu_custom_call" | custom-call | flops 1000000000 | bytes 7000000 | tf_op jit(solution)/shard_map/pallas_call | solution.py:434
  47.2 1.5 %collective-permute-done.15.refs_7_ = bf16[128,128]{1,0:T(8,128)(2,1)S(1)} collective-permute-done((bf16[128,128]{1,0:T(8,128)(2,1)S(1)}, bf16[128,128]{1,0:T(8,128)(2,1)S(1)}, u32[]{:S(2)}, u32[]{:S(2)}) %collective-permute-start.15) | collective-permute-done | bytes 32800 | tf_op jit(solution)/shard_map/ppermute | solution.py:671
  48.8 1.5 %shard_map.110 = (f32[4,80,512]{2,1,0:T(8,128)S(1)}, bf16[4,80,512]{2,1,0:T(8,128)(2,1)S(1)}) custom-call(bf16[128,1152]{1,0:T(8,128)(2,1)S(1)} %copy-done.2, bf16[128,1152]{1,0:T(8,128)(2,1)S(1)} %collective-permute-done.5.refs_1_, bf16[128,1152]{1,0:T(8,128)(2,1)S(1)} %collective-permute-done.6.refs_2_, ...), custom_call_target="tpu_custom_call" | custom-call | flops 600000000 | bytes 4000000 | tf_op jit(solution)/shard_map/pallas_call | solution.py:510
  50.3 1.6 %collective-permute-done.16.got_ref = bf16[4,80,512]{2,1,0:T(8,128)(2,1)S(1)} collective-permute-done((bf16[4,80,512]{2,1,0:T(8,128)(2,1)S(1)}, bf16[4,80,512]{2,1,0:T(8,128)(2,1)S(1)}, u32[]{:S(2)}, u32[]{:S(2)}) %collective-permute-start.16) | collective-permute-done | bytes 327712 | tf_op jit(solution)/shard_map/ppermute | solution.py:671
  52.1 1.4 %collective-permute-start.31 = (bf16[80,256]{1,0:T(8,128)(2,1)S(1)}, bf16[80,256]{1,0:T(8,128)(2,1)S(1)}, u32[]{:S(2)}, u32[]{:S(2)}) collective-permute-start(bf16[80,256]{1,0:T(8,128)(2,1)S(1)} %get-tuple-element.84), channel_id=1, source_target_pairs={{0,4},{1,5},{2,6},{3,7},{4,0},{5,1},{6,2},{7,3},{8,12},{9,13},{10,... | collective-permute-start | bytes 122888 | tf_op jit(solution)/shard_map/ppermute | solution.py:671
  53.5 3.0 %collective-permute-start.32 = (bf16[80,256]{1,0:T(8,128)(2,1)S(1)}, bf16[80,256]{1,0:T(8,128)(2,1)S(1)}, u32[]{:S(2)}, u32[]{:S(2)}) collective-permute-start(bf16[80,256]{1,0:T(8,128)(2,1)S(1)} %get-tuple-element.85), channel_id=1, source_target_pairs={{0,6},{1,7},{2,4},{3,5},{4,2},{5,3},{6,0},{7,1},{8,14},{9,15},{10,... | collective-permute-start | bytes 122888 | tf_op jit(solution)/shard_map/ppermute | solution.py:671
  56.5 1.4 %collective-permute-start.18 = (bf16[80,256]{1,0:T(8,128)(2,1)S(1)}, bf16[80,256]{1,0:T(8,128)(2,1)S(1)}, u32[]{:S(2)}, u32[]{:S(2)}) collective-permute-start(bf16[80,256]{1,0:T(8,128)(2,1)S(1)} %get-tuple-element.80), channel_id=1, source_target_pairs={{0,4},{1,5},{2,6},{3,7},{4,0},{5,1},{6,2},{7,3},{8,12},{9,13},{10,... | collective-permute-start | bytes 122888 | tf_op jit(solution)/shard_map/ppermute | solution.py:671
  57.8 3.0 %collective-permute-start.19 = (bf16[80,256]{1,0:T(8,128)(2,1)S(1)}, bf16[80,256]{1,0:T(8,128)(2,1)S(1)}, u32[]{:S(2)}, u32[]{:S(2)}) collective-permute-start(bf16[80,256]{1,0:T(8,128)(2,1)S(1)} %get-tuple-element.81), channel_id=1, source_target_pairs={{0,6},{1,7},{2,4},{3,5},{4,2},{5,3},{6,0},{7,1},{8,14},{9,15},{10,... | collective-permute-start | bytes 122888 | tf_op jit(solution)/shard_map/ppermute | solution.py:671
  61.0 2.0 %collective-permute-start.34 = (bf16[80,256]{1,0:T(8,128)(2,1)S(1)}, bf16[80,256]{1,0:T(8,128)(2,1)S(1)}, u32[]{:S(2)}, u32[]{:S(2)}) collective-permute-start(bf16[80,256]{1,0:T(8,128)(2,1)S(1)} %shard_map.114.refs_0_), channel_id=1, source_target_pairs={{0,4},{1,5},{2,6},{3,7},{4,0},{5,1},{6,2},{7,3},{8,12},{9,13},{10,... | collective-permute-start | bytes 122888 | tf_op jit(solution)/shard_map/ppermute | solution.py:671
  62.9 2.4 %collective-permute-start.35 = (bf16[80,256]{1,0:T(8,128)(2,1)S(1)}, bf16[80,256]{1,0:T(8,128)(2,1)S(1)}, u32[]{:S(2)}, u32[]{:S(2)}) collective-permute-start(bf16[80,256]{1,0:T(8,128)(2,1)S(1)} %shard_map.114.refs_0_), channel_id=1, source_target_pairs={{0,6},{1,7},{2,4},{3,5},{4,2},{5,3},{6,0},{7,1},{8,14},{9,15},{10,... | collective-permute-start | bytes 122888 | tf_op jit(solution)/shard_map/ppermute | solution.py:671
  65.5 2.0 %collective-permute-start.21 = (bf16[80,256]{1,0:T(8,128)(2,1)S(1)}, bf16[80,256]{1,0:T(8,128)(2,1)S(1)}, u32[]{:S(2)}, u32[]{:S(2)}) collective-permute-start(bf16[80,256]{1,0:T(8,128)(2,1)S(1)} %shard_map.112.refs_0_), channel_id=1, source_target_pairs={{0,4},{1,5},{2,6},{3,7},{4,0},{5,1},{6,2},{7,3},{8,12},{9,13},{10,... | collective-permute-start | bytes 122888 | tf_op jit(solution)/shard_map/ppermute | solution.py:671
  67.4 2.4 %collective-permute-start.22 = (bf16[80,256]{1,0:T(8,128)(2,1)S(1)}, bf16[80,256]{1,0:T(8,128)(2,1)S(1)}, u32[]{:S(2)}, u32[]{:S(2)}) collective-permute-start(bf16[80,256]{1,0:T(8,128)(2,1)S(1)} %shard_map.112.refs_0_), channel_id=1, source_target_pairs={{0,6},{1,7},{2,4},{3,5},{4,2},{5,3},{6,0},{7,1},{8,14},{9,15},{10,... | collective-permute-start | bytes 122888 | tf_op jit(solution)/shard_map/ppermute | solution.py:671
  69.9 1.8 %collective-permute-start.37 = (bf16[320,256]{1,0:T(8,128)(2,1)S(1)}, bf16[320,256]{1,0:T(8,128)(2,1)S(1)}, u32[]{:S(2)}, u32[]{:S(2)}) collective-permute-start(bf16[320,256]{1,0:T(8,128)(2,1)S(1)} %shard_map.115.refs_0_), channel_id=1, source_target_pairs={{0,8},{8,0},{16,24},{24,16},{1,9},{9,1},{17,25},{25,17},{2,10},{10... | collective-permute-start | bytes 491528 | tf_op jit(solution)/shard_map/ppermute | solution.py:671
  71.8 1.5 %collective-permute-done.22.refs_3_ = bf16[80,256]{1,0:T(8,128)(2,1)S(1)} collective-permute-done((bf16[80,256]{1,0:T(8,128)(2,1)S(1)}, bf16[80,256]{1,0:T(8,128)(2,1)S(1)}, u32[]{:S(2)}, u32[]{:S(2)}) %collective-permute-start.22) | collective-permute-done | bytes 40992 | tf_op jit(solution)/shard_map/ppermute | solution.py:671
  73.9 1.5 %collective-permute-start.39 = (bf16[320,256]{1,0:T(8,128)(2,1)S(1)}, bf16[320,256]{1,0:T(8,128)(2,1)S(1)}, u32[]{:S(2)}, u32[]{:S(2)}) collective-permute-start(bf16[320,256]{1,0:T(8,128)(2,1)S(1)} %shard_map.115.refs_0_), channel_id=1, source_target_pairs={{0,16},{8,24},{16,0},{24,8},{1,17},{9,25},{17,1},{25,9},{2,18},{10... | collective-permute-start | bytes 491528 | tf_op jit(solution)/shard_map/ppermute | solution.py:671
  75.4 1.8 %collective-permute-start.24 = (bf16[320,256]{1,0:T(8,128)(2,1)S(1)}, bf16[320,256]{1,0:T(8,128)(2,1)S(1)}, u32[]{:S(2)}, u32[]{:S(2)}) collective-permute-start(bf16[320,256]{1,0:T(8,128)(2,1)S(1)} %shard_map.113.refs_2_.refs_0_), channel_id=1, source_target_pairs={{0,8},{8,0},{16,24},{24,16},{1,9},{9,1},{17,25},{25,17},{2,10},{10... | collective-permute-start | bytes 491528 | tf_op jit(solution)/shard_map/ppermute | solution.py:671
  77.3 3.1 %collective-permute-done.26.refs_2_.refs_4_ = bf16[320,256]{1,0:T(8,128)(2,1)S(1)} collective-permute-done((bf16[320,256]{1,0:T(8,128)(2,1)S(1)}, bf16[320,256]{1,0:T(8,128)(2,1)S(1)}, u32[]{:S(2)}, u32[]{:S(2)}) %collective-permute-start.26) | collective-permute-done | bytes 163872 | tf_op jit(solution)/shard_map/ppermute | solution.py:671
  80.5 1.8 %collective-permute-start.28 = (bf16[320,256]{1,0:T(8,128)(2,1)S(1)}, bf16[320,256]{1,0:T(8,128)(2,1)S(1)}, u32[]{:S(2)}, u32[]{:S(2)}) collective-permute-start(bf16[320,256]{1,0:T(8,128)(2,1)S(1)} %collective-permute-done.26.refs_2_.refs_4_), channel_id=1, source_target_pairs={{0,8},{8,0},{16,24},{24,16},{1,9},{9,1},{17,25},{25,17},{2,10},{10... | collective-permute-start | bytes 491528 | tf_op jit(solution)/shard_map/ppermute | solution.py:671
  82.2 1.8 %collective-permute-done.39.refs_2_.refs_4_ = bf16[320,256]{1,0:T(8,128)(2,1)S(1)} collective-permute-done((bf16[320,256]{1,0:T(8,128)(2,1)S(1)}, bf16[320,256]{1,0:T(8,128)(2,1)S(1)}, u32[]{:S(2)}, u32[]{:S(2)}) %collective-permute-start.39) | collective-permute-done | bytes 163872 | tf_op jit(solution)/shard_map/ppermute | solution.py:671
  84.6 2.4 %collective-permute-done.41.refs_6_ = bf16[320,256]{1,0:T(8,128)(2,1)S(1)} collective-permute-done((bf16[320,256]{1,0:T(8,128)(2,1)S(1)}, bf16[320,256]{1,0:T(8,128)(2,1)S(1)}, u32[]{:S(2)}, u32[]{:S(2)}) %collective-permute-start.41) | collective-permute-done | bytes 163872 | tf_op jit(solution)/shard_map/ppermute | solution.py:671
  92.3 1.6 %shard_map.120 = (f32[2048,512]{1,0:T(8,128)}, f32[512,128]{1,0:T(8,128)}, f32[256,128]{1,0:T(8,128)}) custom-call(bf16[320,256]{1,0:T(8,128)(2,1)S(1)} %shard_map.113.refs_2_.refs_0_, bf16[320,256]{1,0:T(8,128)(2,1)S(1)} %collective-permute-done.23.refs_3_.refs_1_, ...), custom_call_target="tpu_custom_call", output_to_operand_aliasing={{0}: (8, {}), {1}: (9, {})} | custom-call | flops 1000000 | bytes 8000000 | tf_op jit(solution)/shard_map/pallas_call | solution.py:634
  (79 shorter events, 17.3 us)
Async XLA Ops:
  9.5 5.6 %collective-permute-start.1 = (bf16[256,128]{1,0:T(8,128)(2,1)S(1)}, bf16[256,128]{1,0:T(8,128)(2,1)S(1)}, u32[]{:S(2)}, u32[]{:S(2)}) collective-permute-start(bf16[256,128]{1,0:T(8,128)(2,1)S(1)} %shard_map.103.pair_ref), channel_id=1, source_target_pairs={{0,2},{1,9},{2,0},{3,11},{4,6},{5,13},{6,4},{7,15},{8,10},{9,1},{1... | collective-permute-start | bytes 196616 | tf_op jit(solution)/shard_map/ppermute | solution.py:251
  12.5 5.9 %collective-permute-start.2 = (bf16[256,128]{1,0:T(8,128)(2,1)S(1)}, bf16[256,128]{1,0:T(8,128)(2,1)S(1)}, u32[]{:S(2)}, u32[]{:S(2)}) collective-permute-start(bf16[256,128]{1,0:T(8,128)(2,1)S(1)} %shard_map.103.pair_ref), channel_id=1, source_target_pairs={{0,4},{1,17},{2,6},{3,19},{4,0},{5,21},{6,2},{7,23},{8,12},{9,25},... | collective-permute-start | bytes 196616 | tf_op jit(solution)/shard_map/ppermute | solution.py:251
  15.0 6.1 %collective-permute-start.3 = (bf16[256,128]{1,0:T(8,128)(2,1)S(1)}, bf16[256,128]{1,0:T(8,128)(2,1)S(1)}, u32[]{:S(2)}, u32[]{:S(2)}) collective-permute-start(bf16[256,128]{1,0:T(8,128)(2,1)S(1)} %shard_map.103.pair_ref), channel_id=1, source_target_pairs={{0,6},{1,25},{2,4},{3,27},{4,2},{5,29},{6,0},{7,31},{8,14},{9,17},... | collective-permute-start | bytes 196616 | tf_op jit(solution)/shard_map/ppermute | solution.py:251
  21.2 22.7 %collective-permute-start.5 = (bf16[128,1152]{1,0:T(8,128)(2,1)}, bf16[128,1152]{1,0:T(8,128)(2,1)S(1)}, u32[]{:S(2)}, u32[]{:S(2)}) collective-permute-start(bf16[128,1152]{1,0:T(8,128)(2,1)} %get-tuple-element.57), channel_id=1, source_target_pairs={{0,8},{8,0},{16,24},{24,16},{1,9},{9,1},{17,25},{25,17},{2,10},{10... | collective-permute-start | bytes 884744 | tf_op jit(solution)/shard_map/ppermute | solution.py:671
  22.8 24.4 %collective-permute-start.6 = (bf16[128,1152]{1,0:T(8,128)(2,1)}, bf16[128,1152]{1,0:T(8,128)(2,1)S(1)}, u32[]{:S(2)}, u32[]{:S(2)}) collective-permute-start(bf16[128,1152]{1,0:T(8,128)(2,1)} %get-tuple-element.58), channel_id=1, source_target_pairs={{0,16},{8,24},{16,0},{24,8},{1,17},{9,25},{17,1},{25,9},{2,18},{10... | collective-permute-start | bytes 884744 | tf_op jit(solution)/shard_map/ppermute | solution.py:671
  24.3 22.9 %collective-permute-start.7 = (bf16[128,1152]{1,0:T(8,128)(2,1)}, bf16[128,1152]{1,0:T(8,128)(2,1)S(1)}, u32[]{:S(2)}, u32[]{:S(2)}) collective-permute-start(bf16[128,1152]{1,0:T(8,128)(2,1)} %get-tuple-element.59), channel_id=1, source_target_pairs={{0,24},{8,16},{16,8},{24,0},{1,25},{9,17},{17,9},{25,1},{2,26},{10... | collective-permute-start | bytes 884744 | tf_op jit(solution)/shard_map/ppermute | solution.py:671
  27.5 5.4 %collective-permute-start.11 = (f32[16,128]{1,0:T(8,128)S(1)}, f32[16,128]{1,0:T(8,128)S(1)}, u32[]{:S(2)}, u32[]{:S(2)}) collective-permute-start(f32[16,128]{1,0:T(8,128)S(1)} %shard_map.106.pair_ref), channel_id=1, source_target_pairs={{0,6},{1,25},{2,4},{3,27},{4,2},{5,29},{6,0},{7,31},{8,14},{9,17},... | collective-permute-start | bytes 24584 | tf_op jit(solution)/shard_map/ppermute | solution.py:251
  41.0 6.3 %collective-permute-start.13 = (bf16[128,128]{1,0:T(8,128)(2,1)S(1)}, bf16[128,128]{1,0:T(8,128)(2,1)S(1)}, u32[]{:S(2)}, u32[]{:S(2)}) collective-permute-start(bf16[128,128]{1,0:T(8,128)(2,1)S(1)} %shard_map.108.raw_ref.refs_4_), channel_id=1, source_target_pairs={{0,8},{8,0},{16,24},{24,16},{1,9},{9,1},{17,25},{25,17},{2,10},{10... | collective-permute-start | bytes 98312 | tf_op jit(solution)/shard_map/ppermute | solution.py:671
  41.5 5.7 %collective-permute-start.14 = (bf16[128,128]{1,0:T(8,128)(2,1)S(1)}, bf16[128,128]{1,0:T(8,128)(2,1)S(1)}, u32[]{:S(2)}, u32[]{:S(2)}) collective-permute-start(bf16[128,128]{1,0:T(8,128)(2,1)S(1)} %shard_map.108.raw_ref.refs_4_), channel_id=1, source_target_pairs={{0,16},{8,24},{16,0},{24,8},{1,17},{9,25},{17,1},{25,9},{2,18},{10... | collective-permute-start | bytes 98312 | tf_op jit(solution)/shard_map/ppermute | solution.py:671
  52.0 5.8 %collective-permute-start.30 = (bf16[80,256]{1,0:T(8,128)(2,1)S(1)}, bf16[80,256]{1,0:T(8,128)(2,1)S(1)}, u32[]{:S(2)}, u32[]{:S(2)}) collective-permute-start(bf16[80,256]{1,0:T(8,128)(2,1)S(1)} %get-tuple-element.83), channel_id=1, source_target_pairs={{0,2},{1,3},{2,0},{3,1},{4,6},{5,7},{6,4},{7,5},{8,10},{9,11},{10,... | collective-permute-start | bytes 122888 | tf_op jit(solution)/shard_map/ppermute | solution.py:671
  52.1 8.8 %collective-permute-start.31 = (bf16[80,256]{1,0:T(8,128)(2,1)S(1)}, bf16[80,256]{1,0:T(8,128)(2,1)S(1)}, u32[]{:S(2)}, u32[]{:S(2)}) collective-permute-start(bf16[80,256]{1,0:T(8,128)(2,1)S(1)} %get-tuple-element.84), channel_id=1, source_target_pairs={{0,4},{1,5},{2,6},{3,7},{4,0},{5,1},{6,2},{7,3},{8,12},{9,13},{10,... | collective-permute-start | bytes 122888 | tf_op jit(solution)/shard_map/ppermute | solution.py:671
  53.5 7.4 %collective-permute-start.32 = (bf16[80,256]{1,0:T(8,128)(2,1)S(1)}, bf16[80,256]{1,0:T(8,128)(2,1)S(1)}, u32[]{:S(2)}, u32[]{:S(2)}) collective-permute-start(bf16[80,256]{1,0:T(8,128)(2,1)S(1)} %get-tuple-element.85), channel_id=1, source_target_pairs={{0,6},{1,7},{2,4},{3,5},{4,2},{5,3},{6,0},{7,1},{8,14},{9,15},{10,... | collective-permute-start | bytes 122888 | tf_op jit(solution)/shard_map/ppermute | solution.py:671
  56.5 6.5 %collective-permute-start.17 = (bf16[80,256]{1,0:T(8,128)(2,1)S(1)}, bf16[80,256]{1,0:T(8,128)(2,1)S(1)}, u32[]{:S(2)}, u32[]{:S(2)}) collective-permute-start(bf16[80,256]{1,0:T(8,128)(2,1)S(1)} %get-tuple-element.79), channel_id=1, source_target_pairs={{0,2},{1,3},{2,0},{3,1},{4,6},{5,7},{6,4},{7,5},{8,10},{9,11},{10,... | collective-permute-start | bytes 122888 | tf_op jit(solution)/shard_map/ppermute | solution.py:671
  56.5 8.9 %collective-permute-start.18 = (bf16[80,256]{1,0:T(8,128)(2,1)S(1)}, bf16[80,256]{1,0:T(8,128)(2,1)S(1)}, u32[]{:S(2)}, u32[]{:S(2)}) collective-permute-start(bf16[80,256]{1,0:T(8,128)(2,1)S(1)} %get-tuple-element.80), channel_id=1, source_target_pairs={{0,4},{1,5},{2,6},{3,7},{4,0},{5,1},{6,2},{7,3},{8,12},{9,13},{10,... | collective-permute-start | bytes 122888 | tf_op jit(solution)/shard_map/ppermute | solution.py:671
  57.8 7.5 %collective-permute-start.19 = (bf16[80,256]{1,0:T(8,128)(2,1)S(1)}, bf16[80,256]{1,0:T(8,128)(2,1)S(1)}, u32[]{:S(2)}, u32[]{:S(2)}) collective-permute-start(bf16[80,256]{1,0:T(8,128)(2,1)S(1)} %get-tuple-element.81), channel_id=1, source_target_pairs={{0,6},{1,7},{2,4},{3,5},{4,2},{5,3},{6,0},{7,1},{8,14},{9,15},{10,... | collective-permute-start | bytes 122888 | tf_op jit(solution)/shard_map/ppermute | solution.py:671
  60.9 6.5 %collective-permute-start.33 = (bf16[80,256]{1,0:T(8,128)(2,1)S(1)}, bf16[80,256]{1,0:T(8,128)(2,1)S(1)}, u32[]{:S(2)}, u32[]{:S(2)}) collective-permute-start(bf16[80,256]{1,0:T(8,128)(2,1)S(1)} %shard_map.114.refs_0_), channel_id=1, source_target_pairs={{0,2},{1,3},{2,0},{3,1},{4,6},{5,7},{6,4},{7,5},{8,10},{9,11},{10,... | collective-permute-start | bytes 122888 | tf_op jit(solution)/shard_map/ppermute | solution.py:671
  61.0 8.9 %collective-permute-start.34 = (bf16[80,256]{1,0:T(8,128)(2,1)S(1)}, bf16[80,256]{1,0:T(8,128)(2,1)S(1)}, u32[]{:S(2)}, u32[]{:S(2)}) collective-permute-start(bf16[80,256]{1,0:T(8,128)(2,1)S(1)} %shard_map.114.refs_0_), channel_id=1, source_target_pairs={{0,4},{1,5},{2,6},{3,7},{4,0},{5,1},{6,2},{7,3},{8,12},{9,13},{10,... | collective-permute-start | bytes 122888 | tf_op jit(solution)/shard_map/ppermute | solution.py:671
  62.9 6.9 %collective-permute-start.35 = (bf16[80,256]{1,0:T(8,128)(2,1)S(1)}, bf16[80,256]{1,0:T(8,128)(2,1)S(1)}, u32[]{:S(2)}, u32[]{:S(2)}) collective-permute-start(bf16[80,256]{1,0:T(8,128)(2,1)S(1)} %shard_map.114.refs_0_), channel_id=1, source_target_pairs={{0,6},{1,7},{2,4},{3,5},{4,2},{5,3},{6,0},{7,1},{8,14},{9,15},{10,... | collective-permute-start | bytes 122888 | tf_op jit(solution)/shard_map/ppermute | solution.py:671
  65.4 6.4 %collective-permute-start.20 = (bf16[80,256]{1,0:T(8,128)(2,1)S(1)}, bf16[80,256]{1,0:T(8,128)(2,1)S(1)}, u32[]{:S(2)}, u32[]{:S(2)}) collective-permute-start(bf16[80,256]{1,0:T(8,128)(2,1)S(1)} %shard_map.112.refs_0_), channel_id=1, source_target_pairs={{0,2},{1,3},{2,0},{3,1},{4,6},{5,7},{6,4},{7,5},{8,10},{9,11},{10,... | collective-permute-start | bytes 122888 | tf_op jit(solution)/shard_map/ppermute | solution.py:671
  65.5 6.3 %collective-permute-start.21 = (bf16[80,256]{1,0:T(8,128)(2,1)S(1)}, bf16[80,256]{1,0:T(8,128)(2,1)S(1)}, u32[]{:S(2)}, u32[]{:S(2)}) collective-permute-start(bf16[80,256]{1,0:T(8,128)(2,1)S(1)} %shard_map.112.refs_0_), channel_id=1, source_target_pairs={{0,4},{1,5},{2,6},{3,7},{4,0},{5,1},{6,2},{7,3},{8,12},{9,13},{10,... | collective-permute-start | bytes 122888 | tf_op jit(solution)/shard_map/ppermute | solution.py:671
  67.4 5.8 %collective-permute-start.22 = (bf16[80,256]{1,0:T(8,128)(2,1)S(1)}, bf16[80,256]{1,0:T(8,128)(2,1)S(1)}, u32[]{:S(2)}, u32[]{:S(2)}) collective-permute-start(bf16[80,256]{1,0:T(8,128)(2,1)S(1)} %shard_map.112.refs_0_), channel_id=1, source_target_pairs={{0,6},{1,7},{2,4},{3,5},{4,2},{5,3},{6,0},{7,1},{8,14},{9,15},{10,... | collective-permute-start | bytes 122888 | tf_op jit(solution)/shard_map/ppermute | solution.py:671
  69.9 5.5 %collective-permute-start.36 = (bf16[320,256]{1,0:T(8,128)(2,1)S(1)}, bf16[320,256]{1,0:T(8,128)(2,1)S(1)}, u32[]{:S(2)}, u32[]{:S(2)}) collective-permute-start(bf16[320,256]{1,0:T(8,128)(2,1)S(1)} %shard_map.115.refs_0_), channel_id=1, source_target_pairs={{0,1},{1,0},{2,3},{3,2},{4,5},{5,4},{6,7},{7,6},{8,9},{9,8},{10,11... | collective-permute-start | bytes 491528 | tf_op jit(solution)/shard_map/ppermute | solution.py:671
  69.9 7.2 %collective-permute-start.37 = (bf16[320,256]{1,0:T(8,128)(2,1)S(1)}, bf16[320,256]{1,0:T(8,128)(2,1)S(1)}, u32[]{:S(2)}, u32[]{:S(2)}) collective-permute-start(bf16[320,256]{1,0:T(8,128)(2,1)S(1)} %shard_map.115.refs_0_), channel_id=1, source_target_pairs={{0,8},{8,0},{16,24},{24,16},{1,9},{9,1},{17,25},{25,17},{2,10},{10... | collective-permute-start | bytes 491528 | tf_op jit(solution)/shard_map/ppermute | solution.py:671
  73.3 7.1 %collective-permute-start.26 = (bf16[320,256]{1,0:T(8,128)(2,1)S(1)}, bf16[320,256]{1,0:T(8,128)(2,1)S(1)}, u32[]{:S(2)}, u32[]{:S(2)}) collective-permute-start(bf16[320,256]{1,0:T(8,128)(2,1)S(1)} %shard_map.113.refs_2_.refs_0_), channel_id=1, source_target_pairs={{0,16},{8,24},{16,0},{24,8},{1,17},{9,25},{17,1},{25,9},{2,18},{10... | collective-permute-start | bytes 491528 | tf_op jit(solution)/shard_map/ppermute | solution.py:671
  73.9 10.1 %collective-permute-start.39 = (bf16[320,256]{1,0:T(8,128)(2,1)S(1)}, bf16[320,256]{1,0:T(8,128)(2,1)S(1)}, u32[]{:S(2)}, u32[]{:S(2)}) collective-permute-start(bf16[320,256]{1,0:T(8,128)(2,1)S(1)} %shard_map.115.refs_0_), channel_id=1, source_target_pairs={{0,16},{8,24},{16,0},{24,8},{1,17},{9,25},{17,1},{25,9},{2,18},{10... | collective-permute-start | bytes 491528 | tf_op jit(solution)/shard_map/ppermute | solution.py:671
  75.4 8.6 %collective-permute-start.24 = (bf16[320,256]{1,0:T(8,128)(2,1)S(1)}, bf16[320,256]{1,0:T(8,128)(2,1)S(1)}, u32[]{:S(2)}, u32[]{:S(2)}) collective-permute-start(bf16[320,256]{1,0:T(8,128)(2,1)S(1)} %shard_map.113.refs_2_.refs_0_), channel_id=1, source_target_pairs={{0,8},{8,0},{16,24},{24,16},{1,9},{9,1},{17,25},{25,17},{2,10},{10... | collective-permute-start | bytes 491528 | tf_op jit(solution)/shard_map/ppermute | solution.py:671
  77.2 7.3 %collective-permute-start.38 = (bf16[320,256]{1,0:T(8,128)(2,1)S(1)}, bf16[320,256]{1,0:T(8,128)(2,1)S(1)}, u32[]{:S(2)}, u32[]{:S(2)}) collective-permute-start(bf16[320,256]{1,0:T(8,128)(2,1)S(1)} %collective-permute-done.37.refs_0_.refs_2_), channel_id=1, source_target_pairs={{0,1},{1,0},{2,3},{3,2},{4,5},{5,4},{6,7},{7,6},{8,9},{9,8},{10,11... | collective-permute-start | bytes 491528 | tf_op jit(solution)/shard_map/ppermute | solution.py:671
  77.2 9.8 %collective-permute-start.41 = (bf16[320,256]{1,0:T(8,128)(2,1)S(1)}, bf16[320,256]{1,0:T(8,128)(2,1)S(1)}, u32[]{:S(2)}, u32[]{:S(2)}) collective-permute-start(bf16[320,256]{1,0:T(8,128)(2,1)S(1)} %collective-permute-done.37.refs_0_.refs_2_), channel_id=1, source_target_pairs={{0,16},{8,24},{16,0},{24,8},{1,17},{9,25},{17,1},{25,9},{2,18},{10... | collective-permute-start | bytes 491528 | tf_op jit(solution)/shard_map/ppermute | solution.py:671
  80.5 6.5 %collective-permute-start.28 = (bf16[320,256]{1,0:T(8,128)(2,1)S(1)}, bf16[320,256]{1,0:T(8,128)(2,1)S(1)}, u32[]{:S(2)}, u32[]{:S(2)}) collective-permute-start(bf16[320,256]{1,0:T(8,128)(2,1)S(1)} %collective-permute-done.26.refs_2_.refs_4_), channel_id=1, source_target_pairs={{0,8},{8,0},{16,24},{24,16},{1,9},{9,1},{17,25},{25,17},{2,10},{10... | collective-permute-start | bytes 491528 | tf_op jit(solution)/shard_map/ppermute | solution.py:671
  84.0 6.1 %collective-permute-start.25 = (bf16[320,256]{1,0:T(8,128)(2,1)S(1)}, bf16[320,256]{1,0:T(8,128)(2,1)S(1)}, u32[]{:S(2)}, u32[]{:S(2)}) collective-permute-start(bf16[320,256]{1,0:T(8,128)(2,1)S(1)} %collective-permute-done.24.refs_0_.refs_2_), channel_id=1, source_target_pairs={{0,1},{1,0},{2,3},{3,2},{4,5},{5,4},{6,7},{7,6},{8,9},{9,8},{10,11... | collective-permute-start | bytes 491528 | tf_op jit(solution)/shard_map/ppermute | solution.py:671
  84.5 5.6 %collective-permute-start.27 = (bf16[320,256]{1,0:T(8,128)(2,1)S(1)}, bf16[320,256]{1,0:T(8,128)(2,1)S(1)}, u32[]{:S(2)}, u32[]{:S(2)}) collective-permute-start(bf16[320,256]{1,0:T(8,128)(2,1)S(1)} %collective-permute-done.26.refs_2_.refs_4_), channel_id=1, source_target_pairs={{0,1},{1,0},{2,3},{3,2},{4,5},{5,4},{6,7},{7,6},{8,9},{9,8},{10,11... | collective-permute-start | bytes 491528 | tf_op jit(solution)/shard_map/ppermute | solution.py:671
  86.9 5.4 %collective-permute-start.29 = (bf16[320,256]{1,0:T(8,128)(2,1)S(1)}, bf16[320,256]{1,0:T(8,128)(2,1)S(1)}, u32[]{:S(2)}, u32[]{:S(2)}) collective-permute-start(bf16[320,256]{1,0:T(8,128)(2,1)S(1)} %collective-permute-done.28.refs_6_), channel_id=1, source_target_pairs={{0,1},{1,0},{2,3},{3,2},{4,5},{5,4},{6,7},{7,6},{8,9},{9,8},{10,11... | collective-permute-start | bytes 491528 | tf_op jit(solution)/shard_map/ppermute | solution.py:671
  (14 other events, 95.6 us)

commit v8 on v7

--- a/solution.py
+++ b/solution.py
@@ -569,12 +569,10 @@
     slots = lay.peers // 2
     part_cols = lay.width // HALVES
     part_refs, refs = dict(zip(parts, refs)), refs[len(parts) :]
-    if done > 2:
-        mix_ref = refs[2]
     g_in_hbm, g_out_hbm, *refs = refs[done:]
     if closing is not None:
-        g_mix_ref, *refs = refs
-    stage, strip_stage, sems, strip_sems = refs
+        g_mix_hbm, *refs = refs
+    stage, strip_stage, mix_stage, sems, strip_sems, mix_sems = refs
     me_blk, me_dp = lax.axis_index("blk"), lax.axis_index("dp")
     copies = []
 
@@ -583,6 +581,31 @@
         copy.start()
         copies.append(copy)
 
+    if closing is not None:
+        slot = 0
+        for core in range(2):
+            for z in range(slots):
+                strip = z * lay.rows + lay.top
+                owner = me_dp ^ (2 * z + core)
+                for start, rows, cols in lay.mix_parts():
+                    half, first = divmod(cols.start, part_cols)
+                    if half != closing:
+                        continue
+                    terms = [
+                        part_refs[hop, core, half][strip : strip + rows, first : first + 128].astype(F32)
+                        for hop in range(lay.size)
+                    ]
+                    while len(terms) > 1:
+                        terms = [terms[t] + terms[t + 1] for t in range(0, len(terms), 2)]
+                    mix_stage[slot, :rows, :] = terms[0]
+                    copy = pltpu.make_async_copy(
+                        mix_stage.at[slot, :rows],
+                        g_mix_hbm.at[pl.ds(owner * lay.mix_rows + start, rows), :],
+                        mix_sems.at[slot],
+                    )
+                    copy.start()
+                    copies.append(copy)
+                    slot += 1
     for n, (hop, core, half) in enumerate(fresh):
         source = part_refs[hop, core, half]
         cols = slice(half * part_cols, (half + 1) * part_cols)
@@ -601,25 +624,6 @@
                     g_out_hbm.at[pl.ds(owner * lay.out_rows, lay.out_rows), :],
                     strip_sems,
                 )
-    if closing is not None:
-        for core in range(2):
-            for z in range(slots):
-                strip = z * lay.rows + lay.top
-                owner = me_dp ^ (2 * z + core)
-                for start, rows, cols in lay.mix_parts():
-                    half, first = divmod(cols.start, part_cols)
-                    at = pl.ds(owner * lay.mix_rows + start, rows)
-                    if half < closing:
-                        g_mix_ref[at, :] = mix_ref[at, :]
-                    if half != closing:
-                        continue
-                    terms = [
-                        part_refs[hop, core, half][strip : strip + rows, first : first + 128].astype(F32)
-                        for hop in range(lay.size)
-                    ]
-                    while len(terms) > 1:
-                        terms = [terms[t] + terms[t + 1] for t in range(0, len(terms), 2)]
-                    g_mix_ref[at, :] = terms[0]
     for copy in copies:
         copy.wait()
 
@@ -630,19 +634,22 @@
     specs = [ANY, ANY]
     if closing is not None:
         outs.append(shape((lanes, 128), F32))
-        specs.append(VMEM)
+        specs.append(ANY)
+    blocks = lay.peers * lay.mix_blocks
     return pl.pallas_call(
         functools.partial(finish_kernel, lay, tuple(parts), len(done), tuple(fresh), closing),
-        in_specs=[VMEM] * len(parts) + [ANY, ANY, VMEM][: len(done)],
+        in_specs=[VMEM] * len(parts) + [ANY] * len(done),
         out_shape=outs,
         out_specs=specs,
         scratch_shapes=[
             pltpu.VMEM((slots, lay.in_rows, lay.width // HALVES), F32),
             pltpu.VMEM((slots, lay.out_rows, 128), F32),
+            pltpu.VMEM((blocks, lay.strip, 128), F32),
             pltpu.SemaphoreType.DMA((slots,)),
             pltpu.SemaphoreType.DMA((slots,)),
+            pltpu.SemaphoreType.DMA((blocks,)),
         ],
-        input_output_aliases={len(parts) + i: i for i in range(min(2, len(done)))},
+        input_output_aliases={len(parts) + i: i for i in range(len(done))},
         compiler_params=params(24),
         cost_estimate=cost(1e6, 8e6),
     )(*parts.values(), *done)

time: 94.1 us -> 94.2 us (level)
  no operation moved by 1% of the time
where the time goes in v8:
time: 94.2 us; the launch traced here: 94.1 us
  starting transfers between devices  45.3 us (48%)
  waiting for transfers between devices  28.1 us (30%)
  Pallas kernels  19.8 us (21%)
    ppermute x37, starting transfers between devices, swap(): return lax.ppermute(block, axis, [(src, src ^ bit) for src in range(size)])  38.7 us
    ppermute x37, waiting for transfers between devices, swap(): return lax.ppermute(block, axis, [(src, src ^ bit) for src in range(size)])  14.8 us
    ppermute x6, waiting for transfers between devices, cross(): got.append(lax.ppermute(pair, ('blk', 'dp'), routes))  13.2 us
    pallas_call x1, Pallas kernels, encode(): pl.pallas_call(functools.partial(encode_kernel, freqs, size, rounds), in_...  7.38 us
    ppermute x6, starting transfers between devices, cross(): got.append(lax.ppermute(pair, ('blk', 'dp'), routes))  6.58 us
    pallas_call x5, Pallas kernels, finish(): pl.pallas_call(functools.partial(finish_kernel, lay, tuple(parts), len(do...  6.52 us
    pallas_call x1, Pallas kernels, lower(): pl.pallas_call(functools.partial(lower_kernel, freqs), in_specs=[VMEM] *...  2.06 us
  transfers between devices with their start and end apart: 43, of which 14 were waited for; matrix products, arithmetic and copies ran while one was open for 0% of the time, Pallas kernels for 10%

profile of v8, /device:TPU:0, one launch (start us, length us, event | category | flops | bytes accessed | tf_op | source)
XLA Modules:
  0.0 94.1 jit_solution(10851859635042797221)
XLA Ops:
  0.7 7.4 %shard_map.102 = (bf16[128,1152]{1,0:T(8,128)(2,1)}, bf16[128,1152]{1,0:T(8,128)(2,1)}, bf16[128,1152]{1,0:T(8,128)(2,1)}, bf16[128,1152]{1,0:T(8,128)(2,1)}, bf...) custom-call(bf16[128,64,256]{2,1,0:T(8,128)(2,1)} %patch_hbm.1, ...), custom_call_target="tpu_custom_call" | custom-call | flops 3000000000 | bytes 14000000 | tf_op jit(solution)/shard_map/pallas_call | solution.py:191
  9.5 3.0 %collective-permute-start.1 = (bf16[256,128]{1,0:T(8,128)(2,1)S(1)}, bf16[256,128]{1,0:T(8,128)(2,1)S(1)}, u32[]{:S(2)}, u32[]{:S(2)}) collective-permute-start(bf16[256,128]{1,0:T(8,128)(2,1)S(1)} %shard_map.103.pair_ref), channel_id=1, source_target_pairs={{0,2},{1,9},{2,0},{3,11},{4,6},{5,13},{6,4},{7,15},{8,10},{9,1},{1... | collective-permute-start | bytes 196616 | tf_op jit(solution)/shard_map/ppermute | solution.py:251
  12.5 2.6 %collective-permute-start.2 = (bf16[256,128]{1,0:T(8,128)(2,1)S(1)}, bf16[256,128]{1,0:T(8,128)(2,1)S(1)}, u32[]{:S(2)}, u32[]{:S(2)}) collective-permute-start(bf16[256,128]{1,0:T(8,128)(2,1)S(1)} %shard_map.103.pair_ref), channel_id=1, source_target_pairs={{0,4},{1,17},{2,6},{3,19},{4,0},{5,21},{6,2},{7,23},{8,12},{9,25},... | collective-permute-start | bytes 196616 | tf_op jit(solution)/shard_map/ppermute | solution.py:251
  15.0 3.3 %collective-permute-done.2.refs_1_ = bf16[256,128]{1,0:T(8,128)(2,1)S(1)} collective-permute-done((bf16[256,128]{1,0:T(8,128)(2,1)S(1)}, bf16[256,128]{1,0:T(8,128)(2,1)S(1)}, u32[]{:S(2)}, u32[]{:S(2)}) %collective-permute-start.2) | collective-permute-done | bytes 65568 | tf_op jit(solution)/shard_map/ppermute | solution.py:251
  18.3 2.8 %collective-permute-done.3.refs_2_ = bf16[256,128]{1,0:T(8,128)(2,1)S(1)} collective-permute-done((bf16[256,128]{1,0:T(8,128)(2,1)S(1)}, bf16[256,128]{1,0:T(8,128)(2,1)S(1)}, u32[]{:S(2)}, u32[]{:S(2)}) %collective-permute-start.3) | collective-permute-done | bytes 65568 | tf_op jit(solution)/shard_map/ppermute | solution.py:251
  21.2 1.6 %collective-permute-start.5 = (bf16[128,1152]{1,0:T(8,128)(2,1)}, bf16[128,1152]{1,0:T(8,128)(2,1)S(1)}, u32[]{:S(2)}, u32[]{:S(2)}) collective-permute-start(bf16[128,1152]{1,0:T(8,128)(2,1)} %get-tuple-element.57), channel_id=1, source_target_pairs={{0,8},{8,0},{16,24},{24,16},{1,9},{9,1},{17,25},{25,17},{2,10},{10... | collective-permute-start | bytes 884744 | tf_op jit(solution)/shard_map/ppermute | solution.py:678
  22.8 1.5 %collective-permute-start.6 = (bf16[128,1152]{1,0:T(8,128)(2,1)}, bf16[128,1152]{1,0:T(8,128)(2,1)S(1)}, u32[]{:S(2)}, u32[]{:S(2)}) collective-permute-start(bf16[128,1152]{1,0:T(8,128)(2,1)} %get-tuple-element.58), channel_id=1, source_target_pairs={{0,16},{8,24},{16,0},{24,8},{1,17},{9,25},{17,1},{25,9},{2,18},{10... | collective-permute-start | bytes 884744 | tf_op jit(solution)/shard_map/ppermute | solution.py:678
  28.3 3.5 %collective-permute-done.10.refs_1_ = f32[16,128]{1,0:T(8,128)S(1)} collective-permute-done((f32[16,128]{1,0:T(8,128)S(1)}, f32[16,128]{1,0:T(8,128)S(1)}, u32[]{:S(2)}, u32[]{:S(2)}) %collective-permute-start.10) | collective-permute-done | bytes 8224 | tf_op jit(solution)/shard_map/ppermute | solution.py:251
  32.9 2.6 %collective-permute-done.9.refs_0_ = f32[16,128]{1,0:T(8,128)S(1)} collective-permute-done((f32[16,128]{1,0:T(8,128)S(1)}, f32[16,128]{1,0:T(8,128)S(1)}, u32[]{:S(2)}, u32[]{:S(2)}) %collective-permute-start.9) | collective-permute-done | bytes 8224 | tf_op jit(solution)/shard_map/ppermute | solution.py:251
  35.5 3.8 %collective-permute-start.12 = (f32[48,128]{1,0:T(8,128)S(1)}, f32[48,128]{1,0:T(8,128)S(1)}, u32[]{:S(2)}, u32[]{:S(2)}) collective-permute-start(f32[48,128]{1,0:T(8,128)S(1)} %shard_map.107.got_ref), channel_id=1, source_target_pairs={{0,1},{1,0},{2,3},{3,2},{4,5},{5,4},{6,7},{7,6},{8,9},{9,8},{10,11... | collective-permute-start | bytes 73736 | tf_op jit(solution)/shard_map/ppermute | solution.py:678
  41.5 2.4 %collective-permute-start.14 = (bf16[128,128]{1,0:T(8,128)(2,1)S(1)}, bf16[128,128]{1,0:T(8,128)(2,1)S(1)}, u32[]{:S(2)}, u32[]{:S(2)}) collective-permute-start(bf16[128,128]{1,0:T(8,128)(2,1)S(1)} %shard_map.108.raw_ref.refs_4_), channel_id=1, source_target_pairs={{0,16},{8,24},{16,0},{24,8},{1,17},{9,25},{17,1},{25,9},{2,18},{10... | collective-permute-start | bytes 98312 | tf_op jit(solution)/shard_map/ppermute | solution.py:678
  45.1 2.1 %shard_map.109.refs_9_ = f32[256,128]{1,0:T(8,128)S(1)} custom-call(bf16[128,128]{1,0:T(8,128)(2,1)S(1)} %shard_map.108.raw_ref.refs_4_, f32[128,128]{1,0:T(8,128)S(1)} %get-tuple-element.70.rscale_ref, bf16[2048,512]{1,0:T(8,128)(2,1)S(1)} %get-tuple-element.71.in_w, bf16[512,128]{1,0:T(8,128)(2,1)S(1)} %get-tuple-element.69.out_w.refs_8_, ...), custom_call_target="tpu_custom_call" | custom-call | flops 1000000000 | bytes 7000000 | tf_op jit(solution)/shard_map/pallas_call | solution.py:434
  47.2 1.5 %collective-permute-done.15.refs_7_ = bf16[128,128]{1,0:T(8,128)(2,1)S(1)} collective-permute-done((bf16[128,128]{1,0:T(8,128)(2,1)S(1)}, bf16[128,128]{1,0:T(8,128)(2,1)S(1)}, u32[]{:S(2)}, u32[]{:S(2)}) %collective-permute-start.15) | collective-permute-done | bytes 32800 | tf_op jit(solution)/shard_map/ppermute | solution.py:678
  48.8 1.5 %shard_map.110 = (f32[4,80,512]{2,1,0:T(8,128)S(1)}, bf16[4,80,512]{2,1,0:T(8,128)(2,1)S(1)}) custom-call(bf16[128,1152]{1,0:T(8,128)(2,1)S(1)} %copy-done.2, bf16[128,1152]{1,0:T(8,128)(2,1)S(1)} %collective-permute-done.5.refs_1_, bf16[128,1152]{1,0:T(8,128)(2,1)S(1)} %collective-permute-done.6.refs_2_, ...), custom_call_target="tpu_custom_call" | custom-call | flops 600000000 | bytes 4000000 | tf_op jit(solution)/shard_map/pallas_call | solution.py:510
  50.3 1.6 %collective-permute-done.16.got_ref = bf16[4,80,512]{2,1,0:T(8,128)(2,1)S(1)} collective-permute-done((bf16[4,80,512]{2,1,0:T(8,128)(2,1)S(1)}, bf16[4,80,512]{2,1,0:T(8,128)(2,1)S(1)}, u32[]{:S(2)}, u32[]{:S(2)}) %collective-permute-start.16) | collective-permute-done | bytes 327712 | tf_op jit(solution)/shard_map/ppermute | solution.py:678
  53.5 3.0 %collective-permute-start.32 = (bf16[80,256]{1,0:T(8,128)(2,1)S(1)}, bf16[80,256]{1,0:T(8,128)(2,1)S(1)}, u32[]{:S(2)}, u32[]{:S(2)}) collective-permute-start(bf16[80,256]{1,0:T(8,128)(2,1)S(1)} %get-tuple-element.85), channel_id=1, source_target_pairs={{0,6},{1,7},{2,4},{3,5},{4,2},{5,3},{6,0},{7,1},{8,14},{9,15},{10,... | collective-permute-start | bytes 122888 | tf_op jit(solution)/shard_map/ppermute | solution.py:678
  57.8 3.0 %collective-permute-start.19 = (bf16[80,256]{1,0:T(8,128)(2,1)S(1)}, bf16[80,256]{1,0:T(8,128)(2,1)S(1)}, u32[]{:S(2)}, u32[]{:S(2)}) collective-permute-start(bf16[80,256]{1,0:T(8,128)(2,1)S(1)} %get-tuple-element.81), channel_id=1, source_target_pairs={{0,6},{1,7},{2,4},{3,5},{4,2},{5,3},{6,0},{7,1},{8,14},{9,15},{10,... | collective-permute-start | bytes 122888 | tf_op jit(solution)/shard_map/ppermute | solution.py:678
  61.0 2.0 %collective-permute-start.34 = (bf16[80,256]{1,0:T(8,128)(2,1)S(1)}, bf16[80,256]{1,0:T(8,128)(2,1)S(1)}, u32[]{:S(2)}, u32[]{:S(2)}) collective-permute-start(bf16[80,256]{1,0:T(8,128)(2,1)S(1)} %shard_map.114.refs_0_), channel_id=1, source_target_pairs={{0,4},{1,5},{2,6},{3,7},{4,0},{5,1},{6,2},{7,3},{8,12},{9,13},{10,... | collective-permute-start | bytes 122888 | tf_op jit(solution)/shard_map/ppermute | solution.py:678
  62.9 2.4 %collective-permute-start.35 = (bf16[80,256]{1,0:T(8,128)(2,1)S(1)}, bf16[80,256]{1,0:T(8,128)(2,1)S(1)}, u32[]{:S(2)}, u32[]{:S(2)}) collective-permute-start(bf16[80,256]{1,0:T(8,128)(2,1)S(1)} %shard_map.114.refs_0_), channel_id=1, source_target_pairs={{0,6},{1,7},{2,4},{3,5},{4,2},{5,3},{6,0},{7,1},{8,14},{9,15},{10,... | collective-permute-start | bytes 122888 | tf_op jit(solution)/shard_map/ppermute | solution.py:678
  65.5 2.0 %collective-permute-start.21 = (bf16[80,256]{1,0:T(8,128)(2,1)S(1)}, bf16[80,256]{1,0:T(8,128)(2,1)S(1)}, u32[]{:S(2)}, u32[]{:S(2)}) collective-permute-start(bf16[80,256]{1,0:T(8,128)(2,1)S(1)} %shard_map.112.refs_0_), channel_id=1, source_target_pairs={{0,4},{1,5},{2,6},{3,7},{4,0},{5,1},{6,2},{7,3},{8,12},{9,13},{10,... | collective-permute-start | bytes 122888 | tf_op jit(solution)/shard_map/ppermute | solution.py:678
  67.4 2.4 %collective-permute-start.22 = (bf16[80,256]{1,0:T(8,128)(2,1)S(1)}, bf16[80,256]{1,0:T(8,128)(2,1)S(1)}, u32[]{:S(2)}, u32[]{:S(2)}) collective-permute-start(bf16[80,256]{1,0:T(8,128)(2,1)S(1)} %shard_map.112.refs_0_), channel_id=1, source_target_pairs={{0,6},{1,7},{2,4},{3,5},{4,2},{5,3},{6,0},{7,1},{8,14},{9,15},{10,... | collective-permute-start | bytes 122888 | tf_op jit(solution)/shard_map/ppermute | solution.py:678
  69.9 1.8 %collective-permute-start.37 = (bf16[320,256]{1,0:T(8,128)(2,1)S(1)}, bf16[320,256]{1,0:T(8,128)(2,1)S(1)}, u32[]{:S(2)}, u32[]{:S(2)}) collective-permute-start(bf16[320,256]{1,0:T(8,128)(2,1)S(1)} %shard_map.115.refs_0_), channel_id=1, source_target_pairs={{0,8},{8,0},{16,24},{24,16},{1,9},{9,1},{17,25},{25,17},{2,10},{10... | collective-permute-start | bytes 491528 | tf_op jit(solution)/shard_map/ppermute | solution.py:678
  71.8 1.5 %collective-permute-done.22.refs_3_ = bf16[80,256]{1,0:T(8,128)(2,1)S(1)} collective-permute-done((bf16[80,256]{1,0:T(8,128)(2,1)S(1)}, bf16[80,256]{1,0:T(8,128)(2,1)S(1)}, u32[]{:S(2)}, u32[]{:S(2)}) %collective-permute-start.22) | collective-permute-done | bytes 40992 | tf_op jit(solution)/shard_map/ppermute | solution.py:678
  73.9 1.5 %collective-permute-start.39 = (bf16[320,256]{1,0:T(8,128)(2,1)S(1)}, bf16[320,256]{1,0:T(8,128)(2,1)S(1)}, u32[]{:S(2)}, u32[]{:S(2)}) collective-permute-start(bf16[320,256]{1,0:T(8,128)(2,1)S(1)} %shard_map.115.refs_0_), channel_id=1, source_target_pairs={{0,16},{8,24},{16,0},{24,8},{1,17},{9,25},{17,1},{25,9},{2,18},{10... | collective-permute-start | bytes 491528 | tf_op jit(solution)/shard_map/ppermute | solution.py:678
  75.4 1.8 %collective-permute-start.24 = (bf16[320,256]{1,0:T(8,128)(2,1)S(1)}, bf16[320,256]{1,0:T(8,128)(2,1)S(1)}, u32[]{:S(2)}, u32[]{:S(2)}) collective-permute-start(bf16[320,256]{1,0:T(8,128)(2,1)S(1)} %shard_map.113.refs_2_.refs_0_), channel_id=1, source_target_pairs={{0,8},{8,0},{16,24},{24,16},{1,9},{9,1},{17,25},{25,17},{2,10},{10... | collective-permute-start | bytes 491528 | tf_op jit(solution)/shard_map/ppermute | solution.py:678
  77.3 3.1 %collective-permute-done.26.refs_2_.refs_4_ = bf16[320,256]{1,0:T(8,128)(2,1)S(1)} collective-permute-done((bf16[320,256]{1,0:T(8,128)(2,1)S(1)}, bf16[320,256]{1,0:T(8,128)(2,1)S(1)}, u32[]{:S(2)}, u32[]{:S(2)}) %collective-permute-start.26) | collective-permute-done | bytes 163872 | tf_op jit(solution)/shard_map/ppermute | solution.py:678
  80.5 1.8 %collective-permute-start.28 = (bf16[320,256]{1,0:T(8,128)(2,1)S(1)}, bf16[320,256]{1,0:T(8,128)(2,1)S(1)}, u32[]{:S(2)}, u32[]{:S(2)}) collective-permute-start(bf16[320,256]{1,0:T(8,128)(2,1)S(1)} %collective-permute-done.26.refs_2_.refs_4_), channel_id=1, source_target_pairs={{0,8},{8,0},{16,24},{24,16},{1,9},{9,1},{17,25},{25,17},{2,10},{10... | collective-permute-start | bytes 491528 | tf_op jit(solution)/shard_map/ppermute | solution.py:678
  82.2 1.8 %collective-permute-done.39.refs_2_.refs_4_ = bf16[320,256]{1,0:T(8,128)(2,1)S(1)} collective-permute-done((bf16[320,256]{1,0:T(8,128)(2,1)S(1)}, bf16[320,256]{1,0:T(8,128)(2,1)S(1)}, u32[]{:S(2)}, u32[]{:S(2)}) %collective-permute-start.39) | collective-permute-done | bytes 163872 | tf_op jit(solution)/shard_map/ppermute | solution.py:678
  84.6 2.4 %collective-permute-done.41.refs_6_ = bf16[320,256]{1,0:T(8,128)(2,1)S(1)} collective-permute-done((bf16[320,256]{1,0:T(8,128)(2,1)S(1)}, bf16[320,256]{1,0:T(8,128)(2,1)S(1)}, u32[]{:S(2)}, u32[]{:S(2)}) %collective-permute-start.41) | collective-permute-done | bytes 163872 | tf_op jit(solution)/shard_map/ppermute | solution.py:678
  87.5 1.4 %shard_map.116 = (f32[2048,512]{1,0:T(8,128)}, f32[512,128]{1,0:T(8,128)}) custom-call(bf16[320,256]{1,0:T(8,128)(2,1)S(1)} %shard_map.115.refs_0_, bf16[320,256]{1,0:T(8,128)(2,1)S(1)} %collective-permute-done.36.refs_1_, bf16[320,256]{1,0:T(8,128)(2,1)S(1)} %shard_map.113.refs_2_.refs_0_, bf16[320,256]{1,0:T(8,128)(2,1)S(1)} %collective-permute-done.23.refs_3_.refs_1_), custom_call_target="tpu_custom_call" | custom-call | flops 1000000 | bytes 8000000 | tf_op jit(solution)/shard_map/pallas_call | solution.py:639
  88.9 1.5 %shard_map.117 = (f32[2048,512]{1,0:T(8,128)}, f32[512,128]{1,0:T(8,128)}) custom-call(bf16[320,256]{1,0:T(8,128)(2,1)S(1)} %collective-permute-done.37.refs_0_.refs_2_, bf16[320,256]{1,0:T(8,128)(2,1)S(1)} %collective-permute-done.38.refs_1_.refs_3_, ...), custom_call_target="tpu_custom_call", output_to_operand_aliasing={{0}: (4, {}), {1}: (5, {})} | custom-call | flops 1000000 | bytes 8000000 | tf_op jit(solution)/shard_map/pallas_call | solution.py:639
  90.4 1.4 %shard_map.118 = (f32[2048,512]{1,0:T(8,128)}, f32[512,128]{1,0:T(8,128)}) custom-call(bf16[320,256]{1,0:T(8,128)(2,1)S(1)} %collective-permute-done.24.refs_0_.refs_2_, bf16[320,256]{1,0:T(8,128)(2,1)S(1)} %collective-permute-done.25.refs_1_.refs_3_, ...), custom_call_target="tpu_custom_call", output_to_operand_aliasing={{0}: (4, {}), {1}: (5, {})} | custom-call | flops 1000000 | bytes 8000000 | tf_op jit(solution)/shard_map/pallas_call | solution.py:639
  (79 shorter events, 17.5 us)
Async XLA Ops:
  9.5 5.6 %collective-permute-start.1 = (bf16[256,128]{1,0:T(8,128)(2,1)S(1)}, bf16[256,128]{1,0:T(8,128)(2,1)S(1)}, u32[]{:S(2)}, u32[]{:S(2)}) collective-permute-start(bf16[256,128]{1,0:T(8,128)(2,1)S(1)} %shard_map.103.pair_ref), channel_id=1, source_target_pairs={{0,2},{1,9},{2,0},{3,11},{4,6},{5,13},{6,4},{7,15},{8,10},{9,1},{1... | collective-permute-start | bytes 196616 | tf_op jit(solution)/shard_map/ppermute | solution.py:251
  12.5 5.9 %collective-permute-start.2 = (bf16[256,128]{1,0:T(8,128)(2,1)S(1)}, bf16[256,128]{1,0:T(8,128)(2,1)S(1)}, u32[]{:S(2)}, u32[]{:S(2)}) collective-permute-start(bf16[256,128]{1,0:T(8,128)(2,1)S(1)} %shard_map.103.pair_ref), channel_id=1, source_target_pairs={{0,4},{1,17},{2,6},{3,19},{4,0},{5,21},{6,2},{7,23},{8,12},{9,25},... | collective-permute-start | bytes 196616 | tf_op jit(solution)/shard_map/ppermute | solution.py:251
  15.0 6.1 %collective-permute-start.3 = (bf16[256,128]{1,0:T(8,128)(2,1)S(1)}, bf16[256,128]{1,0:T(8,128)(2,1)S(1)}, u32[]{:S(2)}, u32[]{:S(2)}) collective-permute-start(bf16[256,128]{1,0:T(8,128)(2,1)S(1)} %shard_map.103.pair_ref), channel_id=1, source_target_pairs={{0,6},{1,25},{2,4},{3,27},{4,2},{5,29},{6,0},{7,31},{8,14},{9,17},... | collective-permute-start | bytes 196616 | tf_op jit(solution)/shard_map/ppermute | solution.py:251
  21.2 22.7 %collective-permute-start.5 = (bf16[128,1152]{1,0:T(8,128)(2,1)}, bf16[128,1152]{1,0:T(8,128)(2,1)S(1)}, u32[]{:S(2)}, u32[]{:S(2)}) collective-permute-start(bf16[128,1152]{1,0:T(8,128)(2,1)} %get-tuple-element.57), channel_id=1, source_target_pairs={{0,8},{8,0},{16,24},{24,16},{1,9},{9,1},{17,25},{25,17},{2,10},{10... | collective-permute-start | bytes 884744 | tf_op jit(solution)/shard_map/ppermute | solution.py:678
  22.8 24.4 %collective-permute-start.6 = (bf16[128,1152]{1,0:T(8,128)(2,1)}, bf16[128,1152]{1,0:T(8,128)(2,1)S(1)}, u32[]{:S(2)}, u32[]{:S(2)}) collective-permute-start(bf16[128,1152]{1,0:T(8,128)(2,1)} %get-tuple-element.58), channel_id=1, source_target_pairs={{0,16},{8,24},{16,0},{24,8},{1,17},{9,25},{17,1},{25,9},{2,18},{10... | collective-permute-start | bytes 884744 | tf_op jit(solution)/shard_map/ppermute | solution.py:678
  24.3 22.9 %collective-permute-start.7 = (bf16[128,1152]{1,0:T(8,128)(2,1)}, bf16[128,1152]{1,0:T(8,128)(2,1)S(1)}, u32[]{:S(2)}, u32[]{:S(2)}) collective-permute-start(bf16[128,1152]{1,0:T(8,128)(2,1)} %get-tuple-element.59), channel_id=1, source_target_pairs={{0,24},{8,16},{16,8},{24,0},{1,25},{9,17},{17,9},{25,1},{2,26},{10... | collective-permute-start | bytes 884744 | tf_op jit(solution)/shard_map/ppermute | solution.py:678
  27.5 5.4 %collective-permute-start.11 = (f32[16,128]{1,0:T(8,128)S(1)}, f32[16,128]{1,0:T(8,128)S(1)}, u32[]{:S(2)}, u32[]{:S(2)}) collective-permute-start(f32[16,128]{1,0:T(8,128)S(1)} %shard_map.106.pair_ref), channel_id=1, source_target_pairs={{0,6},{1,25},{2,4},{3,27},{4,2},{5,29},{6,0},{7,31},{8,14},{9,17},... | collective-permute-start | bytes 24584 | tf_op jit(solution)/shard_map/ppermute | solution.py:251
  41.0 6.3 %collective-permute-start.13 = (bf16[128,128]{1,0:T(8,128)(2,1)S(1)}, bf16[128,128]{1,0:T(8,128)(2,1)S(1)}, u32[]{:S(2)}, u32[]{:S(2)}) collective-permute-start(bf16[128,128]{1,0:T(8,128)(2,1)S(1)} %shard_map.108.raw_ref.refs_4_), channel_id=1, source_target_pairs={{0,8},{8,0},{16,24},{24,16},{1,9},{9,1},{17,25},{25,17},{2,10},{10... | collective-permute-start | bytes 98312 | tf_op jit(solution)/shard_map/ppermute | solution.py:678
  41.5 5.7 %collective-permute-start.14 = (bf16[128,128]{1,0:T(8,128)(2,1)S(1)}, bf16[128,128]{1,0:T(8,128)(2,1)S(1)}, u32[]{:S(2)}, u32[]{:S(2)}) collective-permute-start(bf16[128,128]{1,0:T(8,128)(2,1)S(1)} %shard_map.108.raw_ref.refs_4_), channel_id=1, source_target_pairs={{0,16},{8,24},{16,0},{24,8},{1,17},{9,25},{17,1},{25,9},{2,18},{10... | collective-permute-start | bytes 98312 | tf_op jit(solution)/shard_map/ppermute | solution.py:678
  52.0 5.8 %collective-permute-start.30 = (bf16[80,256]{1,0:T(8,128)(2,1)S(1)}, bf16[80,256]{1,0:T(8,128)(2,1)S(1)}, u32[]{:S(2)}, u32[]{:S(2)}) collective-permute-start(bf16[80,256]{1,0:T(8,128)(2,1)S(1)} %get-tuple-element.83), channel_id=1, source_target_pairs={{0,2},{1,3},{2,0},{3,1},{4,6},{5,7},{6,4},{7,5},{8,10},{9,11},{10,... | collective-permute-start | bytes 122888 | tf_op jit(solution)/shard_map/ppermute | solution.py:678
  52.1 8.8 %collective-permute-start.31 = (bf16[80,256]{1,0:T(8,128)(2,1)S(1)}, bf16[80,256]{1,0:T(8,128)(2,1)S(1)}, u32[]{:S(2)}, u32[]{:S(2)}) collective-permute-start(bf16[80,256]{1,0:T(8,128)(2,1)S(1)} %get-tuple-element.84), channel_id=1, source_target_pairs={{0,4},{1,5},{2,6},{3,7},{4,0},{5,1},{6,2},{7,3},{8,12},{9,13},{10,... | collective-permute-start | bytes 122888 | tf_op jit(solution)/shard_map/ppermute | solution.py:678
  53.5 7.4 %collective-permute-start.32 = (bf16[80,256]{1,0:T(8,128)(2,1)S(1)}, bf16[80,256]{1,0:T(8,128)(2,1)S(1)}, u32[]{:S(2)}, u32[]{:S(2)}) collective-permute-start(bf16[80,256]{1,0:T(8,128)(2,1)S(1)} %get-tuple-element.85), channel_id=1, source_target_pairs={{0,6},{1,7},{2,4},{3,5},{4,2},{5,3},{6,0},{7,1},{8,14},{9,15},{10,... | collective-permute-start | bytes 122888 | tf_op jit(solution)/shard_map/ppermute | solution.py:678
  56.5 6.5 %collective-permute-start.17 = (bf16[80,256]{1,0:T(8,128)(2,1)S(1)}, bf16[80,256]{1,0:T(8,128)(2,1)S(1)}, u32[]{:S(2)}, u32[]{:S(2)}) collective-permute-start(bf16[80,256]{1,0:T(8,128)(2,1)S(1)} %get-tuple-element.79), channel_id=1, source_target_pairs={{0,2},{1,3},{2,0},{3,1},{4,6},{5,7},{6,4},{7,5},{8,10},{9,11},{10,... | collective-permute-start | bytes 122888 | tf_op jit(solution)/shard_map/ppermute | solution.py:678
  56.5 8.9 %collective-permute-start.18 = (bf16[80,256]{1,0:T(8,128)(2,1)S(1)}, bf16[80,256]{1,0:T(8,128)(2,1)S(1)}, u32[]{:S(2)}, u32[]{:S(2)}) collective-permute-start(bf16[80,256]{1,0:T(8,128)(2,1)S(1)} %get-tuple-element.80), channel_id=1, source_target_pairs={{0,4},{1,5},{2,6},{3,7},{4,0},{5,1},{6,2},{7,3},{8,12},{9,13},{10,... | collective-permute-start | bytes 122888 | tf_op jit(solution)/shard_map/ppermute | solution.py:678
  57.8 7.5 %collective-permute-start.19 = (bf16[80,256]{1,0:T(8,128)(2,1)S(1)}, bf16[80,256]{1,0:T(8,128)(2,1)S(1)}, u32[]{:S(2)}, u32[]{:S(2)}) collective-permute-start(bf16[80,256]{1,0:T(8,128)(2,1)S(1)} %get-tuple-element.81), channel_id=1, source_target_pairs={{0,6},{1,7},{2,4},{3,5},{4,2},{5,3},{6,0},{7,1},{8,14},{9,15},{10,... | collective-permute-start | bytes 122888 | tf_op jit(solution)/shard_map/ppermute | solution.py:678
  60.9 6.5 %collective-permute-start.33 = (bf16[80,256]{1,0:T(8,128)(2,1)S(1)}, bf16[80,256]{1,0:T(8,128)(2,1)S(1)}, u32[]{:S(2)}, u32[]{:S(2)}) collective-permute-start(bf16[80,256]{1,0:T(8,128)(2,1)S(1)} %shard_map.114.refs_0_), channel_id=1, source_target_pairs={{0,2},{1,3},{2,0},{3,1},{4,6},{5,7},{6,4},{7,5},{8,10},{9,11},{10,... | collective-permute-start | bytes 122888 | tf_op jit(solution)/shard_map/ppermute | solution.py:678
  61.0 8.9 %collective-permute-start.34 = (bf16[80,256]{1,0:T(8,128)(2,1)S(1)}, bf16[80,256]{1,0:T(8,128)(2,1)S(1)}, u32[]{:S(2)}, u32[]{:S(2)}) collective-permute-start(bf16[80,256]{1,0:T(8,128)(2,1)S(1)} %shard_map.114.refs_0_), channel_id=1, source_target_pairs={{0,4},{1,5},{2,6},{3,7},{4,0},{5,1},{6,2},{7,3},{8,12},{9,13},{10,... | collective-permute-start | bytes 122888 | tf_op jit(solution)/shard_map/ppermute | solution.py:678
  62.9 6.9 %collective-permute-start.35 = (bf16[80,256]{1,0:T(8,128)(2,1)S(1)}, bf16[80,256]{1,0:T(8,128)(2,1)S(1)}, u32[]{:S(2)}, u32[]{:S(2)}) collective-permute-start(bf16[80,256]{1,0:T(8,128)(2,1)S(1)} %shard_map.114.refs_0_), channel_id=1, source_target_pairs={{0,6},{1,7},{2,4},{3,5},{4,2},{5,3},{6,0},{7,1},{8,14},{9,15},{10,... | collective-permute-start | bytes 122888 | tf_op jit(solution)/shard_map/ppermute | solution.py:678
  65.4 6.4 %collective-permute-start.20 = (bf16[80,256]{1,0:T(8,128)(2,1)S(1)}, bf16[80,256]{1,0:T(8,128)(2,1)S(1)}, u32[]{:S(2)}, u32[]{:S(2)}) collective-permute-start(bf16[80,256]{1,0:T(8,128)(2,1)S(1)} %shard_map.112.refs_0_), channel_id=1, source_target_pairs={{0,2},{1,3},{2,0},{3,1},{4,6},{5,7},{6,4},{7,5},{8,10},{9,11},{10,... | collective-permute-start | bytes 122888 | tf_op jit(solution)/shard_map/ppermute | solution.py:678
  65.5 6.3 %collective-permute-start.21 = (bf16[80,256]{1,0:T(8,128)(2,1)S(1)}, bf16[80,256]{1,0:T(8,128)(2,1)S(1)}, u32[]{:S(2)}, u32[]{:S(2)}) collective-permute-start(bf16[80,256]{1,0:T(8,128)(2,1)S(1)} %shard_map.112.refs_0_), channel_id=1, source_target_pairs={{0,4},{1,5},{2,6},{3,7},{4,0},{5,1},{6,2},{7,3},{8,12},{9,13},{10,... | collective-permute-start | bytes 122888 | tf_op jit(solution)/shard_map/ppermute | solution.py:678
  67.4 5.8 %collective-permute-start.22 = (bf16[80,256]{1,0:T(8,128)(2,1)S(1)}, bf16[80,256]{1,0:T(8,128)(2,1)S(1)}, u32[]{:S(2)}, u32[]{:S(2)}) collective-permute-start(bf16[80,256]{1,0:T(8,128)(2,1)S(1)} %shard_map.112.refs_0_), channel_id=1, source_target_pairs={{0,6},{1,7},{2,4},{3,5},{4,2},{5,3},{6,0},{7,1},{8,14},{9,15},{10,... | collective-permute-start | bytes 122888 | tf_op jit(solution)/shard_map/ppermute | solution.py:678
  69.9 5.5 %collective-permute-start.36 = (bf16[320,256]{1,0:T(8,128)(2,1)S(1)}, bf16[320,256]{1,0:T(8,128)(2,1)S(1)}, u32[]{:S(2)}, u32[]{:S(2)}) collective-permute-start(bf16[320,256]{1,0:T(8,128)(2,1)S(1)} %shard_map.115.refs_0_), channel_id=1, source_target_pairs={{0,1},{1,0},{2,3},{3,2},{4,5},{5,4},{6,7},{7,6},{8,9},{9,8},{10,11... | collective-permute-start | bytes 491528 | tf_op jit(solution)/shard_map/ppermute | solution.py:678
  69.9 7.2 %collective-permute-start.37 = (bf16[320,256]{1,0:T(8,128)(2,1)S(1)}, bf16[320,256]{1,0:T(8,128)(2,1)S(1)}, u32[]{:S(2)}, u32[]{:S(2)}) collective-permute-start(bf16[320,256]{1,0:T(8,128)(2,1)S(1)} %shard_map.115.refs_0_), channel_id=1, source_target_pairs={{0,8},{8,0},{16,24},{24,16},{1,9},{9,1},{17,25},{25,17},{2,10},{10... | collective-permute-start | bytes 491528 | tf_op jit(solution)/shard_map/ppermute | solution.py:678
  73.3 7.1 %collective-permute-start.26 = (bf16[320,256]{1,0:T(8,128)(2,1)S(1)}, bf16[320,256]{1,0:T(8,128)(2,1)S(1)}, u32[]{:S(2)}, u32[]{:S(2)}) collective-permute-start(bf16[320,256]{1,0:T(8,128)(2,1)S(1)} %shard_map.113.refs_2_.refs_0_), channel_id=1, source_target_pairs={{0,16},{8,24},{16,0},{24,8},{1,17},{9,25},{17,1},{25,9},{2,18},{10... | collective-permute-start | bytes 491528 | tf_op jit(solution)/shard_map/ppermute | solution.py:678
  73.9 10.1 %collective-permute-start.39 = (bf16[320,256]{1,0:T(8,128)(2,1)S(1)}, bf16[320,256]{1,0:T(8,128)(2,1)S(1)}, u32[]{:S(2)}, u32[]{:S(2)}) collective-permute-start(bf16[320,256]{1,0:T(8,128)(2,1)S(1)} %shard_map.115.refs_0_), channel_id=1, source_target_pairs={{0,16},{8,24},{16,0},{24,8},{1,17},{9,25},{17,1},{25,9},{2,18},{10... | collective-permute-start | bytes 491528 | tf_op jit(solution)/shard_map/ppermute | solution.py:678
  75.4 8.6 %collective-permute-start.24 = (bf16[320,256]{1,0:T(8,128)(2,1)S(1)}, bf16[320,256]{1,0:T(8,128)(2,1)S(1)}, u32[]{:S(2)}, u32[]{:S(2)}) collective-permute-start(bf16[320,256]{1,0:T(8,128)(2,1)S(1)} %shard_map.113.refs_2_.refs_0_), channel_id=1, source_target_pairs={{0,8},{8,0},{16,24},{24,16},{1,9},{9,1},{17,25},{25,17},{2,10},{10... | collective-permute-start | bytes 491528 | tf_op jit(solution)/shard_map/ppermute | solution.py:678
  77.2 7.3 %collective-permute-start.38 = (bf16[320,256]{1,0:T(8,128)(2,1)S(1)}, bf16[320,256]{1,0:T(8,128)(2,1)S(1)}, u32[]{:S(2)}, u32[]{:S(2)}) collective-permute-start(bf16[320,256]{1,0:T(8,128)(2,1)S(1)} %collective-permute-done.37.refs_0_.refs_2_), channel_id=1, source_target_pairs={{0,1},{1,0},{2,3},{3,2},{4,5},{5,4},{6,7},{7,6},{8,9},{9,8},{10,11... | collective-permute-start | bytes 491528 | tf_op jit(solution)/shard_map/ppermute | solution.py:678
  77.2 9.8 %collective-permute-start.41 = (bf16[320,256]{1,0:T(8,128)(2,1)S(1)}, bf16[320,256]{1,0:T(8,128)(2,1)S(1)}, u32[]{:S(2)}, u32[]{:S(2)}) collective-permute-start(bf16[320,256]{1,0:T(8,128)(2,1)S(1)} %collective-permute-done.37.refs_0_.refs_2_), channel_id=1, source_target_pairs={{0,16},{8,24},{16,0},{24,8},{1,17},{9,25},{17,1},{25,9},{2,18},{10... | collective-permute-start | bytes 491528 | tf_op jit(solution)/shard_map/ppermute | solution.py:678
  80.5 6.5 %collective-permute-start.28 = (bf16[320,256]{1,0:T(8,128)(2,1)S(1)}, bf16[320,256]{1,0:T(8,128)(2,1)S(1)}, u32[]{:S(2)}, u32[]{:S(2)}) collective-permute-start(bf16[320,256]{1,0:T(8,128)(2,1)S(1)} %collective-permute-done.26.refs_2_.refs_4_), channel_id=1, source_target_pairs={{0,8},{8,0},{16,24},{24,16},{1,9},{9,1},{17,25},{25,17},{2,10},{10... | collective-permute-start | bytes 491528 | tf_op jit(solution)/shard_map/ppermute | solution.py:678
  84.0 6.4 %collective-permute-start.25 = (bf16[320,256]{1,0:T(8,128)(2,1)S(1)}, bf16[320,256]{1,0:T(8,128)(2,1)S(1)}, u32[]{:S(2)}, u32[]{:S(2)}) collective-permute-start(bf16[320,256]{1,0:T(8,128)(2,1)S(1)} %collective-permute-done.24.refs_0_.refs_2_), channel_id=1, source_target_pairs={{0,1},{1,0},{2,3},{3,2},{4,5},{5,4},{6,7},{7,6},{8,9},{9,8},{10,11... | collective-permute-start | bytes 491528 | tf_op jit(solution)/shard_map/ppermute | solution.py:678
  84.5 5.9 %collective-permute-start.27 = (bf16[320,256]{1,0:T(8,128)(2,1)S(1)}, bf16[320,256]{1,0:T(8,128)(2,1)S(1)}, u32[]{:S(2)}, u32[]{:S(2)}) collective-permute-start(bf16[320,256]{1,0:T(8,128)(2,1)S(1)} %collective-permute-done.26.refs_2_.refs_4_), channel_id=1, source_target_pairs={{0,1},{1,0},{2,3},{3,2},{4,5},{5,4},{6,7},{7,6},{8,9},{9,8},{10,11... | collective-permute-start | bytes 491528 | tf_op jit(solution)/shard_map/ppermute | solution.py:678
  86.9 6.0 %collective-permute-start.29 = (bf16[320,256]{1,0:T(8,128)(2,1)S(1)}, bf16[320,256]{1,0:T(8,128)(2,1)S(1)}, u32[]{:S(2)}, u32[]{:S(2)}) collective-permute-start(bf16[320,256]{1,0:T(8,128)(2,1)S(1)} %collective-permute-done.28.refs_6_), channel_id=1, source_target_pairs={{0,1},{1,0},{2,3},{3,2},{4,5},{5,4},{6,7},{7,6},{8,9},{9,8},{10,11... | collective-permute-start | bytes 491528 | tf_op jit(solution)/shard_map/ppermute | solution.py:678
  (14 other events, 96.1 us)

commit v9 on v5

--- a/solution.py
+++ b/solution.py
@@ -573,8 +573,8 @@
         refs = refs[2:]
     g_in_hbm, g_out_hbm, *refs = refs
     if closing:
-        g_mix_ref, *refs = refs
-    stage, strip_stage, sems, strip_sems = refs
+        g_mix_hbm, *refs = refs
+    stage, strip_stage, mix_stage, sems, strip_sems, mix_sems = refs
     me_blk, me_dp = lax.axis_index("blk"), lax.axis_index("dp")
     copies = []
 
@@ -602,6 +602,7 @@
                     strip_sems,
                 )
     if closing:
+        slot = 0
         for core in range(2):
             for z in range(slots):
                 strip = z * lay.rows + lay.top
@@ -614,7 +615,14 @@
                     ]
                     while len(terms) > 1:
                         terms = [terms[t] + terms[t + 1] for t in range(0, len(terms), 2)]
-                    g_mix_ref[pl.ds(owner * lay.mix_rows + start, rows), :] = terms[0]
+                    mix_stage[slot, :rows, :] = terms[0]
+                    row = owner * lay.mix_rows + start
+                    copy = pltpu.make_async_copy(
+                        mix_stage.at[slot, :rows], g_mix_hbm.at[pl.ds(row, rows), :], mix_sems.at[slot]
+                    )
+                    copy.start()
+                    copies.append(copy)
+                    slot += 1
     for copy in copies:
         copy.wait()
 
@@ -625,7 +633,8 @@
     specs = [ANY, ANY]
     if closing:
         outs.append(shape((lanes, 128), F32))
-        specs.append(VMEM)
+        specs.append(ANY)
+    blocks = lay.peers * lay.mix_blocks
     return pl.pallas_call(
         functools.partial(finish_kernel, lay, tuple(parts), bool(done), tuple(fresh), closing),
         in_specs=[VMEM] * len(parts) + [ANY] * len(done),
@@ -634,8 +643,10 @@
         scratch_shapes=[
             pltpu.VMEM((slots, lay.in_rows, lay.width // HALVES), F32),
             pltpu.VMEM((slots, lay.out_rows, 128), F32),
+            pltpu.VMEM((blocks, lay.strip, 128), F32),
             pltpu.SemaphoreType.DMA((slots,)),
             pltpu.SemaphoreType.DMA((slots,)),
+            pltpu.SemaphoreType.DMA((blocks,)),
         ],
         input_output_aliases={len(parts) + i: i for i in range(len(done))},
         compiler_params=params(24),

time: 89.2 us -> 89.3 us (level)
  transfers between devices with their start and end apart: 43 -> 43, of which waited for: 17 -> 17; matrix products, arithmetic and copies ran while one was open for 0% -> 0% of each run, Pallas kernels for 10% -> 11%
where the time goes in v9:
time: 89.3 us; the launch traced here: 89.2 us
  starting transfers between devices  43.9 us (49%)
  waiting for transfers between devices  24.6 us (28%)
  Pallas kernels  19.8 us (22%)
    ppermute x37, starting transfers between devices, swap(): return lax.ppermute(block, axis, [(src, src ^ bit) for src in range(size)])  36.2 us
    ppermute x37, waiting for transfers between devices, swap(): return lax.ppermute(block, axis, [(src, src ^ bit) for src in range(size)])  13.1 us
    ppermute x6, waiting for transfers between devices, cross(): got.append(lax.ppermute(pair, ('blk', 'dp'), routes))  11.5 us
    ppermute x6, starting transfers between devices, cross(): got.append(lax.ppermute(pair, ('blk', 'dp'), routes))  7.73 us
    pallas_call x1, Pallas kernels, encode(): pl.pallas_call(functools.partial(encode_kernel, freqs, size, rounds), in_...  7.38 us
    pallas_call x5, Pallas kernels, finish(): pl.pallas_call(functools.partial(finish_kernel, lay, tuple(parts), bool(d...  6.55 us
    pallas_call x1, Pallas kernels, lower(): pl.pallas_call(functools.partial(lower_kernel, freqs), in_specs=[VMEM] *...  2.07 us
  transfers between devices with their start and end apart: 43, of which 17 were waited for; matrix products, arithmetic and copies ran while one was open for 0% of the time, Pallas kernels for 11%

profile of v9, /device:TPU:0, one launch (start us, length us, event | category | flops | bytes accessed | tf_op | source)
XLA Modules:
  0.0 89.2 jit_solution(12783481169951513846)
XLA Ops:
  0.7 7.4 %shard_map.102 = (bf16[128,1152]{1,0:T(8,128)(2,1)}, bf16[128,1152]{1,0:T(8,128)(2,1)}, bf16[128,1152]{1,0:T(8,128)(2,1)}, bf16[128,1152]{1,0:T(8,128)(2,1)}, bf...) custom-call(bf16[128,64,256]{2,1,0:T(8,128)(2,1)} %patch_hbm.1, ...), custom_call_target="tpu_custom_call" | custom-call | flops 3000000000 | bytes 14000000 | tf_op jit(solution)/shard_map/pallas_call | solution.py:191
  9.5 5.0 %collective-permute-start.3 = (bf16[256,128]{1,0:T(8,128)(2,1)S(1)}, bf16[256,128]{1,0:T(8,128)(2,1)S(1)}, u32[]{:S(2)}, u32[]{:S(2)}) collective-permute-start(bf16[256,128]{1,0:T(8,128)(2,1)S(1)} %shard_map.103.pair_ref), channel_id=1, source_target_pairs={{0,6},{1,25},{2,4},{3,27},{4,2},{5,29},{6,0},{7,31},{8,14},{9,17},... | collective-permute-start | bytes 196616 | tf_op jit(solution)/shard_map/ppermute | solution.py:251
  15.1 1.7 %collective-permute-done.3.refs_2_ = bf16[256,128]{1,0:T(8,128)(2,1)S(1)} collective-permute-done((bf16[256,128]{1,0:T(8,128)(2,1)S(1)}, bf16[256,128]{1,0:T(8,128)(2,1)S(1)}, u32[]{:S(2)}, u32[]{:S(2)}) %collective-permute-start.3) | collective-permute-done | bytes 65568 | tf_op jit(solution)/shard_map/ppermute | solution.py:251
  16.8 2.8 %collective-permute-done.2.refs_1_ = bf16[256,128]{1,0:T(8,128)(2,1)S(1)} collective-permute-done((bf16[256,128]{1,0:T(8,128)(2,1)S(1)}, bf16[256,128]{1,0:T(8,128)(2,1)S(1)}, u32[]{:S(2)}, u32[]{:S(2)}) %collective-permute-start.2) | collective-permute-done | bytes 65568 | tf_op jit(solution)/shard_map/ppermute | solution.py:251
  19.7 1.6 %collective-permute-start.5 = (bf16[128,1152]{1,0:T(8,128)(2,1)}, bf16[128,1152]{1,0:T(8,128)(2,1)S(1)}, u32[]{:S(2)}, u32[]{:S(2)}) collective-permute-start(bf16[128,1152]{1,0:T(8,128)(2,1)} %get-tuple-element.56), channel_id=1, source_target_pairs={{0,8},{8,0},{16,24},{24,16},{1,9},{9,1},{17,25},{25,17},{2,10},{10... | collective-permute-start | bytes 884744 | tf_op jit(solution)/shard_map/ppermute | solution.py:677
  21.3 1.5 %collective-permute-start.6 = (bf16[128,1152]{1,0:T(8,128)(2,1)}, bf16[128,1152]{1,0:T(8,128)(2,1)S(1)}, u32[]{:S(2)}, u32[]{:S(2)}) collective-permute-start(bf16[128,1152]{1,0:T(8,128)(2,1)} %get-tuple-element.57), channel_id=1, source_target_pairs={{0,16},{8,24},{16,0},{24,8},{1,17},{9,25},{17,1},{25,9},{2,18},{10... | collective-permute-start | bytes 884744 | tf_op jit(solution)/shard_map/ppermute | solution.py:677
  23.3 1.3 %shard_map.105 = (f32[128,128]{1,0:T(8,128)S(1)}, f32[8,128]{1,0:T(8,128)S(1)}, f32[1,128]{1,0:T(1,128)}, bf16[512,128]{1,0:T(8,128)(2,1)S(1)}, bf16[1024,128]{1,0:T(8,128)(2,1)S(1)}) custom-call(s32[1,128]{1,0:T(1,128)S(1)} %bitcast.3, s32[1,128]{1,0:T(1,128)S(1)} %bitcast.4, bf16[128,128]{1,0:T(8,128)(2,1)S(1)} %get-tuple-element.50.own_ref.units_ref, ...), custom_call_target="tpu_custom_call" | custom-call | flops 400000000 | bytes 1000000 | tf_op jit(solution)/shard_map/pallas_call | solution.py:329
  25.8 1.6 %collective-permute-start.11 = (f32[16,128]{1,0:T(8,128)S(1)}, f32[16,128]{1,0:T(8,128)S(1)}, u32[]{:S(2)}, u32[]{:S(2)}) collective-permute-start(f32[16,128]{1,0:T(8,128)S(1)} %shard_map.106.pair_ref), channel_id=1, source_target_pairs={{0,6},{1,25},{2,4},{3,27},{4,2},{5,29},{6,0},{7,31},{8,14},{9,17},... | collective-permute-start | bytes 24584 | tf_op jit(solution)/shard_map/ppermute | solution.py:251
  27.9 3.4 %collective-permute-done.11.refs_2_ = f32[16,128]{1,0:T(8,128)S(1)} collective-permute-done((f32[16,128]{1,0:T(8,128)S(1)}, f32[16,128]{1,0:T(8,128)S(1)}, u32[]{:S(2)}, u32[]{:S(2)}) %collective-permute-start.11) | collective-permute-done | bytes 8224 | tf_op jit(solution)/shard_map/ppermute | solution.py:251
  32.0 3.0 %collective-permute-done.9.refs_0_ = f32[16,128]{1,0:T(8,128)S(1)} collective-permute-done((f32[16,128]{1,0:T(8,128)S(1)}, f32[16,128]{1,0:T(8,128)S(1)}, u32[]{:S(2)}, u32[]{:S(2)}) %collective-permute-start.9) | collective-permute-done | bytes 8224 | tf_op jit(solution)/shard_map/ppermute | solution.py:251
  34.9 4.0 %collective-permute-start.12 = (f32[48,128]{1,0:T(8,128)S(1)}, f32[48,128]{1,0:T(8,128)S(1)}, u32[]{:S(2)}, u32[]{:S(2)}) collective-permute-start(f32[48,128]{1,0:T(8,128)S(1)} %shard_map.107.got_ref), channel_id=1, source_target_pairs={{0,1},{1,0},{2,3},{3,2},{4,5},{5,4},{6,7},{7,6},{8,9},{9,8},{10,11... | collective-permute-start | bytes 73736 | tf_op jit(solution)/shard_map/ppermute | solution.py:677
  40.6 1.5 %collective-permute-start.15 = (bf16[128,128]{1,0:T(8,128)(2,1)S(1)}, bf16[128,128]{1,0:T(8,128)(2,1)S(1)}, u32[]{:S(2)}, u32[]{:S(2)}) collective-permute-start(bf16[128,128]{1,0:T(8,128)(2,1)S(1)} %shard_map.108.raw_ref.refs_4_), channel_id=1, source_target_pairs={{0,24},{8,16},{16,8},{24,0},{1,25},{9,17},{17,9},{25,1},{2,26},{10... | collective-permute-start | bytes 98312 | tf_op jit(solution)/shard_map/ppermute | solution.py:677
  42.1 1.5 %collective-permute-start.14 = (bf16[128,128]{1,0:T(8,128)(2,1)S(1)}, bf16[128,128]{1,0:T(8,128)(2,1)S(1)}, u32[]{:S(2)}, u32[]{:S(2)}) collective-permute-start(bf16[128,128]{1,0:T(8,128)(2,1)S(1)} %shard_map.108.raw_ref.refs_4_), channel_id=1, source_target_pairs={{0,16},{8,24},{16,0},{24,8},{1,17},{9,25},{17,1},{25,9},{2,18},{10... | collective-permute-start | bytes 98312 | tf_op jit(solution)/shard_map/ppermute | solution.py:677
  44.2 2.1 %shard_map.109.refs_9_ = f32[256,128]{1,0:T(8,128)S(1)} custom-call(bf16[128,128]{1,0:T(8,128)(2,1)S(1)} %shard_map.108.raw_ref.refs_4_, f32[128,128]{1,0:T(8,128)S(1)} %get-tuple-element.69.rscale_ref, bf16[2048,512]{1,0:T(8,128)(2,1)S(1)} %get-tuple-element.70.in_w, bf16[512,128]{1,0:T(8,128)(2,1)S(1)} %get-tuple-element.68.out_w.refs_8_, ...), custom_call_target="tpu_custom_call" | custom-call | flops 1000000000 | bytes 7000000 | tf_op jit(solution)/shard_map/pallas_call | solution.py:434
  46.3 1.2 %collective-permute-done.13.refs_5_ = bf16[128,128]{1,0:T(8,128)(2,1)S(1)} collective-permute-done((bf16[128,128]{1,0:T(8,128)(2,1)S(1)}, bf16[128,128]{1,0:T(8,128)(2,1)S(1)}, u32[]{:S(2)}, u32[]{:S(2)}) %collective-permute-start.13) | collective-permute-done | bytes 32800 | tf_op jit(solution)/shard_map/ppermute | solution.py:677
  47.5 1.5 %shard_map.110 = (f32[4,80,512]{2,1,0:T(8,128)S(1)}, bf16[4,80,512]{2,1,0:T(8,128)(2,1)S(1)}) custom-call(bf16[128,1152]{1,0:T(8,128)(2,1)S(1)} %copy-done.2, bf16[128,1152]{1,0:T(8,128)(2,1)S(1)} %collective-permute-done.5.refs_1_, bf16[128,1152]{1,0:T(8,128)(2,1)S(1)} %collective-permute-done.6.refs_2_, ...), custom_call_target="tpu_custom_call" | custom-call | flops 600000000 | bytes 4000000 | tf_op jit(solution)/shard_map/pallas_call | solution.py:510
  49.1 1.6 %collective-permute-done.16.got_ref = bf16[4,80,512]{2,1,0:T(8,128)(2,1)S(1)} collective-permute-done((bf16[4,80,512]{2,1,0:T(8,128)(2,1)S(1)}, bf16[4,80,512]{2,1,0:T(8,128)(2,1)S(1)}, u32[]{:S(2)}, u32[]{:S(2)}) %collective-permute-start.16) | collective-permute-done | bytes 327712 | tf_op jit(solution)/shard_map/ppermute | solution.py:677
  51.3 1.7 %collective-permute-start.25 = (bf16[80,256]{1,0:T(8,128)(2,1)S(1)}, bf16[80,256]{1,0:T(8,128)(2,1)S(1)}, u32[]{:S(2)}, u32[]{:S(2)}) collective-permute-start(bf16[80,256]{1,0:T(8,128)(2,1)S(1)} %get-tuple-element.83), channel_id=1, source_target_pairs={{0,4},{1,5},{2,6},{3,7},{4,0},{5,1},{6,2},{7,3},{8,12},{9,13},{10,... | collective-permute-start | bytes 122888 | tf_op jit(solution)/shard_map/ppermute | solution.py:677
  53.0 2.2 %collective-permute-start.26 = (bf16[80,256]{1,0:T(8,128)(2,1)S(1)}, bf16[80,256]{1,0:T(8,128)(2,1)S(1)}, u32[]{:S(2)}, u32[]{:S(2)}) collective-permute-start(bf16[80,256]{1,0:T(8,128)(2,1)S(1)} %get-tuple-element.84), channel_id=1, source_target_pairs={{0,6},{1,7},{2,4},{3,5},{4,2},{5,3},{6,0},{7,1},{8,14},{9,15},{10,... | collective-permute-start | bytes 122888 | tf_op jit(solution)/shard_map/ppermute | solution.py:677
  55.2 2.2 %collective-permute-start.18 = (bf16[80,256]{1,0:T(8,128)(2,1)S(1)}, bf16[80,256]{1,0:T(8,128)(2,1)S(1)}, u32[]{:S(2)}, u32[]{:S(2)}) collective-permute-start(bf16[80,256]{1,0:T(8,128)(2,1)S(1)} %get-tuple-element.79), channel_id=1, source_target_pairs={{0,4},{1,5},{2,6},{3,7},{4,0},{5,1},{6,2},{7,3},{8,12},{9,13},{10,... | collective-permute-start | bytes 122888 | tf_op jit(solution)/shard_map/ppermute | solution.py:677
  57.4 2.2 %collective-permute-start.19 = (bf16[80,256]{1,0:T(8,128)(2,1)S(1)}, bf16[80,256]{1,0:T(8,128)(2,1)S(1)}, u32[]{:S(2)}, u32[]{:S(2)}) collective-permute-start(bf16[80,256]{1,0:T(8,128)(2,1)S(1)} %get-tuple-element.80), channel_id=1, source_target_pairs={{0,6},{1,7},{2,4},{3,5},{4,2},{5,3},{6,0},{7,1},{8,14},{9,15},{10,... | collective-permute-start | bytes 122888 | tf_op jit(solution)/shard_map/ppermute | solution.py:677
  59.6 1.7 %collective-permute-start.29 = (bf16[80,256]{1,0:T(8,128)(2,1)S(1)}, bf16[80,256]{1,0:T(8,128)(2,1)S(1)}, u32[]{:S(2)}, u32[]{:S(2)}) collective-permute-start(bf16[80,256]{1,0:T(8,128)(2,1)S(1)} %shard_map.114.refs_0_), channel_id=1, source_target_pairs={{0,6},{1,7},{2,4},{3,5},{4,2},{5,3},{6,0},{7,1},{8,14},{9,15},{10,... | collective-permute-start | bytes 122888 | tf_op jit(solution)/shard_map/ppermute | solution.py:677
  61.3 2.8 %collective-permute-start.27 = (bf16[80,256]{1,0:T(8,128)(2,1)S(1)}, bf16[80,256]{1,0:T(8,128)(2,1)S(1)}, u32[]{:S(2)}, u32[]{:S(2)}) collective-permute-start(bf16[80,256]{1,0:T(8,128)(2,1)S(1)} %shard_map.114.refs_0_), channel_id=1, source_target_pairs={{0,2},{1,3},{2,0},{3,1},{4,6},{5,7},{6,4},{7,5},{8,10},{9,11},{10,... | collective-permute-start | bytes 122888 | tf_op jit(solution)/shard_map/ppermute | solution.py:677
  64.1 1.8 %collective-permute-start.22 = (bf16[80,256]{1,0:T(8,128)(2,1)S(1)}, bf16[80,256]{1,0:T(8,128)(2,1)S(1)}, u32[]{:S(2)}, u32[]{:S(2)}) collective-permute-start(bf16[80,256]{1,0:T(8,128)(2,1)S(1)} %shard_map.112.refs_0_), channel_id=1, source_target_pairs={{0,6},{1,7},{2,4},{3,5},{4,2},{5,3},{6,0},{7,1},{8,14},{9,15},{10,... | collective-permute-start | bytes 122888 | tf_op jit(solution)/shard_map/ppermute | solution.py:677
  65.9 2.7 %collective-permute-start.20 = (bf16[80,256]{1,0:T(8,128)(2,1)S(1)}, bf16[80,256]{1,0:T(8,128)(2,1)S(1)}, u32[]{:S(2)}, u32[]{:S(2)}) collective-permute-start(bf16[80,256]{1,0:T(8,128)(2,1)S(1)} %shard_map.112.refs_0_), channel_id=1, source_target_pairs={{0,2},{1,3},{2,0},{3,1},{4,6},{5,7},{6,4},{7,5},{8,10},{9,11},{10,... | collective-permute-start | bytes 122888 | tf_op jit(solution)/shard_map/ppermute | solution.py:677
  72.8 1.4 %collective-permute-done.37.refs_2_.refs_10_ = bf16[320,256]{1,0:T(8,128)(2,1)S(1)} collective-permute-done((bf16[320,256]{1,0:T(8,128)(2,1)S(1)}, bf16[320,256]{1,0:T(8,128)(2,1)S(1)}, u32[]{:S(2)}, u32[]{:S(2)}) %collective-permute-start.37) | collective-permute-done | bytes 163872 | tf_op jit(solution)/shard_map/ppermute | solution.py:677
  76.4 1.4 %collective-permute-start.39 = (bf16[320,256]{1,0:T(8,128)(2,1)S(1)}, bf16[320,256]{1,0:T(8,128)(2,1)S(1)}, u32[]{:S(2)}, u32[]{:S(2)}) collective-permute-start(bf16[320,256]{1,0:T(8,128)(2,1)S(1)} %collective-permute-done.31.refs_0_.refs_4_), channel_id=1, source_target_pairs={{0,16},{8,24},{16,0},{24,8},{1,17},{9,25},{17,1},{25,9},{2,18},{10... | collective-permute-start | bytes 491528 | tf_op jit(solution)/shard_map/ppermute | solution.py:677
  78.4 2.5 %collective-permute-done.41.refs_14_ = bf16[320,256]{1,0:T(8,128)(2,1)S(1)} collective-permute-done((bf16[320,256]{1,0:T(8,128)(2,1)S(1)}, bf16[320,256]{1,0:T(8,128)(2,1)S(1)}, u32[]{:S(2)}, u32[]{:S(2)}) %collective-permute-start.41) | collective-permute-done | bytes 163872 | tf_op jit(solution)/shard_map/ppermute | solution.py:677
  82.6 1.4 %shard_map.116 = (f32[2048,512]{1,0:T(8,128)}, f32[512,128]{1,0:T(8,128)}) custom-call(bf16[320,256]{1,0:T(8,128)(2,1)S(1)} %shard_map.113.refs_0_, bf16[320,256]{1,0:T(8,128)(2,1)S(1)} %collective-permute-done.23.refs_1_, bf16[320,256]{1,0:T(8,128)(2,1)S(1)} %shard_map.115.refs_2_, bf16[320,256]{1,0:T(8,128)(2,1)S(1)} %collective-permute-done.30.refs_3_), custom_call_target="tpu_custom_call" | custom-call | flops 1000000 | bytes 8000000 | tf_op jit(solution)/shard_map/pallas_call | solution.py:638
  84.0 1.5 %shard_map.117 = (f32[2048,512]{1,0:T(8,128)}, f32[512,128]{1,0:T(8,128)}) custom-call(bf16[320,256]{1,0:T(8,128)(2,1)S(1)} %collective-permute-done.31.refs_0_.refs_4_, bf16[320,256]{1,0:T(8,128)(2,1)S(1)} %collective-permute-done.32.refs_1_.refs_5_, ...), custom_call_target="tpu_custom_call", output_to_operand_aliasing={{0}: (4, {}), {1}: (5, {})} | custom-call | flops 1000000 | bytes 8000000 | tf_op jit(solution)/shard_map/pallas_call | solution.py:638
  85.5 1.4 %shard_map.118 = (f32[2048,512]{1,0:T(8,128)}, f32[512,128]{1,0:T(8,128)}) custom-call(bf16[320,256]{1,0:T(8,128)(2,1)S(1)} %collective-permute-done.35.refs_0_.refs_8_, bf16[320,256]{1,0:T(8,128)(2,1)S(1)} %collective-permute-done.36.refs_1_.refs_9_, ...), custom_call_target="tpu_custom_call", output_to_operand_aliasing={{0}: (4, {}), {1}: (5, {})} | custom-call | flops 1000000 | bytes 8000000 | tf_op jit(solution)/shard_map/pallas_call | solution.py:638
  88.0 1.2 %shard_map.120 = (f32[2048,512]{1,0:T(8,128)}, f32[512,128]{1,0:T(8,128)}, f32[256,128]{1,0:T(8,128)}) custom-call(bf16[320,256]{1,0:T(8,128)(2,1)S(1)} %shard_map.113.refs_0_, bf16[320,256]{1,0:T(8,128)(2,1)S(1)} %collective-permute-done.23.refs_1_, bf16[320,256]{1,0:T(8,128)(2,1)S(1)} %shard_map.115.refs_2_, ...), custom_call_target="tpu_custom_call", output_to_operand_aliasing={{0}: (16, {}), {1}: (17, {})} | custom-call | flops 1000000 | bytes 8000000 | tf_op jit(solution)/shard_map/pallas_call | solution.py:638
  (79 shorter events, 17.8 us)
Async XLA Ops:
  9.5 7.3 %collective-permute-start.3 = (bf16[256,128]{1,0:T(8,128)(2,1)S(1)}, bf16[256,128]{1,0:T(8,128)(2,1)S(1)}, u32[]{:S(2)}, u32[]{:S(2)}) collective-permute-start(bf16[256,128]{1,0:T(8,128)(2,1)S(1)} %shard_map.103.pair_ref), channel_id=1, source_target_pairs={{0,6},{1,25},{2,4},{3,27},{4,2},{5,29},{6,0},{7,31},{8,14},{9,17},... | collective-permute-start | bytes 196616 | tf_op jit(solution)/shard_map/ppermute | solution.py:251
  14.5 5.2 %collective-permute-start.2 = (bf16[256,128]{1,0:T(8,128)(2,1)S(1)}, bf16[256,128]{1,0:T(8,128)(2,1)S(1)}, u32[]{:S(2)}, u32[]{:S(2)}) collective-permute-start(bf16[256,128]{1,0:T(8,128)(2,1)S(1)} %shard_map.103.pair_ref), channel_id=1, source_target_pairs={{0,4},{1,17},{2,6},{3,19},{4,0},{5,21},{6,2},{7,23},{8,12},{9,25},... | collective-permute-start | bytes 196616 | tf_op jit(solution)/shard_map/ppermute | solution.py:251
  14.5 5.2 %collective-permute-start.1 = (bf16[256,128]{1,0:T(8,128)(2,1)S(1)}, bf16[256,128]{1,0:T(8,128)(2,1)S(1)}, u32[]{:S(2)}, u32[]{:S(2)}) collective-permute-start(bf16[256,128]{1,0:T(8,128)(2,1)S(1)} %shard_map.103.pair_ref), channel_id=1, source_target_pairs={{0,2},{1,9},{2,0},{3,11},{4,6},{5,13},{6,4},{7,15},{8,10},{9,1},{1... | collective-permute-start | bytes 196616 | tf_op jit(solution)/shard_map/ppermute | solution.py:251
  19.7 23.8 %collective-permute-start.5 = (bf16[128,1152]{1,0:T(8,128)(2,1)}, bf16[128,1152]{1,0:T(8,128)(2,1)S(1)}, u32[]{:S(2)}, u32[]{:S(2)}) collective-permute-start(bf16[128,1152]{1,0:T(8,128)(2,1)} %get-tuple-element.56), channel_id=1, source_target_pairs={{0,8},{8,0},{16,24},{24,16},{1,9},{9,1},{17,25},{25,17},{2,10},{10... | collective-permute-start | bytes 884744 | tf_op jit(solution)/shard_map/ppermute | solution.py:677
  21.3 24.9 %collective-permute-start.6 = (bf16[128,1152]{1,0:T(8,128)(2,1)}, bf16[128,1152]{1,0:T(8,128)(2,1)S(1)}, u32[]{:S(2)}, u32[]{:S(2)}) collective-permute-start(bf16[128,1152]{1,0:T(8,128)(2,1)} %get-tuple-element.57), channel_id=1, source_target_pairs={{0,16},{8,24},{16,0},{24,8},{1,17},{9,25},{17,1},{25,9},{2,18},{10... | collective-permute-start | bytes 884744 | tf_op jit(solution)/shard_map/ppermute | solution.py:677
  22.8 23.4 %collective-permute-start.7 = (bf16[128,1152]{1,0:T(8,128)(2,1)}, bf16[128,1152]{1,0:T(8,128)(2,1)S(1)}, u32[]{:S(2)}, u32[]{:S(2)}) collective-permute-start(bf16[128,1152]{1,0:T(8,128)(2,1)} %get-tuple-element.58), channel_id=1, source_target_pairs={{0,24},{8,16},{16,8},{24,0},{1,25},{9,17},{17,9},{25,1},{2,26},{10... | collective-permute-start | bytes 884744 | tf_op jit(solution)/shard_map/ppermute | solution.py:677
  25.8 5.4 %collective-permute-start.11 = (f32[16,128]{1,0:T(8,128)S(1)}, f32[16,128]{1,0:T(8,128)S(1)}, u32[]{:S(2)}, u32[]{:S(2)}) collective-permute-start(f32[16,128]{1,0:T(8,128)S(1)} %shard_map.106.pair_ref), channel_id=1, source_target_pairs={{0,6},{1,25},{2,4},{3,27},{4,2},{5,29},{6,0},{7,31},{8,14},{9,17},... | collective-permute-start | bytes 24584 | tf_op jit(solution)/shard_map/ppermute | solution.py:251
  34.9 4.9 %collective-permute-start.12 = (f32[48,128]{1,0:T(8,128)S(1)}, f32[48,128]{1,0:T(8,128)S(1)}, u32[]{:S(2)}, u32[]{:S(2)}) collective-permute-start(f32[48,128]{1,0:T(8,128)S(1)} %shard_map.107.got_ref), channel_id=1, source_target_pairs={{0,1},{1,0},{2,3},{3,2},{4,5},{5,4},{6,7},{7,6},{8,9},{9,8},{10,11... | collective-permute-start | bytes 73736 | tf_op jit(solution)/shard_map/ppermute | solution.py:677
  40.6 5.7 %collective-permute-start.15 = (bf16[128,128]{1,0:T(8,128)(2,1)S(1)}, bf16[128,128]{1,0:T(8,128)(2,1)S(1)}, u32[]{:S(2)}, u32[]{:S(2)}) collective-permute-start(bf16[128,128]{1,0:T(8,128)(2,1)S(1)} %shard_map.108.raw_ref.refs_4_), channel_id=1, source_target_pairs={{0,24},{8,16},{16,8},{24,0},{1,25},{9,17},{17,9},{25,1},{2,26},{10... | collective-permute-start | bytes 98312 | tf_op jit(solution)/shard_map/ppermute | solution.py:677
  50.7 6.6 %collective-permute-start.24 = (bf16[80,256]{1,0:T(8,128)(2,1)S(1)}, bf16[80,256]{1,0:T(8,128)(2,1)S(1)}, u32[]{:S(2)}, u32[]{:S(2)}) collective-permute-start(bf16[80,256]{1,0:T(8,128)(2,1)S(1)} %get-tuple-element.82), channel_id=1, source_target_pairs={{0,2},{1,3},{2,0},{3,1},{4,6},{5,7},{6,4},{7,5},{8,10},{9,11},{10,... | collective-permute-start | bytes 122888 | tf_op jit(solution)/shard_map/ppermute | solution.py:677
  51.3 8.3 %collective-permute-start.25 = (bf16[80,256]{1,0:T(8,128)(2,1)S(1)}, bf16[80,256]{1,0:T(8,128)(2,1)S(1)}, u32[]{:S(2)}, u32[]{:S(2)}) collective-permute-start(bf16[80,256]{1,0:T(8,128)(2,1)S(1)} %get-tuple-element.83), channel_id=1, source_target_pairs={{0,4},{1,5},{2,6},{3,7},{4,0},{5,1},{6,2},{7,3},{8,12},{9,13},{10,... | collective-permute-start | bytes 122888 | tf_op jit(solution)/shard_map/ppermute | solution.py:677
  53.0 6.6 %collective-permute-start.26 = (bf16[80,256]{1,0:T(8,128)(2,1)S(1)}, bf16[80,256]{1,0:T(8,128)(2,1)S(1)}, u32[]{:S(2)}, u32[]{:S(2)}) collective-permute-start(bf16[80,256]{1,0:T(8,128)(2,1)S(1)} %get-tuple-element.84), channel_id=1, source_target_pairs={{0,6},{1,7},{2,4},{3,5},{4,2},{5,3},{6,0},{7,1},{8,14},{9,15},{10,... | collective-permute-start | bytes 122888 | tf_op jit(solution)/shard_map/ppermute | solution.py:677
  55.2 6.1 %collective-permute-start.17 = (bf16[80,256]{1,0:T(8,128)(2,1)S(1)}, bf16[80,256]{1,0:T(8,128)(2,1)S(1)}, u32[]{:S(2)}, u32[]{:S(2)}) collective-permute-start(bf16[80,256]{1,0:T(8,128)(2,1)S(1)} %get-tuple-element.78), channel_id=1, source_target_pairs={{0,2},{1,3},{2,0},{3,1},{4,6},{5,7},{6,4},{7,5},{8,10},{9,11},{10,... | collective-permute-start | bytes 122888 | tf_op jit(solution)/shard_map/ppermute | solution.py:677
  55.2 8.9 %collective-permute-start.18 = (bf16[80,256]{1,0:T(8,128)(2,1)S(1)}, bf16[80,256]{1,0:T(8,128)(2,1)S(1)}, u32[]{:S(2)}, u32[]{:S(2)}) collective-permute-start(bf16[80,256]{1,0:T(8,128)(2,1)S(1)} %get-tuple-element.79), channel_id=1, source_target_pairs={{0,4},{1,5},{2,6},{3,7},{4,0},{5,1},{6,2},{7,3},{8,12},{9,13},{10,... | collective-permute-start | bytes 122888 | tf_op jit(solution)/shard_map/ppermute | solution.py:677
  57.4 6.7 %collective-permute-start.19 = (bf16[80,256]{1,0:T(8,128)(2,1)S(1)}, bf16[80,256]{1,0:T(8,128)(2,1)S(1)}, u32[]{:S(2)}, u32[]{:S(2)}) collective-permute-start(bf16[80,256]{1,0:T(8,128)(2,1)S(1)} %get-tuple-element.80), channel_id=1, source_target_pairs={{0,6},{1,7},{2,4},{3,5},{4,2},{5,3},{6,0},{7,1},{8,14},{9,15},{10,... | collective-permute-start | bytes 122888 | tf_op jit(solution)/shard_map/ppermute | solution.py:677
  59.6 6.3 %collective-permute-start.29 = (bf16[80,256]{1,0:T(8,128)(2,1)S(1)}, bf16[80,256]{1,0:T(8,128)(2,1)S(1)}, u32[]{:S(2)}, u32[]{:S(2)}) collective-permute-start(bf16[80,256]{1,0:T(8,128)(2,1)S(1)} %shard_map.114.refs_0_), channel_id=1, source_target_pairs={{0,6},{1,7},{2,4},{3,5},{4,2},{5,3},{6,0},{7,1},{8,14},{9,15},{10,... | collective-permute-start | bytes 122888 | tf_op jit(solution)/shard_map/ppermute | solution.py:677
  61.3 7.3 %collective-permute-start.28 = (bf16[80,256]{1,0:T(8,128)(2,1)S(1)}, bf16[80,256]{1,0:T(8,128)(2,1)S(1)}, u32[]{:S(2)}, u32[]{:S(2)}) collective-permute-start(bf16[80,256]{1,0:T(8,128)(2,1)S(1)} %shard_map.114.refs_0_), channel_id=1, source_target_pairs={{0,4},{1,5},{2,6},{3,7},{4,0},{5,1},{6,2},{7,3},{8,12},{9,13},{10,... | collective-permute-start | bytes 122888 | tf_op jit(solution)/shard_map/ppermute | solution.py:677
  61.3 7.3 %collective-permute-start.27 = (bf16[80,256]{1,0:T(8,128)(2,1)S(1)}, bf16[80,256]{1,0:T(8,128)(2,1)S(1)}, u32[]{:S(2)}, u32[]{:S(2)}) collective-permute-start(bf16[80,256]{1,0:T(8,128)(2,1)S(1)} %shard_map.114.refs_0_), channel_id=1, source_target_pairs={{0,2},{1,3},{2,0},{3,1},{4,6},{5,7},{6,4},{7,5},{8,10},{9,11},{10,... | collective-permute-start | bytes 122888 | tf_op jit(solution)/shard_map/ppermute | solution.py:677
  64.1 5.9 %collective-permute-start.22 = (bf16[80,256]{1,0:T(8,128)(2,1)S(1)}, bf16[80,256]{1,0:T(8,128)(2,1)S(1)}, u32[]{:S(2)}, u32[]{:S(2)}) collective-permute-start(bf16[80,256]{1,0:T(8,128)(2,1)S(1)} %shard_map.112.refs_0_), channel_id=1, source_target_pairs={{0,6},{1,7},{2,4},{3,5},{4,2},{5,3},{6,0},{7,1},{8,14},{9,15},{10,... | collective-permute-start | bytes 122888 | tf_op jit(solution)/shard_map/ppermute | solution.py:677
  65.9 5.1 %collective-permute-start.21 = (bf16[80,256]{1,0:T(8,128)(2,1)S(1)}, bf16[80,256]{1,0:T(8,128)(2,1)S(1)}, u32[]{:S(2)}, u32[]{:S(2)}) collective-permute-start(bf16[80,256]{1,0:T(8,128)(2,1)S(1)} %shard_map.112.refs_0_), channel_id=1, source_target_pairs={{0,4},{1,5},{2,6},{3,7},{4,0},{5,1},{6,2},{7,3},{8,12},{9,13},{10,... | collective-permute-start | bytes 122888 | tf_op jit(solution)/shard_map/ppermute | solution.py:677
  65.9 5.1 %collective-permute-start.20 = (bf16[80,256]{1,0:T(8,128)(2,1)S(1)}, bf16[80,256]{1,0:T(8,128)(2,1)S(1)}, u32[]{:S(2)}, u32[]{:S(2)}) collective-permute-start(bf16[80,256]{1,0:T(8,128)(2,1)S(1)} %shard_map.112.refs_0_), channel_id=1, source_target_pairs={{0,2},{1,3},{2,0},{3,1},{4,6},{5,7},{6,4},{7,5},{8,10},{9,11},{10,... | collective-permute-start | bytes 122888 | tf_op jit(solution)/shard_map/ppermute | solution.py:677
  68.6 5.7 %collective-permute-start.37 = (bf16[320,256]{1,0:T(8,128)(2,1)S(1)}, bf16[320,256]{1,0:T(8,128)(2,1)S(1)}, u32[]{:S(2)}, u32[]{:S(2)}) collective-permute-start(bf16[320,256]{1,0:T(8,128)(2,1)S(1)} %shard_map.115.refs_2_), channel_id=1, source_target_pairs={{0,16},{8,24},{16,0},{24,8},{1,17},{9,25},{17,1},{25,9},{2,18},{10... | collective-permute-start | bytes 491528 | tf_op jit(solution)/shard_map/ppermute | solution.py:677
  69.2 5.3 %collective-permute-start.35 = (bf16[320,256]{1,0:T(8,128)(2,1)S(1)}, bf16[320,256]{1,0:T(8,128)(2,1)S(1)}, u32[]{:S(2)}, u32[]{:S(2)}) collective-permute-start(bf16[320,256]{1,0:T(8,128)(2,1)S(1)} %shard_map.115.refs_2_), channel_id=1, source_target_pairs={{0,8},{8,0},{16,24},{24,16},{1,9},{9,1},{17,25},{25,17},{2,10},{10... | collective-permute-start | bytes 491528 | tf_op jit(solution)/shard_map/ppermute | solution.py:677
  71.0 5.4 %collective-permute-start.31 = (bf16[320,256]{1,0:T(8,128)(2,1)S(1)}, bf16[320,256]{1,0:T(8,128)(2,1)S(1)}, u32[]{:S(2)}, u32[]{:S(2)}) collective-permute-start(bf16[320,256]{1,0:T(8,128)(2,1)S(1)} %shard_map.113.refs_0_), channel_id=1, source_target_pairs={{0,8},{8,0},{16,24},{24,16},{1,9},{9,1},{17,25},{25,17},{2,10},{10... | collective-permute-start | bytes 491528 | tf_op jit(solution)/shard_map/ppermute | solution.py:677
  71.7 6.1 %collective-permute-start.33 = (bf16[320,256]{1,0:T(8,128)(2,1)S(1)}, bf16[320,256]{1,0:T(8,128)(2,1)S(1)}, u32[]{:S(2)}, u32[]{:S(2)}) collective-permute-start(bf16[320,256]{1,0:T(8,128)(2,1)S(1)} %shard_map.113.refs_0_), channel_id=1, source_target_pairs={{0,16},{8,24},{16,0},{24,8},{1,17},{9,25},{17,1},{25,9},{2,18},{10... | collective-permute-start | bytes 491528 | tf_op jit(solution)/shard_map/ppermute | solution.py:677
  72.8 5.0 %collective-permute-start.30 = (bf16[320,256]{1,0:T(8,128)(2,1)S(1)}, bf16[320,256]{1,0:T(8,128)(2,1)S(1)}, u32[]{:S(2)}, u32[]{:S(2)}) collective-permute-start(bf16[320,256]{1,0:T(8,128)(2,1)S(1)} %shard_map.115.refs_2_), channel_id=1, source_target_pairs={{0,1},{1,0},{2,3},{3,2},{4,5},{5,4},{6,7},{7,6},{8,9},{9,8},{10,11... | collective-permute-start | bytes 491528 | tf_op jit(solution)/shard_map/ppermute | solution.py:677
  74.5 6.3 %collective-permute-start.41 = (bf16[320,256]{1,0:T(8,128)(2,1)S(1)}, bf16[320,256]{1,0:T(8,128)(2,1)S(1)}, u32[]{:S(2)}, u32[]{:S(2)}) collective-permute-start(bf16[320,256]{1,0:T(8,128)(2,1)S(1)} %collective-permute-done.37.refs_2_.refs_10_), channel_id=1, source_target_pairs={{0,8},{8,0},{16,24},{24,16},{1,9},{9,1},{17,25},{25,17},{2,10},{10... | collective-permute-start | bytes 491528 | tf_op jit(solution)/shard_map/ppermute | solution.py:677
  76.4 5.7 %collective-permute-start.39 = (bf16[320,256]{1,0:T(8,128)(2,1)S(1)}, bf16[320,256]{1,0:T(8,128)(2,1)S(1)}, u32[]{:S(2)}, u32[]{:S(2)}) collective-permute-start(bf16[320,256]{1,0:T(8,128)(2,1)S(1)} %collective-permute-done.31.refs_0_.refs_4_), channel_id=1, source_target_pairs={{0,16},{8,24},{16,0},{24,8},{1,17},{9,25},{17,1},{25,9},{2,18},{10... | collective-permute-start | bytes 491528 | tf_op jit(solution)/shard_map/ppermute | solution.py:677
  77.8 6.2 %collective-permute-start.32 = (bf16[320,256]{1,0:T(8,128)(2,1)S(1)}, bf16[320,256]{1,0:T(8,128)(2,1)S(1)}, u32[]{:S(2)}, u32[]{:S(2)}) collective-permute-start(bf16[320,256]{1,0:T(8,128)(2,1)S(1)} %collective-permute-done.31.refs_0_.refs_4_), channel_id=1, source_target_pairs={{0,1},{1,0},{2,3},{3,2},{4,5},{5,4},{6,7},{7,6},{8,9},{9,8},{10,11... | collective-permute-start | bytes 491528 | tf_op jit(solution)/shard_map/ppermute | solution.py:677
  78.3 7.2 %collective-permute-start.38 = (bf16[320,256]{1,0:T(8,128)(2,1)S(1)}, bf16[320,256]{1,0:T(8,128)(2,1)S(1)}, u32[]{:S(2)}, u32[]{:S(2)}) collective-permute-start(bf16[320,256]{1,0:T(8,128)(2,1)S(1)} %collective-permute-done.37.refs_2_.refs_10_), channel_id=1, source_target_pairs={{0,1},{1,0},{2,3},{3,2},{4,5},{5,4},{6,7},{7,6},{8,9},{9,8},{10,11... | collective-permute-start | bytes 491528 | tf_op jit(solution)/shard_map/ppermute | solution.py:677
  82.0 4.8 %collective-permute-start.40 = (bf16[320,256]{1,0:T(8,128)(2,1)S(1)}, bf16[320,256]{1,0:T(8,128)(2,1)S(1)}, u32[]{:S(2)}, u32[]{:S(2)}) collective-permute-start(bf16[320,256]{1,0:T(8,128)(2,1)S(1)} %collective-permute-done.39.refs_0_.refs_12_), channel_id=1, source_target_pairs={{0,1},{1,0},{2,3},{3,2},{4,5},{5,4},{6,7},{7,6},{8,9},{9,8},{10,11... | collective-permute-start | bytes 491528 | tf_op jit(solution)/shard_map/ppermute | solution.py:677
  82.1 6.0 %collective-permute-start.42 = (bf16[320,256]{1,0:T(8,128)(2,1)S(1)}, bf16[320,256]{1,0:T(8,128)(2,1)S(1)}, u32[]{:S(2)}, u32[]{:S(2)}) collective-permute-start(bf16[320,256]{1,0:T(8,128)(2,1)S(1)} %collective-permute-done.41.refs_14_), channel_id=1, source_target_pairs={{0,1},{1,0},{2,3},{3,2},{4,5},{5,4},{6,7},{7,6},{8,9},{9,8},{10,11... | collective-permute-start | bytes 491528 | tf_op jit(solution)/shard_map/ppermute | solution.py:677
  (14 other events, 90.1 us)
